TPU v7x, 32 devices: a whole 2x2x4 slice. The times are simulated.
32 devices in a mesh: ctx: 8 (over z, core), fsdp: 4 (over y, x).
Axes of the slice: x: 2, y: 2, z: 4, core: 2. Of those that a mesh axis runs over, the one named last changes fastest.
Arguments:
- tokens: bfloat16 [4, 1024, 2048], P('fsdp', 'ctx'), may hold values from -6 to 6
- cotangent: bfloat16 [4, 1024, 2048], P('fsdp', 'ctx'), may hold values from -6 to 6
- doc_ids: int32 [4, 1024], P('fsdp'), may hold values from 0 to 3, never falling along the last dimension, each value on 1 to 512 neighbouring positions
- block_order: int32 [16], replicated, may hold values from 0 to 15, each once
- front_weight: bfloat16 [2048, 14336], P(None, 'fsdp'), may hold values from -0.125 to 0.125
- back_weight: bfloat16 [10240, 2048], P(None, 'fsdp'), may hold values from -2 to 2
- front_master: float32 [2048, 14336], P('ctx', 'fsdp'), may hold values from -0.125 to 0.125
- back_master: float32 [10240, 2048], P('ctx', 'fsdp'), may hold values from -0.0625 to 0.0625
- front_first: float32 [2048, 14336], P('ctx', 'fsdp'), may hold values from -64 to 64
- back_first: float32 [10240, 2048], P('ctx', 'fsdp'), may hold values from -64 to 64
- front_second: float32 [2048, 14336], P('ctx', 'fsdp'), may hold values from 100 to 10000
- back_second: float32 [10240, 2048], P('ctx', 'fsdp'), may hold values from 2.048 to 204.8
- vectors: float32 [20480], replicated, may hold values from -2 to 2
- vector_first: float32 [20480], replicated, may hold values from -64 to 64
- vector_second: float32 [20480], replicated, may hold values from 100 to 10000
- learn_rates: float32 [3], replicated, may hold values from 0.02 to 0.2
- adam_step: int32 [1], replicated, may hold values from 1 to 8
Outputs:
- layer_out: bfloat16 [4, 1024, 2048], P('fsdp', 'ctx')
- tokens_grad: bfloat16 [4, 1024, 2048], P('fsdp', 'ctx')
- front_grad: float32 [2048, 14336], P('ctx', 'fsdp')
- back_grad: float32 [10240, 2048], P('ctx', 'fsdp')
- vector_grad: float32 [20480], replicated
- front_new: float32 [2048, 14336], P('ctx', 'fsdp')
- back_new: float32 [10240, 2048], P('ctx', 'fsdp')
- vectors_new: float32 [20480], replicated
- front_first_new: float32 [2048, 14336], P('ctx', 'fsdp')
- back_first_new: float32 [10240, 2048], P('ctx', 'fsdp')
- vector_first_new: float32 [20480], replicated
- front_second_new: float32 [2048, 14336], P('ctx', 'fsdp')
- back_second_new: float32 [10240, 2048], P('ctx', 'fsdp')
- vector_second_new: float32 [20480], replicated
- front_next: bfloat16 [2048, 14336], P(None, 'fsdp')
- back_next: bfloat16 [10240, 2048], P(None, 'fsdp')
Inputs may be any that keep to these rules, and one draw needn't show every extreme that they name: `doc_ids`: within a sequence document numbers never fall; a document has 1 to 512 tokens, and one has exactly 512. `block_order`: A permutation of the block numbers.
All inputs are finite; a program needn't handle non-finite values.
Results may differ from a plain program's by a relative error of at most 0.02.
Values may be sent and summed in bfloat16 or wider, within the bound.
A program may use at most 512 MiB of HBM per device.

v0:
```python
import jax
import jax.numpy as jnp
from jax import lax
from jax.sharding import PartitionSpec as P

D = 2048
HEADS = 32
ROT = 32
HEAD_DIM = 64
IN_COLS = 14336


norm_eps = 1e-05
beta_first = 0.9
beta_second = 0.95
adam_eps = 1e-08
weight_decay = 0.1
masked_score = -1e30


def key_block(amount):
    for candidate in (512, 256, 128):
        return candidate
    return amount


def rotary_tables(positions):
    half_rot = ROT // 2
    frequency = jnp.power(10000.0, -2.0 * jnp.arange(half_rot, dtype=jnp.float32) / ROT)
    angles = positions.astype(jnp.float32)[:, None] * frequency[None, :]
    return (jnp.cos(angles), jnp.sin(angles))


def rotate(values, cosine, sine):
    half_rot = ROT // 2
    lower_half = values[..., :half_rot]
    upper_half = values[..., half_rot:ROT]
    cos_full = cosine[:, None, :]
    sin_full = sine[:, None, :]
    return jnp.concatenate(
        [
            lower_half * cos_full - upper_half * sin_full,
            upper_half * cos_full + lower_half * sin_full,
            values[..., ROT:],
        ],
        axis=-1,
    )


def layer_norm(values, norm_gain, norm_shift):
    row_mean = jnp.mean(values, axis=-1, keepdims=True)
    centered = values - row_mean
    variance = jnp.mean(centered * centered, axis=-1, keepdims=True)
    return centered * lax.rsqrt(variance + norm_eps) * norm_gain + norm_shift


def gelu_tanh(values):
    return jax.nn.gelu(values, approximate=True)


def stored_layout(doc_row, block_order):
    block_count = block_order.shape[0]
    block_tokens = doc_row.shape[0] // block_count
    offsets = jnp.arange(block_tokens, dtype=jnp.int32)
    positions = (block_order[:, None] * block_tokens + offsets[None, :]).reshape(-1)
    segments = jnp.take(doc_row.reshape(block_count, block_tokens), block_order, axis=0).reshape(-1)
    return (positions, segments)


def adam_update(weight, first, second, grad, rate, count_now, decay):
    first_new = beta_first * first + (1.0 - beta_first) * grad
    second_new = beta_second * second + (1.0 - beta_second) * grad * grad
    steps_float = count_now.astype(jnp.float32)
    first_fix = 1.0 - jnp.power(beta_first, steps_float)
    second_fix = 1.0 - jnp.power(beta_second, steps_float)
    change = first_new / first_fix / (jnp.sqrt(second_new / second_fix) + adam_eps) + decay * weight
    return (weight - rate * change, first_new, second_new)


def per_device(
    tokens,
    cotangent,
    doc_ids,
    block_order,
    front_weight,
    back_weight,
    front_master,
    back_master,
    front_first,
    back_first,
    front_second,
    back_second,
    vectors,
    vector_first,
    vector_second,
    learn_rates,
    adam_step,
):
    local_rows = tokens.shape[1]
    score_scale = HEAD_DIM ** (-0.5)
    contract_last = (((1,), (1,)), ((), ()))
    contract_first = (((0,), (0,)), ((), ()))
    bias_front = vectors[:IN_COLS]
    bias_back = vectors[IN_COLS : IN_COLS + D]
    norm_gain = vectors[IN_COLS + D : IN_COLS + 2 * D]
    norm_shift = vectors[IN_COLS + 2 * D :]
    positions_all, segments_all = stored_layout(doc_ids[0], block_order)
    seq_len = positions_all.shape[0]
    first_row = lax.axis_index("ctx") * local_rows
    query_pos = lax.dynamic_slice_in_dim(positions_all, first_row, local_rows)
    query_seg = lax.dynamic_slice_in_dim(segments_all, first_row, local_rows)
    inputs = tokens[0].astype(jnp.float32)
    normed, norm_pull = jax.vjp(layer_norm, inputs, norm_gain, norm_shift)
    normed_low = normed.astype(jnp.bfloat16)
    hidden = (
        jnp.dot(
            normed_low,
            lax.all_gather(front_weight, "fsdp", axis=1, tiled=True),
            preferred_element_type=jnp.float32,
        )
        + bias_front
    )
    cosine, sine = rotary_tables(query_pos)

    def rotate_pair(query_raw, key_raw):
        return (rotate(query_raw, cosine, sine), rotate(key_raw, cosine, sine))

    shaped = (local_rows, HEADS, HEAD_DIM)
    (query_rot, key_rot), rotary_pull = jax.vjp(
        rotate_pair, hidden[:, :D].reshape(shaped), hidden[:, D : 2 * D].reshape(shaped)
    )
    query_low = query_rot.astype(jnp.bfloat16)
    key_low = key_rot.reshape(local_rows, D).astype(jnp.bfloat16)
    value_low = hidden[:, 2 * D : 3 * D].astype(jnp.bfloat16)
    hidden_up = hidden[:, 3 * D :]

    def allowed_pairs(offset, block_len):
        key_pos = lax.dynamic_slice_in_dim(positions_all, offset, block_len)
        key_seg = lax.dynamic_slice_in_dim(segments_all, offset, block_len)
        return (key_pos[None, :] <= query_pos[:, None]) & (key_seg[None, :] == query_seg[:, None])

    start_state = (
        jnp.full((HEADS, local_rows), masked_score, jnp.float32),
        jnp.zeros((HEADS, local_rows), jnp.float32),
        jnp.zeros((HEADS, local_rows, HEAD_DIM), jnp.float32),
    )
    running = start_state
    key_piece = lax.all_gather(key_low, "ctx", axis=0, tiled=True)
    value_piece = lax.all_gather(value_low, "ctx", axis=0, tiled=True)
    amount = key_piece.shape[0]
    block_len = key_block(amount)

    def absorb_one_block(carried, block_number):
        block_start = block_number * block_len
        key_part = lax.dynamic_slice_in_dim(key_piece, block_start, block_len).reshape(
            block_len, HEADS, HEAD_DIM
        )
        value_part = lax.dynamic_slice_in_dim(value_piece, block_start, block_len).reshape(
            block_len, HEADS, HEAD_DIM
        )
        allowed = allowed_pairs(block_start, block_len)
        running_max, running_sum, running_out = carried
        scores = (
            jnp.einsum("qhd,khd->hqk", query_low, key_part, preferred_element_type=jnp.float32)
            * score_scale
        )
        masked = jnp.where(allowed[None], scores, masked_score)
        new_max = jnp.maximum(running_max, jnp.max(masked, axis=-1))
        weights = jnp.where(allowed[None], jnp.exp(masked - new_max[..., None]), 0.0)
        factor = jnp.exp(running_max - new_max)
        running_sum = running_sum * factor + jnp.sum(weights, axis=-1)
        running_out = running_out * factor[..., None] + jnp.einsum(
            "hqk,khd->hqd",
            weights.astype(jnp.bfloat16),
            value_part,
            preferred_element_type=jnp.float32,
        )
        carried = (new_max, running_sum, running_out)
        return (carried, None)

    running, unused = lax.scan(absorb_one_block, running, jnp.arange(amount // block_len))
    final_max, final_sum, final_out = running
    attended = jnp.transpose(final_out / final_sum[..., None], (1, 0, 2))
    log_total = final_max + jnp.log(final_sum)
    attended_low = attended.reshape(local_rows, D).astype(jnp.bfloat16)
    activation, gelu_pull = jax.vjp(gelu_tanh, hidden_up)
    mixed_low = jnp.concatenate([attended_low, activation.astype(jnp.bfloat16)], axis=1)
    projected = jnp.dot(
        mixed_low,
        lax.all_gather(back_weight, "fsdp", axis=1, tiled=True),
        preferred_element_type=jnp.float32,
    )
    layer_out = (inputs + projected + bias_back).astype(jnp.bfloat16)[None]
    grad_low = cotangent[0]
    grad_cols = grad_low
    mixed_grad = lax.dot_general(
        grad_cols,
        lax.all_gather(back_weight, "fsdp", axis=1, tiled=True),
        contract_last,
        preferred_element_type=jnp.float32,
    )
    attended_grad = mixed_grad[:, :D].reshape(shaped).astype(jnp.bfloat16)
    (up_grad,) = gelu_pull(mixed_grad[:, D:])
    row_delta = jnp.sum(attended_grad.astype(jnp.float32) * attended, axis=-1).T
    back_state = (jnp.zeros(shaped, jnp.float32), jnp.zeros((seq_len, 2 * D), jnp.float32))
    running = back_state
    scatter_key_piece = lax.all_gather(key_low, "ctx", axis=0, tiled=True)
    scatter_value_piece = lax.all_gather(value_low, "ctx", axis=0, tiled=True)
    amount = scatter_key_piece.shape[0]
    scatter_block_len = key_block(amount)

    def scatter_one_block(carried, block_number):
        block_start = block_number * scatter_block_len
        key_part = lax.dynamic_slice_in_dim(
            scatter_key_piece, block_start, scatter_block_len
        ).reshape(scatter_block_len, HEADS, HEAD_DIM)
        value_part = lax.dynamic_slice_in_dim(
            scatter_value_piece, block_start, scatter_block_len
        ).reshape(scatter_block_len, HEADS, HEAD_DIM)
        allowed = allowed_pairs(block_start, scatter_block_len)
        query_grad, key_value_grad = carried
        scores = (
            jnp.einsum("qhd,khd->hqk", query_low, key_part, preferred_element_type=jnp.float32)
            * score_scale
        )
        probs = jnp.where(allowed[None], jnp.exp(scores - log_total[..., None]), 0.0)
        value_grad = jnp.einsum(
            "hqk,qhd->khd",
            probs.astype(jnp.bfloat16),
            attended_grad,
            preferred_element_type=jnp.float32,
        )
        prob_grad = jnp.einsum(
            "qhd,khd->hqk", attended_grad, value_part, preferred_element_type=jnp.float32
        )
        score_grad = (probs * (prob_grad - row_delta[..., None])).astype(jnp.bfloat16)
        query_grad = (
            query_grad
            + jnp.einsum("hqk,khd->qhd", score_grad, key_part, preferred_element_type=jnp.float32)
            * score_scale
        )
        key_grad = (
            jnp.einsum("hqk,qhd->khd", score_grad, query_low, preferred_element_type=jnp.float32)
            * score_scale
        )
        block_grads = jnp.concatenate(
            [key_grad.reshape(scatter_block_len, D), value_grad.reshape(scatter_block_len, D)],
            axis=1,
        )
        key_value_grad = lax.dynamic_update_slice_in_dim(
            key_value_grad, block_grads, block_start, 0
        )
        carried = (query_grad, key_value_grad)
        return (carried, None)

    running, unused = lax.scan(scatter_one_block, running, jnp.arange(amount // scatter_block_len))
    query_grad, key_value_all = running
    key_value_own = lax.psum_scatter(
        key_value_all.astype(jnp.bfloat16), "ctx", scatter_dimension=0, tiled=True
    ).astype(jnp.float32)
    query_pre, key_pre = rotary_pull((query_grad, key_value_own[:, :D].reshape(shaped)))
    hidden_grad = jnp.concatenate(
        [
            query_pre.reshape(local_rows, D),
            key_pre.reshape(local_rows, D),
            key_value_own[:, D:],
            up_grad,
        ],
        axis=1,
    ).astype(jnp.bfloat16)
    grad_cols = hidden_grad
    normed_grad = lax.dot_general(
        grad_cols,
        lax.all_gather(front_weight, "fsdp", axis=1, tiled=True),
        contract_last,
        preferred_element_type=jnp.float32,
    )
    input_grad, gain_grad, shift_grad = norm_pull(normed_grad)
    tokens_grad = (grad_low.astype(jnp.float32) + input_grad).astype(jnp.bfloat16)[None]
    front_term = lax.psum_scatter(
        lax.dot_general(
            normed_low, hidden_grad, contract_first, preferred_element_type=jnp.float32
        ).astype(jnp.bfloat16),
        "ctx",
        scatter_dimension=0,
        tiled=True,
    )
    back_term = lax.psum_scatter(
        lax.dot_general(
            mixed_low, grad_low, contract_first, preferred_element_type=jnp.float32
        ).astype(jnp.bfloat16),
        "ctx",
        scatter_dimension=0,
        tiled=True,
    )
    front_grad, back_grad = (
        lax.psum_scatter(front_term, "fsdp", scatter_dimension=1, tiled=True).astype(jnp.float32),
        lax.psum_scatter(back_term, "fsdp", scatter_dimension=1, tiled=True).astype(jnp.float32),
    )
    vector_term = jnp.concatenate(
        [
            jnp.sum(hidden_grad, axis=0, dtype=jnp.float32),
            jnp.sum(grad_low, axis=0, dtype=jnp.float32),
            gain_grad,
            shift_grad,
        ]
    )
    vector_grad = lax.psum(vector_term, ("ctx", "fsdp"))
    count_now = adam_step[0]
    front_new, front_first_new, front_second_new = adam_update(
        front_master, front_first, front_second, front_grad, learn_rates[0], count_now, weight_decay
    )
    back_new, back_first_new, back_second_new = adam_update(
        back_master, back_first, back_second, back_grad, learn_rates[1], count_now, weight_decay
    )
    vectors_new, vector_first_new, vector_second_new = adam_update(
        vectors, vector_first, vector_second, vector_grad, learn_rates[2], count_now, 0.0
    )
    front_next, back_next = (
        lax.all_gather(front_new.astype(jnp.bfloat16), "ctx", axis=0, tiled=True),
        lax.all_gather(back_new.astype(jnp.bfloat16), "ctx", axis=0, tiled=True),
    )
    return (
        layer_out,
        tokens_grad,
        front_grad,
        back_grad,
        vector_grad,
        front_new,
        back_new,
        vectors_new,
        front_first_new,
        back_first_new,
        vector_first_new,
        front_second_new,
        back_second_new,
        vector_second_new,
        front_next,
        back_next,
    )


def solution(mesh):
    in_specs = (
        P("fsdp", "ctx", None),
        P("fsdp", "ctx", None),
        P("fsdp", None),
        P(),
        P(None, "fsdp"),
        P(None, "fsdp"),
        P("ctx", "fsdp"),
        P("ctx", "fsdp"),
        P("ctx", "fsdp"),
        P("ctx", "fsdp"),
        P("ctx", "fsdp"),
        P("ctx", "fsdp"),
        P(),
        P(),
        P(),
        P(),
        P(),
    )
    out_specs = (
        P("fsdp", "ctx", None),
        P("fsdp", "ctx", None),
        P("ctx", "fsdp"),
        P("ctx", "fsdp"),
        P(),
        P("ctx", "fsdp"),
        P("ctx", "fsdp"),
        P(),
        P("ctx", "fsdp"),
        P("ctx", "fsdp"),
        P(),
        P("ctx", "fsdp"),
        P("ctx", "fsdp"),
        P(),
        P(None, "fsdp"),
        P(None, "fsdp"),
    )
    return jax.shard_map(
        per_device, mesh=mesh, in_specs=in_specs, out_specs=out_specs, check_vma=False
    )
```

profile of v0, /device:TPU:0, one launch (start us, length us, event | category | flops | bytes accessed | tf_op | source)
XLA Modules:
  0.0 2660.1 jit_solution(6433679246068548918)
XLA Ops:
  10.5 509.2 %all-gather.7.cloned.1.call-done = bf16[2048,14336]{1,0:T(8,128)(2,1)} async-done(((bf16[2048,3584]{1,0:T(8,128)(2,1)}), bf16[2048,14336]{1,0:T(8,128)(2,1)}) %all-gather.7.cloned.1.call-update) | async-done | bytes 58720272 | tf_op jit(solution)/shard_map/all_gather | solution.py:118
  519.8 31.0 %convolution_add_fusion = f32[128,14336]{1,0:T(8,128)} fusion(bf16[2048,14336]{1,0:T(8,128)(2,1)} %all-gather.7.cloned.1.call-done, f32[14336]{0:T(1024)S(1)} %slice-done, bf16[1,128,2048]{2,1,0:T(8,128)(2,1)S(1)} %copy-done, f32[2048]{0:T(1024)S(1)} %get-tuple-element.415, f32[2048]{0:T(1024)S(1)} %get-tuple-element.416, f32[128]{0:T(128)S(1)} %fusion.56, ...), kind=kOutput, calls=%fused_computation.42 | convolution fusion | flops 7519600640 | bytes 66659328 | tf_op jit(solution)/shard_map/dot_general | solution.py:116
  561.7 327.2 %all-gather.13.cloned.1.call-done = bf16[10240,2048]{1,0:T(8,128)(2,1)} async-done(((bf16[10240,512]{1,0:T(8,128)(2,1)}), bf16[10240,2048]{1,0:T(8,128)(2,1)}) %all-gather.13.cloned.1.call-update) | async-done | bytes 41943056 | tf_op jit(solution)/shard_map/all_gather | solution.py:190
  888.9 21.6 fusion.53
  913.2 24.8 all-gather.11.cloned.1.call-done
  938.0 6.4 copy.76
  944.4 42.2 %all-gather.9.cloned.1.call-done = bf16[1024,2048]{0,1:T(8,128)(2,1)} async-done(((bf16[128,2048]{0,1:T(8,128)(2,1)}), bf16[1024,2048]{0,1:T(8,128)(2,1)}) %all-gather.9.cloned.1.call-update) | async-done | bytes 4194320 | tf_op jit(solution)/shard_map/all_gather | solution.py:148
  986.7 22.1 while.28
  1009.0 4.4 broadcast_in_dim.103.clone
  1013.5 54.4 %while.29 = (s32[]{:T(128)}, f32[128,32,64]{0,2,1:T(8,128)S(1)}, bf16[1024,4096]{1,0:T(8,128)(2,1)}, s32[2]{0:T(128)S(1)}, bf16[1024,2048]{0,1:T(8,128)(2,1)}, /...) while((s32[]{:T(128)}, f32[128,32,64]{0,2,1:T(8,128)S(1)}, ...), condition=%wide.region_8.9_spmd.clone, body=%wide.region_7.8_spmd.clone.sunk | while | flops 1374617600 | bytes 86242552 | solution.py:256
  1019.1 3.4 fusion.133
  1029.7 6.4 copy.106
  1036.1 4.7 constant_dynamic-update-slice_fusion.2
  1056.8 6.4 copy.106
  1063.2 4.7 constant_dynamic-update-slice_fusion.2
  1068.0 6.8 fusion.31
  1076.9 18.6 convolution_convert_fusion.1
  1095.6 60.1 %reduce-scatter.8.cloned.1.call-done = bf16[128,4096]{1,0:T(8,128)(2,1)} async-done(((bf16[1024,4096]{1,0:T(8,128)(2,1)}), bf16[128,4096]{1,0:T(8,128)(2,1)}) %reduce-scatter.8.cloned.1.call-update) | async-done | bytes 1048592 | tf_op jit(solution)/shard_map/reduce_scatter | solution.py:258
  1164.0 24.0 convolution_convert_fusion
  1188.1 372.6 %reduce-scatter.16.cloned.1.call-done = bf16[1280,2048]{1,0:T(8,128)(2,1)} async-done(((bf16[10240,2048]{1,0:T(8,128)(2,1)}), bf16[1280,2048]{1,0:T(8,128)(2,1)}) %reduce-scatter.16.cloned.1.call-update) | async-done | bytes 5242896
  1560.8 562.6 %reduce-scatter.10.cloned.1.call-done = bf16[256,14336]{1,0:T(8,128)(2,1)} async-done(((bf16[2048,14336]{1,0:T(8,128)(2,1)}), bf16[256,14336]{1,0:T(8,128)(2,1)}) %reduce-scatter.10.cloned.1.call-update) | async-done | bytes 7340048 | tf_op jit(solution)/shard_map/reduce_scatter | solution.py:280
  2124.9 27.8 %fusion.48 = (f32[128]{0:T(128)S(1)}, f32[128,2048]{1,0:T(8,128)}) fusion(bf16[1,128,2048]{2,1,0:T(8,128)(2,1)S(1)} %copy-done.1, f32[2048]{0:T(1024)S(1)} %copy-done.14, f32[128]{0:T(128)S(1)} %copy-done.20, bf16[2048,14336]{1,0:T(8,128)(2,1)} %all-gather.7.cloned.1.call-done, bf16[128,8192]{1,0:T(8,128)(2,1)S(1)} %copy-done.3, ...), kind=kOutput, calls=%fused_computation.84 | convolution fusion | flops 7532183552 | bytes 63972352 | tf_op jit(solution)/shard_map/dot_general | solution.py:272
  2158.8 27.5 %reduce-scatter.14.cloned.1.call-done = bf16[1280,512]{1,0:T(8,128)(2,1)} async-done(((bf16[1280,2048]{1,0:T(8,128)(2,1)}), bf16[1280,512]{1,0:T(8,128)(2,1)}) %reduce-scatter.14.cloned.1.call-update) | async-done | bytes 1310736 | tf_op jit(solution)/shard_map/reduce_scatter | solution.py:298
  2186.3 8.3 fusion.63
  2194.7 73.3 %reduce-scatter.12.cloned.1.call-done = bf16[256,3584]{1,0:T(8,128)(2,1)} async-done(((bf16[256,14336]{1,0:T(8,128)(2,1)}), bf16[256,3584]{1,0:T(8,128)(2,1)}) %reduce-scatter.12.cloned.1.call-update) | async-done | bytes 1835024 | tf_op jit(solution)/shard_map/reduce_scatter | solution.py:297
  2268.0 10.9 fusion.65
  2279.0 16.8 fusion.36
  2295.8 99.8 %all-reduce.9.cloned.1.call-done = f32[20480]{0:T(1024)} async-done(((f32[20480]{0:T(1024)}), f32[20480]{0:T(1024)}) %all-reduce.9.cloned.1.call-update) | async-done | bytes 81936 | tf_op jit(solution)/shard_map/psum | solution.py:308
  2397.8 101.5 %all-gather.17.cloned.1.call-done = bf16[10240,512]{1,0:T(8,128)(2,1)} async-done(((bf16[1280,512]{1,0:T(8,128)(2,1)}), bf16[10240,512]{1,0:T(8,128)(2,1)}) %all-gather.17.cloned.1.call-update) | async-done | bytes 10485776 | tf_op jit(solution)/shard_map/all_gather | solution.py:321
  2499.3 134.3 %all-gather.15.cloned.1.call-done = bf16[2048,3584]{1,0:T(8,128)(2,1)} async-done(((bf16[256,3584]{1,0:T(8,128)(2,1)}), bf16[2048,3584]{1,0:T(8,128)(2,1)}) %all-gather.15.cloned.1.call-update) | async-done | bytes 14680080 | tf_op jit(solution)/shard_map/all_gather | solution.py:320
  2635.2 13.7 copy.134
  2648.9 4.1 copy.135
  (197 shorter events, 86.2 us)
Async XLA Ops:
  7.2 512.6 %all-gather.7.cloned.1.call-start = ((), (), s32[]{:S(2)}) async-start(), calls=%async_computation.5 | async-start | bytes 73400320 | tf_op jit(solution)/shard_map/all_gather | solution.py:118
  7.9 511.8 %slice-start = ((f32[20480]{0:T(1024)}), f32[14336]{0:T(1024)S(1)}, s32[]{:S(2)}) async-start(f32[20480]{0:T(1024)} %param.33), calls=%async_computation.17 | async-start | bytes 114688 | tf_op jit(solution)/shard_map/slice | solution.py:103
  7.9 880.9 %all-gather.13.cloned.1.call-start = ((), (), s32[]{:S(2)}) async-start(), calls=%async_computation.8 | async-start | bytes 52428800 | tf_op jit(solution)/shard_map/all_gather | solution.py:190
  8.7 929.3 %all-gather.11.cloned.1.call-start = ((), (), s32[]{:S(2)}) async-start(), calls=%async_computation.7 | async-start | bytes 4718592 | tf_op jit(solution)/shard_map/all_gather | solution.py:149
  9.1 541.7 %copy-start.19 = (f32[128]{0:T(128)}, f32[128]{0:T(128)S(1)}, u32[]{:S(2)}) copy-start(f32[128]{0:T(128)S(1)} %broadcast_multiply_fusion) | copy-start | bytes 1540
  9.9 540.9 %copy-start.21 = (f32[128]{0:T(128)}, f32[128]{0:T(128)S(1)}, u32[]{:S(2)}) copy-start(f32[128]{0:T(128)S(1)} %fusion.56) | copy-start | bytes 1540
  10.5 540.2 %copy-start.13 = (f32[2048]{0:T(1024)}, f32[2048]{0:T(1024)S(1)}, u32[]{:S(2)}) copy-start(f32[2048]{0:T(1024)S(1)} %get-tuple-element.416) | copy-start | bytes 24580
  10.5 540.3 %copy-start.15 = (f32[2048]{0:T(1024)}, f32[2048]{0:T(1024)S(1)}, u32[]{:S(2)}) copy-start(f32[2048]{0:T(1024)S(1)} %get-tuple-element.415) | copy-start | bytes 24580
  519.8 33.3 %copy-start.34 = (s32[16]{0:T(128)S(1)}, s32[16]{0:T(128)}, u32[]{:S(2)}) copy-start(s32[16]{0:T(128)} %param.24) | copy-start | bytes 196
  553.0 433.7 %all-gather.9.cloned.1.call-start = ((), (), s32[]{:S(2)}) async-start(), calls=%async_computation.6 | async-start | bytes 4718592 | tf_op jit(solution)/shard_map/all_gather | solution.py:148
  555.2 333.7 %copy-start.5 = (bf16[1,128,2048]{2,1,0:T(8,128)(2,1)S(1)}, bf16[1,128,2048]{2,1,0:T(8,128)(2,1)}, u32[]{:S(2)}) copy-start(bf16[1,128,2048]{2,1,0:T(8,128)(2,1)} %param.22) | copy-start | bytes 1572868
  559.0 596.7 %reduce-scatter.8.cloned.1.call-start = ((), (), s32[]{:S(2)}) async-start(), calls=%async_computation.9 | async-start | bytes 9437184 | tf_op jit(solution)/shard_map/reduce_scatter | solution.py:258
  1067.9 492.8 %reduce-scatter.16.cloned.1.call-start = ((), (), s32[]{:S(2)}) async-start(), calls=%async_computation.16 | async-start | bytes 47185920
  1095.5 66.5 %copy-start.26 = (f32[128,16]{0,1:T(8,128)S(1)}, f32[128,16]{0,1:T(8,128)}, u32[]{:S(2)}) copy-start(f32[128,16]{0,1:T(8,128)} %copy-done.25) | copy-start | bytes 24580
  1095.5 66.5 %copy-start.28 = (f32[128,16]{0,1:T(8,128)S(1)}, f32[128,16]{0,1:T(8,128)}, u32[]{:S(2)}) copy-start(f32[128,16]{0,1:T(8,128)} %copy-done.27) | copy-start | bytes 24580
  1095.5 1027.9 %reduce-scatter.10.cloned.1.call-start = ((), (), s32[]{:S(2)}) async-start(), calls=%async_computation.10 | async-start | bytes 66060288 | tf_op jit(solution)/shard_map/reduce_scatter | solution.py:280
  1163.7 24.3 copy-start.9
  1164.0 24.1 copy-start.11
  1188.1 998.2 %reduce-scatter.14.cloned.1.call-start = ((), (), s32[]{:S(2)}) async-start(), calls=%async_computation.12 | async-start | bytes 6553600 | tf_op jit(solution)/shard_map/reduce_scatter | solution.py:298
  1560.8 563.5 %copy-start.30 = (f32[3]{0:T(128)S(1)}, f32[3]{0:T(128)}, u32[]{:S(2)}) copy-start(f32[3]{0:T(128)} %param.36) | copy-start | bytes 40
  1560.8 564.1 %copy-start.3 = (bf16[128,8192]{1,0:T(8,128)(2,1)S(1)}, bf16[128,8192]{1,0:T(8,128)(2,1)}, u32[]{:S(2)}) copy-start(bf16[128,8192]{1,0:T(8,128)(2,1)} %get-tuple-element.398) | copy-start | bytes 6291460
  1560.8 707.3 %reduce-scatter.12.cloned.1.call-start = ((), (), s32[]{:S(2)}) async-start(), calls=%async_computation.11 | async-start | bytes 9175040 | tf_op jit(solution)/shard_map/reduce_scatter | solution.py:297
  2123.4 272.1 %all-reduce.9.cloned.1.call-start = ((), (), s32[]{:S(2)}) async-start(), calls=%async_computation.13 | async-start | bytes 163840 | tf_op jit(solution)/shard_map/psum | solution.py:308
  2124.9 27.8 %copy-start.33 = (f32[128]{0:T(128)S(1)}, f32[128]{0:T(128)}, u32[]{:S(2)}) copy-start(f32[128]{0:T(128)} %copy-done.32) | copy-start | bytes 1540
  2158.7 340.6 %all-gather.17.cloned.1.call-start = ((), (), s32[]{:S(2)}) async-start(), calls=%async_computation.15 | async-start | bytes 11796480 | tf_op jit(solution)/shard_map/all_gather | solution.py:321
  2194.6 439.0 %all-gather.15.cloned.1.call-start = ((), (), s32[]{:S(2)}) async-start(), calls=%async_computation.14 | async-start | bytes 16515072 | tf_op jit(solution)/shard_map/all_gather | solution.py:320
  2268.0 10.9 copy-start.2
  2268.0 10.9 copy-start.29
  2278.9 116.6 %copy-start.18 = (f32[20480]{0:T(1024)S(1)}, f32[20480]{0:T(1024)}, u32[]{:S(2)}) copy-start(f32[20480]{0:T(1024)} %param.33) | copy-start | bytes 245764
  2279.0 116.6 %copy-start.23 = (f32[20480]{0:T(1024)S(1)}, f32[20480]{0:T(1024)}, u32[]{:S(2)}) copy-start(f32[20480]{0:T(1024)} %param.35) | copy-start | bytes 245764
  2279.0 116.6 %copy-start.24 = (f32[20480]{0:T(1024)S(1)}, f32[20480]{0:T(1024)}, u32[]{:S(2)}) copy-start(f32[20480]{0:T(1024)} %param.34) | copy-start | bytes 245764
  2635.2 13.7 copy-start.4
  (16 other events, 60.5 us)
Sparse Core Ops, SparseCore 0:
  9.8 509.8 all-gather.6
  521.6 367.2 all-gather.12
  891.1 46.8 all-gather.10
  940.0 46.5 all-gather.8
  1068.0 87.6 reduce-scatter.7
  1158.0 402.6 reduce-scatter.15
  1563.1 560.2 reduce-scatter.9
  2126.4 59.8 reduce-scatter.13
  2189.3 78.7 reduce-scatter.11
  2274.0 121.4 all-reduce.8
  2397.8 101.4 all-gather.16
  2501.4 132.2 all-gather.14
where the time goes:
time: 2670 us; the launch traced here: 2660 us
  waiting for transfers between devices  2340 us (88%)
  matrix products  169 us (6%)
  local copies, waits for them, and re-layouts  82.6 us (3%)
  other arithmetic  52.4 us (2%)
    reduce_scatter x1, waiting for transfers between devices, per_device(): lax.psum_scatter(lax.dot_general(normed_low, hidden_grad, contract_first,...  563 us
    all_gather x1, waiting for transfers between devices, per_device(): lax.all_gather(front_weight, 'fsdp', axis=1, tiled=True)  509 us
    unnamed x13, waiting for transfers between devices  374 us
    all_gather x1, waiting for transfers between devices, per_device(): lax.all_gather(back_weight, 'fsdp', axis=1, tiled=True)  327 us
    all_gather x1, waiting for transfers between devices, per_device(): lax.all_gather(front_new.astype(jnp.bfloat16), 'ctx', axis=0, tiled=True)  134 us
    all_gather x1, waiting for transfers between devices, per_device(): lax.all_gather(back_new.astype(jnp.bfloat16), 'ctx', axis=0, tiled=True)  102 us
    psum x1, waiting for transfers between devices, per_device(): vector_grad = lax.psum(vector_term, ('ctx', 'fsdp'))  99.8 us
    reduce_scatter x1, waiting for transfers between devices, per_device(): lax.psum_scatter(front_term, 'fsdp', scatter_dimension=1, tiled=True)  73.3 us
  transfers between devices with their start and end apart: 12, of which 12 were waited for; matrix products, arithmetic and copies ran while one was open for 8% of the time, Pallas kernels for 0%

commit v1 on v0

v1 whole, which is shorter than its diff:
```python
import functools

import jax
import jax.numpy as jnp
import numpy as np
from jax import lax
from jax.experimental import pallas as pl
from jax.experimental.pallas import tpu as pltpu
from jax.sharding import PartitionSpec as P

D = 2048
HEADS = 32
FF = 8192
ROT = 32
HEAD_DIM = 64
IN_COLS = 14336
BACK_ROWS = 10240

norm_eps = 1e-05
beta_first = 0.9
beta_second = 0.95
adam_eps = 1e-08
weight_decay = 0.1
masked_score = -1e30
bf16 = jnp.bfloat16
f32 = jnp.float32


class Layout:
    def __init__(self, ctx, fsdp):
        self.ctx, self.fsdp, self.planes, self.ranks = ctx, fsdp, ctx // 2, 2 * fsdp
        assert ctx % 2 == 0 and self.planes == fsdp
        self.unit = D // self.ranks
        self.per_shard = IN_COLS // self.unit // fsdp
        r = self.ranks
        first_up = 3 * r
        home = {f: [] for f in range(fsdp)}
        for g in range(first_up, 7 * r, 2):
            assert g // self.per_shard == (g + 1) // self.per_shard
            home[g // self.per_shard].append(g)
        pairs = {p: [None, None] for p in range(r)}
        for f in range(fsdp):
            if len(home[f]) >= 4:
                keep, home[f] = home[f][:4], home[f][4:]
                pairs[2 * f], pairs[2 * f + 1] = keep[:2], keep[2:]
            elif home[f]:
                keep, home[f] = home[f], []
                for i, g in enumerate(keep):
                    pairs[2 * f + i % 2][(i + i // 2) % 2] = g
        for s in range(2):
            for k in range(2):
                used = set()
                for f in range(fsdp):
                    p = 2 * f + k
                    if pairs[p][s] is not None:
                        continue
                    options = sorted(
                        (h for h in range(fsdp) if home[h]),
                        key=lambda h: (h in used, bin(h ^ f).count("1"), -len(home[h])),
                    )
                    used.add(options[0])
                    pairs[p][s] = home[options[0]].pop(0)
        self.pairs = pairs
        self.slots = [
            ([p for p in range(r)], 1),
            ([r + p for p in range(r)], 1),
            ([2 * r + p for p in range(r)], 1),
            ([pairs[p][0] for p in range(r)], 2),
            ([pairs[p][1] for p in range(r)], 2),
        ]
        self.rounds = []
        for units, _ in self.slots:
            rounds = []
            for k in range(2):
                for f in range(fsdp):
                    src = units[2 * f + k] // self.per_shard
                    if src == f:
                        continue
                    for one in rounds:
                        if all((src, k) != (a, c) for a, _, c in one):
                            one.append((src, f, k))
                            break
                    else:
                        rounds.append([(src, f, k)])
            self.rounds.append(rounds)
        self.rank_units = [
            [p, r + p, 2 * r + p, pairs[p][0], pairs[p][0] + 1, pairs[p][1], pairs[p][1] + 1]
            for p in range(r)
        ]
        self.back_units = [[p] + [g - 2 * r for g in self.rank_units[p][3:]] for p in range(r)]
        self.matchings = []
        left = {p: list(range(5)) for p in range(r)}
        own = lambda p, j: self.back_units[p][j] // 5
        for _ in range(5):
            match = {}

            def assign(p, seen):
                for j in left[p]:
                    c = own(p, j)
                    if c in seen:
                        continue
                    seen.add(c)
                    if c not in match or assign(match[c][0], seen):
                        match[c] = (p, j)
                        return True
                return False

            for p in range(r):
                assert assign(p, set())
            for c, (p, j) in match.items():
                left[p].remove(j)
            self.matchings.append(match)

    def device(self, z, k, f):
        return (2 * z + k) * self.fsdp + f


def pick(table, index):
    return jnp.asarray(np.asarray(table, np.int32))[index]


def rotation_tables(positions, width):
    half = ROT // 2
    lane = np.arange(width) % HEAD_DIM
    frequency = jnp.power(
        10000.0, -2.0 * jnp.asarray(lane % half, f32) / ROT
    )
    angles = positions.astype(f32)[:, None] * frequency[None, :]
    rotated = jnp.asarray(lane < ROT)
    lower = jnp.asarray(lane < half)
    cosine = jnp.where(rotated, jnp.cos(angles), 1.0)
    sine = jnp.where(rotated, jnp.sin(angles), 0.0)
    return cosine, jnp.where(lower, -sine, 0.0), jnp.where(lower, 0.0, sine)


def rotate(values, tables):
    half = ROT // 2
    cosine, from_above, from_below = tables
    return (
        values * cosine
        + jnp.roll(values, -half, axis=1) * from_above
        + jnp.roll(values, half, axis=1) * from_below
    )


def rotate_back(values, tables):
    half = ROT // 2
    cosine, from_above, from_below = tables
    return (
        values * cosine
        + jnp.roll(values * from_above, half, axis=1)
        + jnp.roll(values * from_below, -half, axis=1)
    )


def attention_kernel(
    q_ref, k_ref, v_ref, g_ref, pos_q, pos_k, seg_q, seg_k, att_ref, dq_ref, dk_ref, dv_ref
):
    scale = HEAD_DIM ** (-0.5)
    width = q_ref.shape[1]

    @pl.when(pl.program_id(0) == 0)
    def _():
        dk_ref[...] = jnp.zeros_like(dk_ref)
        dv_ref[...] = jnp.zeros_like(dv_ref)

    allowed = (pos_k[...] <= pos_q[...]) & (seg_k[...] == seg_q[...])
    bias = jnp.where(allowed, 0.0, masked_score)
    last = (((1,), (1,)), ((), ()))
    first = (((0,), (0,)), ((), ()))
    for head in range(width // HEAD_DIM):
        cols = slice(head * HEAD_DIM, (head + 1) * HEAD_DIM)
        q, g = q_ref[:, cols], g_ref[:, cols]
        k, v = k_ref[:, cols], v_ref[:, cols]
        scores = lax.dot_general(q, k, last, preferred_element_type=f32) * scale + bias
        weights = jnp.exp(scores - jnp.max(scores, axis=1, keepdims=True))
        probs = weights * (1.0 / jnp.sum(weights, axis=1, keepdims=True))
        probs_low = probs.astype(bf16)
        out = jnp.dot(probs_low, v, preferred_element_type=f32)
        att_ref[:, cols] = out.astype(bf16)
        prob_grad = lax.dot_general(g, v, last, preferred_element_type=f32)
        delta = jnp.sum(g.astype(f32) * out, axis=1, keepdims=True)
        score_grad = (probs * (prob_grad - delta)).astype(bf16)
        dq_ref[:, cols] = jnp.dot(score_grad, k, preferred_element_type=f32) * scale
        dk_ref[:, cols] += lax.dot_general(score_grad, q, first, preferred_element_type=f32) * scale
        dv_ref[:, cols] += lax.dot_general(probs_low, g, first, preferred_element_type=f32)


def attention(query, key, value, grad, positions, segments):
    length, width = query.shape
    block = 256
    rows = pl.BlockSpec((block, width), lambda i: (i, 0))
    whole = pl.BlockSpec((length, width), lambda i: (0, 0))
    column = pl.BlockSpec((block, 1), lambda i: (i, 0))
    line = pl.BlockSpec((1, length), lambda i: (0, 0))
    return pl.pallas_call(
        attention_kernel,
        grid=(length // block,),
        in_specs=[rows, whole, whole, rows, column, line, column, line],
        out_specs=[rows, rows, whole, whole],
        out_shape=[
            jax.ShapeDtypeStruct((length, width), bf16),
            jax.ShapeDtypeStruct((length, width), f32),
            jax.ShapeDtypeStruct((length, width), f32),
            jax.ShapeDtypeStruct((length, width), f32),
        ],
        cost_estimate=pl.CostEstimate(
            flops=14 * length * length * width,
            transcendentals=length * length * width // HEAD_DIM,
            bytes_accessed=20 * length * width,
        ),
    )(query, key, value, grad, positions[:, None], positions[None], segments[:, None], segments[None])


def gelu_parts(u):
    scale = np.float32(np.sqrt(2.0 / np.pi))
    square = u * u
    inner = scale * u * (1.0 + 0.044715 * square)
    t = jnp.tanh(inner)
    value = 0.5 * u * (1.0 + t)
    slope = 0.5 * (1.0 + t) + 0.5 * u * (1.0 - t * t) * scale * (1.0 + 3 * 0.044715 * square)
    return value, slope


def adam_update(weight, first, second, grad, rate, count_now, decay):
    first_new = beta_first * first + (1.0 - beta_first) * grad
    second_new = beta_second * second + (1.0 - beta_second) * grad * grad
    steps_float = count_now.astype(f32)
    first_fix = 1.0 - jnp.power(beta_first, steps_float)
    second_fix = 1.0 - jnp.power(beta_second, steps_float)
    change = first_new / first_fix / (jnp.sqrt(second_new / second_fix) + adam_eps) + decay * weight
    return (weight - rate * change, first_new, second_new)


def after(value, *others):
    return lax.optimization_barrier((value,) + others)[0]


def per_device(
    tokens,
    cotangent,
    doc_ids,
    block_order,
    front_weight,
    back_weight,
    front_master,
    back_master,
    front_first,
    back_first,
    front_second,
    back_second,
    vectors,
    vector_first,
    vector_second,
    learn_rates,
    adam_step,
    *,
    plan,
):
    planes, shards, ranks, unit = plan.planes, plan.fsdp, plan.ranks, plan.unit
    both = ("ctx", "fsdp")
    contract_last = (((1,), (1,)), ((), ()))
    contract_first = (((0,), (0,)), ((), ()))
    c_index, f = lax.axis_index("ctx"), lax.axis_index("fsdp")
    z, k = c_index // 2, c_index % 2
    p = 2 * f + k
    rows = tokens.shape[1]
    plane_rows = 2 * shards * rows
    share = 2 * rows

    bias_front = vectors[:IN_COLS].reshape(-1, unit)
    bias_back = vectors[IN_COLS : IN_COLS + D]
    norm_gain = vectors[IN_COLS + D : IN_COLS + 2 * D]
    norm_shift = vectors[IN_COLS + 2 * D :]

    swap_pairs = [(2 * i + j, 2 * i + 1 - j) for i in range(planes) for j in range(2)]

    def swap_core(value):
        return lax.ppermute(value, "ctx", swap_pairs)

    def to_shard(value, step):
        return lax.ppermute(value, "fsdp", [(i, i ^ step) for i in range(shards)])

    def to_plane(value, step):
        return lax.ppermute(
            value, "ctx", [(2 * i + j, 2 * (i ^ step) + j) for i in range(planes) for j in range(2)]
        )

    def gather_plane(value):
        mine = lax.all_gather(value, "fsdp")
        other = swap_core(mine)
        low = jnp.where(k == 0, mine, other)
        high = jnp.where(k == 0, other, mine)
        return jnp.stack([low, high], axis=1).reshape(plane_rows, D)

    def at(array, index):
        return lax.dynamic_index_in_dim(array, index, 0, keepdims=False)

    blocks = block_order.shape[0]
    block_tokens = doc_ids.shape[1] // blocks
    offsets = jnp.arange(block_tokens, dtype=jnp.int32)
    positions_all = (block_order[:, None] * block_tokens + offsets[None, :]).reshape(planes, share)
    own_positions = at(positions_all, z)
    plane_positions = jnp.tile(own_positions, shards)

    plane_tokens = gather_plane(tokens[0])

    def normalize(values):
        values = values.astype(f32)
        centered = values - jnp.mean(values, axis=-1, keepdims=True)
        factor = lax.rsqrt(jnp.mean(centered * centered, axis=-1, keepdims=True) + norm_eps)
        return centered * factor, factor

    normed = (normalize(plane_tokens)[0] * norm_gain + norm_shift).astype(bf16)

    def slot_weight(slot, gate):
        units, wide = plan.slots[slot]
        width = wide * unit
        table = np.asarray(units)
        source, place = table // plan.per_shard, table % plan.per_shard
        total = None
        for one in plan.rounds[slot]:
            sends = np.zeros(ranks, np.int32)
            links = []
            for src, dst, core in one:
                sends[2 * src + core] = place[2 * dst + core]
                links += [
                    (plan.device(i, core, src), plan.device(i, core, dst)) for i in range(planes)
                ]
            start = after(pick(sends, p) * unit, gate)
            block = lax.dynamic_slice(front_weight, (0, start), (D, width))
            block = lax.ppermute(block, both, links)
            total = block if total is None else total + block
        local = source == np.arange(ranks) // 2
        start = pick(np.where(local, place, 0), p) * unit
        own = lax.dynamic_slice(front_weight, (0, start), (D, width))
        if total is None:
            return own
        if not local.any():
            return total
        return jnp.where(pick(local, p) > 0, own, total)

    gate = normed[0, 0]
    weight_qkv = jnp.concatenate([slot_weight(i, gate) for i in range(3)], axis=1)
    gate = weight_qkv[0, 0]
    plane_grad = gather_plane(after(cotangent[0], gate))
    weight_up = jnp.concatenate([slot_weight(i, gate) for i in range(3, 5)], axis=1)

    def back_rows(rank):
        table = pick(plan.back_units, rank)
        return jnp.concatenate(
            [lax.dynamic_slice(back_weight, (table[j] * unit, 0), (unit, D // shards)) for j in range(5)],
            axis=0,
        )

    col_width = D // shards
    back_local = jnp.zeros((5 * unit, D), bf16)
    for step in range(shards):
        piece = back_rows(after(2 * (f ^ step) + k, gate))
        if step:
            piece = to_shard(piece, step)
        back_local = lax.dynamic_update_slice(back_local, piece, (0, (f ^ step) * col_width))

    unit_table = pick(plan.rank_units, p)
    bias_local = jnp.take(bias_front, unit_table, axis=0).reshape(-1)

    hidden = jnp.dot(normed, weight_qkv, preferred_element_type=f32) + bias_local[: 3 * unit]
    tables = rotation_tables(plane_positions, unit)
    query = rotate(hidden[:, :unit], tables).astype(bf16)
    key = rotate(hidden[:, unit : 2 * unit], tables).astype(bf16)
    qkv = jnp.concatenate([query, key, hidden[:, 2 * unit :].astype(bf16)], axis=1)

    def to_sequence(value):
        shaped = value.reshape(shards, share, -1)
        pieces = [at(shaped, z)]
        for step in range(1, planes):
            pieces.append(to_plane(at(shaped, z ^ step), step))
        return jnp.concatenate(pieces, axis=0)

    def to_plane_rows(value):
        shaped = value.reshape(planes, share, -1)
        pieces = [shaped[0]] + [to_plane(shaped[step], step) for step in range(1, planes)]
        stacked = jnp.stack(pieces)
        return jnp.concatenate([at(stacked, i ^ z) for i in range(planes)], axis=0)

    qkv_seq = to_sequence(qkv)

    mixed_grad = lax.dot_general(plane_grad, back_local, contract_last, preferred_element_type=f32)
    grad_seq = to_sequence(mixed_grad[:, :unit].astype(bf16))

    order = jnp.arange(planes, dtype=jnp.int32) ^ z
    seq_positions = jnp.take(positions_all, order, axis=0).reshape(-1)
    documents = lax.all_gather(doc_ids[0].astype(f32), "fsdp")
    doc_row = at(documents, z).astype(jnp.int32)
    seq_documents = jnp.take(
        jnp.take(doc_row.reshape(blocks, block_tokens), block_order, axis=0).reshape(planes, share),
        order,
        axis=0,
    ).reshape(-1)
    attended, query_grad, key_grad, value_grad = attention(
        qkv_seq[:, :unit],
        qkv_seq[:, unit : 2 * unit],
        qkv_seq[:, 2 * unit :],
        grad_seq,
        seq_positions,
        seq_documents,
    )
    seq_tables = rotation_tables(seq_positions, unit)
    returned = to_plane_rows(
        jnp.concatenate(
            [
                attended,
                rotate_back(query_grad, seq_tables).astype(bf16),
                rotate_back(key_grad, seq_tables).astype(bf16),
                value_grad.astype(bf16),
            ],
            axis=1,
        )
    )

    up = jnp.dot(normed, weight_up, preferred_element_type=f32) + bias_local[3 * unit :]
    activation, slope = gelu_parts(up)
    up_grad = (mixed_grad[:, unit:] * slope).astype(bf16)
    mixed = jnp.concatenate([returned[:, :unit], activation.astype(bf16)], axis=1)
    hidden_grad = jnp.concatenate([returned[:, unit:], up_grad], axis=1)

    def sum_to_owner(value):
        shaped = value.reshape(shards, 2, rows, D)
        kept = lax.dynamic_index_in_dim(shaped, k, 1, keepdims=False)
        sent = lax.dynamic_index_in_dim(shaped, 1 - k, 1, keepdims=False).astype(bf16)
        summed = kept + swap_core(sent).astype(f32)
        total = at(summed, f)
        for step in range(1, shards):
            total = total + to_shard(at(summed, f ^ step).astype(bf16), step).astype(f32)
        return total

    projected = sum_to_owner(jnp.dot(mixed, back_local, preferred_element_type=f32))
    inputs = tokens[0].astype(f32)
    layer_out = (inputs + projected + bias_back).astype(bf16)[None]

    weight_local = jnp.concatenate([weight_qkv, weight_up], axis=1)
    normed_grad = sum_to_owner(
        lax.dot_general(hidden_grad, weight_local, contract_last, preferred_element_type=f32)
    )
    unscaled, factor = normalize(inputs)
    scaled = normed_grad * norm_gain
    input_grad = factor * (
        scaled
        - jnp.mean(scaled, axis=-1, keepdims=True)
        - unscaled * jnp.mean(scaled * unscaled, axis=-1, keepdims=True)
    )
    tokens_grad = (cotangent[0].astype(f32) + input_grad).astype(bf16)[None]

    up_links = lambda s: [
        (2 * i + j, 2 * i + 2 + j) for i in range(min(s, planes - 1)) for j in range(2)
    ]
    mirror = lambda links: [
        (2 * (planes - 1 - a // 2) + a % 2, 2 * (planes - 1 - b // 2) + b % 2) for a, b in links
    ]

    def sum_over_planes(block_of):
        rising = falling = None
        for s in range(1, planes):
            a = jnp.clip(planes - s + z, 0, planes - 1)
            b = jnp.clip(s - 1 - (planes - 1 - z), 0, planes - 1)
            term_a, term_b = block_of(a), block_of(b)
            if rising is not None:
                term_a = (term_a.astype(f32) + rising.astype(f32)).astype(bf16)
                term_b = (term_b.astype(f32) + falling.astype(f32)).astype(bf16)
            rising = lax.ppermute(term_a, "ctx", up_links(s))
            falling = lax.ppermute(term_b, "ctx", mirror(up_links(s)))
        return block_of(z).astype(f32) + rising.astype(f32) + falling.astype(f32)

    back_partial = lax.dot_general(
        mixed, plane_grad, contract_first, preferred_element_type=f32
    ).astype(bf16)
    back_sum = sum_over_planes(
        lambda i: lax.dynamic_slice(back_partial, (0, i * col_width), (5 * unit, col_width))
    ).astype(bf16)
    front_partial = lax.dot_general(
        normed, hidden_grad, contract_first, preferred_element_type=f32
    ).astype(bf16)
    front_rows = D // planes
    front_sum = sum_over_planes(
        lambda i: lax.dynamic_slice(front_partial, (i * front_rows, 0), (front_rows, 7 * unit))
    ).astype(bf16)

    back_grad = jnp.zeros((5 * unit, col_width), bf16)
    for match in plan.matchings:
        slot = np.zeros(ranks, np.int32)
        place = np.zeros(ranks, np.int32)
        links = []
        for owner, (rank, j) in match.items():
            slot[rank] = j
            place[owner] = plan.back_units[rank][j] % 5
            for i in range(planes):
                links.append((plan.device(i, rank % 2, rank // 2), owner * shards + i))
        block = lax.dynamic_slice(back_sum, (pick(slot, p) * unit, 0), (unit, col_width))
        block = lax.ppermute(block, both, links)
        back_grad = lax.dynamic_update_slice(back_grad, block, (pick(place, c_index) * unit, 0))
    back_grad = back_grad.astype(f32)

    natural = jnp.zeros((front_rows, (plan.per_shard + 2) * unit), bf16)
    start = 0
    for (units, wide), rounds in zip(plan.slots, plan.rounds):
        table = np.asarray(units)
        source, place = table // plan.per_shard, table % plan.per_shard
        block = front_sum[:, start : start + wide * unit]
        start += wide * unit
        local = source == np.arange(ranks) // 2
        where = np.where(local, place, plan.per_shard)
        natural = lax.dynamic_update_slice(natural, block, (0, pick(where, p) * unit))
        for one in rounds:
            where = np.full(ranks, plan.per_shard, np.int32)
            links = []
            for src, dst, core in one:
                where[2 * src + core] = place[2 * dst + core]
                links += [
                    (plan.device(i, core, dst), plan.device(i, core, src)) for i in range(planes)
                ]
            moved = lax.ppermute(block, both, links)
            natural = lax.dynamic_update_slice(natural, moved, (0, pick(where, p) * unit))
    natural = natural[:, : plan.per_shard * unit].reshape(2, front_rows // 2, -1)
    front_grad = at(natural, k).astype(f32) + swap_core(at(natural, 1 - k)).astype(f32)

    spread = (jnp.arange(7 * ranks)[:, None] == unit_table[None, :]).astype(f32)
    hidden_sum = jnp.sum(hidden_grad, axis=0, dtype=f32).reshape(7, unit)
    front_vector = jnp.sum(spread[:, :, None] * hidden_sum[None], axis=1).reshape(-1)
    vector_term = jnp.concatenate(
        [
            front_vector,
            jnp.sum(cotangent[0], axis=0, dtype=f32),
            jnp.sum(normed_grad * unscaled, axis=0),
            jnp.sum(normed_grad, axis=0),
        ]
    )
    vector_grad = lax.psum(vector_term, both)

    count_now = adam_step[0]
    back_new, back_first_new, back_second_new = adam_update(
        back_master, back_first, back_second, back_grad, learn_rates[1], count_now, weight_decay
    )
    front_new, front_first_new, front_second_new = adam_update(
        front_master, front_first, front_second, front_grad, learn_rates[0], count_now, weight_decay
    )
    vectors_new, vector_first_new, vector_second_new = adam_update(
        vectors, vector_first, vector_second, vector_grad, learn_rates[2], count_now, 0.0
    )

    def gather_rows(value):
        height = value.shape[0]
        out = jnp.zeros((2 * planes * height, value.shape[1]), value.dtype)

        def place(out, piece, plane):
            valid = (plane >= 0) & (plane < planes)
            where = jnp.where(valid, plane, z)
            mine, other = piece
            out = lax.dynamic_update_slice(out, mine, ((2 * where + k) * height, 0))
            return lax.dynamic_update_slice(out, other, ((2 * where + 1 - k) * height, 0))

        rising = falling = value
        pieces = []
        for s in range(1, planes):
            links = [(2 * i + j, 2 * i + 2 + j) for i in range(s - 1, planes - 1) for j in range(2)]
            rising = lax.ppermute(rising, "ctx", links)
            falling = lax.ppermute(falling, "ctx", mirror(links))
            pieces.append(((rising, swap_core(rising)), z - s))
            pieces.append(((falling, swap_core(falling)), z + s))
        for piece, plane in pieces:
            out = place(out, piece, plane)
        return place(out, (value, swap_core(value)), z)

    back_next = gather_rows(back_new.astype(bf16))
    front_next = gather_rows(front_new.astype(bf16))
    return (
        layer_out,
        tokens_grad,
        front_grad,
        back_grad,
        vector_grad,
        front_new,
        back_new,
        vectors_new,
        front_first_new,
        back_first_new,
        vector_first_new,
        front_second_new,
        back_second_new,
        vector_second_new,
        front_next,
        back_next,
    )


def solution(mesh):
    plan = Layout(mesh.shape["ctx"], mesh.shape["fsdp"])
    tokens_spec = P("fsdp", "ctx", None)
    cols, owned, same = P(None, "fsdp"), P("ctx", "fsdp"), P()
    in_specs = (
        (tokens_spec, tokens_spec, P("fsdp", None), same, cols, cols)
        + (owned,) * 6
        + (same,) * 5
    )
    out_specs = (
        (tokens_spec, tokens_spec, owned, owned, same)
        + (owned, owned, same) * 3
        + (cols, cols)
    )
    return jax.shard_map(
        functools.partial(per_device, plan=plan),
        mesh=mesh,
        in_specs=in_specs,
        out_specs=out_specs,
        check_vma=False,
    )
```

time: 2670 us -> 1190 us (0.45)
  waiting for transfers between devices: 2340 us -> 452 us
  starting transfers between devices: 1.01 us -> 302 us
  matrix products: 169 us -> 57.3 us
  local copies, waits for them, and re-layouts: 82.6 us -> 164 us
  other arithmetic: 52.4 us -> 111 us
  between operations: 15.8 us -> 59.2 us
    all_gather x6 -> x2, waiting for transfers between devices: 1140 us -> 39.8 us  [gather_plane(): mine = lax.all_gather(value, 'fsdp')]
    reduce_scatter x4 -> x0, waiting for transfers between devices: 724 us -> none  [the longest x1 563 us: per_device(): lax.psum_scatter(lax.dot_general(normed_low, hidden_grad, contract_first,...]
    unnamed x13 -> x3, waiting for transfers between devices: 374 us -> 0.71 us
    ppermute x0 -> x86, starting transfers between devices: none -> 302 us  [the longest x9 64.1 us: to_shard(): return lax.ppermute(value, 'fsdp', [(i, i ^ step) for i in range(shards)])]
    ppermute x0 -> x86, waiting for transfers between devices: none -> 281 us  [the longest x6 85.1 us: gather_rows(): falling = lax.ppermute(falling, 'ctx', mirror(links))]
    dot_general x20 -> x7, matrix products: 169 us -> 57.3 us  [the longest x1 12.2 us: per_device(): lax.dot_general(hidden_grad, weight_local, contract_last, preferred_eleme...]
    dynamic_slice x17 -> x50, local copies, waits for them, and re-layouts: 13 us -> 55.4 us  [the longest x45 33.1 us: pick(): return jnp.asarray(np.asarray(table, np.int32))[index]]
    dynamic_update_slice x4 -> x50, local copies, waits for them, and re-layouts: 22.2 us -> 58.1 us  [the longest x14 29.5 us: place(): out = lax.dynamic_update_slice(out, mine, ((2 * where + k) * height, 0))]
  transfers between devices with their start and end apart: 12 -> 89, of which waited for: 12 -> 22; matrix products, arithmetic and copies ran while one was open for 8% -> 24% of each run, Pallas kernels for 0% -> 0%
where the time goes in v1:
time: 1190 us; the launch traced here: 1180 us
  waiting for transfers between devices  452 us (38%)
  starting transfers between devices  302 us (25%)
  local copies, waits for them, and re-layouts  164 us (14%)
  other arithmetic  111 us (9%)
  between operations  59.2 us (5%)
  matrix products  57.3 us (5%)
  Pallas kernels  26.5 us (2%)
    psum x1, waiting for transfers between devices, per_device(): vector_grad = lax.psum(vector_term, both)  130 us
    ppermute x6, waiting for transfers between devices, gather_rows(): falling = lax.ppermute(falling, 'ctx', mirror(links))  85.1 us
    ppermute x9, starting transfers between devices, to_shard(): return lax.ppermute(value, 'fsdp', [(i, i ^ step) for i in range(shards)])  64.1 us
    ppermute x5, starting transfers between devices, per_device(): block = lax.ppermute(block, both, links)  57.4 us
    ppermute x6, waiting for transfers between devices, sum_over_planes(): rising = lax.ppermute(term_a, 'ctx', up_links(s))  50.7 us
    ppermute x6, starting transfers between devices, sum_over_planes(): rising = lax.ppermute(term_a, 'ctx', up_links(s))  48.6 us
    ppermute x9, waiting for transfers between devices, to_plane(): lax.ppermute(value, 'ctx', [(2 * i + j, 2 * (i ^ step) + j) for i in rang...  48.1 us
    ppermute x9, waiting for transfers between devices, to_shard(): return lax.ppermute(value, 'fsdp', [(i, i ^ step) for i in range(shards)])  41 us
  transfers between devices with their start and end apart: 89, of which 22 were waited for; matrix products, arithmetic and copies ran while one was open for 24% of the time, Pallas kernels for 0%

profile of v1, /device:TPU:0, one launch (start us, length us, event | category | flops | bytes accessed | tf_op | source)
XLA Modules:
  0.0 1181.1 jit_solution(10497025138564232550)
XLA Ops:
  8.0 39.8 %all-gather.5.cloned.1.call-done = bf16[4,128,2048]{2,1,0:T(8,128)(2,1)} async-done(((bf16[1,128,2048]{2,1,0:T(8,128)(2,1)}), bf16[4,128,2048]{2,1,0:T(8,128)(2,1)}) %all-gather.5.cloned.1.call-update) | async-done | bytes 2097168 | tf_op jit(solution)/shard_map/all_gather | solution.py:290
  66.4 8.1 all-gather.1
  86.8 11.9 %constant_dynamic-slice_fusion.19 = (bf16[2048,256]{1,0:T(8,128)(2,1)}, bf16[2048,256]{1,0:T(8,128)(2,1)}, bf16[2048,256]{1,0:T(8,128)(2,1)}, bf16[2048,256]{1,0...) fusion(bf16[2048,3584]{1,0:T(8,128)(2,1)} %param.79, ...), kind=kLoop, calls=%fused_computation.279 | loop fusion | bytes 16777248 | tf_op jit(solution)/shard_map/dynamic_slice | solution.py:331
  131.7 18.0 %collective-permute-done.1 = bf16[2048,256]{1,0:T(8,128)(2,1)} collective-permute-done((bf16[2048,256]{1,0:T(8,128)(2,1)S(1)}, bf16[2048,256]{1,0:T(8,128)(2,1)}, u32[]{:S(2)}, u32[]{:S(2)}) %collective-permute-start.1) | collective-permute-done | bytes 1048608 | tf_op jit(solution)/shard_map/ppermute | solution.py:332
  177.6 7.8 collective-permute-start.22
  218.2 10.7 collective-permute-start.13
  232.5 9.3 collective-permute-done.10
  295.1 29.4 %collective-permute-done.14 = bf16[1280,512]{1,0:T(8,128)(2,1)} collective-permute-done((bf16[1280,512]{1,0:T(8,128)(2,1)}, bf16[1280,512]{1,0:T(8,128)(2,1)}, u32[]{:S(2)}, u32[]{:S(2)}) %collective-permute-start.14) | collective-permute-done | bytes 1310752 | tf_op jit(solution)/shard_map/ppermute | solution.py:282
  357.1 26.5 %shard_map.792 = (bf16[1024,256]{1,0:T(8,128)(2,1)}, f32[1024,256]{1,0:T(8,128)}, f32[1024,256]{1,0:T(8,128)}, f32[1024,256]{1,0:T(8,128)}) custom-call(bf16[1024,256]{1,0:T(8,128)(2,1)} %get-tuple-element.160.q_ref, bf16[1024,256]{1,0:T(8,128)(2,1)} %get-tuple-element.159.k_ref, bf16[1024,256]{1,0:T(8,128)(2,1)} %get-tuple-element.158.v_ref, ...), custom_call_target="tpu_custom_call" | custom-call | flops 3758096384 | bytes 5242880 | tf_op jit(solution)/shard_map/pallas_call | solution.py:196
  400.2 8.3 fusion.8
  412.5 29.0 %collective-permute-done.20 = bf16[256,1024]{1,0:T(8,128)(2,1)S(1)} collective-permute-done((bf16[256,1024]{1,0:T(8,128)(2,1)S(1)}, bf16[256,1024]{1,0:T(8,128)(2,1)S(1)}, u32[]{:S(2)}, u32[]{:S(2)}) %collective-permute-start.20) | collective-permute-done | bytes 524320 | tf_op jit(solution)/shard_map/ppermute | solution.py:285
  442.0 8.6 convolution_convert_fusion.1
  471.8 12.2 %fusion.106 = f32[1024,2048]{1,0:T(8,128)} fusion(bf16[2048,1792]{1,0:T(8,128)(2,1)} %get-tuple-element.73, bf16[256,1024]{1,0:T(8,128)(2,1)S(1)} %get-tuple-element.144, bf16[256,1024]{1,0:T(8,128)(2,1)} %copy-done.29, bf16[256,1024]{1,0:T(8,128)(2,1)} %copy-done.31, bf16[256,1024]{1,0:T(8,128)(2,1)S(1)} %get-tuple-element.143, ...), kind=kOutput, calls=%fused_computation.322 | convolution fusion | flops 7534542848 | bytes 19922944 | tf_op jit(solution)/shard_map/dot_general | solution.py:443
  484.0 36.6 %collective-permute-done.49 = bf16[1280,512]{1,0:T(8,128)(2,1)} collective-permute-done((bf16[1280,512]{1,0:T(8,128)(2,1)}, bf16[1280,512]{1,0:T(8,128)(2,1)}, u32[]{:S(2)}, u32[]{:S(2)}) %collective-permute-start.49) | collective-permute-done | bytes 1310752 | tf_op jit(solution)/shard_map/ppermute | solution.py:470
  539.6 11.5 fusion.103
  555.5 11.7 convert_reduce_fusion
  581.9 14.1 %collective-permute-done.33 = bf16[512,1792]{1,0:T(8,128)(2,1)} collective-permute-done((bf16[512,1792]{1,0:T(8,128)(2,1)}, bf16[512,1792]{1,0:T(8,128)(2,1)}, u32[]{:S(2)}, u32[]{:S(2)}) %collective-permute-start.33) | collective-permute-done | bytes 1835040 | tf_op jit(solution)/shard_map/ppermute | solution.py:470
  636.4 23.1 %collective-permute-start.34 = (bf16[512,1792]{1,0:T(8,128)(2,1)S(1)}, bf16[512,1792]{1,0:T(8,128)(2,1)S(1)}, u32[]{:S(2)}, u32[]{:S(2)}) collective-permute-start(bf16[512,1792]{1,0:T(8,128)(2,1)S(1)} %copy-done.35), channel_id=1, source_target_pairs={{0,8},{4,12},{8,16},{12,20},{16,24},{20,28},{1,9},{5,13},{9,17},{1... | collective-permute-start | bytes 5505032 | tf_op jit(solution)/shard_map/ppermute | solution.py:470
  666.7 21.1 %collective-permute-start.55 = (bf16[256,512]{1,0:T(8,128)(2,1)S(1)}, bf16[256,512]{1,0:T(8,128)(2,1)S(1)}, u32[]{:S(2)}, u32[]{:S(2)}) collective-permute-start(bf16[256,512]{1,0:T(8,128)(2,1)S(1)} %get-tuple-element.169), channel_id=1, source_target_pairs={{0,0},{8,1},{16,2},{24,3},{4,16},{12,17},{20,18},{28,19},{3,20},{1... | collective-permute-start | bytes 786440 | tf_op jit(solution)/shard_map/ppermute | solution.py:499
  694.2 31.6 %collective-permute-start.26 = (bf16[128,2048]{1,0:T(8,128)(2,1)S(1)}, bf16[128,2048]{1,0:T(8,128)(2,1)S(1)}, u32[]{:S(2)}, u32[]{:S(2)}) collective-permute-start(bf16[128,2048]{1,0:T(8,128)(2,1)S(1)} %get-tuple-element.128), channel_id=1, source_target_pairs={{0,2},{1,3},{2,0},{3,1},{4,6},{5,7},{6,4},{7,5},{8,10},{9,11},{10,... | collective-permute-start | bytes 1572872 | tf_op jit(solution)/shard_map/ppermute | solution.py:282
  725.9 18.4 %collective-permute-start.57 = (bf16[256,512]{1,0:T(8,128)(2,1)S(1)}, bf16[256,512]{1,0:T(8,128)(2,1)S(1)}, u32[]{:S(2)}, u32[]{:S(2)}) collective-permute-start(bf16[256,512]{1,0:T(8,128)(2,1)S(1)} %get-tuple-element.167), channel_id=1, source_target_pairs={{0,16},{8,17},{16,18},{24,19},{4,0},{12,1},{20,2},{28,3},{6,4},{14... | collective-permute-start | bytes 786440 | tf_op jit(solution)/shard_map/ppermute | solution.py:499
  765.1 13.0 %collective-permute-done.38 = bf16[512,256]{1,0:T(8,128)(2,1)S(1)} collective-permute-done((bf16[512,256]{1,0:T(8,128)(2,1)S(1)}, bf16[512,256]{1,0:T(8,128)(2,1)S(1)}, u32[]{:S(2)}, u32[]{:S(2)}) %collective-permute-start.38) | collective-permute-done | bytes 262176 | tf_op jit(solution)/shard_map/ppermute | solution.py:521
  778.1 8.3 collective-permute-start.41
  798.4 9.4 collective-permute-start.46
  823.4 8.5 collective-permute-start.25
  832.6 11.5 collective-permute-done.25
  851.7 130.2 %all-reduce.2.cloned.1.call-done = f32[20480]{0:T(1024)} async-done(((f32[20480]{0:T(1024)}), f32[20480]{0:T(1024)}) %all-reduce.2.cloned.1.call-update) | async-done | bytes 81936 | tf_op jit(solution)/shard_map/psum | solution.py:537
  1020.8 11.4 collective-permute-done.83
  1038.6 13.2 %collective-permute-done.60 = bf16[256,3584]{1,0:T(8,128)(2,1)} collective-permute-done((bf16[256,3584]{1,0:T(8,128)(2,1)S(1)}, bf16[256,3584]{1,0:T(8,128)(2,1)}, u32[]{:S(2)}, u32[]{:S(2)}) %collective-permute-start.60) | collective-permute-done | bytes 1835040 | tf_op jit(solution)/shard_map/ppermute | solution.py:565
  1053.9 17.5 %collective-permute-done.62 = bf16[256,3584]{1,0:T(8,128)(2,1)} collective-permute-done((bf16[256,3584]{1,0:T(8,128)(2,1)S(1)}, bf16[256,3584]{1,0:T(8,128)(2,1)}, u32[]{:S(2)}, u32[]{:S(2)}) %collective-permute-start.62) | collective-permute-done | bytes 1835040 | tf_op jit(solution)/shard_map/ppermute | solution.py:566
  1088.9 26.4 %collective-permute-done.66 = bf16[256,3584]{1,0:T(8,128)(2,1)} collective-permute-done((bf16[256,3584]{1,0:T(8,128)(2,1)}, bf16[256,3584]{1,0:T(8,128)(2,1)}, u32[]{:S(2)}, u32[]{:S(2)}) %collective-permute-start.66) | collective-permute-done | bytes 1835040 | tf_op jit(solution)/shard_map/ppermute | solution.py:566
  1128.5 29.8 %collective-permute-done.70 = bf16[256,3584]{1,0:T(8,128)(2,1)S(1)} collective-permute-done((bf16[256,3584]{1,0:T(8,128)(2,1)}, bf16[256,3584]{1,0:T(8,128)(2,1)S(1)}, u32[]{:S(2)}, u32[]{:S(2)}) %collective-permute-start.70) | collective-permute-done | bytes 1835040 | tf_op jit(solution)/shard_map/ppermute | solution.py:566
  (588 shorter events, 454.8 us)
Async XLA Ops:
  7.9 280.3 %all-gather.7.cloned.1.call-start = ((), (), s32[]{:S(2)}) async-start(), calls=%async_computation.2 | async-start | bytes 2621440 | tf_op jit(solution)/shard_map/all_gather | solution.py:290
  120.1 57.5 %collective-permute-start.4 = (bf16[2048,256]{1,0:T(8,128)(2,1)}, bf16[2048,256]{1,0:T(8,128)(2,1)}, u32[]{:S(2)}, u32[]{:S(2)}) collective-permute-start(bf16[2048,256]{1,0:T(8,128)(2,1)} %get-tuple-element.89), channel_id=1, source_target_pairs={{0,1},{8,9},{16,17},{24,25},{1,3},{9,11},{17,19},{25,27},{4,5},{12... | collective-permute-start | bytes 3145736 | tf_op jit(solution)/shard_map/ppermute | solution.py:332
  125.9 59.6 %collective-permute-start.5 = (bf16[2048,256]{1,0:T(8,128)(2,1)}, bf16[2048,256]{1,0:T(8,128)(2,1)}, u32[]{:S(2)}, u32[]{:S(2)}) collective-permute-start(bf16[2048,256]{1,0:T(8,128)(2,1)} %get-tuple-element.88), channel_id=1, source_target_pairs={{0,2},{8,10},{16,18},{24,26},{4,6},{12,14},{20,22},{28,30}} | collective-permute-start | bytes 3145736 | tf_op jit(solution)/shard_map/ppermute | solution.py:332
  130.1 58.6 %collective-permute-start.8 = (bf16[2048,256]{1,0:T(8,128)(2,1)}, bf16[2048,256]{1,0:T(8,128)(2,1)}, u32[]{:S(2)}, u32[]{:S(2)}) collective-permute-start(bf16[2048,256]{1,0:T(8,128)(2,1)} %get-tuple-element.86), channel_id=1, source_target_pairs={{1,3},{9,11},{17,19},{25,27},{5,7},{13,15},{21,23},{29,31}} | collective-permute-start | bytes 3145736 | tf_op jit(solution)/shard_map/ppermute | solution.py:332
  170.6 811.2 %all-reduce.2.cloned.1.call-start = ((), (), s32[]{:S(2)}) async-start(), calls=%async_computation.1 | async-start | bytes 163840 | tf_op jit(solution)/shard_map/psum | solution.py:537
  177.6 150.0 %collective-permute-start.22 = (bf16[2048,512]{1,0:T(8,128)(2,1)}, bf16[2048,512]{1,0:T(8,128)(2,1)}, u32[]{:S(2)}, u32[]{:S(2)}) collective-permute-start(bf16[2048,512]{1,0:T(8,128)(2,1)} %get-tuple-element.84), channel_id=1, source_target_pairs={{2,0},{10,8},{18,16},{26,24},{6,4},{14,12},{22,20},{30,28},{7,5},{... | collective-permute-start | bytes 6291464 | tf_op jit(solution)/shard_map/ppermute | solution.py:332
  218.2 74.0 %collective-permute-start.13 = (bf16[1280,512]{1,0:T(8,128)(2,1)}, bf16[1280,512]{1,0:T(8,128)(2,1)}, u32[]{:S(2)}, u32[]{:S(2)}) collective-permute-start(bf16[1280,512]{1,0:T(8,128)(2,1)} %get-tuple-element.95), channel_id=1, source_target_pairs={{0,1},{1,0},{2,3},{3,2},{4,5},{5,4},{6,7},{7,6},{8,9},{9,8},{10,11... | collective-permute-start | bytes 3932168 | tf_op jit(solution)/shard_map/ppermute | solution.py:282
  228.9 59.3 %collective-permute-start.9 = (bf16[256,768]{1,0:T(8,128)(2,1)}, bf16[256,768]{1,0:T(8,128)(2,1)}, u32[]{:S(2)}, u32[]{:S(2)}) collective-permute-start(bf16[256,768]{1,0:T(8,128)(2,1)} %get-tuple-element.164), channel_id=1, source_target_pairs={{0,8},{4,12},{8,0},{12,4},{16,24},{20,28},{24,16},{28,20},{1,9},{5... | collective-permute-start | bytes 1179656 | tf_op jit(solution)/shard_map/ppermute | solution.py:285
  230.2 94.3 %collective-permute-start.14 = (bf16[1280,512]{1,0:T(8,128)(2,1)}, bf16[1280,512]{1,0:T(8,128)(2,1)}, u32[]{:S(2)}, u32[]{:S(2)}) collective-permute-start(bf16[1280,512]{1,0:T(8,128)(2,1)} %get-tuple-element.94), channel_id=1, source_target_pairs={{0,2},{1,3},{2,0},{3,1},{4,6},{5,7},{6,4},{7,5},{8,10},{9,11},{10,... | collective-permute-start | bytes 3932168 | tf_op jit(solution)/shard_map/ppermute | solution.py:282
  241.7 84.4 %collective-permute-start.15 = (bf16[1280,512]{1,0:T(8,128)(2,1)}, bf16[1280,512]{1,0:T(8,128)(2,1)}, u32[]{:S(2)}, u32[]{:S(2)}) collective-permute-start(bf16[1280,512]{1,0:T(8,128)(2,1)} %get-tuple-element.93), channel_id=1, source_target_pairs={{0,3},{1,2},{2,1},{3,0},{4,7},{5,6},{6,5},{7,4},{8,11},{9,10},{10,... | collective-permute-start | bytes 3932168 | tf_op jit(solution)/shard_map/ppermute | solution.py:282
  288.2 46.3 %collective-permute-start.12 = (bf16[4,128,2048]{2,1,0:T(8,128)(2,1)}, bf16[4,128,2048]{2,1,0:T(8,128)(2,1)S(1)}, u32[]{:S(2)}, u32[]{:S(2)}) collective-permute-start(bf16[4,128,2048]{2,1,0:T(8,128)(2,1)} %bitcast.291), channel_id=1, source_target_pairs={{0,4},{4,0},{8,12},{12,8},{16,20},{20,16},{24,28},{28,24},{1,5},{5... | collective-permute-start | bytes 6291464 | tf_op jit(solution)/shard_map/ppermute | solution.py:279
  292.1 54.8 %collective-permute-start.23 = (bf16[2048,512]{1,0:T(8,128)(2,1)S(1)}, bf16[2048,512]{1,0:T(8,128)(2,1)S(1)}, u32[]{:S(2)}, u32[]{:S(2)}) collective-permute-start(bf16[2048,512]{1,0:T(8,128)(2,1)S(1)} %get-tuple-element.83), channel_id=1, source_target_pairs={{2,0},{10,8},{18,16},{26,24},{3,1},{11,9},{19,17},{27,25},{7,4},{1... | collective-permute-start | bytes 6291464 | tf_op jit(solution)/shard_map/ppermute | solution.py:332
  452.7 76.0 %collective-permute-start.32 = (bf16[512,1792]{1,0:T(8,128)(2,1)}, bf16[512,1792]{1,0:T(8,128)(2,1)}, u32[]{:S(2)}, u32[]{:S(2)}) collective-permute-start(bf16[512,1792]{1,0:T(8,128)(2,1)} %get-tuple-element.115), channel_id=1, source_target_pairs={{0,8},{4,12},{1,9},{5,13},{2,10},{6,14},{3,11},{7,15}} | collective-permute-start | bytes 5505032 | tf_op jit(solution)/shard_map/ppermute | solution.py:470
  455.5 126.3 %collective-permute-start.35 = (bf16[512,1792]{1,0:T(8,128)(2,1)}, bf16[512,1792]{1,0:T(8,128)(2,1)}, u32[]{:S(2)}, u32[]{:S(2)}) collective-permute-start(bf16[512,1792]{1,0:T(8,128)(2,1)} %get-tuple-element.116), channel_id=1, source_target_pairs={{24,16},{28,20},{25,17},{29,21},{26,18},{30,22},{27,19},{31,23}} | collective-permute-start | bytes 5505032 | tf_op jit(solution)/shard_map/ppermute | solution.py:471
  467.5 53.1 %collective-permute-start.49 = (bf16[1280,512]{1,0:T(8,128)(2,1)}, bf16[1280,512]{1,0:T(8,128)(2,1)}, u32[]{:S(2)}, u32[]{:S(2)}) collective-permute-start(bf16[1280,512]{1,0:T(8,128)(2,1)} %get-tuple-element.119), channel_id=1, source_target_pairs={{0,8},{4,12},{1,9},{5,13},{2,10},{6,14},{3,11},{7,15}} | collective-permute-start | bytes 3932168 | tf_op jit(solution)/shard_map/ppermute | solution.py:470
  470.0 100.1 %collective-permute-start.52 = (bf16[1280,512]{1,0:T(8,128)(2,1)}, bf16[1280,512]{1,0:T(8,128)(2,1)}, u32[]{:S(2)}, u32[]{:S(2)}) collective-permute-start(bf16[1280,512]{1,0:T(8,128)(2,1)} %get-tuple-element.120), channel_id=1, source_target_pairs={{24,16},{28,20},{25,17},{29,21},{26,18},{30,22},{27,19},{31,23}} | collective-permute-start | bytes 3932168 | tf_op jit(solution)/shard_map/ppermute | solution.py:471
  523.5 46.8 %collective-permute-start.50 = (bf16[1280,512]{1,0:T(8,128)(2,1)}, bf16[1280,512]{1,0:T(8,128)(2,1)}, u32[]{:S(2)}, u32[]{:S(2)}) collective-permute-start(bf16[1280,512]{1,0:T(8,128)(2,1)} %add_convert_fusion.9), channel_id=1, source_target_pairs={{0,8},{4,12},{8,16},{12,20},{1,9},{5,13},{9,17},{13,21},{2,10},{6,... | collective-permute-start | bytes 3932168 | tf_op jit(solution)/shard_map/ppermute | solution.py:470
  532.0 64.0 %collective-permute-start.33 = (bf16[512,1792]{1,0:T(8,128)(2,1)}, bf16[512,1792]{1,0:T(8,128)(2,1)}, u32[]{:S(2)}, u32[]{:S(2)}) collective-permute-start(bf16[512,1792]{1,0:T(8,128)(2,1)} %add_convert_fusion.4), channel_id=1, source_target_pairs={{0,8},{4,12},{8,16},{12,20},{1,9},{5,13},{9,17},{13,21},{2,10},{6,... | collective-permute-start | bytes 5505032 | tf_op jit(solution)/shard_map/ppermute | solution.py:470
  555.1 53.6 %collective-permute-start.28 = (bf16[4,128,2048]{2,1,0:T(8,128)(2,1)}, bf16[4,128,2048]{2,1,0:T(8,128)(2,1)}, u32[]{:S(2)}, u32[]{:S(2)}) collective-permute-start(bf16[4,128,2048]{2,1,0:T(8,128)(2,1)} %fusion.27), channel_id=1, source_target_pairs={{0,4},{4,0},{8,12},{12,8},{16,20},{20,16},{24,28},{28,24},{1,5},{5... | collective-permute-start | bytes 6291464 | tf_op jit(solution)/shard_map/ppermute | solution.py:279
  570.1 56.8 %collective-permute-start.24 = (bf16[4,128,2048]{2,1,0:T(8,128)(2,1)S(1)}, bf16[4,128,2048]{2,1,0:T(8,128)(2,1)S(1)}, u32[]{:S(2)}, u32[]{:S(2)}) collective-permute-start(bf16[4,128,2048]{2,1,0:T(8,128)(2,1)S(1)} %fusion.26), channel_id=1, source_target_pairs={{0,4},{4,0},{8,12},{12,8},{16,20},{20,16},{24,28},{28,24},{1,5},{5... | collective-permute-start | bytes 6291464 | tf_op jit(solution)/shard_map/ppermute | solution.py:279
  616.6 47.9 %collective-permute-start.51 = (bf16[1280,512]{1,0:T(8,128)(2,1)}, bf16[1280,512]{1,0:T(8,128)(2,1)}, u32[]{:S(2)}, u32[]{:S(2)}) collective-permute-start(bf16[1280,512]{1,0:T(8,128)(2,1)} %get-tuple-element.117), channel_id=1, source_target_pairs={{0,8},{4,12},{8,16},{12,20},{16,24},{20,28},{1,9},{5,13},{9,17},{1... | collective-permute-start | bytes 3932168 | tf_op jit(solution)/shard_map/ppermute | solution.py:470
  636.4 107.9 %collective-permute-start.34 = (bf16[512,1792]{1,0:T(8,128)(2,1)S(1)}, bf16[512,1792]{1,0:T(8,128)(2,1)S(1)}, u32[]{:S(2)}, u32[]{:S(2)}) collective-permute-start(bf16[512,1792]{1,0:T(8,128)(2,1)S(1)} %copy-done.35), channel_id=1, source_target_pairs={{0,8},{4,12},{8,16},{12,20},{16,24},{20,28},{1,9},{5,13},{9,17},{1... | collective-permute-start | bytes 5505032 | tf_op jit(solution)/shard_map/ppermute | solution.py:470
  659.5 90.6 %collective-permute-start.37 = (bf16[512,1792]{1,0:T(8,128)(2,1)S(1)}, bf16[512,1792]{1,0:T(8,128)(2,1)S(1)}, u32[]{:S(2)}, u32[]{:S(2)}) collective-permute-start(bf16[512,1792]{1,0:T(8,128)(2,1)S(1)} %add_convert_fusion.1), channel_id=1, source_target_pairs={{24,16},{28,20},{16,8},{20,12},{8,0},{12,4},{25,17},{29,21},{17,9}... | collective-permute-start | bytes 5505032 | tf_op jit(solution)/shard_map/ppermute | solution.py:471
  661.0 171.4 %collective-permute-start.27 = (bf16[128,2048]{1,0:T(8,128)(2,1)S(1)}, bf16[128,2048]{1,0:T(8,128)(2,1)S(1)}, u32[]{:S(2)}, u32[]{:S(2)}) collective-permute-start(bf16[128,2048]{1,0:T(8,128)(2,1)S(1)} %get-tuple-element.127), channel_id=1, source_target_pairs={{0,3},{1,2},{2,1},{3,0},{4,7},{5,6},{6,5},{7,4},{8,11},{9,10},{10,... | collective-permute-start | bytes 1572872 | tf_op jit(solution)/shard_map/ppermute | solution.py:282
  694.2 138.4 %collective-permute-start.26 = (bf16[128,2048]{1,0:T(8,128)(2,1)S(1)}, bf16[128,2048]{1,0:T(8,128)(2,1)S(1)}, u32[]{:S(2)}, u32[]{:S(2)}) collective-permute-start(bf16[128,2048]{1,0:T(8,128)(2,1)S(1)} %get-tuple-element.128), channel_id=1, source_target_pairs={{0,2},{1,3},{2,0},{3,1},{4,6},{5,7},{6,4},{7,5},{8,10},{9,11},{10,... | collective-permute-start | bytes 1572872 | tf_op jit(solution)/shard_map/ppermute | solution.py:282
  832.5 164.6 %collective-permute-start.48 = (bf16[256,3584]{1,0:T(8,128)(2,1)S(1)}, bf16[256,3584]{1,0:T(8,128)(2,1)}, u32[]{:S(2)}, u32[]{:S(2)}) collective-permute-start(bf16[256,3584]{1,0:T(8,128)(2,1)S(1)} %dynamic-slice_bitcast_fusion), channel_id=1, source_target_pairs={{0,4},{4,0},{8,12},{12,8},{16,20},{20,16},{24,28},{28,24},{1,5},{5... | collective-permute-start | bytes 5505032 | tf_op jit(solution)/shard_map/ppermute | solution.py:279
  846.1 147.2 %collective-permute-start.74 = (bf16[1280,512]{1,0:T(8,128)(2,1)}, bf16[1280,512]{1,0:T(8,128)(2,1)}, u32[]{:S(2)}, u32[]{:S(2)}) collective-permute-start(bf16[1280,512]{1,0:T(8,128)(2,1)} %collective-permute-done.73), channel_id=1, source_target_pairs={{0,4},{4,0},{8,12},{12,8},{16,20},{20,16},{24,28},{28,24},{1,5},{5... | collective-permute-start | bytes 3932168 | tf_op jit(solution)/shard_map/ppermute | solution.py:279
  847.4 145.9 %collective-permute-start.77 = (bf16[1280,512]{1,0:T(8,128)(2,1)}, bf16[1280,512]{1,0:T(8,128)(2,1)}, u32[]{:S(2)}, u32[]{:S(2)}) collective-permute-start(bf16[1280,512]{1,0:T(8,128)(2,1)} %collective-permute-done.73), channel_id=1, source_target_pairs={{8,16},{12,20},{16,24},{20,28},{9,17},{13,21},{17,25},{21,29},{10,... | collective-permute-start | bytes 3932168 | tf_op jit(solution)/shard_map/ppermute | solution.py:565
  849.4 144.8 %collective-permute-start.79 = (bf16[1280,512]{1,0:T(8,128)(2,1)}, bf16[1280,512]{1,0:T(8,128)(2,1)}, u32[]{:S(2)}, u32[]{:S(2)}) collective-permute-start(bf16[1280,512]{1,0:T(8,128)(2,1)} %collective-permute-done.75), channel_id=1, source_target_pairs={{16,8},{20,12},{8,0},{12,4},{17,9},{21,13},{9,1},{13,5},{18,10},{2... | collective-permute-start | bytes 3932168 | tf_op jit(solution)/shard_map/ppermute | solution.py:566
  1013.4 58.0 %collective-permute-start.62 = (bf16[256,3584]{1,0:T(8,128)(2,1)S(1)}, bf16[256,3584]{1,0:T(8,128)(2,1)}, u32[]{:S(2)}, u32[]{:S(2)}) collective-permute-start(bf16[256,3584]{1,0:T(8,128)(2,1)S(1)} %get-tuple-element.64), channel_id=1, source_target_pairs={{24,16},{28,20},{16,8},{20,12},{8,0},{12,4},{25,17},{29,21},{17,9}... | collective-permute-start | bytes 5505032 | tf_op jit(solution)/shard_map/ppermute | solution.py:566
  1077.2 93.4 %collective-permute-start.72 = (bf16[256,3584]{1,0:T(8,128)(2,1)S(1)}, bf16[256,3584]{1,0:T(8,128)(2,1)}, u32[]{:S(2)}, u32[]{:S(2)}) collective-permute-start(bf16[256,3584]{1,0:T(8,128)(2,1)S(1)} %get-tuple-element.64), channel_id=1, source_target_pairs={{0,4},{4,0},{8,12},{12,8},{16,20},{20,16},{24,28},{28,24},{1,5},{5... | collective-permute-start | bytes 5505032 | tf_op jit(solution)/shard_map/ppermute | solution.py:279
  1088.1 70.2 %collective-permute-start.65 = (bf16[256,3584]{1,0:T(8,128)(2,1)}, bf16[256,3584]{1,0:T(8,128)(2,1)S(1)}, u32[]{:S(2)}, u32[]{:S(2)}) collective-permute-start(bf16[256,3584]{1,0:T(8,128)(2,1)} %collective-permute-done.64), channel_id=1, source_target_pairs={{0,4},{4,0},{8,12},{12,8},{16,20},{20,16},{24,28},{28,24},{1,5},{5... | collective-permute-start | bytes 5505032 | tf_op jit(solution)/shard_map/ppermute | solution.py:279
  (154 other events, 4876.1 us)
Sparse Core Ops, SparseCore 0:
  9.8 37.8 all-gather.4
  170.8 54.5 all-gather.6
  851.5 130.3 all-reduce.1

commit v2 on v1

--- a/solution.py
+++ b/solution.py
@@ -119,6 +119,13 @@
     return jnp.asarray(np.asarray(table, np.int32))[index]
 
 
+def normalize(values):
+    values = values.astype(f32)
+    centered = values - jnp.mean(values, axis=-1, keepdims=True)
+    factor = lax.rsqrt(jnp.mean(centered * centered, axis=-1, keepdims=True) + norm_eps)
+    return centered * factor, factor
+
+
 def rotation_tables(positions, width):
     half = ROT // 2
     lane = np.arange(width) % HEAD_DIM
@@ -210,6 +217,326 @@
             bytes_accessed=20 * length * width,
         ),
     )(query, key, value, grad, positions[:, None], positions[None], segments[:, None], segments[None])
+
+
+MESH = pl.DeviceIdType.MESH
+
+
+def place_in_mesh():
+    c, f = lax.axis_index("ctx"), lax.axis_index("fsdp")
+    z, k = lax.div(c, 2), lax.rem(c, 2)
+    return c, f, z, k, 2 * f + k
+
+
+def bounce(source, buffer, target, sem):
+    one = pltpu.make_async_copy(source, buffer, sem)
+    one.start()
+    one.wait()
+    two = pltpu.make_async_copy(buffer, target, sem)
+    two.start()
+    two.wait()
+
+
+def gather_kernel(
+    plan, tok, doc, front, back, tok_out, doc_out, w_out, b_out,
+    w_buf, b_buf, tsend, trecv, csend, crecv, wsend, wrecv, bsend, brecv, dsend, drecv, lsem,
+):
+    shards, unit, ranks = plan.fsdp, plan.unit, plan.ranks
+    c, f, z, k, p = place_in_mesh()
+    other = c + 1 - 2 * k
+    width = D // shards
+
+    def cols(block):
+        return pl.ds(pl.multiple_of(block * width, 128), width)
+
+    def remote(src, dst, send, recv, device):
+        return pltpu.make_async_remote_copy(
+            src_ref=src, dst_ref=dst, send_sem=send, recv_sem=recv, device_id=device, device_id_type=MESH
+        )
+
+    def peer(step):
+        return lax.rem(f + step, shards)
+
+    def giver(step):
+        return lax.rem(f + shards - step, shards)
+
+    def send_tokens(step):
+        return remote(tok, tok_out.at[f, k], tsend.at[step], trecv.at[step], (c, peer(step)))
+
+    def get_tokens(step):
+        here = tok_out.at[giver(step), k]
+        return remote(here, here, tsend.at[step], trecv.at[step], (c, peer(step)))
+
+    def share(step):
+        here = tok_out.at[giver(step), k]
+        src = tok if step == 0 else here
+        return remote(src, here, csend.at[step], crecv.at[step], (other, f))
+
+    def get_share(step):
+        here = tok_out.at[giver(step), 1 - k]
+        return remote(here, here, csend.at[step], crecv.at[step], (other, f))
+
+    def rows_of(dst):
+        return pl.ds(pl.multiple_of((2 * dst + k) * unit, unit), unit)
+
+    def send_back(step):
+        return remote(
+            back.at[rows_of(peer(step)), :], b_out.at[:, cols(f)], bsend.at[step], brecv.at[step], (c, peer(step))
+        )
+
+    def get_back(step):
+        here = b_out.at[:, cols(giver(step))]
+        return remote(here, here, bsend.at[step], brecv.at[step], (c, peer(step)))
+
+    def send_doc(step):
+        return remote(doc, doc_out, dsend.at[step], drecv, (c, peer(step)))
+
+    weights = []
+    for slot in range(3):
+        units, _ = plan.slots[slot]
+        for dst in range(ranks):
+            src, at = units[dst] // plan.per_shard, units[dst] % plan.per_shard
+            weights.append((slot, dst, 2 * src + dst % 2, at))
+
+    def send_weight(slot, dst, at):
+        return remote(
+            front.at[:, pl.ds(at * unit, unit)],
+            w_out.at[:, pl.ds(slot * unit, unit)],
+            wsend.at[slot, dst // 2],
+            wrecv.at[slot],
+            (c, dst // 2),
+        )
+
+    own_tok = pltpu.make_async_copy(tok, tok_out.at[f, k], lsem.at[0])
+    own_doc = pltpu.make_async_copy(doc, doc_out, lsem.at[1])
+    for step in range(1, shards):
+        send_tokens(step).start()
+    share(0).start()
+    own_tok.start()
+    for step in range(1, shards):
+        send_back(step).start()
+
+    @pl.when(f == z)
+    def _():
+        own_doc.start()
+        for step in range(1, shards):
+            send_doc(step).start()
+
+    for slot, dst, src, at in weights:
+        if src != dst:
+
+            @pl.when(p == src)
+            def _(slot=slot, dst=dst, at=at):
+                send_weight(slot, dst, at).start()
+
+    for step in range(1, shards):
+        get_tokens(step).wait_recv()
+        share(step).start()
+    for slot, dst, src, at in weights:
+        if src == dst:
+
+            @pl.when(p == dst)
+            def _(slot=slot, at=at):
+                bounce(
+                    front.at[:, pl.ds(at * unit, unit)], w_buf, w_out.at[:, pl.ds(slot * unit, unit)], lsem.at[2]
+                )
+
+    bounce(back.at[rows_of(f), :], b_buf, b_out.at[:, cols(f)], lsem.at[3])
+    own_tok.wait()
+
+    @pl.when(f == z)
+    def _():
+        own_doc.wait()
+        for step in range(1, shards):
+            send_doc(step).wait_send()
+
+    @pl.when(f != z)
+    def _():
+        send_doc(1).wait_recv()
+
+    for step in range(shards):
+        get_share(step).wait_recv()
+        share(step).wait_send()
+    for step in range(1, shards):
+        send_tokens(step).wait_send()
+        send_back(step).wait_send()
+        get_back(step).wait_recv()
+    for slot, dst, src, at in weights:
+        if src != dst:
+
+            @pl.when(p == src)
+            def _(slot=slot, dst=dst, at=at):
+                send_weight(slot, dst, at).wait_send()
+
+            @pl.when(p == dst)
+            def _(slot=slot, dst=dst, at=at):
+                send_weight(slot, dst, at).wait_recv()
+
+
+def gather_first(plan, tokens, documents, front_weight, back_weight):
+    shards, unit = plan.fsdp, plan.unit
+    rows, length = tokens.shape[0], documents.shape[1]
+    vmem, anywhere = pl.BlockSpec(memory_space=pltpu.VMEM), pl.BlockSpec(memory_space=pl.ANY)
+    dma = pltpu.SemaphoreType.DMA
+    return pl.pallas_call(
+        functools.partial(gather_kernel, plan),
+        in_specs=[vmem, vmem, anywhere, anywhere],
+        out_specs=[anywhere] * 4,
+        out_shape=[
+            jax.ShapeDtypeStruct((shards, 2, rows, D), bf16),
+            jax.ShapeDtypeStruct((1, length), f32),
+            jax.ShapeDtypeStruct((D, 3 * unit), bf16),
+            jax.ShapeDtypeStruct((unit, D), bf16),
+        ],
+        scratch_shapes=[
+            pltpu.VMEM((D, unit), bf16),
+            pltpu.VMEM((unit, D // shards), bf16),
+            dma((shards,)),
+            dma((shards,)),
+            dma((shards,)),
+            dma((shards,)),
+            dma((3, shards)),
+            dma((3,)),
+            dma((shards,)),
+            dma((shards,)),
+            dma((shards,)),
+            dma(()),
+            dma((4,)),
+        ],
+        compiler_params=pltpu.CompilerParams(has_side_effects=True),
+    )(tokens, documents, front_weight, back_weight)
+
+
+def back_owner_kernel(plan, src, out, send, recv, lsem):
+    unit, ranks = plan.unit, plan.ranks
+    c, f, z, k, p = place_in_mesh()
+
+    def copy(j, owner, place):
+        return pltpu.make_async_remote_copy(
+            src_ref=src.at[pl.ds(j * unit, unit), :],
+            dst_ref=out.at[pl.ds(place * unit, unit), :],
+            send_sem=send.at[j],
+            recv_sem=recv.at[place],
+            device_id=(owner, z),
+            device_id_type=MESH,
+        )
+
+    blocks = [
+        (rank, j, plan.back_units[rank][j] // 5, plan.back_units[rank][j] % 5)
+        for rank in range(ranks)
+        for j in range(5)
+    ]
+    for rank, j, owner, place in blocks:
+
+        @pl.when((p == rank) & ~((c == owner) & (f == z)))
+        def _(j=j, owner=owner, place=place):
+            copy(j, owner, place).start()
+
+        @pl.when((p == rank) & (c == owner) & (f == z))
+        def _(j=j, place=place):
+            pltpu.make_async_copy(
+                src.at[pl.ds(j * unit, unit), :], out.at[pl.ds(place * unit, unit), :], lsem.at[place]
+            ).start()
+
+    for rank, j, owner, place in blocks:
+
+        @pl.when((p == rank) & ~((c == owner) & (f == z)))
+        def _(j=j, owner=owner, place=place):
+            copy(j, owner, place).wait_send()
+
+        @pl.when((c == owner) & ~((p == rank) & (f == z)))
+        def _(j=j, owner=owner, place=place):
+            copy(j, owner, place).wait_recv()
+
+        @pl.when((p == rank) & (c == owner) & (f == z))
+        def _(j=j, place=place):
+            pltpu.make_async_copy(
+                src.at[pl.ds(j * unit, unit), :], out.at[pl.ds(place * unit, unit), :], lsem.at[place]
+            ).wait()
+
+
+def back_to_owner(plan, value):
+    dma = pltpu.SemaphoreType.DMA
+    return pl.pallas_call(
+        functools.partial(back_owner_kernel, plan),
+        in_specs=[pl.BlockSpec(memory_space=pltpu.VMEM)],
+        out_specs=pl.BlockSpec(memory_space=pl.ANY),
+        out_shape=jax.ShapeDtypeStruct(value.shape, value.dtype),
+        scratch_shapes=[dma((5,)), dma((5,)), dma((5,))],
+        compiler_params=pltpu.CompilerParams(has_side_effects=True),
+    )(value)
+
+
+def front_owner_kernel(plan, src, out, send, recv, lsem):
+    unit, ranks = plan.unit, plan.ranks
+    c, f, z, k, p = place_in_mesh()
+    moves, start = [], 0
+    for slot, (units, wide) in enumerate(plan.slots):
+        for rank in range(ranks):
+            owner, place = units[rank] // plan.per_shard, units[rank] % plan.per_shard
+            moves.append((slot, rank, owner, place, start, wide))
+        start += wide
+
+    def copy(slot, owner, place, begin, wide, half):
+        return pltpu.make_async_remote_copy(
+            src_ref=src.at[half, :, pl.ds(begin * unit, wide * unit)],
+            dst_ref=out.at[:, pl.ds(place * unit, wide * unit)],
+            send_sem=send.at[slot, half],
+            recv_sem=recv.at[place],
+            device_id=(2 * z + half, owner),
+            device_id_type=MESH,
+        )
+
+    def local(place, begin, wide, half):
+        return pltpu.make_async_copy(
+            src.at[half, :, pl.ds(begin * unit, wide * unit)],
+            out.at[:, pl.ds(place * unit, wide * unit)],
+            lsem.at[place],
+        )
+
+    for slot, rank, owner, place, begin, wide in moves:
+        for half in range(2):
+            if 2 * owner + half == rank:
+
+                @pl.when(p == rank)
+                def _(place=place, begin=begin, wide=wide, half=half):
+                    local(place, begin, wide, half).start()
+
+            else:
+
+                @pl.when(p == rank)
+                def _(slot=slot, owner=owner, place=place, begin=begin, wide=wide, half=half):
+                    copy(slot, owner, place, begin, wide, half).start()
+
+    for slot, rank, owner, place, begin, wide in moves:
+        for half in range(2):
+            if 2 * owner + half == rank:
+
+                @pl.when(p == rank)
+                def _(place=place, begin=begin, wide=wide, half=half):
+                    local(place, begin, wide, half).wait()
+
+            else:
+
+                @pl.when(p == rank)
+                def _(slot=slot, owner=owner, place=place, begin=begin, wide=wide, half=half):
+                    copy(slot, owner, place, begin, wide, half).wait_send()
+
+                @pl.when(p == 2 * owner + half)
+                def _(slot=slot, owner=owner, place=place, begin=begin, wide=wide, half=half):
+                    copy(slot, owner, place, begin, wide, half).wait_recv()
+
+
+def front_to_owner(plan, value):
+    dma = pltpu.SemaphoreType.DMA
+    return pl.pallas_call(
+        functools.partial(front_owner_kernel, plan),
+        in_specs=[pl.BlockSpec(memory_space=pltpu.VMEM)],
+        out_specs=pl.BlockSpec(memory_space=pl.ANY),
+        out_shape=jax.ShapeDtypeStruct((value.shape[1], plan.per_shard * plan.unit), value.dtype),
+        scratch_shapes=[dma((5, 2)), dma((plan.per_shard,)), dma((plan.per_shard,))],
+        compiler_params=pltpu.CompilerParams(has_side_effects=True),
+    )(value)
 
 
 def gelu_parts(u):
@@ -303,13 +630,10 @@
     own_positions = at(positions_all, z)
     plane_positions = jnp.tile(own_positions, shards)
 
-    plane_tokens = gather_plane(tokens[0])
-
-    def normalize(values):
-        values = values.astype(f32)
-        centered = values - jnp.mean(values, axis=-1, keepdims=True)
-        factor = lax.rsqrt(jnp.mean(centered * centered, axis=-1, keepdims=True) + norm_eps)
-        return centered * factor, factor
+    plane_tokens, documents, weight_qkv, back_attention = gather_first(
+        plan, tokens[0], doc_ids.astype(f32), front_weight, back_weight
+    )
+    plane_tokens = plane_tokens.reshape(plane_rows, D)
 
     normed = (normalize(plane_tokens)[0] * norm_gain + norm_shift).astype(bf16)
 
@@ -340,8 +664,6 @@
             return total
         return jnp.where(pick(local, p) > 0, own, total)
 
-    gate = normed[0, 0]
-    weight_qkv = jnp.concatenate([slot_weight(i, gate) for i in range(3)], axis=1)
     gate = weight_qkv[0, 0]
     plane_grad = gather_plane(after(cotangent[0], gate))
     weight_up = jnp.concatenate([slot_weight(i, gate) for i in range(3, 5)], axis=1)
@@ -349,17 +671,21 @@
     def back_rows(rank):
         table = pick(plan.back_units, rank)
         return jnp.concatenate(
-            [lax.dynamic_slice(back_weight, (table[j] * unit, 0), (unit, D // shards)) for j in range(5)],
+            [
+                lax.dynamic_slice(back_weight, (table[j] * unit, 0), (2 * unit, D // shards))
+                for j in (1, 3)
+            ],
             axis=0,
         )
 
     col_width = D // shards
-    back_local = jnp.zeros((5 * unit, D), bf16)
+    back_up = jnp.zeros((4 * unit, D), bf16)
     for step in range(shards):
         piece = back_rows(after(2 * (f ^ step) + k, gate))
         if step:
             piece = to_shard(piece, step)
-        back_local = lax.dynamic_update_slice(back_local, piece, (0, (f ^ step) * col_width))
+        back_up = lax.dynamic_update_slice(back_up, piece, (0, (f ^ step) * col_width))
+    back_local = jnp.concatenate([back_attention, back_up], axis=0)
 
     unit_table = pick(plan.rank_units, p)
     bias_local = jnp.take(bias_front, unit_table, axis=0).reshape(-1)
@@ -385,13 +711,14 @@
 
     qkv_seq = to_sequence(qkv)
 
-    mixed_grad = lax.dot_general(plane_grad, back_local, contract_last, preferred_element_type=f32)
-    grad_seq = to_sequence(mixed_grad[:, :unit].astype(bf16))
+    attended_grad = lax.dot_general(
+        plane_grad, back_attention, contract_last, preferred_element_type=f32
+    ).astype(bf16)
+    grad_seq = to_sequence(attended_grad)
 
     order = jnp.arange(planes, dtype=jnp.int32) ^ z
     seq_positions = jnp.take(positions_all, order, axis=0).reshape(-1)
-    documents = lax.all_gather(doc_ids[0].astype(f32), "fsdp")
-    doc_row = at(documents, z).astype(jnp.int32)
+    doc_row = documents[0].astype(jnp.int32)
     seq_documents = jnp.take(
         jnp.take(doc_row.reshape(blocks, block_tokens), block_order, axis=0).reshape(planes, share),
         order,
@@ -420,7 +747,8 @@
 
     up = jnp.dot(normed, weight_up, preferred_element_type=f32) + bias_local[3 * unit :]
     activation, slope = gelu_parts(up)
-    up_grad = (mixed_grad[:, unit:] * slope).astype(bf16)
+    mixed_grad = lax.dot_general(plane_grad, back_up, contract_last, preferred_element_type=f32)
+    up_grad = (mixed_grad * slope).astype(bf16)
     mixed = jnp.concatenate([returned[:, :unit], activation.astype(bf16)], axis=1)
     hidden_grad = jnp.concatenate([returned[:, unit:], up_grad], axis=1)
 
@@ -485,56 +813,32 @@
         lambda i: lax.dynamic_slice(front_partial, (i * front_rows, 0), (front_rows, 7 * unit))
     ).astype(bf16)
 
-    back_grad = jnp.zeros((5 * unit, col_width), bf16)
-    for match in plan.matchings:
-        slot = np.zeros(ranks, np.int32)
-        place = np.zeros(ranks, np.int32)
-        links = []
-        for owner, (rank, j) in match.items():
-            slot[rank] = j
-            place[owner] = plan.back_units[rank][j] % 5
-            for i in range(planes):
-                links.append((plan.device(i, rank % 2, rank // 2), owner * shards + i))
-        block = lax.dynamic_slice(back_sum, (pick(slot, p) * unit, 0), (unit, col_width))
-        block = lax.ppermute(block, both, links)
-        back_grad = lax.dynamic_update_slice(back_grad, block, (pick(place, c_index) * unit, 0))
-    back_grad = back_grad.astype(f32)
-
-    natural = jnp.zeros((front_rows, (plan.per_shard + 2) * unit), bf16)
-    start = 0
-    for (units, wide), rounds in zip(plan.slots, plan.rounds):
-        table = np.asarray(units)
-        source, place = table // plan.per_shard, table % plan.per_shard
-        block = front_sum[:, start : start + wide * unit]
-        start += wide * unit
-        local = source == np.arange(ranks) // 2
-        where = np.where(local, place, plan.per_shard)
-        natural = lax.dynamic_update_slice(natural, block, (0, pick(where, p) * unit))
-        for one in rounds:
-            where = np.full(ranks, plan.per_shard, np.int32)
-            links = []
-            for src, dst, core in one:
-                where[2 * src + core] = place[2 * dst + core]
-                links += [
-                    (plan.device(i, core, dst), plan.device(i, core, src)) for i in range(planes)
-                ]
-            moved = lax.ppermute(block, both, links)
-            natural = lax.dynamic_update_slice(natural, moved, (0, pick(where, p) * unit))
-    natural = natural[:, : plan.per_shard * unit].reshape(2, front_rows // 2, -1)
-    front_grad = at(natural, k).astype(f32) + swap_core(at(natural, 1 - k)).astype(f32)
+    back_grad = back_to_owner(plan, back_sum).astype(f32)
+    front_grad = front_to_owner(plan, front_sum.reshape(2, front_rows // 2, -1)).astype(f32)
+
+    def column_sums(value):
+        ones = jnp.ones((8, value.shape[0]), bf16)
+        return jnp.dot(ones, value, preferred_element_type=f32)[0]
 
     spread = (jnp.arange(7 * ranks)[:, None] == unit_table[None, :]).astype(f32)
-    hidden_sum = jnp.sum(hidden_grad, axis=0, dtype=f32).reshape(7, unit)
+    hidden_sum = column_sums(hidden_grad).reshape(7, unit)
     front_vector = jnp.sum(spread[:, :, None] * hidden_sum[None], axis=1).reshape(-1)
     vector_term = jnp.concatenate(
         [
             front_vector,
-            jnp.sum(cotangent[0], axis=0, dtype=f32),
+            column_sums(cotangent[0]),
             jnp.sum(normed_grad * unscaled, axis=0),
             jnp.sum(normed_grad, axis=0),
         ]
     )
-    vector_grad = lax.psum(vector_term, both)
+    vector_grad = vector_term.reshape(-1, 128)
+    vector_grad = vector_grad + swap_core(vector_grad)
+    step = 1
+    while step < shards:
+        vector_grad = vector_grad + to_shard(vector_grad, step)
+        vector_grad = vector_grad + to_plane(vector_grad, step)
+        step *= 2
+    vector_grad = vector_grad.reshape(-1)
 
     count_now = adam_step[0]
     back_new, back_first_new, back_second_new = adam_update(

time: 1190 us -> 1060 us (0.89)
  Pallas kernels: 26.5 us -> 222 us
  starting transfers between devices: 302 us -> 136 us
  waiting for transfers between devices: 452 us -> 381 us
  local copies, waits for them, and re-layouts: 164 us -> 123 us
  between operations: 59.2 us -> 26.2 us
  other arithmetic: 111 us -> 96.7 us
    pallas_call x0 -> x3, Pallas kernels: none -> 196 us  [the longest x1 111 us: gather_first(): pl.pallas_call(functools.partial(gather_kernel, plan), in_specs=[vmem, vm...]
    psum x1 -> x0, waiting for transfers between devices: 130 us -> none  [per_device(): vector_grad = lax.psum(vector_term, both)]
    ppermute x15 -> x0, starting transfers between devices: 87.1 us -> none  [the longest x5 57.4 us: per_device(): block = lax.ppermute(block, both, links)]
    ppermute x9 -> x11, waiting for transfers between devices: 48.1 us -> 124 us  [to_plane(): lax.ppermute(value, 'ctx', [(2 * i + j, 2 * (i ^ step) + j) for i in rang...]
    ppermute x9 -> x11, starting transfers between devices: 64.1 us -> 12.2 us  [to_shard(): return lax.ppermute(value, 'fsdp', [(i, i ^ step) for i in range(shards)])]
    dynamic_slice x45 -> x7, local copies, waits for them, and re-layouts: 33.1 us -> 3.54 us  [pick(): return jnp.asarray(np.asarray(table, np.int32))[index]]
    ppermute x6, starting transfers between devices: 17.4 us -> 46.4 us  [gather_rows(): rising = lax.ppermute(rising, 'ctx', links)]
    ppermute x6, starting transfers between devices: 48.6 us -> 20.2 us  [sum_over_planes(): rising = lax.ppermute(term_a, 'ctx', up_links(s))]
  transfers between devices with their start and end apart: 89 -> 67, of which waited for: 22 -> 17; matrix products, arithmetic and copies ran while one was open for 24% -> 21% of each run, Pallas kernels for 0% -> 8%
where the time goes in v2:
time: 1060 us; the launch traced here: 1050 us
  waiting for transfers between devices  381 us (36%)
  Pallas kernels  222 us (21%)
  starting transfers between devices  136 us (13%)
  local copies, waits for them, and re-layouts  123 us (12%)
  other arithmetic  96.7 us (9%)
  matrix products  66.5 us (6%)
  between operations  26.2 us (2%)
    ppermute x11, waiting for transfers between devices, to_plane(): lax.ppermute(value, 'ctx', [(2 * i + j, 2 * (i ^ step) + j) for i in rang...  124 us
    ppermute x6, waiting for transfers between devices, gather_rows(): falling = lax.ppermute(falling, 'ctx', mirror(links))  112 us
    pallas_call x1, Pallas kernels, gather_first(): pl.pallas_call(functools.partial(gather_kernel, plan), in_specs=[vmem, vm...  111 us
    ppermute x11, waiting for transfers between devices, to_shard(): return lax.ppermute(value, 'fsdp', [(i, i ^ step) for i in range(shards)])  57.3 us
    pallas_call x1, Pallas kernels, front_to_owner(): pl.pallas_call(functools.partial(front_owner_kernel, plan), in_specs=[pl....  54.6 us
    ppermute x6, waiting for transfers between devices, sum_over_planes(): rising = lax.ppermute(term_a, 'ctx', up_links(s))  53 us
    ppermute x6, starting transfers between devices, gather_rows(): rising = lax.ppermute(rising, 'ctx', links)  46.4 us
    pallas_call x1, Pallas kernels, back_to_owner(): pl.pallas_call(functools.partial(back_owner_kernel, plan), in_specs=[pl.B...  30.3 us
  transfers between devices with their start and end apart: 67, of which 17 were waited for; matrix products, arithmetic and copies ran while one was open for 21% of the time, Pallas kernels for 8%

profile of v2, /device:TPU:0, one launch (start us, length us, event | category | flops | bytes accessed | tf_op | source)
XLA Modules:
  0.0 1052.0 jit_solution(12637130460935298137)
XLA Ops:
  8.5 110.9 %shard_map.441 = (bf16[4,2,128,2048]{3,2,1,0:T(8,128)(2,1)}, f32[1,1024]{1,0:T(1,128)}, bf16[2048,768]{1,0:T(8,128)(2,1)}, bf16[256,2048]{1,0:T(8,128)(2,1)}) custom-call(bf16[128,2048]{1,0:T(8,128)(2,1)} %bitcast.195, f32[1,1024]{1,0:T(1,128)} %convert_element_type.284.doc, bf16[2048,3584]{1,0:T(8,128)(2,1)} %front.1, bf16[10240,512]{1,0:T(8,128)(2,1)} %back.1), custom_call_target="tpu_custom_call" | custom-call | tf_op jit(solution)/shard_map/pallas_call | solution.py:381
  143.9 8.3 fusion.48
  179.0 6.1 dynamic-slice_select_fusion.1
  185.2 13.2 %collective-permute-start.11 = (bf16[2048,512]{1,0:T(8,128)(2,1)}, bf16[2048,512]{1,0:T(8,128)(2,1)S(1)}, u32[]{:S(2)}, u32[]{:S(2)}) collective-permute-start(bf16[2048,512]{1,0:T(8,128)(2,1)} %get-tuple-element.67), channel_id=1, source_target_pairs={{2,0},{10,8},{18,16},{26,24},{3,1},{11,9},{19,17},{27,25},{7,4},{1... | collective-permute-start | bytes 6291464 | tf_op jit(solution)/shard_map/ppermute | solution.py:656
  203.1 20.7 %all-gather.3.cloned.1.call-done = bf16[512,2048]{1,0:T(8,128)(2,1)} async-done(((bf16[128,2048]{1,0:T(8,128)(2,1)}), bf16[512,2048]{1,0:T(8,128)(2,1)}) %all-gather.3.cloned.1.call-update) | async-done | bytes 2097168 | tf_op jit(solution)/shard_map/all_gather | solution.py:617
  234.2 17.3 %collective-permute-done.12 = bf16[1024,512]{1,0:T(8,128)(2,1)S(1)} collective-permute-done((bf16[1024,512]{1,0:T(8,128)(2,1)}, bf16[1024,512]{1,0:T(8,128)(2,1)S(1)}, u32[]{:S(2)}, u32[]{:S(2)}) %collective-permute-start.12) | collective-permute-done | bytes 1048608 | tf_op jit(solution)/shard_map/ppermute | solution.py:609
  251.6 35.9 %collective-permute-done.13 = bf16[1024,512]{1,0:T(8,128)(2,1)S(1)} collective-permute-done((bf16[1024,512]{1,0:T(8,128)(2,1)S(1)}, bf16[1024,512]{1,0:T(8,128)(2,1)S(1)}, u32[]{:S(2)}, u32[]{:S(2)}) %collective-permute-start.13) | collective-permute-done | bytes 1048608 | tf_op jit(solution)/shard_map/ppermute | solution.py:609
  300.9 7.4 multiply_convert_fusion.1
  309.2 26.3 %shard_map.442 = (bf16[1024,256]{1,0:T(8,128)(2,1)}, f32[1024,256]{1,0:T(8,128)}, f32[1024,256]{1,0:T(8,128)}, f32[1024,256]{1,0:T(8,128)}) custom-call(bf16[1024,256]{1,0:T(8,128)(2,1)} %get-tuple-element.112.q_ref, bf16[1024,256]{1,0:T(8,128)(2,1)} %get-tuple-element.111.k_ref, bf16[1024,256]{1,0:T(8,128)(2,1)} %get-tuple-element.110.v_ref, ...), custom_call_target="tpu_custom_call" | custom-call | flops 3758096384 | bytes 5242880 | tf_op jit(solution)/shard_map/pallas_call | solution.py:203
  352.5 7.8 multiply_convert_fusion
  361.6 21.2 %collective-permute-done.8 = bf16[256,1024]{1,0:T(8,128)(2,1)S(1)} collective-permute-done((bf16[256,1024]{1,0:T(8,128)(2,1)S(1)}, bf16[256,1024]{1,0:T(8,128)(2,1)S(1)}, u32[]{:S(2)}, u32[]{:S(2)}) %collective-permute-start.8) | collective-permute-done | bytes 524320 | tf_op jit(solution)/shard_map/ppermute | solution.py:612
  391.4 14.9 %fusion.4 = f32[1024,2048]{1,0:T(8,128)} fusion(bf16[2048,512]{1,0:T(8,128)(2,1)S(1)} %dynamic-slice_select_fusion, bf16[2048,512]{1,0:T(8,128)(2,1)} %get-tuple-element.66, bf16[2048,768]{1,0:T(8,128)(2,1)} %get-tuple-element.33, bf16[256,1024]{0,1:T(8,128)(2,1)} %copy.68, bf16[256,1024]{0,1:T(8,128)(2,1)} %copy.67, bf16[256,1024]{0,1:T(8,128)(2,1)} %copy.66, ...), kind=kOutput, calls=%fused_computation.12 | convolution fusion | flops 7556562944 | bytes 19922944 | tf_op jit(solution)/shard_map/dot_general | solution.py:771
  406.3 10.5 convolution_convert_fusion.1
  416.9 6.5 fusion.30
  423.4 9.2 convolution_convert_fusion
  437.4 10.8 %fusion.14 = f32[1024,2048]{1,0:T(8,128)} fusion(bf16[1024,2048]{1,0:T(8,128)(2,1)S(1)} %copy-done.20, bf16[256,2048]{1,0:T(8,128)(2,1)S(1)} %copy-done.65, bf16[256,1024]{0,1:T(8,128)(2,1)S(1)} %copy-done.32, bf16[256,1024]{0,1:T(8,128)(2,1)S(1)} %copy-done.33, bf16[256,1024]{0,1:T(8,128)(2,1)S(1)} %copy-done.35, bf16[256,1024]{0,1:T(8,128)(2,1)S(1)} %copy-done.37, ...), kind=kOutput, calls=%fused_computation.24 | convolution fusion | flops 5398855680 | bytes 17825792 | tf_op jit(solution)/shard_map/dot_general | solution.py:765
  453.0 11.6 %collective-permute-done.29 = bf16[1280,512]{1,0:T(8,128)(2,1)S(1)} collective-permute-done((bf16[1280,512]{1,0:T(8,128)(2,1)S(1)}, bf16[1280,512]{1,0:T(8,128)(2,1)S(1)}, u32[]{:S(2)}, u32[]{:S(2)}) %collective-permute-start.29) | collective-permute-done | bytes 1310752 | tf_op jit(solution)/shard_map/ppermute | solution.py:798
  483.7 16.3 %collective-permute-done.30 = bf16[1280,512]{1,0:T(8,128)(2,1)} collective-permute-done((bf16[1280,512]{1,0:T(8,128)(2,1)}, bf16[1280,512]{1,0:T(8,128)(2,1)}, u32[]{:S(2)}, u32[]{:S(2)}) %collective-permute-start.30) | collective-permute-done | bytes 1310752 | tf_op jit(solution)/shard_map/ppermute | solution.py:798
  513.0 25.1 %collective-permute-done.23 = bf16[512,1792]{1,0:T(8,128)(2,1)} collective-permute-done((bf16[512,1792]{1,0:T(8,128)(2,1)}, bf16[512,1792]{1,0:T(8,128)(2,1)}, u32[]{:S(2)}, u32[]{:S(2)}) %collective-permute-start.23) | collective-permute-done | bytes 1835040 | tf_op jit(solution)/shard_map/ppermute | solution.py:798
  558.7 53.8 %collective-permute-done.37 = f32[160,128]{1,0:T(8,128)S(1)} collective-permute-done((f32[160,128]{1,0:T(8,128)S(1)}, f32[160,128]{1,0:T(8,128)S(1)}, u32[]{:S(2)}, u32[]{:S(2)}) %collective-permute-start.37) | collective-permute-done | bytes 81952 | tf_op jit(solution)/shard_map/ppermute | solution.py:612
  625.9 30.3 %shard_map.444 = bf16[1280,512]{1,0:T(8,128)(2,1)} custom-call(bf16[1280,512]{1,0:T(8,128)(2,1)} %add_convert_fusion.5.src), custom_call_target="tpu_custom_call" | custom-call | tf_op jit(solution)/shard_map/pallas_call | solution.py:460
  656.2 8.1 fusion.111
  664.3 36.4 %collective-permute-start.53 = (bf16[1280,512]{1,0:T(8,128)(2,1)S(1)}, bf16[1280,512]{1,0:T(8,128)(2,1)}, u32[]{:S(2)}, u32[]{:S(2)}) collective-permute-start(bf16[1280,512]{1,0:T(8,128)(2,1)S(1)} %get-tuple-element.51), channel_id=1, source_target_pairs={{0,8},{4,12},{8,16},{12,20},{16,24},{20,28},{1,9},{5,13},{9,17},{1... | collective-permute-start | bytes 3932168 | tf_op jit(solution)/shard_map/ppermute | solution.py:869
  706.9 5.8 collective-permute-start.39
  716.3 12.5 %collective-permute-done.53 = bf16[1280,512]{1,0:T(8,128)(2,1)} collective-permute-done((bf16[1280,512]{1,0:T(8,128)(2,1)S(1)}, bf16[1280,512]{1,0:T(8,128)(2,1)}, u32[]{:S(2)}, u32[]{:S(2)}) %collective-permute-start.53) | collective-permute-done | bytes 1310752 | tf_op jit(solution)/shard_map/ppermute | solution.py:869
  730.6 48.1 %collective-permute-done.39 = f32[160,128]{1,0:T(8,128)S(1)} collective-permute-done((f32[160,128]{1,0:T(8,128)S(1)}, f32[160,128]{1,0:T(8,128)S(1)}, u32[]{:S(2)}, u32[]{:S(2)}) %collective-permute-start.39) | collective-permute-done | bytes 81952 | tf_op jit(solution)/shard_map/ppermute | solution.py:612
  790.7 54.6 %shard_map.443 = bf16[256,3584]{1,0:T(8,128)(2,1)} custom-call(bf16[2,256,1792]{2,1,0:T(8,128)(2,1)} %bitcast.196), custom_call_target="tpu_custom_call" | custom-call | tf_op jit(solution)/shard_map/pallas_call | solution.py:532
  848.3 10.1 fusion.113
  879.7 58.5 %collective-permute-done.63 = bf16[1280,512]{1,0:T(8,128)(2,1)} collective-permute-done((bf16[1280,512]{1,0:T(8,128)(2,1)}, bf16[1280,512]{1,0:T(8,128)(2,1)}, u32[]{:S(2)}, u32[]{:S(2)}) %collective-permute-start.63) | collective-permute-done | bytes 1310752 | tf_op jit(solution)/shard_map/ppermute | solution.py:870
  945.3 6.4 broadcast_in_dim.126
  965.6 22.5 %collective-permute-done.46 = bf16[256,3584]{1,0:T(8,128)(2,1)} collective-permute-done((bf16[256,3584]{1,0:T(8,128)(2,1)}, bf16[256,3584]{1,0:T(8,128)(2,1)}, u32[]{:S(2)}, u32[]{:S(2)}) %collective-permute-start.46) | collective-permute-done | bytes 1835040 | tf_op jit(solution)/shard_map/ppermute | solution.py:870
  999.8 31.5 %collective-permute-done.50 = bf16[256,3584]{1,0:T(8,128)(2,1)S(1)} collective-permute-done((bf16[256,3584]{1,0:T(8,128)(2,1)}, bf16[256,3584]{1,0:T(8,128)(2,1)S(1)}, u32[]{:S(2)}, u32[]{:S(2)}) %collective-permute-start.50) | collective-permute-done | bytes 1835040 | tf_op jit(solution)/shard_map/ppermute | solution.py:870
  (450 shorter events, 267.3 us)
Async XLA Ops:
  7.2 216.7 %all-gather.3.cloned.1.call-start = ((), (), s32[]{:S(2)}) async-start(), calls=%async_computation | async-start | bytes 2621440 | tf_op jit(solution)/shard_map/all_gather | solution.py:617
  153.5 71.6 %collective-permute-start.2 = (bf16[256,768]{1,0:T(8,128)(2,1)}, bf16[256,768]{1,0:T(8,128)(2,1)}, u32[]{:S(2)}, u32[]{:S(2)}) collective-permute-start(bf16[256,768]{1,0:T(8,128)(2,1)} %get-tuple-element.114), channel_id=1, source_target_pairs={{0,24},{4,28},{8,16},{12,20},{16,8},{20,12},{24,0},{28,4},{1,25},{... | collective-permute-start | bytes 1179656 | tf_op jit(solution)/shard_map/ppermute | solution.py:612
  156.8 69.8 %collective-permute-start.1 = (bf16[256,768]{1,0:T(8,128)(2,1)}, bf16[256,768]{1,0:T(8,128)(2,1)}, u32[]{:S(2)}, u32[]{:S(2)}) collective-permute-start(bf16[256,768]{1,0:T(8,128)(2,1)} %get-tuple-element.115), channel_id=1, source_target_pairs={{0,16},{4,20},{8,24},{12,28},{16,0},{20,4},{24,8},{28,12},{1,17},{... | collective-permute-start | bytes 1179656 | tf_op jit(solution)/shard_map/ppermute | solution.py:612
  156.8 70.6 %collective-permute-start = (bf16[256,768]{1,0:T(8,128)(2,1)}, bf16[256,768]{1,0:T(8,128)(2,1)}, u32[]{:S(2)}, u32[]{:S(2)}) collective-permute-start(bf16[256,768]{1,0:T(8,128)(2,1)} %get-tuple-element.116), channel_id=1, source_target_pairs={{0,8},{4,12},{8,0},{12,4},{16,24},{20,28},{24,16},{28,20},{1,9},{5... | collective-permute-start | bytes 1179656 | tf_op jit(solution)/shard_map/ppermute | solution.py:612
  185.2 102.7 %collective-permute-start.11 = (bf16[2048,512]{1,0:T(8,128)(2,1)}, bf16[2048,512]{1,0:T(8,128)(2,1)S(1)}, u32[]{:S(2)}, u32[]{:S(2)}) collective-permute-start(bf16[2048,512]{1,0:T(8,128)(2,1)} %get-tuple-element.67), channel_id=1, source_target_pairs={{2,0},{10,8},{18,16},{26,24},{3,1},{11,9},{19,17},{27,25},{7,4},{1... | collective-permute-start | bytes 6291464 | tf_op jit(solution)/shard_map/ppermute | solution.py:656
  223.8 69.7 %collective-permute-start.3 = (bf16[4,128,2048]{2,1,0:T(8,128)(2,1)}, bf16[4,128,2048]{2,1,0:T(8,128)(2,1)S(1)}, u32[]{:S(2)}, u32[]{:S(2)}) collective-permute-start(bf16[4,128,2048]{2,1,0:T(8,128)(2,1)} %bitcast.210), channel_id=1, source_target_pairs={{0,4},{4,0},{8,12},{12,8},{16,20},{20,16},{24,28},{28,24},{1,5},{5... | collective-permute-start | bytes 6291464 | tf_op jit(solution)/shard_map/ppermute | solution.py:606
  450.6 100.5 %collective-permute-start.15 = (bf16[4,128,2048]{2,1,0:T(8,128)(2,1)S(1)}, bf16[4,128,2048]{2,1,0:T(8,128)(2,1)}, u32[]{:S(2)}, u32[]{:S(2)}) collective-permute-start(bf16[4,128,2048]{2,1,0:T(8,128)(2,1)S(1)} %fusion.29), channel_id=1, source_target_pairs={{0,4},{4,0},{8,12},{12,8},{16,20},{20,16},{24,28},{28,24},{1,5},{5... | collective-permute-start | bytes 6291464 | tf_op jit(solution)/shard_map/ppermute | solution.py:606
  473.8 64.3 %collective-permute-start.23 = (bf16[512,1792]{1,0:T(8,128)(2,1)}, bf16[512,1792]{1,0:T(8,128)(2,1)}, u32[]{:S(2)}, u32[]{:S(2)}) collective-permute-start(bf16[512,1792]{1,0:T(8,128)(2,1)} %get-tuple-element.78), channel_id=1, source_target_pairs={{0,8},{4,12},{1,9},{5,13},{2,10},{6,14},{3,11},{7,15}} | collective-permute-start | bytes 5505032 | tf_op jit(solution)/shard_map/ppermute | solution.py:798
  506.7 107.8 %collective-permute-start.26 = (bf16[512,1792]{1,0:T(8,128)(2,1)S(1)}, bf16[512,1792]{1,0:T(8,128)(2,1)S(1)}, u32[]{:S(2)}, u32[]{:S(2)}) collective-permute-start(bf16[512,1792]{1,0:T(8,128)(2,1)S(1)} %copy-done.27), channel_id=1, source_target_pairs={{24,16},{28,20},{25,17},{29,21},{26,18},{30,22},{27,19},{31,23}} | collective-permute-start | bytes 5505032 | tf_op jit(solution)/shard_map/ppermute | solution.py:799
  540.1 75.0 %collective-permute-start.24 = (bf16[512,1792]{1,0:T(8,128)(2,1)S(1)}, bf16[512,1792]{1,0:T(8,128)(2,1)}, u32[]{:S(2)}, u32[]{:S(2)}) collective-permute-start(bf16[512,1792]{1,0:T(8,128)(2,1)S(1)} %add_convert_fusion.4), channel_id=1, source_target_pairs={{0,8},{4,12},{8,16},{12,20},{1,9},{5,13},{9,17},{13,21},{2,10},{6,... | collective-permute-start | bytes 5505032 | tf_op jit(solution)/shard_map/ppermute | solution.py:798
  545.7 74.7 %collective-permute-start.31 = (bf16[1280,512]{1,0:T(8,128)(2,1)}, bf16[1280,512]{1,0:T(8,128)(2,1)}, u32[]{:S(2)}, u32[]{:S(2)}) collective-permute-start(bf16[1280,512]{1,0:T(8,128)(2,1)} %get-tuple-element.80), channel_id=1, source_target_pairs={{0,8},{4,12},{8,16},{12,20},{16,24},{20,28},{1,9},{5,13},{9,17},{1... | collective-permute-start | bytes 3932168 | tf_op jit(solution)/shard_map/ppermute | solution.py:798
  551.2 69.8 %collective-permute-start.34 = (bf16[1280,512]{1,0:T(8,128)(2,1)}, bf16[1280,512]{1,0:T(8,128)(2,1)S(1)}, u32[]{:S(2)}, u32[]{:S(2)}) collective-permute-start(bf16[1280,512]{1,0:T(8,128)(2,1)} %add_convert_fusion.6), channel_id=1, source_target_pairs={{24,16},{28,20},{16,8},{20,12},{8,0},{12,4},{25,17},{29,21},{17,9}... | collective-permute-start | bytes 3932168 | tf_op jit(solution)/shard_map/ppermute | solution.py:799
  612.5 90.1 %collective-permute-start.18 = (bf16[128,2048]{1,0:T(8,128)(2,1)}, bf16[128,2048]{1,0:T(8,128)(2,1)}, u32[]{:S(2)}, u32[]{:S(2)}) collective-permute-start(bf16[128,2048]{1,0:T(8,128)(2,1)} %get-tuple-element.88), channel_id=1, source_target_pairs={{0,3},{1,2},{2,1},{3,0},{4,7},{5,6},{6,5},{7,4},{8,11},{9,10},{10,... | collective-permute-start | bytes 1572872 | tf_op jit(solution)/shard_map/ppermute | solution.py:609
  614.5 89.8 %collective-permute-start.17 = (bf16[128,2048]{1,0:T(8,128)(2,1)}, bf16[128,2048]{1,0:T(8,128)(2,1)}, u32[]{:S(2)}, u32[]{:S(2)}) collective-permute-start(bf16[128,2048]{1,0:T(8,128)(2,1)} %get-tuple-element.89), channel_id=1, source_target_pairs={{0,2},{1,3},{2,0},{3,1},{4,6},{5,7},{6,4},{7,5},{8,10},{9,11},{10,... | collective-permute-start | bytes 1572872 | tf_op jit(solution)/shard_map/ppermute | solution.py:609
  615.1 91.8 %collective-permute-start.16 = (bf16[128,2048]{1,0:T(8,128)(2,1)}, bf16[128,2048]{1,0:T(8,128)(2,1)}, u32[]{:S(2)}, u32[]{:S(2)}) collective-permute-start(bf16[128,2048]{1,0:T(8,128)(2,1)} %get-tuple-element.87), channel_id=1, source_target_pairs={{0,1},{1,0},{2,3},{3,2},{4,5},{5,4},{6,7},{7,6},{8,9},{9,8},{10,11... | collective-permute-start | bytes 1572872 | tf_op jit(solution)/shard_map/ppermute | solution.py:609
  620.5 85.1 %collective-permute-start.38 = (f32[160,128]{1,0:T(8,128)S(1)}, f32[160,128]{1,0:T(8,128)S(1)}, u32[]{:S(2)}, u32[]{:S(2)}) collective-permute-start(f32[160,128]{1,0:T(8,128)S(1)} %add.700), channel_id=1, source_target_pairs={{0,2},{1,3},{2,0},{3,1},{4,6},{5,7},{6,4},{7,5},{8,10},{9,11},{10,... | collective-permute-start | bytes 245768 | tf_op jit(solution)/shard_map/ppermute | solution.py:609
  664.3 64.4 %collective-permute-start.53 = (bf16[1280,512]{1,0:T(8,128)(2,1)S(1)}, bf16[1280,512]{1,0:T(8,128)(2,1)}, u32[]{:S(2)}, u32[]{:S(2)}) collective-permute-start(bf16[1280,512]{1,0:T(8,128)(2,1)S(1)} %get-tuple-element.51), channel_id=1, source_target_pairs={{0,8},{4,12},{8,16},{12,20},{16,24},{20,28},{1,9},{5,13},{9,17},{1... | collective-permute-start | bytes 3932168 | tf_op jit(solution)/shard_map/ppermute | solution.py:869
  702.7 84.7 %collective-permute-start.25 = (bf16[512,1792]{1,0:T(8,128)(2,1)S(1)}, bf16[512,1792]{1,0:T(8,128)(2,1)S(1)}, u32[]{:S(2)}, u32[]{:S(2)}) collective-permute-start(bf16[512,1792]{1,0:T(8,128)(2,1)S(1)} %copy-done.28), channel_id=1, source_target_pairs={{0,8},{4,12},{8,16},{12,20},{16,24},{20,28},{1,9},{5,13},{9,17},{1... | collective-permute-start | bytes 5505032 | tf_op jit(solution)/shard_map/ppermute | solution.py:798
  704.2 84.5 %collective-permute-start.28 = (bf16[512,1792]{1,0:T(8,128)(2,1)S(1)}, bf16[512,1792]{1,0:T(8,128)(2,1)S(1)}, u32[]{:S(2)}, u32[]{:S(2)}) collective-permute-start(bf16[512,1792]{1,0:T(8,128)(2,1)S(1)} %add_convert_fusion.1), channel_id=1, source_target_pairs={{24,16},{28,20},{16,8},{20,12},{8,0},{12,4},{25,17},{29,21},{17,9}... | collective-permute-start | bytes 5505032 | tf_op jit(solution)/shard_map/ppermute | solution.py:799
  705.6 74.5 %collective-permute-start.55 = (bf16[1280,512]{1,0:T(8,128)(2,1)S(1)}, bf16[1280,512]{1,0:T(8,128)(2,1)}, u32[]{:S(2)}, u32[]{:S(2)}) collective-permute-start(bf16[1280,512]{1,0:T(8,128)(2,1)S(1)} %get-tuple-element.51), channel_id=1, source_target_pairs={{24,16},{28,20},{16,8},{20,12},{8,0},{12,4},{25,17},{29,21},{17,9}... | collective-permute-start | bytes 3932168 | tf_op jit(solution)/shard_map/ppermute | solution.py:870
  706.9 71.8 %collective-permute-start.39 = (f32[160,128]{1,0:T(8,128)S(1)}, f32[160,128]{1,0:T(8,128)S(1)}, u32[]{:S(2)}, u32[]{:S(2)}) collective-permute-start(f32[160,128]{1,0:T(8,128)S(1)} %add.701), channel_id=1, source_target_pairs={{0,16},{4,20},{8,24},{12,28},{16,0},{20,4},{24,8},{28,12},{1,17},{... | collective-permute-start | bytes 245768 | tf_op jit(solution)/shard_map/ppermute | solution.py:612
  728.7 116.5 %collective-permute-start.57 = (bf16[1280,512]{1,0:T(8,128)(2,1)}, bf16[1280,512]{1,0:T(8,128)(2,1)}, u32[]{:S(2)}, u32[]{:S(2)}) collective-permute-start(bf16[1280,512]{1,0:T(8,128)(2,1)} %collective-permute-done.53), channel_id=1, source_target_pairs={{8,16},{12,20},{16,24},{20,28},{9,17},{13,21},{17,25},{21,29},{10,... | collective-permute-start | bytes 3932168 | tf_op jit(solution)/shard_map/ppermute | solution.py:869
  780.1 78.3 %collective-permute-start.54 = (bf16[1280,512]{1,0:T(8,128)(2,1)}, bf16[1280,512]{1,0:T(8,128)(2,1)}, u32[]{:S(2)}, u32[]{:S(2)}) collective-permute-start(bf16[1280,512]{1,0:T(8,128)(2,1)} %collective-permute-done.53), channel_id=1, source_target_pairs={{0,4},{4,0},{8,12},{12,8},{16,20},{20,16},{24,28},{28,24},{1,5},{5... | collective-permute-start | bytes 3932168 | tf_op jit(solution)/shard_map/ppermute | solution.py:606
  780.1 85.4 %collective-permute-start.56 = (bf16[1280,512]{1,0:T(8,128)(2,1)}, bf16[1280,512]{1,0:T(8,128)(2,1)}, u32[]{:S(2)}, u32[]{:S(2)}) collective-permute-start(bf16[1280,512]{1,0:T(8,128)(2,1)} %collective-permute-done.55), channel_id=1, source_target_pairs={{0,4},{4,0},{8,12},{12,8},{16,20},{20,16},{24,28},{28,24},{1,5},{5... | collective-permute-start | bytes 3932168 | tf_op jit(solution)/shard_map/ppermute | solution.py:606
  787.4 79.3 %collective-permute-start.59 = (bf16[1280,512]{1,0:T(8,128)(2,1)}, bf16[1280,512]{1,0:T(8,128)(2,1)}, u32[]{:S(2)}, u32[]{:S(2)}) collective-permute-start(bf16[1280,512]{1,0:T(8,128)(2,1)} %collective-permute-done.55), channel_id=1, source_target_pairs={{16,8},{20,12},{8,0},{12,4},{17,9},{21,13},{9,1},{13,5},{18,10},{2... | collective-permute-start | bytes 3932168 | tf_op jit(solution)/shard_map/ppermute | solution.py:870
  858.4 82.1 %collective-permute-start.40 = (bf16[256,3584]{1,0:T(8,128)(2,1)S(1)}, bf16[256,3584]{1,0:T(8,128)(2,1)}, u32[]{:S(2)}, u32[]{:S(2)}) collective-permute-start(bf16[256,3584]{1,0:T(8,128)(2,1)S(1)} %get-tuple-element.56), channel_id=1, source_target_pairs={{0,8},{4,12},{8,16},{12,20},{16,24},{20,28},{1,9},{5,13},{9,17},{1... | collective-permute-start | bytes 5505032 | tf_op jit(solution)/shard_map/ppermute | solution.py:869
  865.5 75.6 %collective-permute-start.42 = (bf16[256,3584]{1,0:T(8,128)(2,1)S(1)}, bf16[256,3584]{1,0:T(8,128)(2,1)}, u32[]{:S(2)}, u32[]{:S(2)}) collective-permute-start(bf16[256,3584]{1,0:T(8,128)(2,1)S(1)} %get-tuple-element.56), channel_id=1, source_target_pairs={{24,16},{28,20},{16,8},{20,12},{8,0},{12,4},{25,17},{29,21},{17,9}... | collective-permute-start | bytes 5505032 | tf_op jit(solution)/shard_map/ppermute | solution.py:870
  866.9 71.4 %collective-permute-start.63 = (bf16[1280,512]{1,0:T(8,128)(2,1)}, bf16[1280,512]{1,0:T(8,128)(2,1)}, u32[]{:S(2)}, u32[]{:S(2)}) collective-permute-start(bf16[1280,512]{1,0:T(8,128)(2,1)} %collective-permute-done.59), channel_id=1, source_target_pairs={{8,0},{12,4},{9,1},{13,5},{10,2},{14,6},{11,3},{15,7}} | collective-permute-start | bytes 3932168 | tf_op jit(solution)/shard_map/ppermute | solution.py:870
  873.1 69.8 %collective-permute-start.62 = (bf16[1280,512]{1,0:T(8,128)(2,1)S(1)}, bf16[1280,512]{1,0:T(8,128)(2,1)S(1)}, u32[]{:S(2)}, u32[]{:S(2)}) collective-permute-start(bf16[1280,512]{1,0:T(8,128)(2,1)S(1)} %collective-permute-done.61), channel_id=1, source_target_pairs={{0,4},{4,0},{8,12},{12,8},{16,20},{20,16},{24,28},{28,24},{1,5},{5... | collective-permute-start | bytes 3932168 | tf_op jit(solution)/shard_map/ppermute | solution.py:606
  879.6 82.2 %collective-permute-start.65 = (bf16[1280,512]{1,0:T(8,128)(2,1)S(1)}, bf16[1280,512]{1,0:T(8,128)(2,1)}, u32[]{:S(2)}, u32[]{:S(2)}) collective-permute-start(bf16[1280,512]{1,0:T(8,128)(2,1)S(1)} %copy-done.8), channel_id=1, source_target_pairs={{0,4},{4,0},{8,12},{12,8},{16,20},{20,16},{24,28},{28,24},{1,5},{5... | collective-permute-start | bytes 3932168 | tf_op jit(solution)/shard_map/ppermute | solution.py:606
  961.9 81.7 %collective-permute-start.52 = (bf16[256,3584]{1,0:T(8,128)(2,1)S(1)}, bf16[256,3584]{1,0:T(8,128)(2,1)S(1)}, u32[]{:S(2)}, u32[]{:S(2)}) collective-permute-start(bf16[256,3584]{1,0:T(8,128)(2,1)S(1)} %get-tuple-element.56), channel_id=1, source_target_pairs={{0,4},{4,0},{8,12},{12,8},{16,20},{20,16},{24,28},{28,24},{1,5},{5... | collective-permute-start | bytes 5505032 | tf_op jit(solution)/shard_map/ppermute | solution.py:606
  964.8 66.5 %collective-permute-start.45 = (bf16[256,3584]{1,0:T(8,128)(2,1)}, bf16[256,3584]{1,0:T(8,128)(2,1)S(1)}, u32[]{:S(2)}, u32[]{:S(2)}) collective-permute-start(bf16[256,3584]{1,0:T(8,128)(2,1)} %collective-permute-done.44), channel_id=1, source_target_pairs={{0,4},{4,0},{8,12},{12,8},{16,20},{20,16},{24,28},{28,24},{1,5},{5... | collective-permute-start | bytes 5505032 | tf_op jit(solution)/shard_map/ppermute | solution.py:606
  (117 other events, 2634.5 us)
Sparse Core Ops, SparseCore 0:
  158.0 65.7 all-gather.2

commit v3 on v2

--- a/solution.py
+++ b/solution.py
@@ -407,7 +407,205 @@
     )(tokens, documents, front_weight, back_weight)
 
 
-def back_owner_kernel(plan, src, out, send, recv, lsem):
+def line_sum(plan, block, rising, falling, sends, gets, rows):
+    planes, chunk = plan.planes, 64
+    c, f, z, k, p = place_in_mesh()
+
+    def copy(side, s, src):
+        slots = (rising, falling)[side]
+        return pltpu.make_async_remote_copy(
+            src_ref=src,
+            dst_ref=slots.at[s - 1],
+            send_sem=sends.at[side, s - 1],
+            recv_sem=gets.at[side, s - 1],
+            device_id=(c + 2 - 4 * side, f),
+            device_id_type=MESH,
+        )
+
+    def add(side, s, number):
+        slots = (rising, falling)[side]
+        term = block(number)
+
+        def body(i, carry):
+            at = pl.ds(pl.multiple_of(i * chunk, chunk), chunk)
+            slots[s - 1, at, :] = (slots[s - 1, at, :].astype(f32) + term[at, :].astype(f32)).astype(bf16)
+            return carry
+
+        lax.fori_loop(0, rows // chunk, body, 0)
+
+    def step(s):
+        for side in range(2):
+            place = z if side == 0 else planes - 1 - z
+            number = planes - s + place
+            number = number if side == 0 else planes - 1 - number
+
+            @pl.when(place == 0)
+            def _(side=side, number=number):
+                copy(side, s, block(number)).start()
+
+            if s > 1:
+
+                @pl.when((place > 0) & (place < s) & (place < planes - 1))
+                def _(side=side, number=number):
+                    slots = (rising, falling)[side]
+                    copy(side, s - 1, slots.at[s - 2]).wait_recv()
+                    add(side, s - 1, number)
+                    copy(side, s, slots.at[s - 2]).start()
+
+    def finish(out):
+        last = planes - 1
+        for side in range(2):
+            place = z if side == 0 else planes - 1 - z
+            slots = (rising, falling)[side]
+
+            @pl.when(place > 0)
+            def _(side=side, slots=slots):
+                copy(side, last, slots.at[last - 1]).wait_recv()
+
+        mine = block(z)
+
+        def total(ups, downs):
+            def body(i, carry):
+                at = pl.ds(pl.multiple_of(i * chunk, chunk), chunk)
+                value = mine[at, :].astype(f32)
+                if ups:
+                    value = value + rising[last - 1, at, :].astype(f32)
+                if downs:
+                    value = value + falling[last - 1, at, :].astype(f32)
+                out[at, :] = value.astype(out.dtype)
+                return carry
+
+            lax.fori_loop(0, rows // chunk, body, 0)
+
+        @pl.when(z == 0)
+        def _():
+            total(False, True)
+
+        @pl.when(z == planes - 1)
+        def _():
+            total(True, False)
+
+        @pl.when((z > 0) & (z < planes - 1))
+        def _():
+            total(True, True)
+
+        for side in range(2):
+            place = z if side == 0 else planes - 1 - z
+            slots = (rising, falling)[side]
+            for s in range(1, planes):
+
+                @pl.when((place < s) & (place < planes - 1))
+                def _(side=side, slots=slots, s=s):
+                    copy(side, s, slots.at[s - 1]).wait_send()
+
+    return step, finish
+
+
+def line_gather(plan, own, out, sends, gets, share_sends, share_gets, local, height):
+    planes = plan.planes
+    c, f, z, k, p = place_in_mesh()
+    other = c + 1 - 2 * k
+
+    def rows_of(plane, core):
+        return out.at[pl.ds(pl.multiple_of((2 * plane + core) * height, height), height), :]
+
+    def origin(side, s):
+        return z - s if side == 0 else z + s
+
+    def copy(side, s):
+        plane = origin(side, s - 1)
+        src = own if s == 1 else rows_of(plane, k)
+        return pltpu.make_async_remote_copy(
+            src_ref=src,
+            dst_ref=rows_of(plane, k),
+            send_sem=sends.at[side, s - 1],
+            recv_sem=gets.at[side, s - 1],
+            device_id=(c + 2 - 4 * side, f),
+            device_id_type=MESH,
+        )
+
+    def arrival(side, s):
+        here = rows_of(origin(side, s), k)
+        return pltpu.make_async_remote_copy(
+            src_ref=here,
+            dst_ref=here,
+            send_sem=sends.at[side, s - 1],
+            recv_sem=gets.at[side, s - 1],
+            device_id=(c + 2 - 4 * side, f),
+            device_id_type=MESH,
+        )
+
+    def share(side, s, core):
+        plane = origin(side, s)
+        here = rows_of(plane, core)
+        src = own if s == 0 else here
+        return pltpu.make_async_remote_copy(
+            src_ref=src,
+            dst_ref=here,
+            send_sem=share_sends.at[side, s],
+            recv_sem=share_gets.at[side, s],
+            device_id=(other, f),
+            device_id_type=MESH,
+        )
+
+    keep = pltpu.make_async_copy(own, rows_of(z, k), local)
+
+    def sends_at(side, s):
+        place = z if side == 0 else planes - 1 - z
+        return (place >= s - 1) & (place < planes - 1)
+
+    def gets_at(side, s):
+        place = z if side == 0 else planes - 1 - z
+        return place >= s
+
+    def take(s):
+        for side in range(2):
+
+            @pl.when(gets_at(side, s))
+            def _(side=side):
+                arrival(side, s).wait_recv()
+                if s < planes - 1:
+
+                    @pl.when(sends_at(side, s + 1))
+                    def _():
+                        copy(side, s + 1).start()
+
+                share(side, s, k).start()
+
+    def step(s):
+        if s > 1:
+            take(s - 1)
+            return
+        for side in range(2):
+
+            @pl.when(sends_at(side, 1))
+            def _(side=side):
+                copy(side, 1).start()
+
+        share(0, 0, k).start()
+        keep.start()
+
+    def finish():
+        take(planes - 1)
+        keep.wait()
+        share(0, 0, k).wait_send()
+        share(0, 0, 1 - k).wait_recv()
+        for side in range(2):
+            for s in range(1, planes):
+
+                @pl.when(sends_at(side, s))
+                def _(side=side, s=s):
+                    copy(side, s).wait_send()
+
+                @pl.when(gets_at(side, s))
+                def _(side=side, s=s):
+                    share(side, s, k).wait_send()
+                    share(side, s, 1 - k).wait_recv()
+
+    return step, finish
+
+
+def back_owners(plan, src, out, send, recv, lsem):
     unit, ranks = plan.unit, plan.ranks
     c, f, z, k, p = place_in_mesh()
 
@@ -421,65 +619,60 @@
             device_id_type=MESH,
         )
 
+    def local(j, place):
+        return pltpu.make_async_copy(
+            src.at[pl.ds(j * unit, unit), :], out.at[pl.ds(place * unit, unit), :], lsem.at[place]
+        )
+
     blocks = [
         (rank, j, plan.back_units[rank][j] // 5, plan.back_units[rank][j] % 5)
         for rank in range(ranks)
         for j in range(5)
     ]
-    for rank, j, owner, place in blocks:
-
-        @pl.when((p == rank) & ~((c == owner) & (f == z)))
-        def _(j=j, owner=owner, place=place):
-            copy(j, owner, place).start()
-
-        @pl.when((p == rank) & (c == owner) & (f == z))
-        def _(j=j, place=place):
-            pltpu.make_async_copy(
-                src.at[pl.ds(j * unit, unit), :], out.at[pl.ds(place * unit, unit), :], lsem.at[place]
-            ).start()
-
-    for rank, j, owner, place in blocks:
-
-        @pl.when((p == rank) & ~((c == owner) & (f == z)))
-        def _(j=j, owner=owner, place=place):
-            copy(j, owner, place).wait_send()
-
-        @pl.when((c == owner) & ~((p == rank) & (f == z)))
-        def _(j=j, owner=owner, place=place):
-            copy(j, owner, place).wait_recv()
-
-        @pl.when((p == rank) & (c == owner) & (f == z))
-        def _(j=j, place=place):
-            pltpu.make_async_copy(
-                src.at[pl.ds(j * unit, unit), :], out.at[pl.ds(place * unit, unit), :], lsem.at[place]
-            ).wait()
-
-
-def back_to_owner(plan, value):
-    dma = pltpu.SemaphoreType.DMA
-    return pl.pallas_call(
-        functools.partial(back_owner_kernel, plan),
-        in_specs=[pl.BlockSpec(memory_space=pltpu.VMEM)],
-        out_specs=pl.BlockSpec(memory_space=pl.ANY),
-        out_shape=jax.ShapeDtypeStruct(value.shape, value.dtype),
-        scratch_shapes=[dma((5,)), dma((5,)), dma((5,))],
-        compiler_params=pltpu.CompilerParams(has_side_effects=True),
-    )(value)
-
-
-def front_owner_kernel(plan, src, out, send, recv, lsem):
+
+    def start():
+        for rank, j, owner, place in blocks:
+
+            @pl.when((p == rank) & ~((c == owner) & (f == z)))
+            def _(j=j, owner=owner, place=place):
+                copy(j, owner, place).start()
+
+            @pl.when((p == rank) & (c == owner) & (f == z))
+            def _(j=j, place=place):
+                local(j, place).start()
+
+    def finish():
+        for rank, j, owner, place in blocks:
+
+            @pl.when((p == rank) & ~((c == owner) & (f == z)))
+            def _(j=j, owner=owner, place=place):
+                copy(j, owner, place).wait_send()
+
+            @pl.when((c == owner) & ~((p == rank) & (f == z)))
+            def _(j=j, owner=owner, place=place):
+                copy(j, owner, place).wait_recv()
+
+            @pl.when((p == rank) & (c == owner) & (f == z))
+            def _(j=j, place=place):
+                local(j, place).wait()
+
+    return start, finish
+
+
+def front_owners(plan, src, out, send, recv, lsem):
     unit, ranks = plan.unit, plan.ranks
     c, f, z, k, p = place_in_mesh()
-    moves, start = [], 0
+    height = src.shape[0] // 2
+    moves, start_at = [], 0
     for slot, (units, wide) in enumerate(plan.slots):
         for rank in range(ranks):
             owner, place = units[rank] // plan.per_shard, units[rank] % plan.per_shard
-            moves.append((slot, rank, owner, place, start, wide))
-        start += wide
+            moves.append((slot, rank, owner, place, start_at, wide))
+        start_at += wide
 
     def copy(slot, owner, place, begin, wide, half):
         return pltpu.make_async_remote_copy(
-            src_ref=src.at[half, :, pl.ds(begin * unit, wide * unit)],
+            src_ref=src.at[pl.ds(half * height, height), pl.ds(begin * unit, wide * unit)],
             dst_ref=out.at[:, pl.ds(place * unit, wide * unit)],
             send_sem=send.at[slot, half],
             recv_sem=recv.at[place],
@@ -489,54 +682,165 @@
 
     def local(place, begin, wide, half):
         return pltpu.make_async_copy(
-            src.at[half, :, pl.ds(begin * unit, wide * unit)],
+            src.at[pl.ds(half * height, height), pl.ds(begin * unit, wide * unit)],
             out.at[:, pl.ds(place * unit, wide * unit)],
             lsem.at[place],
         )
 
-    for slot, rank, owner, place, begin, wide in moves:
-        for half in range(2):
-            if 2 * owner + half == rank:
-
-                @pl.when(p == rank)
-                def _(place=place, begin=begin, wide=wide, half=half):
-                    local(place, begin, wide, half).start()
-
-            else:
-
-                @pl.when(p == rank)
-                def _(slot=slot, owner=owner, place=place, begin=begin, wide=wide, half=half):
-                    copy(slot, owner, place, begin, wide, half).start()
-
-    for slot, rank, owner, place, begin, wide in moves:
-        for half in range(2):
-            if 2 * owner + half == rank:
-
-                @pl.when(p == rank)
-                def _(place=place, begin=begin, wide=wide, half=half):
-                    local(place, begin, wide, half).wait()
-
-            else:
-
-                @pl.when(p == rank)
-                def _(slot=slot, owner=owner, place=place, begin=begin, wide=wide, half=half):
-                    copy(slot, owner, place, begin, wide, half).wait_send()
-
-                @pl.when(p == 2 * owner + half)
-                def _(slot=slot, owner=owner, place=place, begin=begin, wide=wide, half=half):
-                    copy(slot, owner, place, begin, wide, half).wait_recv()
-
-
-def front_to_owner(plan, value):
+    def start():
+        for slot, rank, owner, place, begin, wide in moves:
+            for half in range(2):
+                if 2 * owner + half == rank:
+
+                    @pl.when(p == rank)
+                    def _(place=place, begin=begin, wide=wide, half=half):
+                        local(place, begin, wide, half).start()
+
+                else:
+
+                    @pl.when(p == rank)
+                    def _(slot=slot, owner=owner, place=place, begin=begin, wide=wide, half=half):
+                        copy(slot, owner, place, begin, wide, half).start()
+
+    def finish():
+        for slot, rank, owner, place, begin, wide in moves:
+            for half in range(2):
+                if 2 * owner + half == rank:
+
+                    @pl.when(p == rank)
+                    def _(place=place, begin=begin, wide=wide, half=half):
+                        local(place, begin, wide, half).wait()
+
+                else:
+
+                    @pl.when(p == rank)
+                    def _(slot=slot, owner=owner, place=place, begin=begin, wide=wide, half=half):
+                        copy(slot, owner, place, begin, wide, half).wait_send()
+
+                    @pl.when(p == 2 * owner + half)
+                    def _(slot=slot, owner=owner, place=place, begin=begin, wide=wide, half=half):
+                        copy(slot, owner, place, begin, wide, half).wait_recv()
+
+    return start, finish
+
+
+VMEM_BLOCK = pl.BlockSpec(memory_space=pltpu.VMEM)
+ANY_BLOCK = pl.BlockSpec(memory_space=pl.ANY)
+
+
+def sum_scratch(plan, rows, columns):
+    dma = pltpu.SemaphoreType.DMA
+    steps = plan.planes - 1
+    slots = pltpu.VMEM((steps, rows, columns), bf16)
+    return [slots, slots, dma((2, steps)), dma((2, steps))]
+
+
+def gather_scratch(plan):
+    dma = pltpu.SemaphoreType.DMA
+    return [dma((2, plan.planes - 1))] * 2 + [dma((2, plan.planes))] * 2 + [dma(())]
+
+
+def busy(microseconds):
+    return pl.CostEstimate(flops=int(microseconds * 900e6), transcendentals=0, bytes_accessed=0)
+
+
+def back_sum_kernel(plan, width, src, out, *scratch):
+    def block(i):
+        return src.at[:, pl.ds(pl.multiple_of(i * width, 128), width)]
+
+    step, finish = line_sum(plan, block, *scratch, src.shape[0])
+    for s in range(1, plan.planes):
+        step(s)
+    finish(out)
+
+
+def back_sums(plan, partial):
+    rows, width = partial.shape[0], D // plan.planes
+    return pl.pallas_call(
+        functools.partial(back_sum_kernel, plan, width),
+        in_specs=[VMEM_BLOCK],
+        out_specs=VMEM_BLOCK,
+        out_shape=jax.ShapeDtypeStruct((rows, width), bf16),
+        scratch_shapes=sum_scratch(plan, rows, width),
+        compiler_params=pltpu.CompilerParams(has_side_effects=True),
+        cost_estimate=busy(90),
+    )(partial)
+
+
+def front_sum_kernel(plan, rows, src, back, out, owned, *scratch):
+    start, done = back_owners(plan, back, owned, *scratch[:3])
+    step, finish = line_sum(
+        plan, lambda i: src.at[pl.ds(pl.multiple_of(i * rows, rows), rows), :], *scratch[3:], rows
+    )
+    step(1)
+    start()
+    for s in range(2, plan.planes):
+        step(s)
+    finish(out)
+    done()
+
+
+def front_sums(plan, partial, back_sum):
+    dma = pltpu.SemaphoreType.DMA
+    rows, width = partial.shape[0] // plan.planes, partial.shape[1]
+    return pl.pallas_call(
+        functools.partial(front_sum_kernel, plan, rows),
+        in_specs=[VMEM_BLOCK, VMEM_BLOCK],
+        out_specs=[VMEM_BLOCK, ANY_BLOCK],
+        out_shape=[
+            jax.ShapeDtypeStruct((rows, width), bf16),
+            jax.ShapeDtypeStruct(back_sum.shape, bf16),
+        ],
+        scratch_shapes=[dma((5,))] * 3 + sum_scratch(plan, rows, width),
+        compiler_params=pltpu.CompilerParams(has_side_effects=True),
+        cost_estimate=busy(120),
+    )(partial, back_sum)
+
+
+def back_next_kernel(plan, own, src, out, owned, *scratch):
+    start, done = front_owners(plan, src, owned, *scratch[:3])
+    step, finish = line_gather(plan, own, out, *scratch[3:], own.shape[0])
+    step(1)
+    start()
+    for s in range(2, plan.planes):
+        step(s)
+    finish()
+    done()
+
+
+def back_nexts(plan, own, front_sum):
     dma = pltpu.SemaphoreType.DMA
     return pl.pallas_call(
-        functools.partial(front_owner_kernel, plan),
-        in_specs=[pl.BlockSpec(memory_space=pltpu.VMEM)],
-        out_specs=pl.BlockSpec(memory_space=pl.ANY),
-        out_shape=jax.ShapeDtypeStruct((value.shape[1], plan.per_shard * plan.unit), value.dtype),
-        scratch_shapes=[dma((5, 2)), dma((plan.per_shard,)), dma((plan.per_shard,))],
+        functools.partial(back_next_kernel, plan),
+        in_specs=[VMEM_BLOCK, VMEM_BLOCK],
+        out_specs=[ANY_BLOCK, ANY_BLOCK],
+        out_shape=[
+            jax.ShapeDtypeStruct((2 * plan.planes * own.shape[0], own.shape[1]), bf16),
+            jax.ShapeDtypeStruct((front_sum.shape[0] // 2, plan.per_shard * plan.unit), bf16),
+        ],
+        scratch_shapes=[dma((5, 2)), dma((plan.per_shard,)), dma((plan.per_shard,))] + gather_scratch(plan),
         compiler_params=pltpu.CompilerParams(has_side_effects=True),
-    )(value)
+        cost_estimate=busy(90),
+    )(own, front_sum)
+
+
+def front_next_kernel(plan, own, out, *scratch):
+    step, finish = line_gather(plan, own, out, *scratch, own.shape[0])
+    for s in range(1, plan.planes):
+        step(s)
+    finish()
+
+
+def front_nexts(plan, own):
+    return pl.pallas_call(
+        functools.partial(front_next_kernel, plan),
+        in_specs=[VMEM_BLOCK],
+        out_specs=ANY_BLOCK,
+        out_shape=jax.ShapeDtypeStruct((2 * plan.planes * own.shape[0], own.shape[1]), bf16),
+        scratch_shapes=gather_scratch(plan),
+        compiler_params=pltpu.CompilerParams(has_side_effects=True),
+        cost_estimate=busy(120),
+    )(own)
 
 
 def gelu_parts(u):
@@ -779,42 +1083,24 @@
     )
     tokens_grad = (cotangent[0].astype(f32) + input_grad).astype(bf16)[None]
 
-    up_links = lambda s: [
-        (2 * i + j, 2 * i + 2 + j) for i in range(min(s, planes - 1)) for j in range(2)
-    ]
-    mirror = lambda links: [
-        (2 * (planes - 1 - a // 2) + a % 2, 2 * (planes - 1 - b // 2) + b % 2) for a, b in links
-    ]
-
-    def sum_over_planes(block_of):
-        rising = falling = None
-        for s in range(1, planes):
-            a = jnp.clip(planes - s + z, 0, planes - 1)
-            b = jnp.clip(s - 1 - (planes - 1 - z), 0, planes - 1)
-            term_a, term_b = block_of(a), block_of(b)
-            if rising is not None:
-                term_a = (term_a.astype(f32) + rising.astype(f32)).astype(bf16)
-                term_b = (term_b.astype(f32) + falling.astype(f32)).astype(bf16)
-            rising = lax.ppermute(term_a, "ctx", up_links(s))
-            falling = lax.ppermute(term_b, "ctx", mirror(up_links(s)))
-        return block_of(z).astype(f32) + rising.astype(f32) + falling.astype(f32)
-
     back_partial = lax.dot_general(
         mixed, plane_grad, contract_first, preferred_element_type=f32
-    ).astype(bf16)
-    back_sum = sum_over_planes(
-        lambda i: lax.dynamic_slice(back_partial, (0, i * col_width), (5 * unit, col_width))
     ).astype(bf16)
     front_partial = lax.dot_general(
         normed, hidden_grad, contract_first, preferred_element_type=f32
     ).astype(bf16)
-    front_rows = D // planes
-    front_sum = sum_over_planes(
-        lambda i: lax.dynamic_slice(front_partial, (i * front_rows, 0), (front_rows, 7 * unit))
-    ).astype(bf16)
-
-    back_grad = back_to_owner(plan, back_sum).astype(f32)
-    front_grad = front_to_owner(plan, front_sum.reshape(2, front_rows // 2, -1)).astype(f32)
+    back_sum = back_sums(plan, back_partial)
+    front_sum, back_owned = front_sums(plan, front_partial, back_sum)
+    back_grad = back_owned.astype(f32)
+    back_new, back_first_new, back_second_new = adam_update(
+        back_master, back_first, back_second, back_grad, learn_rates[1], adam_step[0], weight_decay
+    )
+    back_next, front_owned = back_nexts(plan, back_new.astype(bf16), front_sum)
+    front_grad = front_owned.astype(f32)
+    front_new, front_first_new, front_second_new = adam_update(
+        front_master, front_first, front_second, front_grad, learn_rates[0], adam_step[0], weight_decay
+    )
+    front_next = front_nexts(plan, front_new.astype(bf16))
 
     def column_sums(value):
         ones = jnp.ones((8, value.shape[0]), bf16)
@@ -841,41 +1127,10 @@
     vector_grad = vector_grad.reshape(-1)
 
     count_now = adam_step[0]
-    back_new, back_first_new, back_second_new = adam_update(
-        back_master, back_first, back_second, back_grad, learn_rates[1], count_now, weight_decay
-    )
-    front_new, front_first_new, front_second_new = adam_update(
-        front_master, front_first, front_second, front_grad, learn_rates[0], count_now, weight_decay
-    )
     vectors_new, vector_first_new, vector_second_new = adam_update(
         vectors, vector_first, vector_second, vector_grad, learn_rates[2], count_now, 0.0
     )
 
-    def gather_rows(value):
-        height = value.shape[0]
-        out = jnp.zeros((2 * planes * height, value.shape[1]), value.dtype)
-
-        def place(out, piece, plane):
-            valid = (plane >= 0) & (plane < planes)
-            where = jnp.where(valid, plane, z)
-            mine, other = piece
-            out = lax.dynamic_update_slice(out, mine, ((2 * where + k) * height, 0))
-            return lax.dynamic_update_slice(out, other, ((2 * where + 1 - k) * height, 0))
-
-        rising = falling = value
-        pieces = []
-        for s in range(1, planes):
-            links = [(2 * i + j, 2 * i + 2 + j) for i in range(s - 1, planes - 1) for j in range(2)]
-            rising = lax.ppermute(rising, "ctx", links)
-            falling = lax.ppermute(falling, "ctx", mirror(links))
-            pieces.append(((rising, swap_core(rising)), z - s))
-            pieces.append(((falling, swap_core(falling)), z + s))
-        for piece, plane in pieces:
-            out = place(out, piece, plane)
-        return place(out, (value, swap_core(value)), z)
-
-    back_next = gather_rows(back_new.astype(bf16))
-    front_next = gather_rows(front_new.astype(bf16))
     return (
         layer_out,
         tokens_grad,

time: 1060 us -> 1040 us (0.981)
  Pallas kernels: 222 us -> 626 us
  waiting for transfers between devices: 381 us -> 128 us
  starting transfers between devices: 136 us -> 32.2 us
  local copies, waits for them, and re-layouts: 123 us -> 65 us
    pallas_call x2 -> x4, Pallas kernels: 84.9 us -> 489 us  [the longest x1 153 us: front_sums(): pl.pallas_call(functools.partial(front_sum_kernel, plan, rows), in_specs=...]
    ppermute x24 -> x0, waiting for transfers between devices: 178 us -> none  [the longest x6 112 us: gather_rows(): falling = lax.ppermute(falling, 'ctx', mirror(links))]
    ppermute x11, waiting for transfers between devices: 124 us -> 21.5 us  [to_plane(): lax.ppermute(value, 'ctx', [(2 * i + j, 2 * (i ^ step) + j) for i in rang...]
    ppermute x24 -> x0, starting transfers between devices: 82.2 us -> none  [the longest x6 46.4 us: gather_rows(): rising = lax.ppermute(rising, 'ctx', links)]
    dynamic_update_slice x28 -> x0, local copies, waits for them, and re-layouts: 54.3 us -> none  [the longest x14 30.1 us: place(): out = lax.dynamic_update_slice(out, mine, ((2 * where + k) * height, 0))]
    ppermute x11, waiting for transfers between devices: 57.3 us -> 95 us  [to_shard(): return lax.ppermute(value, 'fsdp', [(i, i ^ step) for i in range(shards)])]
    all_gather x1, waiting for transfers between devices: 20.7 us -> 0.01 us  [gather_plane(): mine = lax.all_gather(value, 'fsdp')]
    convert_element_type x10 -> x2, other arithmetic: 39 us -> 19.5 us  [the longest x1 11.6 us: per_device(): front_next = front_nexts(plan, front_new.astype(bf16))]
  transfers between devices with their start and end apart: 67 -> 29, of which waited for: 17 -> 7; matrix products, arithmetic and copies ran while one was open for 21% -> 11% of each run, Pallas kernels for 8% -> 38%
where the time goes in v3:
time: 1040 us
  Pallas kernels  626 us (60%)
  waiting for transfers between devices  128 us (12%)
  other arithmetic  89.6 us (9%)
  matrix products  71.9 us (7%)
  local copies, waits for them, and re-layouts  65 us (6%)
  starting transfers between devices  32.2 us (3%)
  between operations  25.5 us (2%)
    pallas_call x1, Pallas kernels, front_sums(): pl.pallas_call(functools.partial(front_sum_kernel, plan, rows), in_specs=...  153 us
    pallas_call x1, Pallas kernels, front_nexts(): pl.pallas_call(functools.partial(front_next_kernel, plan), in_specs=[VMEM...  133 us
    pallas_call x1, Pallas kernels, gather_first(): pl.pallas_call(functools.partial(gather_kernel, plan), in_specs=[vmem, vm...  111 us
    pallas_call x1, Pallas kernels, back_nexts(): pl.pallas_call(functools.partial(back_next_kernel, plan), in_specs=[VMEM_...  106 us
    pallas_call x1, Pallas kernels, back_sums(): pl.pallas_call(functools.partial(back_sum_kernel, plan, width), in_specs=...  97.1 us
    ppermute x11, waiting for transfers between devices, to_shard(): return lax.ppermute(value, 'fsdp', [(i, i ^ step) for i in range(shards)])  95 us
    pallas_call x1, Pallas kernels, attention(): pl.pallas_call(attention_kernel, grid=(length // block,), in_specs=[rows,...  26.3 us
    ppermute x11, waiting for transfers between devices, to_plane(): lax.ppermute(value, 'ctx', [(2 * i + j, 2 * (i ^ step) + j) for i in rang...  21.5 us
  transfers between devices with their start and end apart: 29, of which 7 were waited for; matrix products, arithmetic and copies ran while one was open for 11% of the time, Pallas kernels for 38%

profile of v3, /device:TPU:0, one launch (start us, length us, event | category | flops | bytes accessed | tf_op | source)
XLA Modules:
  0.0 1038.4 jit_solution(6095535066683346364)
XLA Ops:
  8.5 110.9 %shard_map.441 = (bf16[4,2,128,2048]{3,2,1,0:T(8,128)(2,1)}, f32[1,1024]{1,0:T(1,128)}, bf16[2048,768]{1,0:T(8,128)(2,1)}, bf16[256,2048]{1,0:T(8,128)(2,1)}) custom-call(bf16[128,2048]{1,0:T(8,128)(2,1)} %bitcast.190, f32[1,1024]{1,0:T(1,128)} %convert_element_type.188.doc, bf16[2048,3584]{1,0:T(8,128)(2,1)} %front.1, bf16[10240,512]{1,0:T(8,128)(2,1)} %back.1), custom_call_target="tpu_custom_call" | custom-call | tf_op jit(solution)/shard_map/pallas_call | solution.py:381
  120.7 4.1 constant_dynamic-slice_fusion.13
  145.1 8.6 fusion.48
  179.7 11.5 %collective-permute-done.10 = bf16[2048,512]{1,0:T(8,128)(2,1)} collective-permute-done((bf16[2048,512]{1,0:T(8,128)(2,1)}, bf16[2048,512]{1,0:T(8,128)(2,1)}, u32[]{:S(2)}, u32[]{:S(2)}) %collective-permute-start.10) | collective-permute-done | bytes 2097184 | tf_op jit(solution)/shard_map/ppermute | solution.py:960
  191.2 6.3 dynamic-slice_select_fusion.1
  199.7 3.6 constant_dynamic-slice_fusion.1
  216.4 15.3 %collective-permute-done.12 = bf16[1024,512]{1,0:T(8,128)(2,1)S(1)} collective-permute-done((bf16[1024,512]{1,0:T(8,128)(2,1)S(1)}, bf16[1024,512]{1,0:T(8,128)(2,1)S(1)}, u32[]{:S(2)}, u32[]{:S(2)}) %collective-permute-start.12) | collective-permute-done | bytes 1048608 | tf_op jit(solution)/shard_map/ppermute | solution.py:913
  231.9 60.2 %collective-permute-done.13 = bf16[1024,512]{1,0:T(8,128)(2,1)S(1)} collective-permute-done((bf16[1024,512]{1,0:T(8,128)(2,1)S(1)}, bf16[1024,512]{1,0:T(8,128)(2,1)S(1)}, u32[]{:S(2)}, u32[]{:S(2)}) %collective-permute-start.13) | collective-permute-done | bytes 1048608 | tf_op jit(solution)/shard_map/ppermute | solution.py:913
  293.7 4.3 dynamic-slice_select_fusion
  305.4 7.5 multiply_convert_fusion.1
  313.7 26.3 %shard_map.442 = (bf16[1024,256]{1,0:T(8,128)(2,1)}, f32[1024,256]{1,0:T(8,128)}, f32[1024,256]{1,0:T(8,128)}, f32[1024,256]{1,0:T(8,128)}) custom-call(bf16[1024,256]{1,0:T(8,128)(2,1)} %get-tuple-element.112.q_ref, bf16[1024,256]{1,0:T(8,128)(2,1)} %get-tuple-element.111.k_ref, bf16[1024,256]{1,0:T(8,128)(2,1)} %get-tuple-element.110.v_ref, ...), custom_call_target="tpu_custom_call" | custom-call | flops 3758096384 | bytes 5242880 | tf_op jit(solution)/shard_map/pallas_call | solution.py:203
  340.0 5.1 fusion.73
  347.2 15.5 %fusion.65 = (bf16[1024,256]{1,0:T(8,128)(2,1)S(1)}, bf16[1024,256]{1,0:T(8,128)(2,1)S(1)}) fusion(f32[1024,256]{1,0:T(8,128)S(1)} %copy-done.8, f32[1024,240]{1,0:T(8,128)S(1)} %bitcast.193, f32[1024,16]{1,0:T(8,128)S(1)} %slice.260, f32[1024,16]{1,0:T(8,128)S(1)} %slice.263, f32[1024,240]{1,0:T(8,128)S(1)} %slice.262, f32[1024]{0:T(1024)S(1)} %bitcast.221, ...), kind=kLoop, calls=%fused_computation.110 | loop fusion | flops 3670016 | bytes 7345408 | tf_op jit(solution)/shard_map/convert_element_type | solution.py:1044
  367.7 7.8 multiply_convert_fusion
  375.4 13.7 %collective-permute-done.8 = bf16[256,1024]{1,0:T(8,128)(2,1)S(1)} collective-permute-done((bf16[256,1024]{1,0:T(8,128)(2,1)S(1)}, bf16[256,1024]{1,0:T(8,128)(2,1)S(1)}, u32[]{:S(2)}, u32[]{:S(2)}) %collective-permute-start.8) | collective-permute-done | bytes 524320 | tf_op jit(solution)/shard_map/ppermute | solution.py:916
  397.8 11.6 %convolution_convert_fusion.src = bf16[1280,2048]{1,0:T(8,128)(2,1)} fusion(bf16[1024,2048]{1,0:T(8,128)(2,1)} %bitcast.202, bf16[256,1024]{0,1:T(8,128)(2,1)} %copy.68, bf16[256,1024]{0,1:T(8,128)(2,1)} %copy.67, bf16[256,1024]{0,1:T(8,128)(2,1)} %copy.66, bf16[256,1024]{0,1:T(8,128)(2,1)} %copy.65, bf16[1024,1024]{0,1:T(8,128)(2,1)} %get-tuple-element.154), kind=kOutput, calls=%fused_computation.10 | convolution fusion | flops 5390991360 | bytes 13631488 | tf_op jit(solution)/shard_map/dot_general | solution.py:1086
  409.5 9.1 fusion.14
  418.5 15.4 %fusion.4 = f32[1024,2048]{1,0:T(8,128)} fusion(bf16[2048,512]{1,0:T(8,128)(2,1)S(1)} %dynamic-slice_select_fusion, bf16[2048,512]{1,0:T(8,128)(2,1)} %get-tuple-element.74, bf16[2048,768]{1,0:T(8,128)(2,1)} %get-tuple-element.37, bf16[256,1024]{0,1:T(8,128)(2,1)} %copy.68, bf16[256,1024]{0,1:T(8,128)(2,1)} %copy.67, bf16[256,1024]{0,1:T(8,128)(2,1)} %copy.66, ...), kind=kOutput, calls=%fused_computation.12 | convolution fusion | flops 7556562944 | bytes 19922944 | tf_op jit(solution)/shard_map/dot_general | solution.py:1075
  433.9 12.1 %convolution_convert_fusion.1.src = bf16[2048,1792]{1,0:T(8,128)(2,1)} fusion(bf16[1024,2048]{1,0:T(8,128)(2,1)S(1)} %copy-done.12, bf16[256,1024]{0,1:T(8,128)(2,1)} %copy.68, bf16[256,1024]{0,1:T(8,128)(2,1)} %copy.67, bf16[256,1024]{0,1:T(8,128)(2,1)} %copy.66, bf16[256,1024]{0,1:T(8,128)(2,1)} %copy.65, bf16[1024,1024]{0,1:T(8,128)(2,1)} %multiply_convert_fusion), kind=kOutput, calls=%fused_computation.11 | convolution fusion | flops 7538212864 | bytes 15728640 | tf_op jit(solution)/shard_map/dot_general | solution.py:1089
  446.0 97.1 %shard_map.443.back = bf16[1280,512]{1,0:T(8,128)(2,1)} custom-call(bf16[1280,2048]{1,0:T(8,128)(2,1)} %convolution_convert_fusion.src), custom_call_target="tpu_custom_call" | custom-call | flops 80999997440 | tf_op jit(solution)/shard_map/pallas_call | solution.py:759
  543.1 3.9 fusion.30
  546.9 3.9 fusion.29
  551.3 153.5 %shard_map.444 = (bf16[512,1792]{1,0:T(8,128)(2,1)}, bf16[1280,512]{1,0:T(8,128)(2,1)}) custom-call(bf16[2048,1792]{1,0:T(8,128)(2,1)} %convolution_convert_fusion.1.src, bf16[1280,512]{1,0:T(8,128)(2,1)} %shard_map.443.back), custom_call_target="tpu_custom_call" | custom-call | flops 108000002048 | tf_op jit(solution)/shard_map/pallas_call | solution.py:786
  704.8 8.0 fusion.114
  712.8 105.7 %shard_map.445 = (bf16[10240,512]{1,0:T(8,128)(2,1)}, bf16[256,3584]{1,0:T(8,128)(2,1)}) custom-call(bf16[1280,512]{1,0:T(8,128)(2,1)} %get-tuple-element.68.own, bf16[512,1792]{1,0:T(8,128)(2,1)} %get-tuple-element.52.src), custom_call_target="tpu_custom_call" | custom-call | flops 80999997440 | tf_op jit(solution)/shard_map/pallas_call | solution.py:813
  818.5 11.6 %fusion.111 = (bf16[256,3584]{1,0:T(8,128)(2,1)}, f32[256,3584]{1,0:T(8,128)}, f32[256,3584]{1,0:T(8,128)}, f32[256,3584]{1,0:T(8,128)}, f32[256,3584]{1,0:T(8,128)}) fusion(f32[256,3584]{1,0:T(8,128)} %param.42, f32[]{:T(128)} %bitcast.65, f32[]{:T(128)} %bitcast.64, f32[]{:T(128)} %bitcast.69, f32[256,3584]{1,0:T(8,128)} %param.46, ...), kind=kLoop, calls=%fused_computation.231 | loop fusion | flops 15597568 | bytes 29360140 | tf_op jit(solution)/shard_map/convert_element_type | solution.py:1103
  838.1 132.7 %shard_map.446 = bf16[2048,3584]{1,0:T(8,128)(2,1)} custom-call(bf16[256,3584]{1,0:T(8,128)(2,1)} %get-tuple-element.59.own), custom_call_target="tpu_custom_call" | custom-call | flops 108000002048 | tf_op jit(solution)/shard_map/pallas_call | solution.py:835
  977.1 3.6 bitcast_add_fusion.1
  986.2 4.4 collective-permute-done.25
  992.2 19.5 %collective-permute-done.26 = f32[160,128]{1,0:T(8,128)S(1)} collective-permute-done((f32[160,128]{1,0:T(8,128)S(1)}, f32[160,128]{1,0:T(8,128)S(1)}, u32[]{:S(2)}, u32[]{:S(2)}) %collective-permute-start.26) | collective-permute-done | bytes 81952 | tf_op jit(solution)/shard_map/ppermute | solution.py:913
  1018.5 7.4 copy.91
  1027.3 4.1 copy.92
  (318 shorter events, 108.8 us)
Async XLA Ops:
  7.2 197.1 %all-gather.3.cloned.1.call-start = ((), (), s32[]{:S(2)}) async-start(), calls=%async_computation | async-start | bytes 2621440 | tf_op jit(solution)/shard_map/all_gather | solution.py:921
  124.8 66.4 %collective-permute-start.10 = (bf16[2048,512]{1,0:T(8,128)(2,1)}, bf16[2048,512]{1,0:T(8,128)(2,1)}, u32[]{:S(2)}, u32[]{:S(2)}) collective-permute-start(bf16[2048,512]{1,0:T(8,128)(2,1)} %constant_dynamic-slice_fusion.13), channel_id=1, source_target_pairs={{2,0},{10,8},{18,16},{26,24},{6,4},{14,12},{22,20},{30,28},{7,5},{... | collective-permute-start | bytes 6291464 | tf_op jit(solution)/shard_map/ppermute | solution.py:960
  155.0 50.6 %collective-permute-start.2 = (bf16[256,768]{1,0:T(8,128)(2,1)}, bf16[256,768]{1,0:T(8,128)(2,1)}, u32[]{:S(2)}, u32[]{:S(2)}) collective-permute-start(bf16[256,768]{1,0:T(8,128)(2,1)} %get-tuple-element.114), channel_id=1, source_target_pairs={{0,24},{4,28},{8,16},{12,20},{16,8},{20,12},{24,0},{28,4},{1,25},{... | collective-permute-start | bytes 1179656 | tf_op jit(solution)/shard_map/ppermute | solution.py:916
  158.1 48.9 %collective-permute-start.1 = (bf16[256,768]{1,0:T(8,128)(2,1)}, bf16[256,768]{1,0:T(8,128)(2,1)}, u32[]{:S(2)}, u32[]{:S(2)}) collective-permute-start(bf16[256,768]{1,0:T(8,128)(2,1)} %get-tuple-element.115), channel_id=1, source_target_pairs={{0,16},{4,20},{8,24},{12,28},{16,0},{20,4},{24,8},{28,12},{1,17},{... | collective-permute-start | bytes 1179656 | tf_op jit(solution)/shard_map/ppermute | solution.py:916
  158.1 52.6 %collective-permute-start = (bf16[256,768]{1,0:T(8,128)(2,1)}, bf16[256,768]{1,0:T(8,128)(2,1)}, u32[]{:S(2)}, u32[]{:S(2)}) collective-permute-start(bf16[256,768]{1,0:T(8,128)(2,1)} %get-tuple-element.116), channel_id=1, source_target_pairs={{0,8},{4,12},{8,0},{12,4},{16,24},{20,28},{24,16},{28,20},{1,9},{5... | collective-permute-start | bytes 1179656 | tf_op jit(solution)/shard_map/ppermute | solution.py:916
  197.6 94.8 %collective-permute-start.11 = (bf16[2048,512]{1,0:T(8,128)(2,1)}, bf16[2048,512]{1,0:T(8,128)(2,1)S(1)}, u32[]{:S(2)}, u32[]{:S(2)}) collective-permute-start(bf16[2048,512]{1,0:T(8,128)(2,1)} %get-tuple-element.75), channel_id=1, source_target_pairs={{2,0},{10,8},{18,16},{26,24},{3,1},{11,9},{19,17},{27,25},{7,4},{1... | collective-permute-start | bytes 6291464 | tf_op jit(solution)/shard_map/ppermute | solution.py:960
  204.3 93.7 %collective-permute-start.3 = (bf16[4,128,2048]{2,1,0:T(8,128)(2,1)}, bf16[4,128,2048]{2,1,0:T(8,128)(2,1)S(1)}, u32[]{:S(2)}, u32[]{:S(2)}) collective-permute-start(bf16[4,128,2048]{2,1,0:T(8,128)(2,1)} %bitcast.204), channel_id=1, source_target_pairs={{0,4},{4,0},{8,12},{12,8},{16,20},{20,16},{24,28},{28,24},{1,5},{5... | collective-permute-start | bytes 6291464 | tf_op jit(solution)/shard_map/ppermute | solution.py:910
  205.6 26.1 %collective-permute-start.12 = (bf16[1024,512]{1,0:T(8,128)(2,1)S(1)}, bf16[1024,512]{1,0:T(8,128)(2,1)S(1)}, u32[]{:S(2)}, u32[]{:S(2)}) collective-permute-start(bf16[1024,512]{1,0:T(8,128)(2,1)S(1)} %pad_maximum_fusion.8), channel_id=1, source_target_pairs={{0,1},{1,0},{2,3},{3,2},{4,5},{5,4},{6,7},{7,6},{8,9},{9,8},{10,11... | collective-permute-start | bytes 3145736 | tf_op jit(solution)/shard_map/ppermute | solution.py:913
  207.0 85.0 %collective-permute-start.13 = (bf16[1024,512]{1,0:T(8,128)(2,1)S(1)}, bf16[1024,512]{1,0:T(8,128)(2,1)S(1)}, u32[]{:S(2)}, u32[]{:S(2)}) collective-permute-start(bf16[1024,512]{1,0:T(8,128)(2,1)S(1)} %pad_maximum_fusion.9), channel_id=1, source_target_pairs={{0,2},{1,3},{2,0},{3,1},{4,6},{5,7},{6,4},{7,5},{8,10},{9,11},{10,... | collective-permute-start | bytes 3145736 | tf_op jit(solution)/shard_map/ppermute | solution.py:913
  210.7 81.5 %collective-permute-start.14 = (bf16[1024,512]{1,0:T(8,128)(2,1)S(1)}, bf16[1024,512]{1,0:T(8,128)(2,1)S(1)}, u32[]{:S(2)}, u32[]{:S(2)}) collective-permute-start(bf16[1024,512]{1,0:T(8,128)(2,1)S(1)} %copy-done.24), channel_id=1, source_target_pairs={{0,3},{1,2},{2,1},{3,0},{4,7},{5,6},{6,5},{7,4},{8,11},{9,10},{10,... | collective-permute-start | bytes 3145736 | tf_op jit(solution)/shard_map/ppermute | solution.py:913
  300.9 11.9 %collective-permute-start.6 = (bf16[256,256]{1,0:T(8,128)(2,1)S(1)}, bf16[256,256]{1,0:T(8,128)(2,1)S(1)}, u32[]{:S(2)}, u32[]{:S(2)}) collective-permute-start(bf16[256,256]{1,0:T(8,128)(2,1)S(1)} %get-tuple-element.124), channel_id=1, source_target_pairs={{0,24},{4,28},{8,16},{12,20},{16,8},{20,12},{24,0},{28,4},{1,25},{... | collective-permute-start | bytes 393224 | tf_op jit(solution)/shard_map/ppermute | solution.py:916
  303.8 9.1 collective-permute-start.5
  303.8 9.1 collective-permute-start.4
  363.2 12.2 %collective-permute-start.9 = (bf16[256,1024]{1,0:T(8,128)(2,1)S(1)}, bf16[256,1024]{1,0:T(8,128)(2,1)S(1)}, u32[]{:S(2)}, u32[]{:S(2)}) collective-permute-start(bf16[256,1024]{1,0:T(8,128)(2,1)S(1)} %get-tuple-element.107), channel_id=1, source_target_pairs={{0,24},{4,28},{8,16},{12,20},{16,8},{20,12},{24,0},{28,4},{1,25},{... | collective-permute-start | bytes 1572872 | tf_op jit(solution)/shard_map/ppermute | solution.py:916
  366.0 23.1 %collective-permute-start.8 = (bf16[256,1024]{1,0:T(8,128)(2,1)S(1)}, bf16[256,1024]{1,0:T(8,128)(2,1)S(1)}, u32[]{:S(2)}, u32[]{:S(2)}) collective-permute-start(bf16[256,1024]{1,0:T(8,128)(2,1)S(1)} %get-tuple-element.108), channel_id=1, source_target_pairs={{0,16},{4,20},{8,24},{12,28},{16,0},{20,4},{24,8},{28,12},{1,17},{... | collective-permute-start | bytes 1572872 | tf_op jit(solution)/shard_map/ppermute | solution.py:916
  366.0 23.1 %collective-permute-start.7 = (bf16[256,1024]{1,0:T(8,128)(2,1)S(1)}, bf16[256,1024]{1,0:T(8,128)(2,1)S(1)}, u32[]{:S(2)}, u32[]{:S(2)}) collective-permute-start(bf16[256,1024]{1,0:T(8,128)(2,1)S(1)} %get-tuple-element.109), channel_id=1, source_target_pairs={{0,8},{4,12},{8,0},{12,4},{16,24},{20,28},{24,16},{28,20},{1,9},{5... | collective-permute-start | bytes 1572872 | tf_op jit(solution)/shard_map/ppermute | solution.py:916
  550.8 154.0 %copy-start.18 = (f32[1280,512]{1,0:T(8,128)S(1)}, f32[1280,512]{1,0:T(8,128)}, u32[]{:S(2)}) copy-start(f32[1280,512]{1,0:T(8,128)} %param.43) | copy-start | bytes 7864324
  550.8 426.3 %collective-permute-start.15 = (bf16[4,128,2048]{2,1,0:T(8,128)(2,1)}, bf16[4,128,2048]{2,1,0:T(8,128)(2,1)}, u32[]{:S(2)}, u32[]{:S(2)}) collective-permute-start(bf16[4,128,2048]{2,1,0:T(8,128)(2,1)} %fusion.29), channel_id=1, source_target_pairs={{0,4},{4,0},{8,12},{12,8},{16,20},{20,16},{24,28},{28,24},{1,5},{5... | collective-permute-start | bytes 6291464 | tf_op jit(solution)/shard_map/ppermute | solution.py:910
  550.8 279.3 %collective-permute-start.19 = (bf16[4,128,2048]{2,1,0:T(8,128)(2,1)}, bf16[4,128,2048]{2,1,0:T(8,128)(2,1)}, u32[]{:S(2)}, u32[]{:S(2)}) collective-permute-start(bf16[4,128,2048]{2,1,0:T(8,128)(2,1)} %fusion.30), channel_id=1, source_target_pairs={{0,4},{4,0},{8,12},{12,8},{16,20},{20,16},{24,28},{28,24},{1,5},{5... | collective-permute-start | bytes 6291464 | tf_op jit(solution)/shard_map/ppermute | solution.py:910
  834.5 139.6 %collective-permute-start.20 = (bf16[128,2048]{1,0:T(8,128)(2,1)S(1)}, bf16[128,2048]{1,0:T(8,128)(2,1)}, u32[]{:S(2)}, u32[]{:S(2)}) collective-permute-start(bf16[128,2048]{1,0:T(8,128)(2,1)S(1)} %get-tuple-element.84), channel_id=1, source_target_pairs={{0,1},{1,0},{2,3},{3,2},{4,5},{5,4},{6,7},{7,6},{8,9},{9,8},{10,11... | collective-permute-start | bytes 1572872 | tf_op jit(solution)/shard_map/ppermute | solution.py:913
  836.0 138.2 %collective-permute-start.22 = (bf16[128,2048]{1,0:T(8,128)(2,1)S(1)}, bf16[128,2048]{1,0:T(8,128)(2,1)}, u32[]{:S(2)}, u32[]{:S(2)}) collective-permute-start(bf16[128,2048]{1,0:T(8,128)(2,1)S(1)} %get-tuple-element.85), channel_id=1, source_target_pairs={{0,3},{1,2},{2,1},{3,0},{4,7},{5,6},{6,5},{7,4},{8,11},{9,10},{10,... | collective-permute-start | bytes 1572872 | tf_op jit(solution)/shard_map/ppermute | solution.py:913
  837.5 136.7 %collective-permute-start.21 = (bf16[128,2048]{1,0:T(8,128)(2,1)S(1)}, bf16[128,2048]{1,0:T(8,128)(2,1)}, u32[]{:S(2)}, u32[]{:S(2)}) collective-permute-start(bf16[128,2048]{1,0:T(8,128)(2,1)S(1)} %get-tuple-element.86), channel_id=1, source_target_pairs={{0,2},{1,3},{2,0},{3,1},{4,6},{5,7},{6,4},{7,5},{8,10},{9,11},{10,... | collective-permute-start | bytes 1572872 | tf_op jit(solution)/shard_map/ppermute | solution.py:913
  838.1 132.7 %copy-start.26 = (bf16[256,1024]{0,1:T(8,128)(2,1)S(1)}, bf16[256,1024]{0,1:T(8,128)(2,1)}, u32[]{:S(2)}) copy-start(bf16[256,1024]{0,1:T(8,128)(2,1)} %copy.65) | copy-start | bytes 1572868
  838.1 132.7 %copy-start.28 = (bf16[256,1024]{0,1:T(8,128)(2,1)S(1)}, bf16[256,1024]{0,1:T(8,128)(2,1)}, u32[]{:S(2)}) copy-start(bf16[256,1024]{0,1:T(8,128)(2,1)} %copy.68) | copy-start | bytes 1572868
  976.7 4.0 collective-permute-start.23
  980.7 5.4 collective-permute-start.24
  982.6 29.2 %collective-permute-start.16 = (bf16[128,2048]{1,0:T(8,128)(2,1)S(1)}, bf16[128,2048]{1,0:T(8,128)(2,1)S(1)}, u32[]{:S(2)}, u32[]{:S(2)}) collective-permute-start(bf16[128,2048]{1,0:T(8,128)(2,1)S(1)} %get-tuple-element.87), channel_id=1, source_target_pairs={{0,1},{1,0},{2,3},{3,2},{4,5},{5,4},{6,7},{7,6},{8,9},{9,8},{10,11... | collective-permute-start | bytes 1572872 | tf_op jit(solution)/shard_map/ppermute | solution.py:913
  983.2 28.6 %collective-permute-start.18 = (bf16[128,2048]{1,0:T(8,128)(2,1)S(1)}, bf16[128,2048]{1,0:T(8,128)(2,1)S(1)}, u32[]{:S(2)}, u32[]{:S(2)}) collective-permute-start(bf16[128,2048]{1,0:T(8,128)(2,1)S(1)} %get-tuple-element.88), channel_id=1, source_target_pairs={{0,3},{1,2},{2,1},{3,0},{4,7},{5,6},{6,5},{7,4},{8,11},{9,10},{10,... | collective-permute-start | bytes 1572872 | tf_op jit(solution)/shard_map/ppermute | solution.py:913
  985.6 26.2 %collective-permute-start.17 = (bf16[128,2048]{1,0:T(8,128)(2,1)S(1)}, bf16[128,2048]{1,0:T(8,128)(2,1)S(1)}, u32[]{:S(2)}, u32[]{:S(2)}) collective-permute-start(bf16[128,2048]{1,0:T(8,128)(2,1)S(1)} %get-tuple-element.89), channel_id=1, source_target_pairs={{0,2},{1,3},{2,0},{3,1},{4,6},{5,7},{6,4},{7,5},{8,10},{9,11},{10,... | collective-permute-start | bytes 1572872 | tf_op jit(solution)/shard_map/ppermute | solution.py:913
  986.1 4.5 collective-permute-start.25
  990.7 21.0 %collective-permute-start.26 = (f32[160,128]{1,0:T(8,128)S(1)}, f32[160,128]{1,0:T(8,128)S(1)}, u32[]{:S(2)}, u32[]{:S(2)}) collective-permute-start(f32[160,128]{1,0:T(8,128)S(1)} %add.458), channel_id=1, source_target_pairs={{0,2},{1,3},{2,0},{3,1},{4,6},{5,7},{6,4},{7,5},{8,10},{9,11},{10,... | collective-permute-start | bytes 245768 | tf_op jit(solution)/shard_map/ppermute | solution.py:913
  1011.7 5.4 collective-permute-start.27
  (70 other events, 888.9 us)
Sparse Core Ops, SparseCore 0:
  119.6 53.1 all-gather.2

commit v4 on v3

--- a/solution.py
+++ b/solution.py
@@ -222,6 +222,14 @@
 MESH = pl.DeviceIdType.MESH
 
 
+VMEM_BLOCK = pl.BlockSpec(memory_space=pltpu.VMEM)
+ANY_BLOCK = pl.BlockSpec(memory_space=pl.ANY)
+
+
+def busy(microseconds):
+    return pl.CostEstimate(flops=int(microseconds * 900e6), transcendentals=0, bytes_accessed=0)
+
+
 def place_in_mesh():
     c, f = lax.axis_index("ctx"), lax.axis_index("fsdp")
     z, k = lax.div(c, 2), lax.rem(c, 2)
@@ -238,13 +246,14 @@
 
 
 def gather_kernel(
-    plan, tok, doc, front, back, tok_out, doc_out, w_out, b_out,
+    plan, tok, cot, doc, front, back, tok_out, cot_out, doc_out, w_out, b_out,
     w_buf, b_buf, tsend, trecv, csend, crecv, wsend, wrecv, bsend, brecv, dsend, drecv, lsem,
 ):
     shards, unit, ranks = plan.fsdp, plan.unit, plan.ranks
     c, f, z, k, p = place_in_mesh()
     other = c + 1 - 2 * k
     width = D // shards
+    both = ((tok, tok_out), (cot, cot_out))
 
     def cols(block):
         return pl.ds(pl.multiple_of(block * width, 128), width)
@@ -260,21 +269,22 @@
     def giver(step):
         return lax.rem(f + shards - step, shards)
 
-    def send_tokens(step):
-        return remote(tok, tok_out.at[f, k], tsend.at[step], trecv.at[step], (c, peer(step)))
-
-    def get_tokens(step):
-        here = tok_out.at[giver(step), k]
-        return remote(here, here, tsend.at[step], trecv.at[step], (c, peer(step)))
-
-    def share(step):
-        here = tok_out.at[giver(step), k]
-        src = tok if step == 0 else here
-        return remote(src, here, csend.at[step], crecv.at[step], (other, f))
-
-    def get_share(step):
-        here = tok_out.at[giver(step), 1 - k]
-        return remote(here, here, csend.at[step], crecv.at[step], (other, f))
+    def send_tokens(n, step):
+        src, out = both[n]
+        return remote(src, out.at[f, k], tsend.at[n, step], trecv.at[n, step], (c, peer(step)))
+
+    def get_tokens(n, step):
+        here = both[n][1].at[giver(step), k]
+        return remote(here, here, tsend.at[n, step], trecv.at[n, step], (c, peer(step)))
+
+    def share(n, step):
+        src, out = both[n]
+        here = out.at[giver(step), k]
+        return remote(src if step == 0 else here, here, csend.at[n, step], crecv.at[n, step], (other, f))
+
+    def get_share(n, step):
+        here = both[n][1].at[giver(step), 1 - k]
+        return remote(here, here, csend.at[n, step], crecv.at[n, step], (other, f))
 
     def rows_of(dst):
         return pl.ds(pl.multiple_of((2 * dst + k) * unit, unit), unit)
@@ -291,28 +301,14 @@
     def send_doc(step):
         return remote(doc, doc_out, dsend.at[step], drecv, (c, peer(step)))
 
-    weights = []
-    for slot in range(3):
-        units, _ = plan.slots[slot]
-        for dst in range(ranks):
-            src, at = units[dst] // plan.per_shard, units[dst] % plan.per_shard
-            weights.append((slot, dst, 2 * src + dst % 2, at))
-
-    def send_weight(slot, dst, at):
-        return remote(
-            front.at[:, pl.ds(at * unit, unit)],
-            w_out.at[:, pl.ds(slot * unit, unit)],
-            wsend.at[slot, dst // 2],
-            wrecv.at[slot],
-            (c, dst // 2),
-        )
-
-    own_tok = pltpu.make_async_copy(tok, tok_out.at[f, k], lsem.at[0])
+    start_weights, finish_weights = weight_moves(plan, range(3), front, w_out, w_buf, wsend, wrecv, lsem.at[2])
+    own = [pltpu.make_async_copy(src, out.at[f, k], lsem.at[4 * n]) for n, (src, out) in enumerate(both)]
     own_doc = pltpu.make_async_copy(doc, doc_out, lsem.at[1])
-    for step in range(1, shards):
-        send_tokens(step).start()
-    share(0).start()
-    own_tok.start()
+    for n in range(2):
+        for step in range(1, shards):
+            send_tokens(n, step).start()
+        share(n, 0).start()
+        own[n].start()
     for step in range(1, shards):
         send_back(step).start()
 
@@ -322,27 +318,14 @@
         for step in range(1, shards):
             send_doc(step).start()
 
-    for slot, dst, src, at in weights:
-        if src != dst:
-
-            @pl.when(p == src)
-            def _(slot=slot, dst=dst, at=at):
-                send_weight(slot, dst, at).start()
-
-    for step in range(1, shards):
-        get_tokens(step).wait_recv()
-        share(step).start()
-    for slot, dst, src, at in weights:
-        if src == dst:
-
-            @pl.when(p == dst)
-            def _(slot=slot, at=at):
-                bounce(
-                    front.at[:, pl.ds(at * unit, unit)], w_buf, w_out.at[:, pl.ds(slot * unit, unit)], lsem.at[2]
-                )
-
+    start_weights()
+    for n in range(2):
+        for step in range(1, shards):
+            get_tokens(n, step).wait_recv()
+            share(n, step).start()
     bounce(back.at[rows_of(f), :], b_buf, b_out.at[:, cols(f)], lsem.at[3])
-    own_tok.wait()
+    for n in range(2):
+        own[n].wait()
 
     @pl.when(f == z)
     def _():
@@ -354,35 +337,152 @@
     def _():
         send_doc(1).wait_recv()
 
-    for step in range(shards):
-        get_share(step).wait_recv()
-        share(step).wait_send()
+    for n in range(2):
+        for step in range(shards):
+            get_share(n, step).wait_recv()
+            share(n, step).wait_send()
+        for step in range(1, shards):
+            send_tokens(n, step).wait_send()
     for step in range(1, shards):
-        send_tokens(step).wait_send()
         send_back(step).wait_send()
         get_back(step).wait_recv()
-    for slot, dst, src, at in weights:
-        if src != dst:
-
-            @pl.when(p == src)
-            def _(slot=slot, dst=dst, at=at):
-                send_weight(slot, dst, at).wait_send()
-
-            @pl.when(p == dst)
-            def _(slot=slot, dst=dst, at=at):
-                send_weight(slot, dst, at).wait_recv()
-
-
-def gather_first(plan, tokens, documents, front_weight, back_weight):
+    finish_weights()
+
+
+def moves_between(moves, device_of):
+    c, f, z, k, p = place_in_mesh()
+
+    def remote(move):
+        src, dst, source, target, send, recv, _, _ = move
+        return pltpu.make_async_remote_copy(
+            src_ref=source, dst_ref=target, send_sem=send, recv_sem=recv, device_id=device_of(c, dst), device_id_type=MESH
+        )
+
+    def start():
+        for move in moves:
+            if move[0] != move[1]:
+
+                @pl.when(p == move[0])
+                def _(move=move):
+                    remote(move).start()
+
+        for move in moves:
+            if move[0] == move[1]:
+
+                @pl.when(p == move[0])
+                def _(move=move):
+                    bounce(move[2], move[6], move[3], move[7])
+
+    def finish():
+        for move in moves:
+            if move[0] != move[1]:
+
+                @pl.when(p == move[0])
+                def _(move=move):
+                    remote(move).wait_send()
+
+                @pl.when(p == move[1])
+                def _(move=move):
+                    remote(move).wait_recv()
+
+    return start, finish
+
+
+def weight_moves(plan, slots, front, out, buffer, send, recv, local):
+    unit, moves, begin = plan.unit, [], 0
+    for number, slot in enumerate(slots):
+        units, wide = plan.slots[slot]
+        for dst in range(plan.ranks):
+            src, at = units[dst] // plan.per_shard, units[dst] % plan.per_shard
+            moves.append(
+                (
+                    2 * src + dst % 2,
+                    dst,
+                    front.at[:, pl.ds(at * unit, wide * unit)],
+                    out.at[:, pl.ds(begin * unit, wide * unit)],
+                    send.at[number, dst // 2],
+                    recv.at[number],
+                    buffer,
+                    local,
+                )
+            )
+        begin += wide
+    return moves_between(moves, lambda c, dst: (c, dst // 2))
+
+
+def back_moves(plan, back, out, buffer, send, recv, local):
+    unit, width, moves = plan.unit, D // plan.fsdp, []
+    for dst in range(plan.ranks):
+        for src in range(plan.fsdp):
+            for number in range(2):
+                row = plan.back_units[dst][1 + 2 * number]
+                moves.append(
+                    (
+                        2 * src + dst % 2,
+                        dst,
+                        back.at[pl.ds(row * unit, 2 * unit), :],
+                        out.at[pl.ds(2 * number * unit, 2 * unit), pl.ds(src * width, width)],
+                        send.at[number, dst // 2],
+                        recv.at[number, src],
+                        buffer,
+                        local,
+                    )
+                )
+    return moves_between(moves, lambda c, dst: (c, dst // 2))
+
+
+def line_exchange(plan, src, out, send, recv, local):
+    planes = plan.planes
+    c, f, z, k, p = place_in_mesh()
+
+    def copy(step):
+        to = lax.rem(z + step, planes)
+        return pltpu.make_async_remote_copy(
+            src_ref=src.at[to],
+            dst_ref=out.at[z],
+            send_sem=send.at[step],
+            recv_sem=recv.at[step],
+            device_id=(2 * to + k, f),
+            device_id_type=MESH,
+        )
+
+    def arrival(step):
+        here = out.at[lax.rem(z + planes - step, planes)]
+        return pltpu.make_async_remote_copy(
+            src_ref=here,
+            dst_ref=here,
+            send_sem=send.at[step],
+            recv_sem=recv.at[step],
+            device_id=(2 * lax.rem(z + step, planes) + k, f),
+            device_id_type=MESH,
+        )
+
+    keep = pltpu.make_async_copy(src.at[z], out.at[z], local)
+
+    def start():
+        for step in range(planes - 1, 0, -1):
+            copy(step).start()
+        keep.start()
+
+    def finish():
+        keep.wait()
+        for step in range(1, planes):
+            copy(step).wait_send()
+            arrival(step).wait_recv()
+
+    return start, finish
+
+
+def gather_first(plan, tokens, cotangent, documents, front_weight, back_weight):
     shards, unit = plan.fsdp, plan.unit
     rows, length = tokens.shape[0], documents.shape[1]
-    vmem, anywhere = pl.BlockSpec(memory_space=pltpu.VMEM), pl.BlockSpec(memory_space=pl.ANY)
     dma = pltpu.SemaphoreType.DMA
     return pl.pallas_call(
         functools.partial(gather_kernel, plan),
-        in_specs=[vmem, vmem, anywhere, anywhere],
-        out_specs=[anywhere] * 4,
+        in_specs=[VMEM_BLOCK] * 3 + [ANY_BLOCK] * 2,
+        out_specs=[ANY_BLOCK] * 5,
         out_shape=[
+            jax.ShapeDtypeStruct((shards, 2, rows, D), bf16),
             jax.ShapeDtypeStruct((shards, 2, rows, D), bf16),
             jax.ShapeDtypeStruct((1, length), f32),
             jax.ShapeDtypeStruct((D, 3 * unit), bf16),
@@ -391,20 +491,50 @@
         scratch_shapes=[
             pltpu.VMEM((D, unit), bf16),
             pltpu.VMEM((unit, D // shards), bf16),
-            dma((shards,)),
-            dma((shards,)),
-            dma((shards,)),
-            dma((shards,)),
+            dma((2, shards)),
+            dma((2, shards)),
+            dma((2, shards)),
+            dma((2, shards)),
             dma((3, shards)),
             dma((3,)),
             dma((shards,)),
             dma((shards,)),
             dma((shards,)),
             dma(()),
-            dma((4,)),
+            dma((5,)),
         ],
         compiler_params=pltpu.CompilerParams(has_side_effects=True),
-    )(tokens, documents, front_weight, back_weight)
+        cost_estimate=busy(130),
+    )(tokens, cotangent, documents, front_weight, back_weight)
+
+
+def exchange_kernel(plan, make, src, weight, out, w_out, buffer, send, recv, local, wsend, wrecv):
+    start, finish = line_exchange(plan, src, out, send, recv, local.at[0])
+    start_weights, finish_weights = make(weight, w_out, buffer, wsend, wrecv, local.at[1])
+    start()
+    start_weights()
+    finish()
+    finish_weights()
+
+
+def exchange_with(plan, values, weight, moves, shape, buffer, recv_shape):
+    dma = pltpu.SemaphoreType.DMA
+    return pl.pallas_call(
+        functools.partial(exchange_kernel, plan, moves),
+        in_specs=[VMEM_BLOCK, ANY_BLOCK],
+        out_specs=[ANY_BLOCK, ANY_BLOCK],
+        out_shape=[jax.ShapeDtypeStruct(values.shape, bf16), jax.ShapeDtypeStruct(shape, bf16)],
+        scratch_shapes=[
+            pltpu.VMEM(buffer, bf16),
+            dma((plan.planes,)),
+            dma((plan.planes,)),
+            dma((2,)),
+            dma((2, plan.fsdp)),
+            dma(recv_shape),
+        ],
+        compiler_params=pltpu.CompilerParams(has_side_effects=True),
+        cost_estimate=busy(50),
+    )(values, weight)
 
 
 def line_sum(plan, block, rising, falling, sends, gets, rows):
@@ -724,10 +854,6 @@
     return start, finish
 
 
-VMEM_BLOCK = pl.BlockSpec(memory_space=pltpu.VMEM)
-ANY_BLOCK = pl.BlockSpec(memory_space=pl.ANY)
-
-
 def sum_scratch(plan, rows, columns):
     dma = pltpu.SemaphoreType.DMA
     steps = plan.planes - 1
@@ -738,10 +864,6 @@
 def gather_scratch(plan):
     dma = pltpu.SemaphoreType.DMA
     return [dma((2, plan.planes - 1))] * 2 + [dma((2, plan.planes))] * 2 + [dma(())]
-
-
-def busy(microseconds):
-    return pl.CostEstimate(flops=int(microseconds * 900e6), transcendentals=0, bytes_accessed=0)
 
 
 def back_sum_kernel(plan, width, src, out, *scratch):
@@ -824,23 +946,94 @@
     )(own, front_sum)
 
 
-def front_next_kernel(plan, own, out, *scratch):
+def vector_sum(plan, own, out, terms, sums, send, recv):
+    planes, ranks = plan.planes, plan.ranks
+    c, f, z, k, p = place_in_mesh()
+
+    def in_plane(step, target):
+        to = lax.rem(p + step, ranks)
+        return pltpu.make_async_remote_copy(
+            src_ref=own,
+            dst_ref=terms.at[target],
+            send_sem=send.at[step],
+            recv_sem=recv.at[step],
+            device_id=(2 * z + lax.rem(to, 2), lax.div(to, 2)),
+            device_id_type=MESH,
+        )
+
+    def over_planes(step, target):
+        to = lax.rem(z + step, planes)
+        return pltpu.make_async_remote_copy(
+            src_ref=out,
+            dst_ref=sums.at[target],
+            send_sem=send.at[ranks + step],
+            recv_sem=recv.at[ranks + step],
+            device_id=(2 * to + k, f),
+            device_id_type=MESH,
+        )
+
+    def start():
+        for step in range(1, ranks):
+            in_plane(step, p).start()
+        terms[p] = own[...]
+
+    def middle():
+        for step in range(1, ranks):
+            in_plane(step, lax.rem(p + ranks - step, ranks)).wait_recv()
+        total = terms[0]
+        for rank in range(1, ranks):
+            total = total + terms[rank]
+        out[...] = total
+        sums[z] = total
+        for step in range(1, planes):
+            over_planes(step, z).start()
+
+    def finish():
+        for step in range(1, ranks):
+            in_plane(step, p).wait_send()
+        for step in range(1, planes):
+            over_planes(step, z).wait_send()
+            over_planes(step, lax.rem(z + planes - step, planes)).wait_recv()
+        total = sums[0]
+        for plane in range(1, planes):
+            total = total + sums[plane]
+        out[...] = total
+
+    return start, middle, finish
+
+
+def front_next_kernel(plan, own, vector, out, vector_out, terms, sums, vsend, vrecv, *scratch):
+    begin, middle, end = vector_sum(plan, vector, vector_out, terms, sums, vsend, vrecv)
     step, finish = line_gather(plan, own, out, *scratch, own.shape[0])
-    for s in range(1, plan.planes):
+    begin()
+    step(1)
+    middle()
+    for s in range(2, plan.planes):
         step(s)
     finish()
-
-
-def front_nexts(plan, own):
+    end()
+
+
+def front_nexts(plan, own, vector):
+    dma = pltpu.SemaphoreType.DMA
     return pl.pallas_call(
         functools.partial(front_next_kernel, plan),
-        in_specs=[VMEM_BLOCK],
-        out_specs=ANY_BLOCK,
-        out_shape=jax.ShapeDtypeStruct((2 * plan.planes * own.shape[0], own.shape[1]), bf16),
-        scratch_shapes=gather_scratch(plan),
+        in_specs=[VMEM_BLOCK, VMEM_BLOCK],
+        out_specs=[ANY_BLOCK, VMEM_BLOCK],
+        out_shape=[
+            jax.ShapeDtypeStruct((2 * plan.planes * own.shape[0], own.shape[1]), bf16),
+            jax.ShapeDtypeStruct(vector.shape, f32),
+        ],
+        scratch_shapes=[
+            pltpu.VMEM((plan.ranks,) + vector.shape, f32),
+            pltpu.VMEM((plan.planes,) + vector.shape, f32),
+            dma((plan.ranks + plan.planes,)),
+            dma((plan.ranks + plan.planes,)),
+        ]
+        + gather_scratch(plan),
         compiler_params=pltpu.CompilerParams(has_side_effects=True),
         cost_estimate=busy(120),
-    )(own)
+    )(own, vector)
 
 
 def gelu_parts(u):
@@ -912,18 +1105,6 @@
     def to_shard(value, step):
         return lax.ppermute(value, "fsdp", [(i, i ^ step) for i in range(shards)])
 
-    def to_plane(value, step):
-        return lax.ppermute(
-            value, "ctx", [(2 * i + j, 2 * (i ^ step) + j) for i in range(planes) for j in range(2)]
-        )
-
-    def gather_plane(value):
-        mine = lax.all_gather(value, "fsdp")
-        other = swap_core(mine)
-        low = jnp.where(k == 0, mine, other)
-        high = jnp.where(k == 0, other, mine)
-        return jnp.stack([low, high], axis=1).reshape(plane_rows, D)
-
     def at(array, index):
         return lax.dynamic_index_in_dim(array, index, 0, keepdims=False)
 
@@ -934,62 +1115,13 @@
     own_positions = at(positions_all, z)
     plane_positions = jnp.tile(own_positions, shards)
 
-    plane_tokens, documents, weight_qkv, back_attention = gather_first(
-        plan, tokens[0], doc_ids.astype(f32), front_weight, back_weight
+    plane_tokens, plane_grad, documents, weight_qkv, back_attention = gather_first(
+        plan, tokens[0], cotangent[0], doc_ids.astype(f32), front_weight, back_weight
     )
     plane_tokens = plane_tokens.reshape(plane_rows, D)
+    plane_grad = plane_grad.reshape(plane_rows, D)
 
     normed = (normalize(plane_tokens)[0] * norm_gain + norm_shift).astype(bf16)
-
-    def slot_weight(slot, gate):
-        units, wide = plan.slots[slot]
-        width = wide * unit
-        table = np.asarray(units)
-        source, place = table // plan.per_shard, table % plan.per_shard
-        total = None
-        for one in plan.rounds[slot]:
-            sends = np.zeros(ranks, np.int32)
-            links = []
-            for src, dst, core in one:
-                sends[2 * src + core] = place[2 * dst + core]
-                links += [
-                    (plan.device(i, core, src), plan.device(i, core, dst)) for i in range(planes)
-                ]
-            start = after(pick(sends, p) * unit, gate)
-            block = lax.dynamic_slice(front_weight, (0, start), (D, width))
-            block = lax.ppermute(block, both, links)
-            total = block if total is None else total + block
-        local = source == np.arange(ranks) // 2
-        start = pick(np.where(local, place, 0), p) * unit
-        own = lax.dynamic_slice(front_weight, (0, start), (D, width))
-        if total is None:
-            return own
-        if not local.any():
-            return total
-        return jnp.where(pick(local, p) > 0, own, total)
-
-    gate = weight_qkv[0, 0]
-    plane_grad = gather_plane(after(cotangent[0], gate))
-    weight_up = jnp.concatenate([slot_weight(i, gate) for i in range(3, 5)], axis=1)
-
-    def back_rows(rank):
-        table = pick(plan.back_units, rank)
-        return jnp.concatenate(
-            [
-                lax.dynamic_slice(back_weight, (table[j] * unit, 0), (2 * unit, D // shards))
-                for j in (1, 3)
-            ],
-            axis=0,
-        )
-
-    col_width = D // shards
-    back_up = jnp.zeros((4 * unit, D), bf16)
-    for step in range(shards):
-        piece = back_rows(after(2 * (f ^ step) + k, gate))
-        if step:
-            piece = to_shard(piece, step)
-        back_up = lax.dynamic_update_slice(back_up, piece, (0, (f ^ step) * col_width))
-    back_local = jnp.concatenate([back_attention, back_up], axis=0)
 
     unit_table = pick(plan.rank_units, p)
     bias_local = jnp.take(bias_front, unit_table, axis=0).reshape(-1)
@@ -998,56 +1130,53 @@
     tables = rotation_tables(plane_positions, unit)
     query = rotate(hidden[:, :unit], tables).astype(bf16)
     key = rotate(hidden[:, unit : 2 * unit], tables).astype(bf16)
-    qkv = jnp.concatenate([query, key, hidden[:, 2 * unit :].astype(bf16)], axis=1)
-
-    def to_sequence(value):
-        shaped = value.reshape(shards, share, -1)
-        pieces = [at(shaped, z)]
-        for step in range(1, planes):
-            pieces.append(to_plane(at(shaped, z ^ step), step))
-        return jnp.concatenate(pieces, axis=0)
-
-    def to_plane_rows(value):
-        shaped = value.reshape(planes, share, -1)
-        pieces = [shaped[0]] + [to_plane(shaped[step], step) for step in range(1, planes)]
-        stacked = jnp.stack(pieces)
-        return jnp.concatenate([at(stacked, i ^ z) for i in range(planes)], axis=0)
-
-    qkv_seq = to_sequence(qkv)
-
     attended_grad = lax.dot_general(
         plane_grad, back_attention, contract_last, preferred_element_type=f32
     ).astype(bf16)
-    grad_seq = to_sequence(attended_grad)
-
-    order = jnp.arange(planes, dtype=jnp.int32) ^ z
-    seq_positions = jnp.take(positions_all, order, axis=0).reshape(-1)
+    qkvg = jnp.concatenate([query, key, hidden[:, 2 * unit :].astype(bf16), attended_grad], axis=1)
+    qkvg, weight_up = exchange_with(
+        plan,
+        qkvg.reshape(planes, share, -1),
+        front_weight,
+        functools.partial(weight_moves, plan, range(3, 5)),
+        (D, 4 * unit),
+        (D, 2 * unit),
+        (2,),
+    )
+    qkvg = qkvg.reshape(planes * share, -1)
+
+    seq_positions = positions_all.reshape(-1)
     doc_row = documents[0].astype(jnp.int32)
-    seq_documents = jnp.take(
-        jnp.take(doc_row.reshape(blocks, block_tokens), block_order, axis=0).reshape(planes, share),
-        order,
-        axis=0,
-    ).reshape(-1)
+    seq_documents = jnp.take(doc_row.reshape(blocks, block_tokens), block_order, axis=0).reshape(-1)
     attended, query_grad, key_grad, value_grad = attention(
-        qkv_seq[:, :unit],
-        qkv_seq[:, unit : 2 * unit],
-        qkv_seq[:, 2 * unit :],
-        grad_seq,
+        qkvg[:, :unit],
+        qkvg[:, unit : 2 * unit],
+        qkvg[:, 2 * unit : 3 * unit],
+        qkvg[:, 3 * unit :],
         seq_positions,
         seq_documents,
     )
     seq_tables = rotation_tables(seq_positions, unit)
-    returned = to_plane_rows(
-        jnp.concatenate(
-            [
-                attended,
-                rotate_back(query_grad, seq_tables).astype(bf16),
-                rotate_back(key_grad, seq_tables).astype(bf16),
-                value_grad.astype(bf16),
-            ],
-            axis=1,
-        )
-    )
+    returned = jnp.concatenate(
+        [
+            attended,
+            rotate_back(query_grad, seq_tables).astype(bf16),
+            rotate_back(key_grad, seq_tables).astype(bf16),
+            value_grad.astype(bf16),
+        ],
+        axis=1,
+    )
+    returned, back_up = exchange_with(
+        plan,
+        returned.reshape(planes, share, -1),
+        back_weight,
+        functools.partial(back_moves, plan),
+        (4 * unit, D),
+        (2 * unit, D // shards),
+        (2, shards),
+    )
+    returned = returned.reshape(plane_rows, -1)
+    back_local = jnp.concatenate([back_attention, back_up], axis=0)
 
     up = jnp.dot(normed, weight_up, preferred_element_type=f32) + bias_local[3 * unit :]
     activation, slope = gelu_parts(up)
@@ -1100,8 +1229,6 @@
     front_new, front_first_new, front_second_new = adam_update(
         front_master, front_first, front_second, front_grad, learn_rates[0], adam_step[0], weight_decay
     )
-    front_next = front_nexts(plan, front_new.astype(bf16))
-
     def column_sums(value):
         ones = jnp.ones((8, value.shape[0]), bf16)
         return jnp.dot(ones, value, preferred_element_type=f32)[0]
@@ -1117,13 +1244,7 @@
             jnp.sum(normed_grad, axis=0),
         ]
     )
-    vector_grad = vector_term.reshape(-1, 128)
-    vector_grad = vector_grad + swap_core(vector_grad)
-    step = 1
-    while step < shards:
-        vector_grad = vector_grad + to_shard(vector_grad, step)
-        vector_grad = vector_grad + to_plane(vector_grad, step)
-        step *= 2
+    front_next, vector_grad = front_nexts(plan, front_new.astype(bf16), vector_term.reshape(-1, 128))
     vector_grad = vector_grad.reshape(-1)
 
     count_now = adam_step[0]

time: 1040 us -> 1040 us (level); the launches traced: 1040 us -> 1030 us
  Pallas kernels: 626 us -> 812 us
  waiting for transfers between devices: 128 us -> 15.6 us
  other arithmetic: 89.6 us -> 65.1 us
  starting transfers between devices: 32.2 us -> 8.36 us
  between operations: 25.5 us -> 2.69 us
    pallas_call x1 -> x3, Pallas kernels: 111 us -> 289 us  [the longest x2 156 us: exchange_with(): pl.pallas_call(functools.partial(exchange_kernel, plan, moves), in_specs=...]
    ppermute x11 -> x6, waiting for transfers between devices: 95 us -> 15.6 us  [to_shard(): return lax.ppermute(value, 'fsdp', [(i, i ^ step) for i in range(shards)])]
    ppermute x13 -> x0, waiting for transfers between devices: 33 us -> none  [the longest x11 21.5 us: to_plane(): lax.ppermute(value, 'ctx', [(2 * i + j, 2 * (i ^ step) + j) for i in rang...]
    ppermute x13 -> x0, starting transfers between devices: 16.3 us -> none  [the longest x11 13.4 us: to_plane(): lax.ppermute(value, 'ctx', [(2 * i + j, 2 * (i ^ step) + j) for i in rang...]
    dynamic_slice x9 -> x0, local copies, waits for them, and re-layouts: 11.3 us -> none  [the longest x1 4.13 us: slot_weight(): block = lax.dynamic_slice(front_weight, (0, start), (D, width))]
    select_n x3 -> x0, other arithmetic: 10.7 us -> none  [the longest x2 10.6 us: slot_weight(): return jnp.where(pick(local, p) > 0, own, total)]
    unnamed x156 -> x126, local copies, waits for them, and re-layouts: 21.3 us -> 29.9 us
  transfers between devices with their start and end apart: 29 -> 8, of which waited for: 7 -> 3; matrix products, arithmetic and copies ran while one was open for 11% -> 8% of each run, Pallas kernels for 38% -> 48%
where the time goes in v4:
time: 1040 us; the launch traced here: 1030 us
  Pallas kernels  812 us (78%)
  matrix products  66.1 us (6%)
  other arithmetic  65.1 us (6%)
  local copies, waits for them, and re-layouts  58.2 us (6%)
  waiting for transfers between devices  15.6 us (2%)
    pallas_call x2, Pallas kernels, exchange_with(): pl.pallas_call(functools.partial(exchange_kernel, plan, moves), in_specs=...  156 us
    pallas_call x1, Pallas kernels, front_sums(): pl.pallas_call(functools.partial(front_sum_kernel, plan, rows), in_specs=...  154 us
    pallas_call x1, Pallas kernels, front_nexts(): pl.pallas_call(functools.partial(front_next_kernel, plan), in_specs=[VMEM...  138 us
    pallas_call x1, Pallas kernels, gather_first(): pl.pallas_call(functools.partial(gather_kernel, plan), in_specs=[VMEM_BLO...  134 us
    pallas_call x1, Pallas kernels, back_nexts(): pl.pallas_call(functools.partial(back_next_kernel, plan), in_specs=[VMEM_...  106 us
    pallas_call x1, Pallas kernels, back_sums(): pl.pallas_call(functools.partial(back_sum_kernel, plan, width), in_specs=...  98.3 us
    unnamed x126, local copies, waits for them, and re-layouts  29.9 us
    pallas_call x1, Pallas kernels, attention(): pl.pallas_call(attention_kernel, grid=(length // block,), in_specs=[rows,...  26.3 us
  transfers between devices with their start and end apart: 8, of which 3 were waited for; matrix products, arithmetic and copies ran while one was open for 8% of the time, Pallas kernels for 48%

profile of v4, /device:TPU:0, one launch (start us, length us, event | category | flops | bytes accessed | tf_op | source)
XLA Modules:
  0.0 1027.7 jit_solution(11415989273639618032)
XLA Ops:
  10.2 133.7 %shard_map.351 = (bf16[4,2,128,2048]{3,2,1,0:T(8,128)(2,1)}, bf16[4,2,128,2048]{3,2,1,0:T(8,128)(2,1)}, f32[1,1024]{1,0:T(1,128)}, bf16[2048,768]{1,0:T(8,128)(2,1)}, bf16[256,2048]{1,0:T(8,128)(2,1)}) custom-call(bf16[128,2048]{1,0:T(8,128)(2,1)} %bitcast.120, bf16[128,2048]{1,0:T(8,128)(2,1)} %bitcast.132, f32[1,1024]{1,0:T(1,128)} %convert_element_type.188.doc, ...), custom_call_target="tpu_custom_call" | custom-call | flops 117000003584 | tf_op jit(solution)/shard_map/pallas_call | solution.py:480
  147.3 3.0 convert_reduce_fusion
  153.8 3.4 convolution_add_fusion
  159.8 2.6 fusion.101
  162.8 3.9 convolution_convert_fusion.2
  167.1 5.3 fusion.33
  174.0 101.1 %shard_map.352 = (bf16[4,256,1024]{2,1,0:T(8,128)(2,1)}, bf16[2048,1024]{1,0:T(8,128)(2,1)}) custom-call(bf16[4,256,1024]{2,1,0:T(8,128)(2,1)} %bitcast.130, bf16[2048,3584]{1,0:T(8,128)(2,1)} %weight.2), custom_call_target="tpu_custom_call" | custom-call | flops 44999999488 | tf_op jit(solution)/shard_map/pallas_call | solution.py:522
  275.2 2.9 fusion.102
  278.1 26.3 %shard_map.353 = (bf16[1024,256]{1,0:T(8,128)(2,1)}, f32[1024,256]{1,0:T(8,128)}, f32[1024,256]{1,0:T(8,128)}, f32[1024,256]{1,0:T(8,128)}) custom-call(bf16[1024,256]{1,0:T(8,128)(2,1)} %get-tuple-element.91.q_ref, bf16[1024,256]{1,0:T(8,128)(2,1)} %get-tuple-element.90.k_ref, bf16[1024,256]{1,0:T(8,128)(2,1)} %get-tuple-element.89.v_ref, ...), custom_call_target="tpu_custom_call" | custom-call | flops 3758096384 | bytes 5242880 | tf_op jit(solution)/shard_map/pallas_call | solution.py:203
  304.3 5.1 fusion.58
  315.9 5.5 fusion.50
  323.1 54.6 %shard_map.354 = (bf16[4,256,1024]{2,1,0:T(8,128)(2,1)}, bf16[1024,2048]{1,0:T(8,128)(2,1)}) custom-call(bf16[4,256,1024]{2,1,0:T(8,128)(2,1)} %bitcast.131, bf16[10240,512]{1,0:T(8,128)(2,1)} %weight.3), custom_call_target="tpu_custom_call" | custom-call | flops 44999999488 | tf_op jit(solution)/shard_map/pallas_call | solution.py:522
  379.0 11.3 %multiply_convert_fusion.1 = (bf16[1024,1024]{0,1:T(8,128)(2,1)S(1)}, f32[1024,1024]{0,1:T(8,128)}) fusion(f32[1024]{0:T(1024)S(1)} %bitcast.141, bf16[1024,2048]{1,0:T(8,128)(2,1)} %copy-done.10, bf16[2048,1024]{1,0:T(8,128)(2,1)} %get-tuple-element.46), kind=kOutput, calls=%fused_computation.25 | convolution fusion | flops 4305453056 | bytes 14684160 | tf_op jit(solution)/shard_map/dot_general | solution.py:1181
  390.3 5.9 fusion.8
  401.3 11.2 %multiply_convert_fusion = bf16[1024,1024]{0,1:T(8,128)(2,1)S(1)} fusion(f32[1024,1024]{0,1:T(8,128)} %get-tuple-element.113, bf16[1024,2048]{1,0:T(8,128)(2,1)} %bitcast.144, bf16[1024,2048]{1,0:T(8,128)(2,1)} %get-tuple-element.47, f32[1024]{0:T(1024)S(1)} %bitcast.142), kind=kOutput, calls=%fused_computation.24 | convolution fusion | flops 4314890240 | bytes 14684160 | tf_op jit(solution)/shard_map/dot_general | solution.py:1183
  412.6 8.1 fusion.4
  420.7 3.4 copy-done.6
  427.2 2.9 convolution_reduce_fusion
  430.2 9.1 convolution_convert_fusion.src
  439.3 10.0 convolution_convert_fusion.1.src
  452.8 98.3 %shard_map.355.back = bf16[1280,512]{1,0:T(8,128)(2,1)} custom-call(bf16[1280,2048]{1,0:T(8,128)(2,1)} %convolution_convert_fusion.src), custom_call_target="tpu_custom_call" | custom-call | flops 80999997440 | tf_op jit(solution)/shard_map/pallas_call | solution.py:881
  551.1 153.6 %shard_map.356 = (bf16[512,1792]{1,0:T(8,128)(2,1)}, bf16[1280,512]{1,0:T(8,128)(2,1)}) custom-call(bf16[2048,1792]{1,0:T(8,128)(2,1)} %convolution_convert_fusion.1.src, bf16[1280,512]{1,0:T(8,128)(2,1)} %shard_map.355.back), custom_call_target="tpu_custom_call" | custom-call | flops 108000002048 | tf_op jit(solution)/shard_map/pallas_call | solution.py:908
  704.7 7.9 fusion.97
  712.7 106.0 %shard_map.357 = (bf16[10240,512]{1,0:T(8,128)(2,1)}, bf16[256,3584]{1,0:T(8,128)(2,1)}) custom-call(bf16[1280,512]{1,0:T(8,128)(2,1)} %get-tuple-element.66.own, bf16[512,1792]{1,0:T(8,128)(2,1)} %get-tuple-element.49.src), custom_call_target="tpu_custom_call" | custom-call | flops 80999997440 | tf_op jit(solution)/shard_map/pallas_call | solution.py:935
  819.0 11.6 %fusion.95 = (bf16[256,3584]{1,0:T(8,128)(2,1)}, f32[256,3584]{1,0:T(8,128)}, f32[256,3584]{1,0:T(8,128)}, f32[256,3584]{1,0:T(8,128)}, f32[256,3584]{1,0:T(8,128)}) fusion(f32[256,3584]{1,0:T(8,128)} %param.30, f32[]{:T(128)} %bitcast.32, f32[]{:T(128)} %bitcast.31, f32[]{:T(128)} %bitcast.33, f32[256,3584]{1,0:T(8,128)} %param.34, f32[256,3584]{1,0:T(8,128)} %param.32, ...), kind=kLoop, calls=%fused_computation.166 | loop fusion | flops 15597568 | bytes 29360140 | tf_op jit(solution)/shard_map/convert_element_type | solution.py:1247
  830.6 2.6 bitcast_add_fusion
  845.5 2.8 collective-permute-done.5
  849.8 10.7 %collective-permute-done.7 = bf16[128,2048]{1,0:T(8,128)(2,1)S(1)} collective-permute-done((bf16[128,2048]{1,0:T(8,128)(2,1)S(1)}, bf16[128,2048]{1,0:T(8,128)(2,1)S(1)}, u32[]{:S(2)}, u32[]{:S(2)}) %collective-permute-start.7) | collective-permute-done | bytes 524320 | tf_op jit(solution)/shard_map/ppermute | solution.py:1106
  863.9 138.2 %shard_map.358 = (bf16[2048,3584]{1,0:T(8,128)(2,1)}, f32[160,128]{1,0:T(8,128)}) custom-call(bf16[256,3584]{1,0:T(8,128)(2,1)} %get-tuple-element.61.own, f32[160,128]{1,0:T(8,128)} %maximum_bitcast_fusion.vector), custom_call_target="tpu_custom_call" | custom-call | flops 108000002048 | tf_op jit(solution)/shard_map/pallas_call | solution.py:1019
  1004.4 3.6 fusion.75
  1008.6 14.6 %copy.74 = bf16[2048,3584]{1,0:T(8,128)(2,1)} copy(bf16[2048,3584]{1,0:T(8,128)(2,1)} %get-tuple-element.146) | data formatting | bytes 29360128
  1023.2 4.1 copy.75
  (204 shorter events, 61.7 us)
Async XLA Ops:
  4.9 147.1 %copy-start.31 = (f32[2048]{0:T(1024)}, f32[2048]{0:T(1024)S(1)}, u32[]{:S(2)}) copy-start(f32[2048]{0:T(1024)S(1)} %get-tuple-element.100) | copy-start | bytes 24580
  378.9 11.3 %copy-start.26 = (bf16[1024,256]{0,1:T(8,128)(2,1)}, bf16[1024,256]{0,1:T(8,128)(2,1)S(1)}, u32[]{:S(2)}) copy-start(bf16[1024,256]{0,1:T(8,128)(2,1)S(1)} %copy.62) | copy-start | bytes 1572868
  378.9 11.3 %copy-start.49 = (bf16[1024,2048]{1,0:T(8,128)(2,1)S(1)}, bf16[1024,2048]{1,0:T(8,128)(2,1)}, u32[]{:S(2)}) copy-start(bf16[1024,2048]{1,0:T(8,128)(2,1)} %get-tuple-element.47) | copy-start | bytes 12582916
  379.0 11.3 %copy-start.50 = (bf16[256,2048]{1,0:T(8,128)(2,1)S(1)}, bf16[256,2048]{1,0:T(8,128)(2,1)}, u32[]{:S(2)}) copy-start(bf16[256,2048]{1,0:T(8,128)(2,1)} %get-tuple-element.38) | copy-start | bytes 3145732
  400.4 436.8 %collective-permute-start = (bf16[4,128,2048]{2,1,0:T(8,128)(2,1)}, bf16[4,128,2048]{2,1,0:T(8,128)(2,1)}, u32[]{:S(2)}, u32[]{:S(2)}) collective-permute-start(bf16[4,128,2048]{2,1,0:T(8,128)(2,1)} %fusion.14), channel_id=1, source_target_pairs={{0,4},{4,0},{8,12},{12,8},{16,20},{20,16},{24,28},{28,24},{1,5},{5... | collective-permute-start | bytes 6291464 | tf_op jit(solution)/shard_map/ppermute | solution.py:1103
  401.3 11.3 %copy-start.53 = (bf16[2048,768]{1,0:T(8,128)(2,1)S(1)}, bf16[2048,768]{1,0:T(8,128)(2,1)}, u32[]{:S(2)}) copy-start(bf16[2048,768]{1,0:T(8,128)(2,1)} %get-tuple-element.36) | copy-start | bytes 9437188
  401.3 11.3 %copy-start.54 = (bf16[2048,1024]{1,0:T(8,128)(2,1)S(1)}, bf16[2048,1024]{1,0:T(8,128)(2,1)}, u32[]{:S(2)}) copy-start(bf16[2048,1024]{1,0:T(8,128)(2,1)} %get-tuple-element.46) | copy-start | bytes 12582916
  425.7 404.9 %collective-permute-start.4 = (bf16[4,128,2048]{2,1,0:T(8,128)(2,1)}, bf16[4,128,2048]{2,1,0:T(8,128)(2,1)}, u32[]{:S(2)}, u32[]{:S(2)}) collective-permute-start(bf16[4,128,2048]{2,1,0:T(8,128)(2,1)} %fusion.15), channel_id=1, source_target_pairs={{0,4},{4,0},{8,12},{12,8},{16,20},{20,16},{24,28},{28,24},{1,5},{5... | collective-permute-start | bytes 6291464 | tf_op jit(solution)/shard_map/ppermute | solution.py:1103
  430.2 9.1 copy-start.11
  439.3 11.6 %copy-start.41 = (f32[3]{0:T(128)S(1)}, f32[3]{0:T(128)}, u32[]{:S(2)}) copy-start(f32[3]{0:T(128)} %param.39) | copy-start | bytes 40
  551.1 153.6 %copy-start.18 = (f32[1280,512]{1,0:T(8,128)S(1)}, f32[1280,512]{1,0:T(8,128)}, u32[]{:S(2)}) copy-start(f32[1280,512]{1,0:T(8,128)} %param.31) | copy-start | bytes 7864324
  712.7 106.0 %copy-start.36 = (f32[7,256]{1,0:T(8,128)S(1)}, f32[7,256]{1,0:T(8,128)}, u32[]{:S(2)}) copy-start(f32[7,256]{1,0:T(8,128)} %mul.368) | copy-start | bytes 21508
  712.7 106.0 %copy-start.37 = (f32[56,7]{0,1:T(8,128)S(1)}, f32[56,7]{0,1:T(8,128)}, u32[]{:S(2)}) copy-start(f32[56,7]{0,1:T(8,128)} %fusion.77) | copy-start | bytes 4708
  712.7 106.2 %copy-start.24 = (bf16[1,128,2048]{2,1,0:T(8,128)(2,1)S(1)}, bf16[1,128,2048]{2,1,0:T(8,128)(2,1)}, u32[]{:S(2)}) copy-start(bf16[1,128,2048]{2,1,0:T(8,128)(2,1)} %param.25) | copy-start | bytes 1572868
  819.0 11.6 %copy-start.7 = (f32[1024,2048]{1,0:T(8,128)S(1)}, f32[1024,2048]{1,0:T(8,128)}, u32[]{:S(2)}) copy-start(f32[1024,2048]{1,0:T(8,128)} %copy-done.6) | copy-start | bytes 25165828
  833.5 14.9 %collective-permute-start.5 = (bf16[128,2048]{1,0:T(8,128)(2,1)S(1)}, bf16[128,2048]{1,0:T(8,128)(2,1)S(1)}, u32[]{:S(2)}, u32[]{:S(2)}) collective-permute-start(bf16[128,2048]{1,0:T(8,128)(2,1)S(1)} %get-tuple-element.72), channel_id=1, source_target_pairs={{0,1},{1,0},{2,3},{3,2},{4,5},{5,4},{6,7},{7,6},{8,9},{9,8},{10,11... | collective-permute-start | bytes 1572872 | tf_op jit(solution)/shard_map/ppermute | solution.py:1106
  835.0 25.5 %collective-permute-start.7 = (bf16[128,2048]{1,0:T(8,128)(2,1)S(1)}, bf16[128,2048]{1,0:T(8,128)(2,1)S(1)}, u32[]{:S(2)}, u32[]{:S(2)}) collective-permute-start(bf16[128,2048]{1,0:T(8,128)(2,1)S(1)} %get-tuple-element.73), channel_id=1, source_target_pairs={{0,3},{1,2},{2,1},{3,0},{4,7},{5,6},{6,5},{7,4},{8,11},{9,10},{10,... | collective-permute-start | bytes 1572872 | tf_op jit(solution)/shard_map/ppermute | solution.py:1106
  836.4 26.1 %copy-start.3 = (bf16[1,128,2048]{2,1,0:T(8,128)(2,1)S(1)}, bf16[1,128,2048]{2,1,0:T(8,128)(2,1)}, u32[]{:S(2)}) copy-start(bf16[1,128,2048]{2,1,0:T(8,128)(2,1)} %param.24) | copy-start | bytes 1572868
  836.4 26.1 %copy-start.32 = (f32[2048]{0:T(1024)S(1)}, f32[2048]{0:T(1024)}, u32[]{:S(2)}) copy-start(f32[2048]{0:T(1024)} %copy-done.31) | copy-start | bytes 24580
  836.4 26.1 %copy-start.43 = (f32[128]{0:T(128)S(1)}, f32[128]{0:T(128)}, u32[]{:S(2)}) copy-start(f32[128]{0:T(128)} %copy-done.42) | copy-start | bytes 1540
  836.4 26.1 %copy-start.45 = (f32[128]{0:T(128)S(1)}, f32[128]{0:T(128)}, u32[]{:S(2)}) copy-start(f32[128]{0:T(128)} %add_rsqrt_fusion.1) | copy-start | bytes 1540
  836.4 26.1 %collective-permute-start.6 = (bf16[128,2048]{1,0:T(8,128)(2,1)S(1)}, bf16[128,2048]{1,0:T(8,128)(2,1)S(1)}, u32[]{:S(2)}, u32[]{:S(2)}) collective-permute-start(bf16[128,2048]{1,0:T(8,128)(2,1)S(1)} %get-tuple-element.74), channel_id=1, source_target_pairs={{0,2},{1,3},{2,0},{3,1},{4,6},{5,7},{6,4},{7,5},{8,10},{9,11},{10,... | collective-permute-start | bytes 1572872 | tf_op jit(solution)/shard_map/ppermute | solution.py:1106
  842.7 161.6 %collective-permute-start.1 = (bf16[128,2048]{1,0:T(8,128)(2,1)}, bf16[128,2048]{1,0:T(8,128)(2,1)}, u32[]{:S(2)}, u32[]{:S(2)}) collective-permute-start(bf16[128,2048]{1,0:T(8,128)(2,1)} %get-tuple-element.75), channel_id=1, source_target_pairs={{0,1},{1,0},{2,3},{3,2},{4,5},{5,4},{6,7},{7,6},{8,9},{9,8},{10,11... | collective-permute-start | bytes 1572872 | tf_op jit(solution)/shard_map/ppermute | solution.py:1106
  844.1 160.2 %collective-permute-start.3 = (bf16[128,2048]{1,0:T(8,128)(2,1)S(1)}, bf16[128,2048]{1,0:T(8,128)(2,1)}, u32[]{:S(2)}, u32[]{:S(2)}) collective-permute-start(bf16[128,2048]{1,0:T(8,128)(2,1)S(1)} %get-tuple-element.76), channel_id=1, source_target_pairs={{0,3},{1,2},{2,1},{3,0},{4,7},{5,6},{6,5},{7,4},{8,11},{9,10},{10,... | collective-permute-start | bytes 1572872 | tf_op jit(solution)/shard_map/ppermute | solution.py:1106
  848.4 156.0 %collective-permute-start.2 = (bf16[128,2048]{1,0:T(8,128)(2,1)S(1)}, bf16[128,2048]{1,0:T(8,128)(2,1)}, u32[]{:S(2)}, u32[]{:S(2)}) collective-permute-start(bf16[128,2048]{1,0:T(8,128)(2,1)S(1)} %get-tuple-element.77), channel_id=1, source_target_pairs={{0,2},{1,3},{2,0},{3,1},{4,6},{5,7},{6,4},{7,5},{8,10},{9,11},{10,... | collective-permute-start | bytes 1572872 | tf_op jit(solution)/shard_map/ppermute | solution.py:1106
  863.9 138.2 %copy-start.29 = (f32[20480]{0:T(1024)S(1)}, f32[20480]{0:T(1024)}, u32[]{:S(2)}) copy-start(f32[20480]{0:T(1024)} %param.36) | copy-start | bytes 245764
  863.9 138.2 %copy-start.33 = (f32[20480]{0:T(1024)S(1)}, f32[20480]{0:T(1024)}, u32[]{:S(2)}) copy-start(f32[20480]{0:T(1024)} %param.38) | copy-start | bytes 245764
  863.9 138.2 %copy-start.34 = (f32[20480]{0:T(1024)S(1)}, f32[20480]{0:T(1024)}, u32[]{:S(2)}) copy-start(f32[20480]{0:T(1024)} %param.37) | copy-start | bytes 245764
  863.9 140.4 %copy-start.35 = (f32[2048]{0:T(1024)S(1)}, f32[2048]{0:T(1024)}, u32[]{:S(2)}) copy-start(f32[2048]{0:T(1024)} %get-tuple-element.98) | copy-start | bytes 24580
  1004.4 18.8 %slice-start = ((s8[10485760]{0:T(1024)(128)(4,1)}), s8[2097152]{0:T(1024)(128)(4,1)S(1)}, s32[]{:S(2)}) async-start(s8[10485760]{0:T(1024)(128)(4,1)} %bitcast.118), calls=%async_computation | async-start | bytes 4194304
  1008.6 14.6 %slice-start.1 = ((s8[10485760]{0:T(1024)(128)(4,1)}), s8[4194304]{0:T(1024)(128)(4,1)S(1)}, s32[]{:S(2)}) async-start(s8[10485760]{0:T(1024)(128)(4,1)} %bitcast.118), calls=%async_computation.1 | async-start | bytes 8388608
  1008.6 14.6 %slice-start.2 = ((s8[10485760]{0:T(1024)(128)(4,1)}), s8[4194304]{0:T(1024)(128)(4,1)S(1)}, s32[]{:S(2)}) async-start(s8[10485760]{0:T(1024)(128)(4,1)} %bitcast.118), calls=%async_computation.2 | async-start | bytes 8388608
  (34 other events, 149.2 us)

commit v5 on v4

--- a/solution.py
+++ b/solution.py
@@ -247,7 +247,7 @@
 
 def gather_kernel(
     plan, tok, cot, doc, front, back, tok_out, cot_out, doc_out, w_out, b_out,
-    w_buf, b_buf, tsend, trecv, csend, crecv, wsend, wrecv, bsend, brecv, dsend, drecv, lsem,
+    w_buf, b_buf, tsend, trecv, csend, crecv, wsend, wrecv, rsend, rrecv, bsend, brecv, dsend, drecv, lsem,
 ):
     shards, unit, ranks = plan.fsdp, plan.unit, plan.ranks
     c, f, z, k, p = place_in_mesh()
@@ -301,7 +301,9 @@
     def send_doc(step):
         return remote(doc, doc_out, dsend.at[step], drecv, (c, peer(step)))
 
-    start_weights, finish_weights = weight_moves(plan, range(3), front, w_out, w_buf, wsend, wrecv, lsem.at[2])
+    start_weights, relay_weights, finish_weights = weight_moves(
+        plan, front, w_out, w_buf, wsend, wrecv, rsend, rrecv, lsem.at[2]
+    )
     own = [pltpu.make_async_copy(src, out.at[f, k], lsem.at[4 * n]) for n, (src, out) in enumerate(both)]
     own_doc = pltpu.make_async_copy(doc, doc_out, lsem.at[1])
     for n in range(2):
@@ -323,6 +325,7 @@
         for step in range(1, shards):
             get_tokens(n, step).wait_recv()
             share(n, step).start()
+    relay_weights()
     bounce(back.at[rows_of(f), :], b_buf, b_out.at[:, cols(f)], lsem.at[3])
     for n in range(2):
         own[n].wait()
@@ -388,26 +391,83 @@
     return start, finish
 
 
-def weight_moves(plan, slots, front, out, buffer, send, recv, local):
+def weight_moves(plan, front, out, buffer, send, recv, relay_send, relay_recv, local):
     unit, moves, begin = plan.unit, [], 0
-    for number, slot in enumerate(slots):
-        units, wide = plan.slots[slot]
+    c, f, z, k, p = place_in_mesh()
+    half, parity = D // 2, lax.rem(z, 2)
+
+    def rows(part):
+        return pl.ds(pl.multiple_of(part * half, half), half)
+
+    for slot, (units, wide) in enumerate(plan.slots):
         for dst in range(plan.ranks):
             src, at = units[dst] // plan.per_shard, units[dst] % plan.per_shard
             moves.append(
-                (
-                    2 * src + dst % 2,
-                    dst,
-                    front.at[:, pl.ds(at * unit, wide * unit)],
-                    out.at[:, pl.ds(begin * unit, wide * unit)],
-                    send.at[number, dst // 2],
-                    recv.at[number],
-                    buffer,
-                    local,
-                )
+                (slot, 2 * src + dst % 2, dst, pl.ds(at * unit, wide * unit), pl.ds(begin * unit, wide * unit), wide * unit)
             )
         begin += wide
-    return moves_between(moves, lambda c, dst: (c, dst // 2))
+
+    def copy(move):
+        slot, _, dst, source, target, _ = move
+        return pltpu.make_async_remote_copy(
+            src_ref=front.at[rows(parity), source],
+            dst_ref=out.at[rows(parity), target],
+            send_sem=send.at[slot, dst // 2],
+            recv_sem=recv.at[slot],
+            device_id=(c, dst // 2),
+            device_id_type=MESH,
+        )
+
+    def pass_on(move, part):
+        slot, _, _, _, target, _ = move
+        here = out.at[rows(part), target]
+        return pltpu.make_async_remote_copy(
+            src_ref=here,
+            dst_ref=here,
+            send_sem=relay_send.at[slot],
+            recv_sem=relay_recv.at[slot],
+            device_id=(c + 2 - 4 * parity, f),
+            device_id_type=MESH,
+        )
+
+    def start():
+        for move in moves:
+            if move[1] != move[2]:
+
+                @pl.when(p == move[1])
+                def _(move=move):
+                    copy(move).start()
+
+    def relay():
+        for move in moves:
+            if move[1] != move[2]:
+
+                @pl.when(p == move[2])
+                def _(move=move):
+                    copy(move).wait_recv()
+                    pass_on(move, parity).start()
+
+    def finish():
+        for move in moves:
+            if move[1] == move[2]:
+
+                @pl.when(p == move[2])
+                def _(move=move):
+                    bounce(front.at[:, move[3]], buffer.at[:, pl.ds(0, move[5])], out.at[:, move[4]], local)
+
+        for move in moves:
+            if move[1] != move[2]:
+
+                @pl.when(p == move[1])
+                def _(move=move):
+                    copy(move).wait_send()
+
+                @pl.when(p == move[2])
+                def _(move=move):
+                    pass_on(move, parity).wait_send()
+                    pass_on(move, 1 - parity).wait_recv()
+
+    return start, relay, finish
 
 
 def back_moves(plan, back, out, buffer, send, recv, local):
@@ -485,18 +545,20 @@
             jax.ShapeDtypeStruct((shards, 2, rows, D), bf16),
             jax.ShapeDtypeStruct((shards, 2, rows, D), bf16),
             jax.ShapeDtypeStruct((1, length), f32),
-            jax.ShapeDtypeStruct((D, 3 * unit), bf16),
+            jax.ShapeDtypeStruct((D, 7 * unit), bf16),
             jax.ShapeDtypeStruct((unit, D), bf16),
         ],
         scratch_shapes=[
-            pltpu.VMEM((D, unit), bf16),
+            pltpu.VMEM((D, 2 * unit), bf16),
             pltpu.VMEM((unit, D // shards), bf16),
             dma((2, shards)),
             dma((2, shards)),
             dma((2, shards)),
             dma((2, shards)),
-            dma((3, shards)),
-            dma((3,)),
+            dma((5, shards)),
+            dma((5,)),
+            dma((5,)),
+            dma((5,)),
             dma((shards,)),
             dma((shards,)),
             dma((shards,)),
@@ -508,33 +570,53 @@
     )(tokens, cotangent, documents, front_weight, back_weight)
 
 
-def exchange_kernel(plan, make, src, weight, out, w_out, buffer, send, recv, local, wsend, wrecv):
+def exchange_kernel(plan, src, back, out, b_out, buffer, send, recv, local, bsend, brecv):
     start, finish = line_exchange(plan, src, out, send, recv, local.at[0])
-    start_weights, finish_weights = make(weight, w_out, buffer, wsend, wrecv, local.at[1])
+    start_rows, finish_rows = back_moves(plan, back, b_out, buffer, bsend, brecv, local.at[1])
     start()
-    start_weights()
+    start_rows()
     finish()
-    finish_weights()
-
-
-def exchange_with(plan, values, weight, moves, shape, buffer, recv_shape):
+    finish_rows()
+
+
+def exchange_first(plan, values, back_weight):
     dma = pltpu.SemaphoreType.DMA
+    unit, shards = plan.unit, plan.fsdp
     return pl.pallas_call(
-        functools.partial(exchange_kernel, plan, moves),
+        functools.partial(exchange_kernel, plan),
         in_specs=[VMEM_BLOCK, ANY_BLOCK],
         out_specs=[ANY_BLOCK, ANY_BLOCK],
-        out_shape=[jax.ShapeDtypeStruct(values.shape, bf16), jax.ShapeDtypeStruct(shape, bf16)],
+        out_shape=[jax.ShapeDtypeStruct(values.shape, bf16), jax.ShapeDtypeStruct((4 * unit, D), bf16)],
         scratch_shapes=[
-            pltpu.VMEM(buffer, bf16),
+            pltpu.VMEM((2 * unit, D // shards), bf16),
             dma((plan.planes,)),
             dma((plan.planes,)),
             dma((2,)),
-            dma((2, plan.fsdp)),
-            dma(recv_shape),
+            dma((2, shards)),
+            dma((2, shards)),
         ],
         compiler_params=pltpu.CompilerParams(has_side_effects=True),
         cost_estimate=busy(50),
-    )(values, weight)
+    )(values, back_weight)
+
+
+def exchange_back_kernel(plan, src, out, send, recv, local):
+    start, finish = line_exchange(plan, src, out, send, recv, local)
+    start()
+    finish()
+
+
+def exchange_back(plan, values):
+    dma = pltpu.SemaphoreType.DMA
+    return pl.pallas_call(
+        functools.partial(exchange_back_kernel, plan),
+        in_specs=[VMEM_BLOCK],
+        out_specs=ANY_BLOCK,
+        out_shape=jax.ShapeDtypeStruct(values.shape, bf16),
+        scratch_shapes=[dma((plan.planes,)), dma((plan.planes,)), dma(())],
+        compiler_params=pltpu.CompilerParams(has_side_effects=True),
+        cost_estimate=busy(50),
+    )(values)
 
 
 def line_sum(plan, block, rising, falling, sends, gets, rows):
@@ -1115,7 +1197,7 @@
     own_positions = at(positions_all, z)
     plane_positions = jnp.tile(own_positions, shards)
 
-    plane_tokens, plane_grad, documents, weight_qkv, back_attention = gather_first(
+    plane_tokens, plane_grad, documents, weight_local, back_attention = gather_first(
         plan, tokens[0], cotangent[0], doc_ids.astype(f32), front_weight, back_weight
     )
     plane_tokens = plane_tokens.reshape(plane_rows, D)
@@ -1126,7 +1208,7 @@
     unit_table = pick(plan.rank_units, p)
     bias_local = jnp.take(bias_front, unit_table, axis=0).reshape(-1)
 
-    hidden = jnp.dot(normed, weight_qkv, preferred_element_type=f32) + bias_local[: 3 * unit]
+    hidden = jnp.dot(normed, weight_local[:, : 3 * unit], preferred_element_type=f32) + bias_local[: 3 * unit]
     tables = rotation_tables(plane_positions, unit)
     query = rotate(hidden[:, :unit], tables).astype(bf16)
     key = rotate(hidden[:, unit : 2 * unit], tables).astype(bf16)
@@ -1134,15 +1216,7 @@
         plane_grad, back_attention, contract_last, preferred_element_type=f32
     ).astype(bf16)
     qkvg = jnp.concatenate([query, key, hidden[:, 2 * unit :].astype(bf16), attended_grad], axis=1)
-    qkvg, weight_up = exchange_with(
-        plan,
-        qkvg.reshape(planes, share, -1),
-        front_weight,
-        functools.partial(weight_moves, plan, range(3, 5)),
-        (D, 4 * unit),
-        (D, 2 * unit),
-        (2,),
-    )
+    qkvg, back_up = exchange_first(plan, qkvg.reshape(planes, share, -1), back_weight)
     qkvg = qkvg.reshape(planes * share, -1)
 
     seq_positions = positions_all.reshape(-1)
@@ -1166,51 +1240,35 @@
         ],
         axis=1,
     )
-    returned, back_up = exchange_with(
-        plan,
-        returned.reshape(planes, share, -1),
-        back_weight,
-        functools.partial(back_moves, plan),
-        (4 * unit, D),
-        (2 * unit, D // shards),
-        (2, shards),
-    )
+    returned = exchange_back(plan, returned.reshape(planes, share, -1))
     returned = returned.reshape(plane_rows, -1)
     back_local = jnp.concatenate([back_attention, back_up], axis=0)
 
-    up = jnp.dot(normed, weight_up, preferred_element_type=f32) + bias_local[3 * unit :]
+    up = jnp.dot(normed, weight_local[:, 3 * unit :], preferred_element_type=f32) + bias_local[3 * unit :]
     activation, slope = gelu_parts(up)
     mixed_grad = lax.dot_general(plane_grad, back_up, contract_last, preferred_element_type=f32)
     up_grad = (mixed_grad * slope).astype(bf16)
     mixed = jnp.concatenate([returned[:, :unit], activation.astype(bf16)], axis=1)
     hidden_grad = jnp.concatenate([returned[:, unit:], up_grad], axis=1)
 
-    def sum_to_owner(value):
+    def sum_over_cores(value):
         shaped = value.reshape(shards, 2, rows, D)
         kept = lax.dynamic_index_in_dim(shaped, k, 1, keepdims=False)
         sent = lax.dynamic_index_in_dim(shaped, 1 - k, 1, keepdims=False).astype(bf16)
-        summed = kept + swap_core(sent).astype(f32)
-        total = at(summed, f)
+        return kept + swap_core(sent).astype(f32)
+
+    def sum_over_shards(*values):
+        totals = [at(value, f) for value in values]
         for step in range(1, shards):
-            total = total + to_shard(at(summed, f ^ step).astype(bf16), step).astype(f32)
-        return total
-
-    projected = sum_to_owner(jnp.dot(mixed, back_local, preferred_element_type=f32))
-    inputs = tokens[0].astype(f32)
-    layer_out = (inputs + projected + bias_back).astype(bf16)[None]
-
-    weight_local = jnp.concatenate([weight_qkv, weight_up], axis=1)
-    normed_grad = sum_to_owner(
+            pieces = jnp.stack([at(value, f ^ step).astype(bf16) for value in values])
+            pieces = to_shard(pieces, step).astype(f32)
+            totals = [total + piece for total, piece in zip(totals, pieces)]
+        return totals
+
+    projected_cores = sum_over_cores(jnp.dot(mixed, back_local, preferred_element_type=f32))
+    normed_grad_cores = sum_over_cores(
         lax.dot_general(hidden_grad, weight_local, contract_last, preferred_element_type=f32)
     )
-    unscaled, factor = normalize(inputs)
-    scaled = normed_grad * norm_gain
-    input_grad = factor * (
-        scaled
-        - jnp.mean(scaled, axis=-1, keepdims=True)
-        - unscaled * jnp.mean(scaled * unscaled, axis=-1, keepdims=True)
-    )
-    tokens_grad = (cotangent[0].astype(f32) + input_grad).astype(bf16)[None]
 
     back_partial = lax.dot_general(
         mixed, plane_grad, contract_first, preferred_element_type=f32
@@ -1219,7 +1277,24 @@
         normed, hidden_grad, contract_first, preferred_element_type=f32
     ).astype(bf16)
     back_sum = back_sums(plan, back_partial)
+    back_sum, projected_cores, normed_grad_cores = lax.optimization_barrier(
+        (back_sum, projected_cores, normed_grad_cores)
+    )
+    projected, normed_grad = sum_over_shards(projected_cores, normed_grad_cores)
     front_sum, back_owned = front_sums(plan, front_partial, back_sum)
+    front_sum, projected, normed_grad = lax.optimization_barrier((front_sum, projected, normed_grad))
+
+    inputs = tokens[0].astype(f32)
+    layer_out = (inputs + projected + bias_back).astype(bf16)[None]
+    unscaled, factor = normalize(inputs)
+    scaled = normed_grad * norm_gain
+    input_grad = factor * (
+        scaled
+        - jnp.mean(scaled, axis=-1, keepdims=True)
+        - unscaled * jnp.mean(scaled * unscaled, axis=-1, keepdims=True)
+    )
+    tokens_grad = (cotangent[0].astype(f32) + input_grad).astype(bf16)[None]
+
     back_grad = back_owned.astype(f32)
     back_new, back_first_new, back_second_new = adam_update(
         back_master, back_first, back_second, back_grad, learn_rates[1], adam_step[0], weight_decay

time: 1040 us -> 1010 us (0.971)
  Pallas kernels: 812 us -> 779 us
  waiting for transfers between devices: 15.6 us -> 0.01 us
  matrix products: 66.1 us -> 79.6 us
  other arithmetic: 65.1 us -> 77 us
    pallas_call x2, Pallas kernels: 156 us -> 108 us  [the longest x1 54.4 us: exchange_back(): pl.pallas_call(functools.partial(exchange_back_kernel, plan), in_specs=[V...]
    ppermute x6 -> x3, waiting for transfers between devices: 15.6 us -> 0.01 us  [to_shard(): return lax.ppermute(value, 'fsdp', [(i, i ^ step) for i in range(shards)])]
    pallas_call x1, Pallas kernels: 134 us -> 149 us  [gather_first(): pl.pallas_call(functools.partial(gather_kernel, plan), in_specs=[VMEM_BLO...]
    unnamed x126 -> x132, local copies, waits for them, and re-layouts: 29.9 us -> 29.5 us
  transfers between devices with their start and end apart: 8 -> 5, of which waited for: 3 -> 0; matrix products, arithmetic and copies ran while one was open for 8% -> 7% of each run, Pallas kernels for 48% -> 25%
where the time goes in v5:
time: 1010 us; the launch traced here: 997 us
  Pallas kernels  779 us (77%)
  matrix products  79.6 us (8%)
  other arithmetic  77 us (8%)
  local copies, waits for them, and re-layouts  54.9 us (5%)
    pallas_call x1, Pallas kernels, front_sums(): pl.pallas_call(functools.partial(front_sum_kernel, plan, rows), in_specs=...  154 us
    pallas_call x1, Pallas kernels, gather_first(): pl.pallas_call(functools.partial(gather_kernel, plan), in_specs=[VMEM_BLO...  149 us
    pallas_call x1, Pallas kernels, front_nexts(): pl.pallas_call(functools.partial(front_next_kernel, plan), in_specs=[VMEM...  139 us
    pallas_call x1, Pallas kernels, back_nexts(): pl.pallas_call(functools.partial(back_next_kernel, plan), in_specs=[VMEM_...  106 us
    pallas_call x1, Pallas kernels, back_sums(): pl.pallas_call(functools.partial(back_sum_kernel, plan, width), in_specs=...  97.2 us
    pallas_call x1, Pallas kernels, exchange_back(): pl.pallas_call(functools.partial(exchange_back_kernel, plan), in_specs=[V...  54.4 us
    pallas_call x1, Pallas kernels, exchange_first(): pl.pallas_call(functools.partial(exchange_kernel, plan), in_specs=[VMEM_B...  53.5 us
    unnamed x132, local copies, waits for them, and re-layouts  29.5 us
  transfers between devices with their start and end apart: 5, of which 0 were waited for; matrix products, arithmetic and copies ran while one was open for 7% of the time, Pallas kernels for 25%

profile of v5, /device:TPU:0, one launch (start us, length us, event | category | flops | bytes accessed | tf_op | source)
XLA Modules:
  0.0 996.7 jit_solution(2413303782662724406)
XLA Ops:
  10.2 149.0 %shard_map.351 = (bf16[4,2,128,2048]{3,2,1,0:T(8,128)(2,1)}, bf16[4,2,128,2048]{3,2,1,0:T(8,128)(2,1)}, f32[1,1024]{1,0:T(1,128)}, bf16[2048,1792]{1,0:T(8,128)(2,1)}, bf16[256,2048]{1,0:T(8,128)(2,1)}) custom-call(bf16[128,2048]{1,0:T(8,128)(2,1)} %bitcast.94, bf16[128,2048]{1,0:T(8,128)(2,1)} %bitcast.106, f32[1,1024]{1,0:T(1,128)} %convert_element_type.167.doc, ...), custom_call_target="tpu_custom_call" | custom-call | flops 117000003584 | tf_op jit(solution)/shard_map/pallas_call | solution.py:540
  162.6 3.0 convert_reduce_fusion
  169.1 6.8 fusion.16
  178.4 2.6 fusion.96
  181.5 3.9 convolution_convert_fusion.2
  185.8 5.3 fusion.37
  192.7 53.5 %shard_map.352 = (bf16[4,256,1024]{2,1,0:T(8,128)(2,1)}, bf16[1024,2048]{1,0:T(8,128)(2,1)}) custom-call(bf16[4,256,1024]{2,1,0:T(8,128)(2,1)} %bitcast.104, bf16[10240,512]{1,0:T(8,128)(2,1)} %back.3), custom_call_target="tpu_custom_call" | custom-call | flops 44999999488 | tf_op jit(solution)/shard_map/pallas_call | solution.py:585
  246.3 2.9 fusion.97
  249.2 26.3 %shard_map.353 = (bf16[1024,256]{1,0:T(8,128)(2,1)}, f32[1024,256]{1,0:T(8,128)}, f32[1024,256]{1,0:T(8,128)}, f32[1024,256]{1,0:T(8,128)}) custom-call(bf16[1024,256]{1,0:T(8,128)(2,1)} %get-tuple-element.100.q_ref, bf16[1024,256]{1,0:T(8,128)(2,1)} %get-tuple-element.99.k_ref, bf16[1024,256]{1,0:T(8,128)(2,1)} %get-tuple-element.98.v_ref, ...), custom_call_target="tpu_custom_call" | custom-call | flops 3758096384 | bytes 5242880 | tf_op jit(solution)/shard_map/pallas_call | solution.py:203
  275.4 5.1 fusion.62
  287.0 5.5 fusion.54
  294.2 54.4 %shard_map.354 = bf16[4,256,1024]{2,1,0:T(8,128)(2,1)} custom-call(bf16[4,256,1024]{2,1,0:T(8,128)(2,1)} %bitcast.105), custom_call_target="tpu_custom_call" | custom-call | flops 44999999488 | tf_op jit(solution)/shard_map/pallas_call | solution.py:611
  349.8 12.0 %multiply_convert_fusion = (bf16[1024,1024]{0,1:T(8,128)(2,1)}, f32[1024,1024]{0,1:T(8,128)}) fusion(f32[1024]{0:T(1024)S(1)} %bitcast.115, bf16[1024,2048]{1,0:T(8,128)(2,1)} %copy-done.12, bf16[2048,1792]{1,0:T(8,128)(2,1)} %get-tuple-element.40), kind=kOutput, calls=%fused_computation.20 | convolution fusion | flops 4305453056 | bytes 14684160 | tf_op jit(solution)/shard_map/dot_general | solution.py:1247
  361.8 8.6 fusion.4
  372.0 2.5 copy-done.8
  375.5 11.7 %multiply_convert_fusion.1 = bf16[1024,1024]{0,1:T(8,128)(2,1)S(1)} fusion(f32[1024,1024]{0,1:T(8,128)} %get-tuple-element.122, bf16[1024,2048]{1,0:T(8,128)(2,1)} %bitcast.118, bf16[1024,2048]{1,0:T(8,128)(2,1)} %get-tuple-element.49, f32[1024]{0:T(1024)S(1)} %bitcast.116), kind=kOutput, calls=%fused_computation.21 | convolution fusion | flops 4314890240 | bytes 14684160 | tf_op jit(solution)/shard_map/dot_general | solution.py:1249
  387.2 10.8 %fusion.24 = f32[1024,2048]{1,0:T(8,128)S(1)} fusion(bf16[2048,1792]{1,0:T(8,128)(2,1)} %get-tuple-element.40, bf16[1024,1024]{0,1:T(8,128)(2,1)S(1)} %multiply_convert_fusion.1, bf16[1024,768]{0,1:T(8,128)(2,1)S(1)} %copy.62), kind=kOutput, calls=%fused_computation.55 | convolution fusion | flops 7523532800 | bytes 19398656 | tf_op jit(solution)/shard_map/dot_general | solution.py:1270
  398.0 3.4 copy-done.9
  403.3 3.4 convolution_reduce_fusion
  406.7 9.0 convolution_convert_fusion.src
  417.6 97.2 %shard_map.355.back = bf16[1280,512]{1,0:T(8,128)(2,1)} custom-call(bf16[1280,2048]{1,0:T(8,128)(2,1)} %convolution_convert_fusion.src), custom_call_target="tpu_custom_call" | custom-call | flops 80999997440 | tf_op jit(solution)/shard_map/pallas_call | solution.py:963
  516.2 12.7 %convolution_convert_fusion.1.src = bf16[2048,1792]{1,0:T(8,128)(2,1)} fusion(bf16[1024,2048]{1,0:T(8,128)(2,1)} %copy-done.12, bf16[1024,1024]{0,1:T(8,128)(2,1)} %copy-done.56, bf16[1024,768]{0,1:T(8,128)(2,1)} %copy-done.29), kind=kOutput, calls=%fused_computation.9 | convolution fusion | flops 7527202816 | bytes 15204352 | tf_op jit(solution)/shard_map/dot_general | solution.py:1276
  528.9 3.4 bitcast_add_fusion.1
  532.4 4.9 bitcast_add_fusion
  545.2 153.6 %shard_map.356 = (bf16[512,1792]{1,0:T(8,128)(2,1)}, bf16[1280,512]{1,0:T(8,128)(2,1)}) custom-call(bf16[2048,1792]{1,0:T(8,128)(2,1)} %convolution_convert_fusion.1.src, bf16[1280,512]{1,0:T(8,128)(2,1)} %shard_map.355.back), custom_call_target="tpu_custom_call" | custom-call | flops 108000002048 | tf_op jit(solution)/shard_map/pallas_call | solution.py:990
  698.8 7.9 fusion.93
  711.2 3.4 fusion.68
  717.1 105.7 %shard_map.357 = (bf16[10240,512]{1,0:T(8,128)(2,1)}, bf16[256,3584]{1,0:T(8,128)(2,1)}) custom-call(bf16[1280,512]{1,0:T(8,128)(2,1)} %get-tuple-element.74.own, bf16[512,1792]{1,0:T(8,128)(2,1)} %get-tuple-element.57.src), custom_call_target="tpu_custom_call" | custom-call | flops 80999997440 | tf_op jit(solution)/shard_map/pallas_call | solution.py:1017
  823.5 10.8 %fusion.91 = (bf16[256,3584]{1,0:T(8,128)(2,1)}, f32[256,3584]{1,0:T(8,128)}, f32[256,3584]{1,0:T(8,128)}, f32[256,3584]{1,0:T(8,128)}, f32[256,3584]{1,0:T(8,128)}) fusion(f32[256,3584]{1,0:T(8,128)} %param.30, f32[]{:T(128)} %bitcast.26, f32[]{:T(128)} %bitcast.25, f32[]{:T(128)} %bitcast.27, f32[256,3584]{1,0:T(8,128)} %param.34, f32[256,3584]{1,0:T(8,128)} %param.32, ...), kind=kLoop, calls=%fused_computation.166 | loop fusion | flops 15597568 | bytes 29360140 | tf_op jit(solution)/shard_map/convert_element_type | solution.py:1322
  834.5 139.0 %shard_map.358 = (bf16[2048,3584]{1,0:T(8,128)(2,1)}, f32[160,128]{1,0:T(8,128)}) custom-call(bf16[256,3584]{1,0:T(8,128)(2,1)} %get-tuple-element.69.own, f32[160,128]{1,0:T(8,128)} %maximum_bitcast_fusion.vector), custom_call_target="tpu_custom_call" | custom-call | flops 108000002048 | tf_op jit(solution)/shard_map/pallas_call | solution.py:1101
  978.3 14.1 %copy.74 = bf16[2048,3584]{1,0:T(8,128)(2,1)} copy(bf16[2048,3584]{1,0:T(8,128)(2,1)} %get-tuple-element.156) | data formatting | bytes 29360128
  992.4 4.1 copy.75
  (211 shorter events, 57.8 us)
Async XLA Ops:
  4.9 162.4 %copy-start.36 = (f32[2048]{0:T(1024)}, f32[2048]{0:T(1024)S(1)}, u32[]{:S(2)}) copy-start(f32[2048]{0:T(1024)S(1)} %get-tuple-element.109) | copy-start | bytes 24580
  349.8 12.0 %copy-start.30 = (bf16[1024,256]{0,1:T(8,128)(2,1)}, bf16[1024,256]{0,1:T(8,128)(2,1)S(1)}, u32[]{:S(2)}) copy-start(bf16[1024,256]{0,1:T(8,128)(2,1)S(1)} %copy.63) | copy-start | bytes 1572868
  349.8 12.0 %copy-start.57 = (bf16[256,2048]{1,0:T(8,128)(2,1)S(1)}, bf16[256,2048]{1,0:T(8,128)(2,1)}, u32[]{:S(2)}) copy-start(bf16[256,2048]{1,0:T(8,128)(2,1)} %get-tuple-element.42) | copy-start | bytes 3145732
  374.5 154.4 %collective-permute-start = (bf16[4,128,2048]{2,1,0:T(8,128)(2,1)}, bf16[4,128,2048]{2,1,0:T(8,128)(2,1)}, u32[]{:S(2)}, u32[]{:S(2)}) collective-permute-start(bf16[4,128,2048]{2,1,0:T(8,128)(2,1)} %fusion.14), channel_id=1, source_target_pairs={{0,4},{4,0},{8,12},{12,8},{16,20},{20,16},{24,28},{28,24},{1,5},{5... | collective-permute-start | bytes 6291464 | tf_op jit(solution)/shard_map/ppermute | solution.py:1185
  375.5 11.7 %copy-start.29 = (bf16[1024,768]{0,1:T(8,128)(2,1)}, bf16[1024,768]{0,1:T(8,128)(2,1)S(1)}, u32[]{:S(2)}) copy-start(bf16[1024,768]{0,1:T(8,128)(2,1)S(1)} %copy.62) | copy-start | bytes 4718596
  387.2 10.8 %copy-start.56 = (bf16[1024,1024]{0,1:T(8,128)(2,1)}, bf16[1024,1024]{0,1:T(8,128)(2,1)S(1)}, u32[]{:S(2)}) copy-start(bf16[1024,1024]{0,1:T(8,128)(2,1)S(1)} %multiply_convert_fusion.1) | copy-start | bytes 6291460
  401.7 130.6 %collective-permute-start.1 = (bf16[4,128,2048]{2,1,0:T(8,128)(2,1)S(1)}, bf16[4,128,2048]{2,1,0:T(8,128)(2,1)}, u32[]{:S(2)}, u32[]{:S(2)}) collective-permute-start(bf16[4,128,2048]{2,1,0:T(8,128)(2,1)S(1)} %fusion.15), channel_id=1, source_target_pairs={{0,4},{4,0},{8,12},{12,8},{16,20},{20,16},{24,28},{28,24},{1,5},{5... | collective-permute-start | bytes 6291464 | tf_op jit(solution)/shard_map/ppermute | solution.py:1185
  417.6 97.2 %copy-start.46 = (f32[3]{0:T(128)S(1)}, f32[3]{0:T(128)}, u32[]{:S(2)}) copy-start(f32[3]{0:T(128)} %param.39) | copy-start | bytes 40
  417.6 97.8 %copy-start.26 = (bf16[1,128,2048]{2,1,0:T(8,128)(2,1)S(1)}, bf16[1,128,2048]{2,1,0:T(8,128)(2,1)}, u32[]{:S(2)}) copy-start(bf16[1,128,2048]{2,1,0:T(8,128)(2,1)} %param.25) | copy-start | bytes 1572868
  515.4 199.2 %copy-start.51 = (f32[128]{0:T(128)}, f32[128]{0:T(128)S(1)}, u32[]{:S(2)}) copy-start(f32[128]{0:T(128)S(1)} %add_rsqrt_fusion.1) | copy-start | bytes 1540
  539.6 167.1 %collective-permute-start.3 = (bf16[2,128,2048]{2,1,0:T(8,128)(2,1)}, bf16[2,128,2048]{2,1,0:T(8,128)(2,1)}, u32[]{:S(2)}, u32[]{:S(2)}) collective-permute-start(bf16[2,128,2048]{2,1,0:T(8,128)(2,1)} %pad_maximum_fusion.10), channel_id=1, source_target_pairs={{0,2},{1,3},{2,0},{3,1},{4,6},{5,7},{6,4},{7,5},{8,10},{9,11},{10,... | collective-permute-start | bytes 3145736 | tf_op jit(solution)/shard_map/ppermute | solution.py:1188
  542.2 166.0 %collective-permute-start.4 = (bf16[2,128,2048]{2,1,0:T(8,128)(2,1)}, bf16[2,128,2048]{2,1,0:T(8,128)(2,1)}, u32[]{:S(2)}, u32[]{:S(2)}) collective-permute-start(bf16[2,128,2048]{2,1,0:T(8,128)(2,1)} %pad_maximum_fusion.11), channel_id=1, source_target_pairs={{0,3},{1,2},{2,1},{3,0},{4,7},{5,6},{6,5},{7,4},{8,11},{9,10},{10,... | collective-permute-start | bytes 3145736 | tf_op jit(solution)/shard_map/ppermute | solution.py:1188
  544.7 154.1 %copy-start.20 = (f32[1280,512]{1,0:T(8,128)S(1)}, f32[1280,512]{1,0:T(8,128)}, u32[]{:S(2)}) copy-start(f32[1280,512]{1,0:T(8,128)} %param.31) | copy-start | bytes 7864324
  544.7 165.0 %collective-permute-start.2 = (bf16[2,128,2048]{2,1,0:T(8,128)(2,1)}, bf16[2,128,2048]{2,1,0:T(8,128)(2,1)}, u32[]{:S(2)}, u32[]{:S(2)}) collective-permute-start(bf16[2,128,2048]{2,1,0:T(8,128)(2,1)} %pad_maximum_fusion.9), channel_id=1, source_target_pairs={{0,1},{1,0},{2,3},{3,2},{4,5},{5,4},{6,7},{7,6},{8,9},{9,8},{10,11... | collective-permute-start | bytes 3145736 | tf_op jit(solution)/shard_map/ppermute | solution.py:1188
  717.1 105.7 %copy-start.35 = (f32[7,2,8,128]{3,1,2,0:T(2,128)S(1)}, f32[7,2,8,128]{3,1,2,0:T(2,128)}, u32[]{:S(2)}) copy-start(f32[7,2,8,128]{3,1,2,0:T(2,128)} %copy.68) | copy-start | bytes 172036
  717.1 105.7 %copy-start.41 = (f32[1,2048]{1,0:T(1,128)S(1)}, f32[1,2048]{1,0:T(1,128)}, u32[]{:S(2)}) copy-start(f32[1,2048]{1,0:T(1,128)} %fusion.80) | copy-start | bytes 24580
  834.4 139.1 %copy-start.33 = (f32[20480]{0:T(1024)S(1)}, f32[20480]{0:T(1024)}, u32[]{:S(2)}) copy-start(f32[20480]{0:T(1024)} %param.36) | copy-start | bytes 245764
  834.4 139.1 %copy-start.39 = (f32[20480]{0:T(1024)S(1)}, f32[20480]{0:T(1024)}, u32[]{:S(2)}) copy-start(f32[20480]{0:T(1024)} %param.38) | copy-start | bytes 245764
  834.4 139.1 %copy-start.40 = (f32[20480]{0:T(1024)S(1)}, f32[20480]{0:T(1024)}, u32[]{:S(2)}) copy-start(f32[20480]{0:T(1024)} %param.37) | copy-start | bytes 245764
  834.4 141.6 %copy-start.4 = (f32[128,2048]{1,0:T(8,128)S(1)}, f32[128,2048]{1,0:T(8,128)}, u32[]{:S(2)}) copy-start(f32[128,2048]{1,0:T(8,128)} %copy-done.3) | copy-start | bytes 3145732
  834.4 141.6 %copy-start.7 = (bf16[1,128,2048]{2,1,0:T(8,128)(2,1)S(1)}, bf16[1,128,2048]{2,1,0:T(8,128)(2,1)}, u32[]{:S(2)}) copy-start(bf16[1,128,2048]{2,1,0:T(8,128)(2,1)} %param.24) | copy-start | bytes 1572868
  834.4 141.6 %copy-start.19 = (f32[128,2048]{1,0:T(8,128)S(1)}, f32[128,2048]{1,0:T(8,128)}, u32[]{:S(2)}) copy-start(f32[128,2048]{1,0:T(8,128)} %get-tuple-element.54) | copy-start | bytes 3145732
  834.4 141.6 %copy-start.27 = (bf16[1,128,2048]{2,1,0:T(8,128)(2,1)S(1)}, bf16[1,128,2048]{2,1,0:T(8,128)(2,1)}, u32[]{:S(2)}) copy-start(bf16[1,128,2048]{2,1,0:T(8,128)(2,1)} %param.25) | copy-start | bytes 1572868
  834.4 141.6 %copy-start.38 = (f32[2048]{0:T(1024)S(1)}, f32[2048]{0:T(1024)}, u32[]{:S(2)}) copy-start(f32[2048]{0:T(1024)} %copy-done.36) | copy-start | bytes 24580
  834.4 141.6 %copy-start.42 = (f32[2048]{0:T(1024)S(1)}, f32[2048]{0:T(1024)}, u32[]{:S(2)}) copy-start(f32[2048]{0:T(1024)} %get-tuple-element.107) | copy-start | bytes 24580
  834.4 141.6 %copy-start.49 = (f32[128]{0:T(128)S(1)}, f32[128]{0:T(128)}, u32[]{:S(2)}) copy-start(f32[128]{0:T(128)} %copy-done.47) | copy-start | bytes 1540
  834.5 141.6 %copy-start.52 = (f32[128]{0:T(128)S(1)}, f32[128]{0:T(128)}, u32[]{:S(2)}) copy-start(f32[128]{0:T(128)} %copy-done.51) | copy-start | bytes 1540
  834.5 141.6 %copy-start.53 = (f32[128]{0:T(128)S(1)}, f32[128]{0:T(128)}, u32[]{:S(2)}) copy-start(f32[128]{0:T(128)} %broadcast_multiply_fusion.1) | copy-start | bytes 1540
  834.5 141.5 %copy-start.54 = (f32[128]{0:T(128)S(1)}, f32[128]{0:T(128)}, u32[]{:S(2)}) copy-start(f32[128]{0:T(128)} %broadcast_multiply_fusion.2) | copy-start | bytes 1540
  973.5 18.8 %slice-start = ((s8[10485760]{0:T(1024)(128)(4,1)}), s8[4194304]{0:T(1024)(128)(4,1)S(1)}, s32[]{:S(2)}) async-start(s8[10485760]{0:T(1024)(128)(4,1)} %bitcast.92), calls=%async_computation | async-start | bytes 8388608
  978.3 14.1 %slice-start.1 = ((s8[10485760]{0:T(1024)(128)(4,1)}), s8[4194304]{0:T(1024)(128)(4,1)S(1)}, s32[]{:S(2)}) async-start(s8[10485760]{0:T(1024)(128)(4,1)} %bitcast.92), calls=%async_computation.1 | async-start | bytes 8388608
  978.3 14.1 %slice-start.2 = ((s8[10485760]{0:T(1024)(128)(4,1)}), s8[2097152]{0:T(1024)(128)(4,1)S(1)}, s32[]{:S(2)}) async-start(s8[10485760]{0:T(1024)(128)(4,1)} %bitcast.92), calls=%async_computation.2 | async-start | bytes 4194304
  (34 other events, 135.0 us)

commit v6 on v5

--- a/solution.py
+++ b/solution.py
@@ -306,6 +306,7 @@
     )
     own = [pltpu.make_async_copy(src, out.at[f, k], lsem.at[4 * n]) for n, (src, out) in enumerate(both)]
     own_doc = pltpu.make_async_copy(doc, doc_out, lsem.at[1])
+    start_weights()
     for n in range(2):
         for step in range(1, shards):
             send_tokens(n, step).start()
@@ -320,12 +321,11 @@
         for step in range(1, shards):
             send_doc(step).start()
 
-    start_weights()
+    relay_weights()
     for n in range(2):
         for step in range(1, shards):
             get_tokens(n, step).wait_recv()
             share(n, step).start()
-    relay_weights()
     bounce(back.at[rows_of(f), :], b_buf, b_out.at[:, cols(f)], lsem.at[3])
     for n in range(2):
         own[n].wait()
@@ -570,23 +570,58 @@
     )(tokens, cotangent, documents, front_weight, back_weight)
 
 
-def exchange_kernel(plan, src, back, out, b_out, buffer, send, recv, local, bsend, brecv):
+def tiles(rows, columns, tall, wide, first, last, body):
+    across = columns // wide
+
+    def one(i, carry):
+        row = pl.multiple_of(lax.div(i, across) * tall, tall)
+        column = pl.multiple_of(lax.rem(i, across) * wide, wide)
+        body(row, column)
+        return carry
+
+    lax.fori_loop(first, last, one, 0)
+
+
+def exchange_kernel(
+    plan, src, normed, weight, bias, back, out, b_out, act, slope, buffer, send, recv, local, bsend, brecv
+):
+    unit = plan.unit
     start, finish = line_exchange(plan, src, out, send, recv, local.at[0])
     start_rows, finish_rows = back_moves(plan, back, b_out, buffer, bsend, brecv, local.at[1])
     start()
     start_rows()
+    tall = 512
+
+    def units(row, column):
+        at, here = pl.ds(row, tall), pl.ds(column, unit)
+        u = jnp.dot(
+            normed[at, :],
+            weight[:, pl.ds(pl.multiple_of(column + 3 * unit, unit), unit)],
+            preferred_element_type=f32,
+        )
+        value, steep = gelu_parts(u + bias[:, here])
+        act[at, here] = value.astype(bf16)
+        slope[at, here] = steep
+
+    tiles(act.shape[0], 4 * unit, tall, unit, 0, act.shape[0] // tall * 4, units)
     finish()
     finish_rows()
 
 
-def exchange_first(plan, values, back_weight):
+def exchange_first(plan, values, normed, weight, bias, back_weight):
     dma = pltpu.SemaphoreType.DMA
     unit, shards = plan.unit, plan.fsdp
+    length = normed.shape[0]
     return pl.pallas_call(
         functools.partial(exchange_kernel, plan),
-        in_specs=[VMEM_BLOCK, ANY_BLOCK],
-        out_specs=[ANY_BLOCK, ANY_BLOCK],
-        out_shape=[jax.ShapeDtypeStruct(values.shape, bf16), jax.ShapeDtypeStruct((4 * unit, D), bf16)],
+        in_specs=[VMEM_BLOCK] * 4 + [ANY_BLOCK],
+        out_specs=[ANY_BLOCK, ANY_BLOCK, VMEM_BLOCK, VMEM_BLOCK],
+        out_shape=[
+            jax.ShapeDtypeStruct(values.shape, bf16),
+            jax.ShapeDtypeStruct((4 * unit, D), bf16),
+            jax.ShapeDtypeStruct((length, 4 * unit), bf16),
+            jax.ShapeDtypeStruct((length, 4 * unit), f32),
+        ],
         scratch_shapes=[
             pltpu.VMEM((2 * unit, D // shards), bf16),
             dma((plan.planes,)),
@@ -597,26 +632,39 @@
         ],
         compiler_params=pltpu.CompilerParams(has_side_effects=True),
         cost_estimate=busy(50),
-    )(values, back_weight)
-
-
-def exchange_back_kernel(plan, src, out, send, recv, local):
+    )(values, normed, weight, bias, back_weight)
+
+
+def exchange_back_kernel(plan, src, grad, rows, slope, out, up_grad, send, recv, local):
+    unit, tall = plan.unit, 512
     start, finish = line_exchange(plan, src, out, send, recv, local)
     start()
+
+    def units(row, column):
+        at, here = pl.ds(row, tall), pl.ds(column, unit)
+        mixed_grad = lax.dot_general(
+            grad[at, :], rows[here, :], (((1,), (1,)), ((), ())), preferred_element_type=f32
+        )
+        up_grad[at, here] = (mixed_grad * slope[at, here]).astype(bf16)
+
+    tiles(grad.shape[0], 4 * unit, tall, unit, 0, grad.shape[0] // tall * 4, units)
     finish()
 
 
-def exchange_back(plan, values):
+def exchange_back(plan, values, grad, rows, slope):
     dma = pltpu.SemaphoreType.DMA
     return pl.pallas_call(
         functools.partial(exchange_back_kernel, plan),
-        in_specs=[VMEM_BLOCK],
-        out_specs=ANY_BLOCK,
-        out_shape=jax.ShapeDtypeStruct(values.shape, bf16),
+        in_specs=[VMEM_BLOCK] * 4,
+        out_specs=[ANY_BLOCK, VMEM_BLOCK],
+        out_shape=[
+            jax.ShapeDtypeStruct(values.shape, bf16),
+            jax.ShapeDtypeStruct(slope.shape, bf16),
+        ],
         scratch_shapes=[dma((plan.planes,)), dma((plan.planes,)), dma(())],
         compiler_params=pltpu.CompilerParams(has_side_effects=True),
         cost_estimate=busy(50),
-    )(values)
+    )(values, grad, rows, slope)
 
 
 def line_sum(plan, block, rising, falling, sends, gets, rows):
@@ -948,27 +996,48 @@
     return [dma((2, plan.planes - 1))] * 2 + [dma((2, plan.planes))] * 2 + [dma(())]
 
 
-def back_sum_kernel(plan, width, src, out, *scratch):
+def back_sum_kernel(plan, width, src, normed, grad, out, partial, *scratch):
+    unit, tall = plan.unit, 512
+
     def block(i):
         return src.at[:, pl.ds(pl.multiple_of(i * width, 128), width)]
 
+    def term(row, column):
+        here = pl.ds(column, unit)
+        partial[pl.ds(row, tall), here] = lax.dot_general(
+            normed[:, pl.ds(row, tall)], grad[:, here], (((0,), (0,)), ((), ())), preferred_element_type=f32
+        ).astype(bf16)
+
+    count = D // tall * 7
     step, finish = line_sum(plan, block, *scratch, src.shape[0])
     for s in range(1, plan.planes):
         step(s)
+        tiles(
+            D,
+            7 * unit,
+            tall,
+            unit,
+            count * (s - 1) // (plan.planes - 1),
+            count * s // (plan.planes - 1),
+            term,
+        )
     finish(out)
 
 
-def back_sums(plan, partial):
+def back_sums(plan, partial, normed, hidden_grad):
     rows, width = partial.shape[0], D // plan.planes
     return pl.pallas_call(
         functools.partial(back_sum_kernel, plan, width),
-        in_specs=[VMEM_BLOCK],
-        out_specs=VMEM_BLOCK,
-        out_shape=jax.ShapeDtypeStruct((rows, width), bf16),
+        in_specs=[VMEM_BLOCK] * 3,
+        out_specs=[VMEM_BLOCK] * 2,
+        out_shape=[
+            jax.ShapeDtypeStruct((rows, width), bf16),
+            jax.ShapeDtypeStruct((D, hidden_grad.shape[1]), bf16),
+        ],
         scratch_shapes=sum_scratch(plan, rows, width),
         compiler_params=pltpu.CompilerParams(has_side_effects=True),
         cost_estimate=busy(90),
-    )(partial)
+    )(partial, normed, hidden_grad)
 
 
 def front_sum_kernel(plan, rows, src, back, out, owned, *scratch):
@@ -1216,7 +1285,9 @@
         plane_grad, back_attention, contract_last, preferred_element_type=f32
     ).astype(bf16)
     qkvg = jnp.concatenate([query, key, hidden[:, 2 * unit :].astype(bf16), attended_grad], axis=1)
-    qkvg, back_up = exchange_first(plan, qkvg.reshape(planes, share, -1), back_weight)
+    qkvg, back_up, activation, slope = exchange_first(
+        plan, qkvg.reshape(planes, share, -1), normed, weight_local, bias_local[None, 3 * unit :], back_weight
+    )
     qkvg = qkvg.reshape(planes * share, -1)
 
     seq_positions = positions_all.reshape(-1)
@@ -1240,15 +1311,13 @@
         ],
         axis=1,
     )
-    returned = exchange_back(plan, returned.reshape(planes, share, -1))
+    returned, up_grad = exchange_back(
+        plan, returned.reshape(planes, share, -1), plane_grad, back_up, slope
+    )
     returned = returned.reshape(plane_rows, -1)
     back_local = jnp.concatenate([back_attention, back_up], axis=0)
 
-    up = jnp.dot(normed, weight_local[:, 3 * unit :], preferred_element_type=f32) + bias_local[3 * unit :]
-    activation, slope = gelu_parts(up)
-    mixed_grad = lax.dot_general(plane_grad, back_up, contract_last, preferred_element_type=f32)
-    up_grad = (mixed_grad * slope).astype(bf16)
-    mixed = jnp.concatenate([returned[:, :unit], activation.astype(bf16)], axis=1)
+    mixed = jnp.concatenate([returned[:, :unit], activation], axis=1)
     hidden_grad = jnp.concatenate([returned[:, unit:], up_grad], axis=1)
 
     def sum_over_cores(value):
@@ -1273,10 +1342,7 @@
     back_partial = lax.dot_general(
         mixed, plane_grad, contract_first, preferred_element_type=f32
     ).astype(bf16)
-    front_partial = lax.dot_general(
-        normed, hidden_grad, contract_first, preferred_element_type=f32
-    ).astype(bf16)
-    back_sum = back_sums(plan, back_partial)
+    back_sum, front_partial = back_sums(plan, back_partial, normed, hidden_grad)
     back_sum, projected_cores, normed_grad_cores = lax.optimization_barrier(
         (back_sum, projected_cores, normed_grad_cores)
     )

time: 1010 us -> 954 us (0.945)
  matrix products: 79.6 us -> 37.8 us
  Pallas kernels: 779 us -> 764 us
    dot_general x3 -> x0, matrix products: 36.3 us -> none  [the longest x1 12.7 us: per_device(): lax.dot_general(normed, hidden_grad, contract_first, preferred_element_ty...]
    pallas_call x1, Pallas kernels: 149 us -> 118 us  [gather_first(): pl.pallas_call(functools.partial(gather_kernel, plan), in_specs=[VMEM_BLO...]
    unnamed x132 -> x122, local copies, waits for them, and re-layouts: 29.5 us -> 27.7 us
  transfers between devices with their start and end apart: 5 -> 5, of which waited for: 0 -> 0; matrix products, arithmetic and copies ran while one was open for 7% -> 4% of each run, Pallas kernels for 25% -> 27%
where the time goes in v6:
time: 954 us; the launch traced here: 945 us
  Pallas kernels  764 us (80%)
  other arithmetic  78.9 us (8%)
  local copies, waits for them, and re-layouts  57.7 us (6%)
  matrix products  37.8 us (4%)
    pallas_call x1, Pallas kernels, front_sums(): pl.pallas_call(functools.partial(front_sum_kernel, plan, rows), in_specs=...  154 us
    pallas_call x1, Pallas kernels, front_nexts(): pl.pallas_call(functools.partial(front_next_kernel, plan), in_specs=[VMEM...  139 us
    pallas_call x1, Pallas kernels, gather_first(): pl.pallas_call(functools.partial(gather_kernel, plan), in_specs=[VMEM_BLO...  118 us
    pallas_call x1, Pallas kernels, back_nexts(): pl.pallas_call(functools.partial(back_next_kernel, plan), in_specs=[VMEM_...  106 us
    pallas_call x1, Pallas kernels, back_sums(): pl.pallas_call(functools.partial(back_sum_kernel, plan, width), in_specs=...  102 us
    pallas_call x1, Pallas kernels, exchange_first(): pl.pallas_call(functools.partial(exchange_kernel, plan), in_specs=[VMEM_B...  60.4 us
    pallas_call x1, Pallas kernels, exchange_back(): pl.pallas_call(functools.partial(exchange_back_kernel, plan), in_specs=[V...  59.3 us
    unnamed x122, local copies, waits for them, and re-layouts  27.7 us
  transfers between devices with their start and end apart: 5, of which 0 were waited for; matrix products, arithmetic and copies ran while one was open for 4% of the time, Pallas kernels for 27%

profile of v6, /device:TPU:0, one launch (start us, length us, event | category | flops | bytes accessed | tf_op | source)
XLA Modules:
  0.0 945.0 jit_solution(14268210206568006603)
XLA Ops:
  9.6 118.3 %shard_map.351 = (bf16[4,2,128,2048]{3,2,1,0:T(8,128)(2,1)}, bf16[4,2,128,2048]{3,2,1,0:T(8,128)(2,1)}, f32[1,1024]{1,0:T(1,128)}, bf16[2048,1792]{1,0:T(8,128)(2,1)}, bf16[256,2048]{1,0:T(8,128)(2,1)}) custom-call(bf16[128,2048]{1,0:T(8,128)(2,1)} %bitcast.91, bf16[128,2048]{1,0:T(8,128)(2,1)} %bitcast.103, f32[1,1024]{1,0:T(1,128)} %convert_element_type.158.doc, ...), custom_call_target="tpu_custom_call" | custom-call | flops 117000003584 | tf_op jit(solution)/shard_map/pallas_call | solution.py:540
  131.3 3.0 convert_reduce_fusion
  136.0 1.8 fusion.3.normed
  137.9 6.8 fusion.14
  147.2 2.6 fusion.91
  150.8 3.9 convolution_convert_fusion.1
  155.1 5.3 fusion.34
  162.1 60.4 %shard_map.352 = (bf16[4,256,1024]{2,1,0:T(8,128)(2,1)}, bf16[1024,2048]{1,0:T(8,128)(2,1)}, bf16[1024,1024]{1,0:T(8,128)(2,1)}, f32[1024,1024]{1,0:T(8,128)}) custom-call(bf16[4,256,1024]{2,1,0:T(8,128)(2,1)} %bitcast.101, bf16[1024,2048]{1,0:T(8,128)(2,1)} %copy-done.11, bf16[2048,1792]{1,0:T(8,128)(2,1)} %get-tuple-element.46.weight, ...), custom_call_target="tpu_custom_call" | custom-call | flops 44999999488 | tf_op jit(solution)/shard_map/pallas_call | solution.py:615
  222.5 2.9 fusion.92
  225.4 26.3 %shard_map.353 = (bf16[1024,256]{1,0:T(8,128)(2,1)}, f32[1024,256]{1,0:T(8,128)}, f32[1024,256]{1,0:T(8,128)}, f32[1024,256]{1,0:T(8,128)}) custom-call(bf16[1024,256]{1,0:T(8,128)(2,1)} %get-tuple-element.112.q_ref, bf16[1024,256]{1,0:T(8,128)(2,1)} %get-tuple-element.111.k_ref, bf16[1024,256]{1,0:T(8,128)(2,1)} %get-tuple-element.110.v_ref, ...), custom_call_target="tpu_custom_call" | custom-call | flops 3758096384 | bytes 5242880 | tf_op jit(solution)/shard_map/pallas_call | solution.py:203
  251.7 5.1 fusion.59
  263.3 5.4 fusion.51
  270.4 59.3 %shard_map.354 = (bf16[4,256,1024]{2,1,0:T(8,128)(2,1)}, bf16[1024,1024]{1,0:T(8,128)(2,1)}) custom-call(bf16[4,256,1024]{2,1,0:T(8,128)(2,1)} %bitcast.102, bf16[1024,2048]{1,0:T(8,128)(2,1)} %bitcast.114, bf16[1024,2048]{1,0:T(8,128)(2,1)} %get-tuple-element.55.rows, f32[1024,1024]{1,0:T(8,128)} %get-tuple-element.56.slope), custom_call_target="tpu_custom_call" | custom-call | flops 44999999488 | tf_op jit(solution)/shard_map/pallas_call | solution.py:656
  331.3 10.9 %fusion.84 = f32[1024,2048]{1,0:T(8,128)S(1)} fusion(bf16[2048,1792]{1,0:T(8,128)(2,1)} %get-tuple-element.46.weight, bf16[1024,1024]{1,0:T(8,128)(2,1)} %get-tuple-element.59, bf16[1024,768]{1,0:T(8,128)(2,1)S(1)} %slice.208), kind=kOutput, calls=%fused_computation.156 | convolution fusion | flops 7523532800 | bytes 19398656 | tf_op jit(solution)/shard_map/dot_general | solution.py:1339
  343.8 3.1 slice.207
  346.9 5.6 fusion.4
  352.6 3.5 copy-done.8
  357.7 2.1 pad_maximum_fusion.grad
  361.2 7.7 convolution_convert_fusion.src
  368.9 101.7 %shard_map.355 = (bf16[1280,512]{1,0:T(8,128)(2,1)}, bf16[2048,1792]{1,0:T(8,128)(2,1)}) custom-call(bf16[1280,2048]{1,0:T(8,128)(2,1)} %convolution_convert_fusion.src, bf16[1024,2048]{1,0:T(8,128)(2,1)} %copy-done.11, bf16[1024,1792]{1,0:T(8,128)(2,1)} %pad_maximum_fusion.grad), custom_call_target="tpu_custom_call" | custom-call | flops 80999997440 | tf_op jit(solution)/shard_map/pallas_call | solution.py:1029
  471.5 2.2 convolution_reduce_fusion
  477.2 3.4 bitcast_add_fusion
  480.6 4.9 bitcast_add_fusion.1
  493.5 153.6 %shard_map.356 = (bf16[512,1792]{1,0:T(8,128)(2,1)}, bf16[1280,512]{1,0:T(8,128)(2,1)}) custom-call(bf16[2048,1792]{1,0:T(8,128)(2,1)} %get-tuple-element.60.src, bf16[1280,512]{1,0:T(8,128)(2,1)} %get-tuple-element.62.back), custom_call_target="tpu_custom_call" | custom-call | flops 108000002048 | tf_op jit(solution)/shard_map/pallas_call | solution.py:1059
  647.1 7.9 fusion.88
  659.4 3.4 fusion.65
  665.3 105.7 %shard_map.357 = (bf16[10240,512]{1,0:T(8,128)(2,1)}, bf16[256,3584]{1,0:T(8,128)(2,1)}) custom-call(bf16[1280,512]{1,0:T(8,128)(2,1)} %get-tuple-element.86.own, bf16[512,1792]{1,0:T(8,128)(2,1)} %get-tuple-element.69.src), custom_call_target="tpu_custom_call" | custom-call | flops 80999997440 | tf_op jit(solution)/shard_map/pallas_call | solution.py:1086
  771.7 10.6 %fusion.86 = (bf16[256,3584]{1,0:T(8,128)(2,1)}, f32[256,3584]{1,0:T(8,128)}, f32[256,3584]{1,0:T(8,128)}, f32[256,3584]{1,0:T(8,128)}, f32[256,3584]{1,0:T(8,128)}) fusion(f32[256,3584]{1,0:T(8,128)} %param.30, f32[]{:T(128)} %bitcast.26, f32[]{:T(128)} %bitcast.25, f32[]{:T(128)} %bitcast.27, f32[256,3584]{1,0:T(8,128)} %param.34, f32[256,3584]{1,0:T(8,128)} %param.32, ...), kind=kLoop, calls=%fused_computation.157 | loop fusion | flops 15597568 | bytes 29360140 | tf_op jit(solution)/shard_map/convert_element_type | solution.py:1388
  782.5 139.0 %shard_map.358 = (bf16[2048,3584]{1,0:T(8,128)(2,1)}, f32[160,128]{1,0:T(8,128)}) custom-call(bf16[256,3584]{1,0:T(8,128)(2,1)} %get-tuple-element.81.own, f32[160,128]{1,0:T(8,128)} %maximum_bitcast_fusion.vector), custom_call_target="tpu_custom_call" | custom-call | flops 108000002048 | tf_op jit(solution)/shard_map/pallas_call | solution.py:1170
  921.5 2.6 multiply_subtract_fusion.2
  926.4 14.1 %copy.66 = bf16[2048,3584]{1,0:T(8,128)(2,1)} copy(bf16[2048,3584]{1,0:T(8,128)(2,1)} %get-tuple-element.166) | data formatting | bytes 29360128
  940.5 4.1 copy.67
  (199 shorter events, 54.9 us)
Async XLA Ops:
  4.9 131.1 %copy-start.33 = (f32[2048]{0:T(1024)}, f32[2048]{0:T(1024)S(1)}, u32[]{:S(2)}) copy-start(f32[2048]{0:T(1024)S(1)} %get-tuple-element.121) | copy-start | bytes 24580
  137.9 6.8 copy-start.11
  263.3 5.5 copy-start.29
  331.3 15.6 %copy-start.53 = (bf16[1024,2048]{1,0:T(8,128)(2,1)S(1)}, bf16[1024,2048]{1,0:T(8,128)(2,1)}, u32[]{:S(2)}) copy-start(bf16[1024,2048]{1,0:T(8,128)(2,1)} %get-tuple-element.55.rows) | copy-start | bytes 12582916
  342.1 10.4 %copy-start.7 = (f32[1024,2048]{1,0:T(8,128)}, f32[1024,2048]{1,0:T(8,128)S(1)}, u32[]{:S(2)}) copy-start(f32[1024,2048]{1,0:T(8,128)S(1)} %fusion.84) | copy-start | bytes 25165828
  343.8 133.3 %collective-permute-start.1 = (bf16[4,128,2048]{2,1,0:T(8,128)(2,1)}, bf16[4,128,2048]{2,1,0:T(8,128)(2,1)}, u32[]{:S(2)}, u32[]{:S(2)}) collective-permute-start(bf16[4,128,2048]{2,1,0:T(8,128)(2,1)} %fusion.13), channel_id=1, source_target_pairs={{0,4},{4,0},{8,12},{12,8},{16,20},{20,16},{24,28},{28,24},{1,5},{5... | collective-permute-start | bytes 6291464 | tf_op jit(solution)/shard_map/ppermute | solution.py:1254
  357.7 122.9 %collective-permute-start = (bf16[4,128,2048]{2,1,0:T(8,128)(2,1)}, bf16[4,128,2048]{2,1,0:T(8,128)(2,1)}, u32[]{:S(2)}, u32[]{:S(2)}) collective-permute-start(bf16[4,128,2048]{2,1,0:T(8,128)(2,1)} %fusion.12), channel_id=1, source_target_pairs={{0,4},{4,0},{8,12},{12,8},{16,20},{20,16},{24,28},{28,24},{1,5},{5... | collective-permute-start | bytes 6291464 | tf_op jit(solution)/shard_map/ppermute | solution.py:1254
  470.6 5.7 copy-start.26
  476.0 186.8 %copy-start.43 = (f32[128]{0:T(128)}, f32[128]{0:T(128)S(1)}, u32[]{:S(2)}) copy-start(f32[128]{0:T(128)S(1)} %broadcast_multiply_fusion.3) | copy-start | bytes 1540
  476.4 186.4 %copy-start.46 = (f32[128]{0:T(128)}, f32[128]{0:T(128)S(1)}, u32[]{:S(2)}) copy-start(f32[128]{0:T(128)S(1)} %add_rsqrt_fusion.1) | copy-start | bytes 1540
  487.9 167.1 %collective-permute-start.3 = (bf16[2,128,2048]{2,1,0:T(8,128)(2,1)}, bf16[2,128,2048]{2,1,0:T(8,128)(2,1)}, u32[]{:S(2)}, u32[]{:S(2)}) collective-permute-start(bf16[2,128,2048]{2,1,0:T(8,128)(2,1)} %pad_maximum_fusion.7), channel_id=1, source_target_pairs={{0,2},{1,3},{2,0},{3,1},{4,6},{5,7},{6,4},{7,5},{8,10},{9,11},{10,... | collective-permute-start | bytes 3145736 | tf_op jit(solution)/shard_map/ppermute | solution.py:1257
  490.4 166.0 %collective-permute-start.4 = (bf16[2,128,2048]{2,1,0:T(8,128)(2,1)}, bf16[2,128,2048]{2,1,0:T(8,128)(2,1)}, u32[]{:S(2)}, u32[]{:S(2)}) collective-permute-start(bf16[2,128,2048]{2,1,0:T(8,128)(2,1)} %pad_maximum_fusion.8), channel_id=1, source_target_pairs={{0,3},{1,2},{2,1},{3,0},{4,7},{5,6},{6,5},{7,4},{8,11},{9,10},{10,... | collective-permute-start | bytes 3145736 | tf_op jit(solution)/shard_map/ppermute | solution.py:1257
  492.9 165.0 %collective-permute-start.2 = (bf16[2,128,2048]{2,1,0:T(8,128)(2,1)}, bf16[2,128,2048]{2,1,0:T(8,128)(2,1)}, u32[]{:S(2)}, u32[]{:S(2)}) collective-permute-start(bf16[2,128,2048]{2,1,0:T(8,128)(2,1)} %pad_maximum_fusion.6), channel_id=1, source_target_pairs={{0,1},{1,0},{2,3},{3,2},{4,5},{5,4},{6,7},{7,6},{8,9},{9,8},{10,11... | collective-permute-start | bytes 3145736 | tf_op jit(solution)/shard_map/ppermute | solution.py:1257
  493.5 153.6 %copy-start.19 = (f32[1280,512]{1,0:T(8,128)S(1)}, f32[1280,512]{1,0:T(8,128)}, u32[]{:S(2)}) copy-start(f32[1280,512]{1,0:T(8,128)} %param.31) | copy-start | bytes 7864324
  665.3 105.7 %copy-start.32 = (f32[7,2,8,128]{3,1,2,0:T(2,128)S(1)}, f32[7,2,8,128]{3,1,2,0:T(2,128)}, u32[]{:S(2)}) copy-start(f32[7,2,8,128]{3,1,2,0:T(2,128)} %copy.60) | copy-start | bytes 172036
  665.3 105.7 %copy-start.38 = (f32[1,2048]{1,0:T(1,128)S(1)}, f32[1,2048]{1,0:T(1,128)}, u32[]{:S(2)}) copy-start(f32[1,2048]{1,0:T(1,128)} %fusion.77) | copy-start | bytes 24580
  782.3 139.1 %copy-start.30 = (f32[20480]{0:T(1024)S(1)}, f32[20480]{0:T(1024)}, u32[]{:S(2)}) copy-start(f32[20480]{0:T(1024)} %param.36) | copy-start | bytes 245764
  782.3 139.1 %copy-start.36 = (f32[20480]{0:T(1024)S(1)}, f32[20480]{0:T(1024)}, u32[]{:S(2)}) copy-start(f32[20480]{0:T(1024)} %param.38) | copy-start | bytes 245764
  782.3 139.1 %copy-start.37 = (f32[20480]{0:T(1024)S(1)}, f32[20480]{0:T(1024)}, u32[]{:S(2)}) copy-start(f32[20480]{0:T(1024)} %param.37) | copy-start | bytes 245764
  782.3 141.8 %copy-start.4 = (f32[128,2048]{1,0:T(8,128)S(1)}, f32[128,2048]{1,0:T(8,128)}, u32[]{:S(2)}) copy-start(f32[128,2048]{1,0:T(8,128)} %copy-done.3) | copy-start | bytes 3145732
  782.4 141.8 %copy-start.6 = (bf16[1,128,2048]{2,1,0:T(8,128)(2,1)S(1)}, bf16[1,128,2048]{2,1,0:T(8,128)(2,1)}, u32[]{:S(2)}) copy-start(bf16[1,128,2048]{2,1,0:T(8,128)(2,1)} %param.24) | copy-start | bytes 1572868
  782.4 141.7 %copy-start.18 = (f32[128,2048]{1,0:T(8,128)S(1)}, f32[128,2048]{1,0:T(8,128)}, u32[]{:S(2)}) copy-start(f32[128,2048]{1,0:T(8,128)} %get-tuple-element.66) | copy-start | bytes 3145732
  782.4 141.7 %copy-start.27 = (bf16[1,128,2048]{2,1,0:T(8,128)(2,1)S(1)}, bf16[1,128,2048]{2,1,0:T(8,128)(2,1)}, u32[]{:S(2)}) copy-start(bf16[1,128,2048]{2,1,0:T(8,128)(2,1)} %param.25) | copy-start | bytes 1572868
  782.4 141.7 %copy-start.35 = (f32[2048]{0:T(1024)S(1)}, f32[2048]{0:T(1024)}, u32[]{:S(2)}) copy-start(f32[2048]{0:T(1024)} %copy-done.33) | copy-start | bytes 24580
  782.4 141.7 %copy-start.39 = (f32[2048]{0:T(1024)S(1)}, f32[2048]{0:T(1024)}, u32[]{:S(2)}) copy-start(f32[2048]{0:T(1024)} %get-tuple-element.119) | copy-start | bytes 24580
  782.4 141.7 %copy-start.44 = (f32[128]{0:T(128)S(1)}, f32[128]{0:T(128)}, u32[]{:S(2)}) copy-start(f32[128]{0:T(128)} %copy-done.43) | copy-start | bytes 1540
  782.4 141.7 %copy-start.47 = (f32[128]{0:T(128)S(1)}, f32[128]{0:T(128)}, u32[]{:S(2)}) copy-start(f32[128]{0:T(128)} %copy-done.46) | copy-start | bytes 1540
  782.4 141.7 %copy-start.48 = (f32[128]{0:T(128)S(1)}, f32[128]{0:T(128)}, u32[]{:S(2)}) copy-start(f32[128]{0:T(128)} %broadcast_multiply_fusion.1) | copy-start | bytes 1540
  782.5 141.7 %copy-start.49 = (f32[128]{0:T(128)S(1)}, f32[128]{0:T(128)}, u32[]{:S(2)}) copy-start(f32[128]{0:T(128)} %broadcast_multiply_fusion.2) | copy-start | bytes 1540
  921.5 19.0 %slice-start = ((s8[10485760]{0:T(1024)(128)(4,1)}), s8[4194304]{0:T(1024)(128)(4,1)S(1)}, s32[]{:S(2)}) async-start(s8[10485760]{0:T(1024)(128)(4,1)} %bitcast.89), calls=%async_computation | async-start | bytes 8388608
  926.4 14.1 %slice-start.1 = ((s8[10485760]{0:T(1024)(128)(4,1)}), s8[4194304]{0:T(1024)(128)(4,1)S(1)}, s32[]{:S(2)}) async-start(s8[10485760]{0:T(1024)(128)(4,1)} %bitcast.89), calls=%async_computation.1 | async-start | bytes 8388608
  926.4 14.1 %slice-start.2 = ((s8[10485760]{0:T(1024)(128)(4,1)}), s8[2097152]{0:T(1024)(128)(4,1)S(1)}, s32[]{:S(2)}) async-start(s8[10485760]{0:T(1024)(128)(4,1)} %bitcast.89), calls=%async_computation.2 | async-start | bytes 4194304
  (30 other events, 115.2 us)

commit v7 on v6

--- a/solution.py
+++ b/solution.py
@@ -761,13 +761,13 @@
     return step, finish
 
 
-def line_gather(plan, own, out, sends, gets, share_sends, share_gets, local, height):
-    planes = plan.planes
+def line_gather(plan, own, out, sends, gets, share_sends, share_gets, local, pitch, offset=0):
+    planes, height = plan.planes, own.shape[0]
     c, f, z, k, p = place_in_mesh()
     other = c + 1 - 2 * k
 
     def rows_of(plane, core):
-        return out.at[pl.ds(pl.multiple_of((2 * plane + core) * height, height), height), :]
+        return out.at[pl.ds(pl.multiple_of((2 * plane + core) * pitch + offset, height), height), :]
 
     def origin(side, s):
         return z - s if side == 0 else z + s
@@ -996,17 +996,21 @@
     return [dma((2, plan.planes - 1))] * 2 + [dma((2, plan.planes))] * 2 + [dma(())]
 
 
-def back_sum_kernel(plan, width, src, normed, grad, out, partial, *scratch):
-    unit, tall = plan.unit, 512
+def back_sum_kernel(plan, width, src, normed, grad, out, upper, lower, *scratch):
+    unit, tall = plan.unit, D // (2 * plan.planes)
+    half = tall // 2
 
     def block(i):
         return src.at[:, pl.ds(pl.multiple_of(i * width, 128), width)]
 
     def term(row, column):
         here = pl.ds(column, unit)
-        partial[pl.ds(row, tall), here] = lax.dot_general(
+        value = lax.dot_general(
             normed[:, pl.ds(row, tall)], grad[:, here], (((0,), (0,)), ((), ())), preferred_element_type=f32
         ).astype(bf16)
+        at = pl.ds(pl.multiple_of(lax.div(row, 2), half), half)
+        upper[at, here] = value[:half]
+        lower[at, here] = value[half:]
 
     count = D // tall * 7
     step, finish = line_sum(plan, block, *scratch, src.shape[0])
@@ -1026,25 +1030,25 @@
 
 def back_sums(plan, partial, normed, hidden_grad):
     rows, width = partial.shape[0], D // plan.planes
+    half = jax.ShapeDtypeStruct((D // 2, hidden_grad.shape[1]), bf16)
     return pl.pallas_call(
         functools.partial(back_sum_kernel, plan, width),
         in_specs=[VMEM_BLOCK] * 3,
-        out_specs=[VMEM_BLOCK] * 2,
-        out_shape=[
-            jax.ShapeDtypeStruct((rows, width), bf16),
-            jax.ShapeDtypeStruct((D, hidden_grad.shape[1]), bf16),
-        ],
+        out_specs=[VMEM_BLOCK] * 3,
+        out_shape=[jax.ShapeDtypeStruct((rows, width), bf16), half, half],
         scratch_shapes=sum_scratch(plan, rows, width),
         compiler_params=pltpu.CompilerParams(has_side_effects=True),
         cost_estimate=busy(90),
     )(partial, normed, hidden_grad)
 
 
+def front_block(plan, src, rows):
+    return lambda i: src.at[pl.ds(pl.multiple_of(i * rows, rows), rows), :]
+
+
 def front_sum_kernel(plan, rows, src, back, out, owned, *scratch):
     start, done = back_owners(plan, back, owned, *scratch[:3])
-    step, finish = line_sum(
-        plan, lambda i: src.at[pl.ds(pl.multiple_of(i * rows, rows), rows), :], *scratch[3:], rows
-    )
+    step, finish = line_sum(plan, front_block(plan, src, rows), *scratch[3:], rows)
     step(1)
     start()
     for s in range(2, plan.planes):
@@ -1066,13 +1070,50 @@
         ],
         scratch_shapes=[dma((5,))] * 3 + sum_scratch(plan, rows, width),
         compiler_params=pltpu.CompilerParams(has_side_effects=True),
-        cost_estimate=busy(120),
+        cost_estimate=busy(80),
     )(partial, back_sum)
 
 
-def back_next_kernel(plan, own, src, out, owned, *scratch):
+def owner_scratch(plan):
+    dma = pltpu.SemaphoreType.DMA
+    return [dma((5, 2)), dma((plan.per_shard,)), dma((plan.per_shard,))]
+
+
+def back_next_kernel(plan, rows, own, upper, src, out, owned, total, *scratch):
+    start, done = front_owners(plan, upper, owned, *scratch[:3])
+    step, finish = line_gather(plan, own, out, *scratch[3:8], own.shape[0])
+    step_sum, finish_sum = line_sum(plan, front_block(plan, src, rows), *scratch[8:], rows)
+    step_sum(1)
+    step(1)
+    start()
+    for s in range(2, plan.planes):
+        step_sum(s)
+        step(s)
+    finish_sum(total)
+    finish()
+    done()
+
+
+def back_nexts(plan, own, upper, partial):
+    rows, width = partial.shape[0] // plan.planes, partial.shape[1]
+    return pl.pallas_call(
+        functools.partial(back_next_kernel, plan, rows),
+        in_specs=[VMEM_BLOCK] * 3,
+        out_specs=[ANY_BLOCK, ANY_BLOCK, VMEM_BLOCK],
+        out_shape=[
+            jax.ShapeDtypeStruct((2 * plan.planes * own.shape[0], own.shape[1]), bf16),
+            jax.ShapeDtypeStruct((rows // 2, plan.per_shard * plan.unit), bf16),
+            jax.ShapeDtypeStruct((rows, width), bf16),
+        ],
+        scratch_shapes=owner_scratch(plan) + gather_scratch(plan) + sum_scratch(plan, rows, width),
+        compiler_params=pltpu.CompilerParams(has_side_effects=True),
+        cost_estimate=busy(110),
+    )(own, upper, partial)
+
+
+def upper_next_kernel(plan, own, src, out, owned, *scratch):
     start, done = front_owners(plan, src, owned, *scratch[:3])
-    step, finish = line_gather(plan, own, out, *scratch[3:], own.shape[0])
+    step, finish = line_gather(plan, own, out, *scratch[3:], 2 * own.shape[0])
     step(1)
     start()
     for s in range(2, plan.planes):
@@ -1081,20 +1122,19 @@
     done()
 
 
-def back_nexts(plan, own, front_sum):
-    dma = pltpu.SemaphoreType.DMA
+def upper_nexts(plan, own, lower):
     return pl.pallas_call(
-        functools.partial(back_next_kernel, plan),
+        functools.partial(upper_next_kernel, plan),
         in_specs=[VMEM_BLOCK, VMEM_BLOCK],
         out_specs=[ANY_BLOCK, ANY_BLOCK],
         out_shape=[
-            jax.ShapeDtypeStruct((2 * plan.planes * own.shape[0], own.shape[1]), bf16),
-            jax.ShapeDtypeStruct((front_sum.shape[0] // 2, plan.per_shard * plan.unit), bf16),
+            jax.ShapeDtypeStruct((4 * plan.planes * own.shape[0], own.shape[1]), bf16),
+            jax.ShapeDtypeStruct((lower.shape[0] // 2, plan.per_shard * plan.unit), bf16),
         ],
-        scratch_shapes=[dma((5, 2)), dma((plan.per_shard,)), dma((plan.per_shard,))] + gather_scratch(plan),
+        scratch_shapes=owner_scratch(plan) + gather_scratch(plan),
         compiler_params=pltpu.CompilerParams(has_side_effects=True),
-        cost_estimate=busy(90),
-    )(own, front_sum)
+        cost_estimate=busy(70),
+    )(own, lower)
 
 
 def vector_sum(plan, own, out, terms, sums, send, recv):
@@ -1153,9 +1193,9 @@
     return start, middle, finish
 
 
-def front_next_kernel(plan, own, vector, out, vector_out, terms, sums, vsend, vrecv, *scratch):
+def front_next_kernel(plan, own, vector, upper, out, vector_out, terms, sums, vsend, vrecv, *scratch):
     begin, middle, end = vector_sum(plan, vector, vector_out, terms, sums, vsend, vrecv)
-    step, finish = line_gather(plan, own, out, *scratch, own.shape[0])
+    step, finish = line_gather(plan, own, out, *scratch, 2 * own.shape[0], own.shape[0])
     begin()
     step(1)
     middle()
@@ -1165,14 +1205,14 @@
     end()
 
 
-def front_nexts(plan, own, vector):
+def front_nexts(plan, own, vector, upper):
     dma = pltpu.SemaphoreType.DMA
     return pl.pallas_call(
         functools.partial(front_next_kernel, plan),
-        in_specs=[VMEM_BLOCK, VMEM_BLOCK],
+        in_specs=[VMEM_BLOCK, VMEM_BLOCK, ANY_BLOCK],
         out_specs=[ANY_BLOCK, VMEM_BLOCK],
         out_shape=[
-            jax.ShapeDtypeStruct((2 * plan.planes * own.shape[0], own.shape[1]), bf16),
+            jax.ShapeDtypeStruct((4 * plan.planes * own.shape[0], own.shape[1]), bf16),
             jax.ShapeDtypeStruct(vector.shape, f32),
         ],
         scratch_shapes=[
@@ -1182,9 +1222,10 @@
             dma((plan.ranks + plan.planes,)),
         ]
         + gather_scratch(plan),
+        input_output_aliases={2: 0},
         compiler_params=pltpu.CompilerParams(has_side_effects=True),
         cost_estimate=busy(120),
-    )(own, vector)
+    )(own, vector, upper)
 
 
 def gelu_parts(u):
@@ -1342,13 +1383,13 @@
     back_partial = lax.dot_general(
         mixed, plane_grad, contract_first, preferred_element_type=f32
     ).astype(bf16)
-    back_sum, front_partial = back_sums(plan, back_partial, normed, hidden_grad)
+    back_sum, upper_partial, lower_partial = back_sums(plan, back_partial, normed, hidden_grad)
     back_sum, projected_cores, normed_grad_cores = lax.optimization_barrier(
         (back_sum, projected_cores, normed_grad_cores)
     )
     projected, normed_grad = sum_over_shards(projected_cores, normed_grad_cores)
-    front_sum, back_owned = front_sums(plan, front_partial, back_sum)
-    front_sum, projected, normed_grad = lax.optimization_barrier((front_sum, projected, normed_grad))
+    upper_sum, back_owned = front_sums(plan, upper_partial, back_sum)
+    upper_sum, projected, normed_grad = lax.optimization_barrier((upper_sum, projected, normed_grad))
 
     inputs = tokens[0].astype(f32)
     layer_out = (inputs + projected + bias_back).astype(bf16)[None]
@@ -1365,11 +1406,23 @@
     back_new, back_first_new, back_second_new = adam_update(
         back_master, back_first, back_second, back_grad, learn_rates[1], adam_step[0], weight_decay
     )
-    back_next, front_owned = back_nexts(plan, back_new.astype(bf16), front_sum)
-    front_grad = front_owned.astype(f32)
+    back_next, upper_owned, lower_sum = back_nexts(plan, back_new.astype(bf16), upper_sum, lower_partial)
+    half = upper_owned.shape[0]
+    upper_new = adam_update(
+        front_master[:half],
+        front_first[:half],
+        front_second[:half],
+        upper_owned.astype(f32),
+        learn_rates[0],
+        adam_step[0],
+        weight_decay,
+    )[0]
+    upper_next, lower_owned = upper_nexts(plan, upper_new.astype(bf16), lower_sum)
+    front_grad = jnp.concatenate([upper_owned, lower_owned], axis=0).astype(f32)
     front_new, front_first_new, front_second_new = adam_update(
         front_master, front_first, front_second, front_grad, learn_rates[0], adam_step[0], weight_decay
     )
+
     def column_sums(value):
         ones = jnp.ones((8, value.shape[0]), bf16)
         return jnp.dot(ones, value, preferred_element_type=f32)[0]
@@ -1385,7 +1438,9 @@
             jnp.sum(normed_grad, axis=0),
         ]
     )
-    front_next, vector_grad = front_nexts(plan, front_new.astype(bf16), vector_term.reshape(-1, 128))
+    front_next, vector_grad = front_nexts(
+        plan, front_new[half:].astype(bf16), vector_term.reshape(-1, 128), upper_next
+    )
     vector_grad = vector_grad.reshape(-1)
 
     count_now = adam_step[0]

time: 954 us -> 958 us (level)
    pallas_call x1 -> x2, Pallas kernels: 106 us -> 225 us  [the longest x1 152 us: back_nexts(): pl.pallas_call(functools.partial(back_next_kernel, plan, rows), in_specs=...]
    pallas_call x1, Pallas kernels: 154 us -> 92.6 us  [front_sums(): pl.pallas_call(functools.partial(front_sum_kernel, plan, rows), in_specs=...]
    pallas_call x1, Pallas kernels: 139 us -> 78.3 us  [front_nexts(): pl.pallas_call(functools.partial(front_next_kernel, plan), in_specs=[VMEM...]
    unnamed x122 -> x130, local copies, waits for them, and re-layouts: 27.7 us -> 27.7 us
  transfers between devices with their start and end apart: 5 -> 5, of which waited for: 0 -> 0; matrix products, arithmetic and copies ran while one was open for 4% -> 4% of each run, Pallas kernels for 27% -> 20%
where the time goes in v7:
time: 958 us; the launch traced here: 949 us
  Pallas kernels  762 us (80%)
  other arithmetic  84.3 us (9%)
  local copies, waits for them, and re-layouts  58.8 us (6%)
  matrix products  37.7 us (4%)
    pallas_call x1, Pallas kernels, back_nexts(): pl.pallas_call(functools.partial(back_next_kernel, plan, rows), in_specs=...  152 us
    pallas_call x1, Pallas kernels, gather_first(): pl.pallas_call(functools.partial(gather_kernel, plan), in_specs=[VMEM_BLO...  118 us
    pallas_call x1, Pallas kernels, back_sums(): pl.pallas_call(functools.partial(back_sum_kernel, plan, width), in_specs=...  102 us
    pallas_call x1, Pallas kernels, front_sums(): pl.pallas_call(functools.partial(front_sum_kernel, plan, rows), in_specs=...  92.6 us
    pallas_call x1, Pallas kernels, front_nexts(): pl.pallas_call(functools.partial(front_next_kernel, plan), in_specs=[VMEM...  78.3 us
    pallas_call x1, Pallas kernels, upper_nexts(): pl.pallas_call(functools.partial(upper_next_kernel, plan), in_specs=[VMEM...  73 us
    pallas_call x1, Pallas kernels, exchange_first(): pl.pallas_call(functools.partial(exchange_kernel, plan), in_specs=[VMEM_B...  60.7 us
    pallas_call x1, Pallas kernels, exchange_back(): pl.pallas_call(functools.partial(exchange_back_kernel, plan), in_specs=[V...  59.3 us
  transfers between devices with their start and end apart: 5, of which 0 were waited for; matrix products, arithmetic and copies ran while one was open for 4% of the time, Pallas kernels for 20%

profile of v7, /device:TPU:0, one launch (start us, length us, event | category | flops | bytes accessed | tf_op | source)
XLA Modules:
  0.0 949.4 jit_solution(16834960812160714588)
XLA Ops:
  9.6 118.3 %shard_map.351 = (bf16[4,2,128,2048]{3,2,1,0:T(8,128)(2,1)}, bf16[4,2,128,2048]{3,2,1,0:T(8,128)(2,1)}, f32[1,1024]{1,0:T(1,128)}, bf16[2048,1792]{1,0:T(8,128)(2,1)}, bf16[256,2048]{1,0:T(8,128)(2,1)}) custom-call(bf16[128,2048]{1,0:T(8,128)(2,1)} %bitcast.91, bf16[128,2048]{1,0:T(8,128)(2,1)} %bitcast.103, f32[1,1024]{1,0:T(1,128)} %convert_element_type.163.doc, ...), custom_call_target="tpu_custom_call" | custom-call | flops 117000003584 | tf_op jit(solution)/shard_map/pallas_call | solution.py:540
  131.3 3.0 convert_reduce_fusion
  137.9 6.8 fusion.25
  147.2 2.6 fusion.101
  150.8 3.9 convolution_convert_fusion.1
  155.1 5.3 fusion.45
  162.1 60.7 %shard_map.352 = (bf16[4,256,1024]{2,1,0:T(8,128)(2,1)}, bf16[1024,2048]{1,0:T(8,128)(2,1)}, bf16[1024,1024]{1,0:T(8,128)(2,1)}, f32[1024,1024]{1,0:T(8,128)}) custom-call(bf16[4,256,1024]{2,1,0:T(8,128)(2,1)} %bitcast.101, bf16[1024,2048]{1,0:T(8,128)(2,1)} %copy-done.12, bf16[2048,1792]{1,0:T(8,128)(2,1)} %get-tuple-element.50.weight, ...), custom_call_target="tpu_custom_call" | custom-call | flops 44999999488 | tf_op jit(solution)/shard_map/pallas_call | solution.py:615
  222.8 2.9 fusion.102
  225.7 26.3 %shard_map.353 = (bf16[1024,256]{1,0:T(8,128)(2,1)}, f32[1024,256]{1,0:T(8,128)}, f32[1024,256]{1,0:T(8,128)}, f32[1024,256]{1,0:T(8,128)}) custom-call(bf16[1024,256]{1,0:T(8,128)(2,1)} %get-tuple-element.119.q_ref, bf16[1024,256]{1,0:T(8,128)(2,1)} %get-tuple-element.118.k_ref, bf16[1024,256]{1,0:T(8,128)(2,1)} %get-tuple-element.117.v_ref, ...), custom_call_target="tpu_custom_call" | custom-call | flops 3758096384 | bytes 5242880 | tf_op jit(solution)/shard_map/pallas_call | solution.py:203
  252.0 5.1 fusion.70
  263.6 5.4 fusion.62
  270.7 59.3 %shard_map.354 = (bf16[4,256,1024]{2,1,0:T(8,128)(2,1)}, bf16[1024,1024]{1,0:T(8,128)(2,1)}) custom-call(bf16[4,256,1024]{2,1,0:T(8,128)(2,1)} %bitcast.102, bf16[1024,2048]{1,0:T(8,128)(2,1)} %bitcast.114, bf16[1024,2048]{1,0:T(8,128)(2,1)} %get-tuple-element.59.rows, f32[1024,1024]{1,0:T(8,128)} %get-tuple-element.60.slope), custom_call_target="tpu_custom_call" | custom-call | flops 44999999488 | tf_op jit(solution)/shard_map/pallas_call | solution.py:656
  331.5 10.9 %fusion.95 = f32[1024,2048]{1,0:T(8,128)S(1)} fusion(bf16[2048,1792]{1,0:T(8,128)(2,1)} %get-tuple-element.50.weight, bf16[1024,1024]{1,0:T(8,128)(2,1)} %get-tuple-element.63, bf16[1024,768]{1,0:T(8,128)(2,1)S(1)} %slice.226), kind=kOutput, calls=%fused_computation.171 | convolution fusion | flops 7523532800 | bytes 19398656 | tf_op jit(solution)/shard_map/dot_general | solution.py:1380
  344.1 3.1 slice.225
  347.2 5.6 fusion.4
  352.8 3.5 copy-done.9
  361.5 7.6 convolution_convert_fusion.src
  369.1 102.0 %shard_map.355 = (bf16[1280,512]{1,0:T(8,128)(2,1)}, bf16[1024,1792]{1,0:T(8,128)(2,1)}, bf16[1024,1792]{1,0:T(8,128)(2,1)}) custom-call(bf16[1280,2048]{1,0:T(8,128)(2,1)} %convolution_convert_fusion.src, bf16[1024,2048]{1,0:T(8,128)(2,1)} %copy-done.12, bf16[1024,1792]{1,0:T(8,128)(2,1)} %pad_maximum_fusion.grad), custom_call_target="tpu_custom_call" | custom-call | flops 80999997440 | tf_op jit(solution)/shard_map/pallas_call | solution.py:1034
  472.0 2.2 convolution_reduce_fusion
  477.7 3.4 bitcast_add_fusion
  481.1 4.9 bitcast_add_fusion.1
  494.0 92.6 %shard_map.356 = (bf16[256,1792]{1,0:T(8,128)(2,1)}, bf16[1280,512]{1,0:T(8,128)(2,1)}) custom-call(bf16[1024,1792]{1,0:T(8,128)(2,1)} %get-tuple-element.64.src, bf16[1280,512]{1,0:T(8,128)(2,1)} %get-tuple-element.66.back), custom_call_target="tpu_custom_call" | custom-call | flops 71999995904 | tf_op jit(solution)/shard_map/pallas_call | solution.py:1063
  586.6 7.9 fusion.98
  598.9 3.4 fusion.76
  605.5 151.7 %shard_map.357 = (bf16[10240,512]{1,0:T(8,128)(2,1)}, bf16[128,3584]{1,0:T(8,128)(2,1)}, bf16[256,1792]{1,0:T(8,128)(2,1)}) custom-call(bf16[1280,512]{1,0:T(8,128)(2,1)} %get-tuple-element.93.own, bf16[256,1792]{1,0:T(8,128)(2,1)} %get-tuple-element.73.upper, bf16[1024,1792]{1,0:T(8,128)(2,1)} %get-tuple-element.74.src), custom_call_target="tpu_custom_call" | custom-call | flops 99000000512 | tf_op jit(solution)/shard_map/pallas_call | solution.py:1099
  757.2 5.9 fusion.24.own
  763.1 73.0 %shard_map.358 = (bf16[2048,3584]{1,0:T(8,128)(2,1)}, bf16[128,3584]{1,0:T(8,128)(2,1)}) custom-call(bf16[128,3584]{1,0:T(8,128)(2,1)} %fusion.24.own, bf16[256,1792]{1,0:T(8,128)(2,1)} %get-tuple-element.76.src), custom_call_target="tpu_custom_call" | custom-call | flops 62999998464 | tf_op jit(solution)/shard_map/pallas_call | solution.py:1126
  836.1 9.1 multiply_subtract_fusion
  847.4 78.3 %shard_map.359 = (bf16[2048,3584]{1,0:T(8,128)(2,1)}, f32[160,128]{1,0:T(8,128)}) custom-call(bf16[128,3584]{1,0:T(8,128)(2,1)} %slice.246.own, f32[160,128]{1,0:T(8,128)} %maximum_bitcast_fusion.vector, bf16[2048,3584]{1,0:T(8,128)(2,1)} %get-tuple-element.78.upper), custom_call_target="tpu_custom_call", output_to_operand_aliasing={{0}: (2, {})} | custom-call | flops 108000002048 | tf_op jit(solution)/shard_map/pallas_call | solution.py:1210
  925.8 2.6 multiply_subtract_fusion.2
  930.8 14.1 %copy.68 = bf16[2048,3584]{1,0:T(8,128)(2,1)} copy(bf16[2048,3584]{1,0:T(8,128)(2,1)} %get-tuple-element.173) | data formatting | bytes 29360128
  944.9 4.1 copy.69
  (210 shorter events, 61.0 us)
Async XLA Ops:
  4.9 131.1 %copy-start.35 = (f32[2048]{0:T(1024)}, f32[2048]{0:T(1024)S(1)}, u32[]{:S(2)}) copy-start(f32[2048]{0:T(1024)S(1)} %get-tuple-element.128) | copy-start | bytes 24580
  331.5 15.6 %copy-start.57 = (bf16[1024,2048]{1,0:T(8,128)(2,1)S(1)}, bf16[1024,2048]{1,0:T(8,128)(2,1)}, u32[]{:S(2)}) copy-start(bf16[1024,2048]{1,0:T(8,128)(2,1)} %get-tuple-element.59.rows) | copy-start | bytes 12582916
  342.4 10.4 %copy-start.8 = (f32[1024,2048]{1,0:T(8,128)}, f32[1024,2048]{1,0:T(8,128)S(1)}, u32[]{:S(2)}) copy-start(f32[1024,2048]{1,0:T(8,128)S(1)} %fusion.95) | copy-start | bytes 25165828
  344.1 133.6 %collective-permute-start.1 = (bf16[4,128,2048]{2,1,0:T(8,128)(2,1)}, bf16[4,128,2048]{2,1,0:T(8,128)(2,1)}, u32[]{:S(2)}, u32[]{:S(2)}) collective-permute-start(bf16[4,128,2048]{2,1,0:T(8,128)(2,1)} %fusion.13), channel_id=1, source_target_pairs={{0,4},{4,0},{8,12},{12,8},{16,20},{20,16},{24,28},{28,24},{1,5},{5... | collective-permute-start | bytes 6291464 | tf_op jit(solution)/shard_map/ppermute | solution.py:1295
  358.0 123.1 %collective-permute-start = (bf16[4,128,2048]{2,1,0:T(8,128)(2,1)}, bf16[4,128,2048]{2,1,0:T(8,128)(2,1)}, u32[]{:S(2)}, u32[]{:S(2)}) collective-permute-start(bf16[4,128,2048]{2,1,0:T(8,128)(2,1)} %fusion.12), channel_id=1, source_target_pairs={{0,4},{4,0},{8,12},{12,8},{16,20},{20,16},{24,28},{28,24},{1,5},{5... | collective-permute-start | bytes 6291464 | tf_op jit(solution)/shard_map/ppermute | solution.py:1295
  476.6 125.8 %copy-start.47 = (f32[128]{0:T(128)}, f32[128]{0:T(128)S(1)}, u32[]{:S(2)}) copy-start(f32[128]{0:T(128)S(1)} %broadcast_multiply_fusion.3) | copy-start | bytes 1540
  476.9 125.5 %copy-start.50 = (f32[128]{0:T(128)}, f32[128]{0:T(128)S(1)}, u32[]{:S(2)}) copy-start(f32[128]{0:T(128)S(1)} %add_rsqrt_fusion.1) | copy-start | bytes 1540
  488.4 106.1 %collective-permute-start.3 = (bf16[2,128,2048]{2,1,0:T(8,128)(2,1)}, bf16[2,128,2048]{2,1,0:T(8,128)(2,1)}, u32[]{:S(2)}, u32[]{:S(2)}) collective-permute-start(bf16[2,128,2048]{2,1,0:T(8,128)(2,1)} %pad_maximum_fusion.7), channel_id=1, source_target_pairs={{0,2},{1,3},{2,0},{3,1},{4,6},{5,7},{6,4},{7,5},{8,10},{9,11},{10,... | collective-permute-start | bytes 3145736 | tf_op jit(solution)/shard_map/ppermute | solution.py:1298
  491.0 105.0 %collective-permute-start.4 = (bf16[2,128,2048]{2,1,0:T(8,128)(2,1)}, bf16[2,128,2048]{2,1,0:T(8,128)(2,1)}, u32[]{:S(2)}, u32[]{:S(2)}) collective-permute-start(bf16[2,128,2048]{2,1,0:T(8,128)(2,1)} %pad_maximum_fusion.8), channel_id=1, source_target_pairs={{0,3},{1,2},{2,1},{3,0},{4,7},{5,6},{6,5},{7,4},{8,11},{9,10},{10,... | collective-permute-start | bytes 3145736 | tf_op jit(solution)/shard_map/ppermute | solution.py:1298
  493.5 104.0 %collective-permute-start.2 = (bf16[2,128,2048]{2,1,0:T(8,128)(2,1)}, bf16[2,128,2048]{2,1,0:T(8,128)(2,1)}, u32[]{:S(2)}, u32[]{:S(2)}) collective-permute-start(bf16[2,128,2048]{2,1,0:T(8,128)(2,1)} %pad_maximum_fusion.6), channel_id=1, source_target_pairs={{0,1},{1,0},{2,3},{3,2},{4,5},{5,4},{6,7},{7,6},{8,9},{9,8},{10,11... | collective-permute-start | bytes 3145736 | tf_op jit(solution)/shard_map/ppermute | solution.py:1298
  494.0 92.6 %copy-start.21 = (f32[1280,512]{1,0:T(8,128)S(1)}, f32[1280,512]{1,0:T(8,128)}, u32[]{:S(2)}) copy-start(f32[1280,512]{1,0:T(8,128)} %param.31) | copy-start | bytes 7864324
  763.1 73.0 %copy-start.20 = (bf16[128,3584]{1,0:T(8,128)(2,1)S(1)}, bf16[128,3584]{1,0:T(8,128)(2,1)}, u32[]{:S(2)}) copy-start(bf16[128,3584]{1,0:T(8,128)(2,1)} %get-tuple-element.75) | copy-start | bytes 2752516
  836.0 10.2 %copy-start.34 = (f32[7,2,8,128]{3,1,2,0:T(2,128)S(1)}, f32[7,2,8,128]{3,1,2,0:T(2,128)}, u32[]{:S(2)}) copy-start(f32[7,2,8,128]{3,1,2,0:T(2,128)} %copy.61) | copy-start | bytes 172036
  836.1 10.2 %copy-start.40 = (f32[1,2048]{1,0:T(1,128)S(1)}, f32[1,2048]{1,0:T(1,128)}, u32[]{:S(2)}) copy-start(f32[1,2048]{1,0:T(1,128)} %fusion.88) | copy-start | bytes 24580
  836.1 10.2 %copy-start.41 = (f32[2048]{0:T(1024)S(1)}, f32[2048]{0:T(1024)}, u32[]{:S(2)}) copy-start(f32[2048]{0:T(1024)} %get-tuple-element.82) | copy-start | bytes 24580
  836.1 10.2 %copy-start.42 = (f32[2048]{0:T(1024)S(1)}, f32[2048]{0:T(1024)}, u32[]{:S(2)}) copy-start(f32[2048]{0:T(1024)} %get-tuple-element.85) | copy-start | bytes 24580
  847.3 78.5 %copy-start.32 = (f32[20480]{0:T(1024)S(1)}, f32[20480]{0:T(1024)}, u32[]{:S(2)}) copy-start(f32[20480]{0:T(1024)} %param.36) | copy-start | bytes 245764
  847.3 78.5 %copy-start.38 = (f32[20480]{0:T(1024)S(1)}, f32[20480]{0:T(1024)}, u32[]{:S(2)}) copy-start(f32[20480]{0:T(1024)} %param.38) | copy-start | bytes 245764
  847.3 78.5 %copy-start.39 = (f32[20480]{0:T(1024)S(1)}, f32[20480]{0:T(1024)}, u32[]{:S(2)}) copy-start(f32[20480]{0:T(1024)} %param.37) | copy-start | bytes 245764
  847.3 81.2 %copy-start.4 = (f32[128,2048]{1,0:T(8,128)S(1)}, f32[128,2048]{1,0:T(8,128)}, u32[]{:S(2)}) copy-start(f32[128,2048]{1,0:T(8,128)} %copy-done.3) | copy-start | bytes 3145732
  847.3 81.1 %copy-start.6 = (bf16[1,128,2048]{2,1,0:T(8,128)(2,1)S(1)}, bf16[1,128,2048]{2,1,0:T(8,128)(2,1)}, u32[]{:S(2)}) copy-start(bf16[1,128,2048]{2,1,0:T(8,128)(2,1)} %param.24) | copy-start | bytes 1572868
  847.3 81.1 %copy-start.19 = (f32[128,2048]{1,0:T(8,128)S(1)}, f32[128,2048]{1,0:T(8,128)}, u32[]{:S(2)}) copy-start(f32[128,2048]{1,0:T(8,128)} %get-tuple-element.70) | copy-start | bytes 3145732
  847.3 81.1 %copy-start.29 = (bf16[1,128,2048]{2,1,0:T(8,128)(2,1)S(1)}, bf16[1,128,2048]{2,1,0:T(8,128)(2,1)}, u32[]{:S(2)}) copy-start(bf16[1,128,2048]{2,1,0:T(8,128)(2,1)} %param.25) | copy-start | bytes 1572868
  847.3 81.1 %copy-start.37 = (f32[2048]{0:T(1024)S(1)}, f32[2048]{0:T(1024)}, u32[]{:S(2)}) copy-start(f32[2048]{0:T(1024)} %copy-done.35) | copy-start | bytes 24580
  847.4 81.1 %copy-start.43 = (f32[2048]{0:T(1024)S(1)}, f32[2048]{0:T(1024)}, u32[]{:S(2)}) copy-start(f32[2048]{0:T(1024)} %get-tuple-element.126) | copy-start | bytes 24580
  847.4 81.1 %copy-start.48 = (f32[128]{0:T(128)S(1)}, f32[128]{0:T(128)}, u32[]{:S(2)}) copy-start(f32[128]{0:T(128)} %copy-done.47) | copy-start | bytes 1540
  847.4 81.1 %copy-start.51 = (f32[128]{0:T(128)S(1)}, f32[128]{0:T(128)}, u32[]{:S(2)}) copy-start(f32[128]{0:T(128)} %copy-done.50) | copy-start | bytes 1540
  847.4 81.1 %copy-start.52 = (f32[128]{0:T(128)S(1)}, f32[128]{0:T(128)}, u32[]{:S(2)}) copy-start(f32[128]{0:T(128)} %broadcast_multiply_fusion.1) | copy-start | bytes 1540
  847.4 81.1 %copy-start.53 = (f32[128]{0:T(128)S(1)}, f32[128]{0:T(128)}, u32[]{:S(2)}) copy-start(f32[128]{0:T(128)} %broadcast_multiply_fusion.2) | copy-start | bytes 1540
  925.8 19.0 %slice-start = ((s8[10485760]{0:T(1024)(128)(4,1)}), s8[4194304]{0:T(1024)(128)(4,1)S(1)}, s32[]{:S(2)}) async-start(s8[10485760]{0:T(1024)(128)(4,1)} %bitcast.89), calls=%async_computation | async-start | bytes 8388608
  930.8 14.1 %slice-start.1 = ((s8[10485760]{0:T(1024)(128)(4,1)}), s8[4194304]{0:T(1024)(128)(4,1)S(1)}, s32[]{:S(2)}) async-start(s8[10485760]{0:T(1024)(128)(4,1)} %bitcast.89), calls=%async_computation.1 | async-start | bytes 8388608
  930.8 14.1 %slice-start.2 = ((s8[10485760]{0:T(1024)(128)(4,1)}), s8[2097152]{0:T(1024)(128)(4,1)S(1)}, s32[]{:S(2)}) async-start(s8[10485760]{0:T(1024)(128)(4,1)} %bitcast.89), calls=%async_computation.2 | async-start | bytes 4194304
  (34 other events, 135.5 us)

commit v8 on v6

--- a/solution.py
+++ b/solution.py
@@ -150,73 +150,82 @@
     )
 
 
-def rotate_back(values, tables):
-    half = ROT // 2
-    cosine, from_above, from_below = tables
-    return (
-        values * cosine
-        + jnp.roll(values * from_above, half, axis=1)
-        + jnp.roll(values * from_below, -half, axis=1)
-    )
-
-
 def attention_kernel(
-    q_ref, k_ref, v_ref, g_ref, pos_q, pos_k, seg_q, seg_k, att_ref, dq_ref, dk_ref, dv_ref
+    x_ref, pos_q, pos_k, seg_q, seg_k, cosine, from_above, from_below, out_ref, dq_ref, dk_ref, dv_ref
 ):
     scale = HEAD_DIM ** (-0.5)
-    width = q_ref.shape[1]
+    half = ROT // 2
+    block, width = dq_ref.shape
+    length = dk_ref.shape[0]
+    rows = pl.ds(pl.multiple_of(pl.program_id(0) * block, block), block)
 
     @pl.when(pl.program_id(0) == 0)
     def _():
         dk_ref[...] = jnp.zeros_like(dk_ref)
         dv_ref[...] = jnp.zeros_like(dv_ref)
+
+    def turn_back(values, at):
+        return (
+            values * cosine[at, :]
+            + pltpu.roll(values * from_above[at, :], half, 1)
+            + pltpu.roll(values * from_below[at, :], width - half, 1)
+        ).astype(bf16)
 
     allowed = (pos_k[...] <= pos_q[...]) & (seg_k[...] == seg_q[...])
     bias = jnp.where(allowed, 0.0, masked_score)
     last = (((1,), (1,)), ((), ()))
     first = (((0,), (0,)), ((), ()))
     for head in range(width // HEAD_DIM):
-        cols = slice(head * HEAD_DIM, (head + 1) * HEAD_DIM)
-        q, g = q_ref[:, cols], g_ref[:, cols]
-        k, v = k_ref[:, cols], v_ref[:, cols]
+        q_cols, k_cols, v_cols, g_cols = (
+            slice(n * width + head * HEAD_DIM, n * width + (head + 1) * HEAD_DIM) for n in range(4)
+        )
+        q, g = x_ref[rows, q_cols], x_ref[rows, g_cols]
+        k, v = x_ref[:, k_cols], x_ref[:, v_cols]
         scores = lax.dot_general(q, k, last, preferred_element_type=f32) * scale + bias
         weights = jnp.exp(scores - jnp.max(scores, axis=1, keepdims=True))
         probs = weights * (1.0 / jnp.sum(weights, axis=1, keepdims=True))
         probs_low = probs.astype(bf16)
         out = jnp.dot(probs_low, v, preferred_element_type=f32)
-        att_ref[:, cols] = out.astype(bf16)
+        out_ref[rows, q_cols] = out.astype(bf16)
         prob_grad = lax.dot_general(g, v, last, preferred_element_type=f32)
         delta = jnp.sum(g.astype(f32) * out, axis=1, keepdims=True)
         score_grad = (probs * (prob_grad - delta)).astype(bf16)
-        dq_ref[:, cols] = jnp.dot(score_grad, k, preferred_element_type=f32) * scale
-        dk_ref[:, cols] += lax.dot_general(score_grad, q, first, preferred_element_type=f32) * scale
-        dv_ref[:, cols] += lax.dot_general(probs_low, g, first, preferred_element_type=f32)
-
-
-def attention(query, key, value, grad, positions, segments):
-    length, width = query.shape
+        dq_ref[:, q_cols] = jnp.dot(score_grad, k, preferred_element_type=f32) * scale
+        dk_ref[:, q_cols] += lax.dot_general(score_grad, q, first, preferred_element_type=f32) * scale
+        dv_ref[:, q_cols] += lax.dot_general(probs_low, g, first, preferred_element_type=f32)
+    out_ref[rows, width : 2 * width] = turn_back(dq_ref[...], rows)
+
+    @pl.when(pl.program_id(0) == pl.num_programs(0) - 1)
+    def _():
+        for number in range(length // block):
+            at = slice(number * block, (number + 1) * block)
+            out_ref[at, 2 * width : 3 * width] = turn_back(dk_ref[at, :], at)
+            out_ref[at, 3 * width :] = dv_ref[at, :].astype(bf16)
+
+
+def attention(values, positions, segments, tables):
+    length, width = values.shape[0], values.shape[1] // 4
     block = 256
-    rows = pl.BlockSpec((block, width), lambda i: (i, 0))
-    whole = pl.BlockSpec((length, width), lambda i: (0, 0))
+    whole = lambda columns: pl.BlockSpec((length, columns), lambda i: (0, 0))
     column = pl.BlockSpec((block, 1), lambda i: (i, 0))
     line = pl.BlockSpec((1, length), lambda i: (0, 0))
     return pl.pallas_call(
         attention_kernel,
         grid=(length // block,),
-        in_specs=[rows, whole, whole, rows, column, line, column, line],
-        out_specs=[rows, rows, whole, whole],
-        out_shape=[
-            jax.ShapeDtypeStruct((length, width), bf16),
-            jax.ShapeDtypeStruct((length, width), f32),
-            jax.ShapeDtypeStruct((length, width), f32),
-            jax.ShapeDtypeStruct((length, width), f32),
+        in_specs=[whole(4 * width), column, line, column, line] + [whole(width)] * 3,
+        out_specs=whole(4 * width),
+        out_shape=jax.ShapeDtypeStruct((length, 4 * width), bf16),
+        scratch_shapes=[
+            pltpu.VMEM((block, width), f32),
+            pltpu.VMEM((length, width), f32),
+            pltpu.VMEM((length, width), f32),
         ],
         cost_estimate=pl.CostEstimate(
             flops=14 * length * length * width,
             transcendentals=length * length * width // HEAD_DIM,
             bytes_accessed=20 * length * width,
         ),
-    )(query, key, value, grad, positions[:, None], positions[None], segments[:, None], segments[None])
+    )(values, positions[:, None], positions[None], segments[:, None], segments[None], *tables)
 
 
 MESH = pl.DeviceIdType.MESH
@@ -1293,24 +1302,7 @@
     seq_positions = positions_all.reshape(-1)
     doc_row = documents[0].astype(jnp.int32)
     seq_documents = jnp.take(doc_row.reshape(blocks, block_tokens), block_order, axis=0).reshape(-1)
-    attended, query_grad, key_grad, value_grad = attention(
-        qkvg[:, :unit],
-        qkvg[:, unit : 2 * unit],
-        qkvg[:, 2 * unit : 3 * unit],
-        qkvg[:, 3 * unit :],
-        seq_positions,
-        seq_documents,
-    )
-    seq_tables = rotation_tables(seq_positions, unit)
-    returned = jnp.concatenate(
-        [
-            attended,
-            rotate_back(query_grad, seq_tables).astype(bf16),
-            rotate_back(key_grad, seq_tables).astype(bf16),
-            value_grad.astype(bf16),
-        ],
-        axis=1,
-    )
+    returned = attention(qkvg, seq_positions, seq_documents, rotation_tables(seq_positions, unit))
     returned, up_grad = exchange_back(
         plan, returned.reshape(planes, share, -1), plane_grad, back_up, slope
     )

time: 954 us -> 940 us (0.985)
    convert_element_type x3 -> x0, other arithmetic: 12.2 us -> none  [the longest x1 5.45 us: per_device(): rotate_back(query_grad, seq_tables).astype(bf16)]
    select_n x0 -> x1, other arithmetic: none -> 10.1 us  [rotation_tables(): return (cosine, jnp.where(lower, -sine, 0.0), jnp.where(lower, 0.0, sine))]
    unnamed x122 -> x110, local copies, waits for them, and re-layouts: 27.7 us -> 27.2 us
  transfers between devices with their start and end apart: 5 -> 5, of which waited for: 0 -> 0; matrix products, arithmetic and copies ran while one was open for 4% -> 5% of each run, Pallas kernels for 27% -> 27%
where the time goes in v8:
time: 940 us; the launch traced here: 930 us
  Pallas kernels  767 us (82%)
  other arithmetic  69.9 us (7%)
  local copies, waits for them, and re-layouts  49.6 us (5%)
  matrix products  37.8 us (4%)
    pallas_call x1, Pallas kernels, front_sums(): pl.pallas_call(functools.partial(front_sum_kernel, plan, rows), in_specs=...  154 us
    pallas_call x1, Pallas kernels, front_nexts(): pl.pallas_call(functools.partial(front_next_kernel, plan), in_specs=[VMEM...  139 us
    pallas_call x1, Pallas kernels, gather_first(): pl.pallas_call(functools.partial(gather_kernel, plan), in_specs=[VMEM_BLO...  118 us
    pallas_call x1, Pallas kernels, back_nexts(): pl.pallas_call(functools.partial(back_next_kernel, plan), in_specs=[VMEM_...  106 us
    pallas_call x1, Pallas kernels, back_sums(): pl.pallas_call(functools.partial(back_sum_kernel, plan, width), in_specs=...  102 us
    pallas_call x1, Pallas kernels, exchange_first(): pl.pallas_call(functools.partial(exchange_kernel, plan), in_specs=[VMEM_B...  60.5 us
    pallas_call x1, Pallas kernels, exchange_back(): pl.pallas_call(functools.partial(exchange_back_kernel, plan), in_specs=[V...  59.5 us
    pallas_call x1, Pallas kernels, attention(): pl.pallas_call(attention_kernel, grid=(length // block,), in_specs=[whole...  28.7 us
  transfers between devices with their start and end apart: 5, of which 0 were waited for; matrix products, arithmetic and copies ran while one was open for 5% of the time, Pallas kernels for 27%

profile of v8, /device:TPU:0, one launch (start us, length us, event | category | flops | bytes accessed | tf_op | source)
XLA Modules:
  0.0 930.4 jit_solution(13093271059736992508)
XLA Ops:
  9.6 118.3 %shard_map.351 = (bf16[4,2,128,2048]{3,2,1,0:T(8,128)(2,1)}, bf16[4,2,128,2048]{3,2,1,0:T(8,128)(2,1)}, f32[1,1024]{1,0:T(1,128)}, bf16[2048,1792]{1,0:T(8,128)(2,1)}, bf16[256,2048]{1,0:T(8,128)(2,1)}) custom-call(bf16[128,2048]{1,0:T(8,128)(2,1)} %bitcast.89, bf16[128,2048]{1,0:T(8,128)(2,1)} %bitcast.97, f32[1,1024]{1,0:T(1,128)} %convert_element_type.149.doc, ...), custom_call_target="tpu_custom_call" | custom-call | flops 117000003584 | tf_op jit(solution)/shard_map/pallas_call | solution.py:549
  131.3 3.0 convert_reduce_fusion
  136.0 1.8 fusion.3.normed
  137.9 6.8 fusion.14
  145.5 1.6 fusion.78
  147.2 2.6 fusion.79
  150.8 3.9 convolution_convert_fusion.1
  155.1 10.1 %fusion.48 = (f32[1024,256]{1,0:T(8,128)}, f32[1024,256]{1,0:T(8,128)}, f32[1024,256]{1,0:T(8,128)}, bf16[1024,256]{1,0:T(8,128)(2,1)S(1)}, bf16[1024,256]{1,0:T(8,128)(2,1)S(1)}) fusion(f32[1024]{0:T(1024)S(1)} %convert_element_type.163, f32[256]{0:T(256)S(1)} %copy-done.39, pred[256]{0:T(512)(128)(4,1)S(1)} %copy-done.40, pred[256]{0:T(512)(128)(4,1)S(1)} %copy-done.41, ...), kind=kLoop, calls=%fused_computation.74 | loop fusion | flops 7340032 | bytes 10495488 | tf_op jit(solution)/shard_map/jit(_where)/select_n | solution.py:140
  166.8 60.5 %shard_map.352 = (bf16[4,256,1024]{2,1,0:T(8,128)(2,1)}, bf16[1024,2048]{1,0:T(8,128)(2,1)}, bf16[1024,1024]{1,0:T(8,128)(2,1)}, f32[1024,1024]{1,0:T(8,128)}) custom-call(bf16[4,256,1024]{2,1,0:T(8,128)(2,1)} %bitcast.96, bf16[1024,2048]{1,0:T(8,128)(2,1)} %copy-done.9, bf16[2048,1792]{1,0:T(8,128)(2,1)} %get-tuple-element.42.weight, f32[1,1024]{1,0:T(1,128)} %bitcast.106, ...), custom_call_target="tpu_custom_call" | custom-call | flops 44999999488 | tf_op jit(solution)/shard_map/pallas_call | solution.py:624
  227.3 28.7 %shard_map.353 = bf16[1024,1024]{1,0:T(8,128)(2,1)} custom-call(bf16[1024,1024]{1,0:T(8,128)(2,1)} %bitcast.110, s32[1024,1]{1,0:T(8,128)} %add.327.pos_q, s32[1,1024]{1,0:T(1,128)} %add.288.pos_k, s32[1024,1]{1,0:T(8,128)} %select_n.144.seg_q, s32[1,1024]{1,0:T(1,128)} %select_n.133.seg_k, f32[1024,256]{1,0:T(8,128)} %get-tuple-element.108.cosine, ...), custom_call_target="tpu_custom_call" | custom-call | flops 3758096384 | bytes 5242880 | tf_op jit(solution)/shard_map/pallas_call | solution.py:212
  256.0 59.5 %shard_map.354 = (bf16[4,256,1024]{2,1,0:T(8,128)(2,1)}, bf16[1024,1024]{1,0:T(8,128)(2,1)}) custom-call(bf16[4,256,1024]{2,1,0:T(8,128)(2,1)} %bitcast.111, bf16[1024,2048]{1,0:T(8,128)(2,1)} %bitcast.108, bf16[1024,2048]{1,0:T(8,128)(2,1)} %get-tuple-element.47.rows, f32[1024,1024]{1,0:T(8,128)} %get-tuple-element.48.slope), custom_call_target="tpu_custom_call" | custom-call | flops 44999999488 | tf_op jit(solution)/shard_map/pallas_call | solution.py:665
  317.1 10.9 %fusion.72 = f32[1024,2048]{1,0:T(8,128)S(1)} fusion(bf16[2048,1792]{1,0:T(8,128)(2,1)} %get-tuple-element.42.weight, bf16[1024,1024]{1,0:T(8,128)(2,1)} %get-tuple-element.51, bf16[1024,768]{1,0:T(8,128)(2,1)S(1)} %slice.148), kind=kOutput, calls=%fused_computation.143 | convolution fusion | flops 7523532800 | bytes 19398656 | tf_op jit(solution)/shard_map/dot_general | solution.py:1331
  328.0 1.6 fusion.13
  329.6 3.1 slice.147
  332.7 5.6 fusion.4
  338.4 3.5 copy-done.8
  341.9 1.6 fusion.12
  343.5 2.1 pad_maximum_fusion.grad
  347.0 7.6 convolution_convert_fusion.src
  354.7 101.7 %shard_map.355 = (bf16[1280,512]{1,0:T(8,128)(2,1)}, bf16[2048,1792]{1,0:T(8,128)(2,1)}) custom-call(bf16[1280,2048]{1,0:T(8,128)(2,1)} %convolution_convert_fusion.src, bf16[1024,2048]{1,0:T(8,128)(2,1)} %copy-done.9, bf16[1024,1792]{1,0:T(8,128)(2,1)} %pad_maximum_fusion.grad), custom_call_target="tpu_custom_call" | custom-call | flops 80999997440 | tf_op jit(solution)/shard_map/pallas_call | solution.py:1038
  457.2 2.2 convolution_reduce_fusion
  462.9 3.4 bitcast_add_fusion
  466.3 4.9 bitcast_add_fusion.1
  479.2 153.6 %shard_map.356 = (bf16[512,1792]{1,0:T(8,128)(2,1)}, bf16[1280,512]{1,0:T(8,128)(2,1)}) custom-call(bf16[2048,1792]{1,0:T(8,128)(2,1)} %get-tuple-element.52.src, bf16[1280,512]{1,0:T(8,128)(2,1)} %get-tuple-element.54.back), custom_call_target="tpu_custom_call" | custom-call | flops 108000002048 | tf_op jit(solution)/shard_map/pallas_call | solution.py:1068
  632.8 7.9 fusion.76
  645.2 3.4 fusion.53
  651.0 105.7 %shard_map.357 = (bf16[10240,512]{1,0:T(8,128)(2,1)}, bf16[256,3584]{1,0:T(8,128)(2,1)}) custom-call(bf16[1280,512]{1,0:T(8,128)(2,1)} %get-tuple-element.78.own, bf16[512,1792]{1,0:T(8,128)(2,1)} %get-tuple-element.61.src), custom_call_target="tpu_custom_call" | custom-call | flops 80999997440 | tf_op jit(solution)/shard_map/pallas_call | solution.py:1095
  757.4 10.7 %fusion.74 = (bf16[256,3584]{1,0:T(8,128)(2,1)}, f32[256,3584]{1,0:T(8,128)}, f32[256,3584]{1,0:T(8,128)}, f32[256,3584]{1,0:T(8,128)}, f32[256,3584]{1,0:T(8,128)}) fusion(f32[256,3584]{1,0:T(8,128)} %param.30, f32[]{:T(128)} %bitcast.26, f32[]{:T(128)} %bitcast.25, f32[]{:T(128)} %bitcast.27, f32[256,3584]{1,0:T(8,128)} %param.34, f32[256,3584]{1,0:T(8,128)} %param.32, ...), kind=kLoop, calls=%fused_computation.144 | loop fusion | flops 15597568 | bytes 29360140 | tf_op jit(solution)/shard_map/convert_element_type | solution.py:1380
  768.3 139.0 %shard_map.358 = (bf16[2048,3584]{1,0:T(8,128)(2,1)}, f32[160,128]{1,0:T(8,128)}) custom-call(bf16[256,3584]{1,0:T(8,128)(2,1)} %get-tuple-element.73.own, f32[160,128]{1,0:T(8,128)} %maximum_bitcast_fusion.vector), custom_call_target="tpu_custom_call" | custom-call | flops 108000002048 | tf_op jit(solution)/shard_map/pallas_call | solution.py:1179
  907.3 2.4 multiply_subtract_fusion.2
  912.0 14.1 %copy.66 = bf16[2048,3584]{1,0:T(8,128)(2,1)} copy(bf16[2048,3584]{1,0:T(8,128)(2,1)} %get-tuple-element.151) | data formatting | bytes 29360128
  926.1 4.1 copy.67
  (176 shorter events, 41.8 us)
Async XLA Ops:
  4.9 131.1 %copy-start.27 = (f32[2048]{0:T(1024)}, f32[2048]{0:T(1024)S(1)}, u32[]{:S(2)}) copy-start(f32[2048]{0:T(1024)S(1)} %get-tuple-element.105) | copy-start | bytes 24580
  137.8 6.8 copy-start.9
  155.1 10.1 %copy-start.23 = (bf16[1024,256]{1,0:T(8,128)(2,1)S(1)}, bf16[1024,256]{1,0:T(8,128)(2,1)}, u32[]{:S(2)}) copy-start(bf16[1024,256]{1,0:T(8,128)(2,1)} %slice.157) | copy-start | bytes 1572868
  317.1 15.6 %copy-start.47 = (bf16[1024,2048]{1,0:T(8,128)(2,1)S(1)}, bf16[1024,2048]{1,0:T(8,128)(2,1)}, u32[]{:S(2)}) copy-start(bf16[1024,2048]{1,0:T(8,128)(2,1)} %get-tuple-element.47.rows) | copy-start | bytes 12582916
  327.9 10.4 %copy-start.7 = (f32[1024,2048]{1,0:T(8,128)}, f32[1024,2048]{1,0:T(8,128)S(1)}, u32[]{:S(2)}) copy-start(f32[1024,2048]{1,0:T(8,128)S(1)} %fusion.72) | copy-start | bytes 25165828
  329.6 133.3 %collective-permute-start.1 = (bf16[4,128,2048]{2,1,0:T(8,128)(2,1)}, bf16[4,128,2048]{2,1,0:T(8,128)(2,1)}, u32[]{:S(2)}, u32[]{:S(2)}) collective-permute-start(bf16[4,128,2048]{2,1,0:T(8,128)(2,1)} %fusion.13), channel_id=1, source_target_pairs={{0,4},{4,0},{8,12},{12,8},{16,20},{20,16},{24,28},{28,24},{1,5},{5... | collective-permute-start | bytes 6291464 | tf_op jit(solution)/shard_map/ppermute | solution.py:1263
  343.5 122.8 %collective-permute-start = (bf16[4,128,2048]{2,1,0:T(8,128)(2,1)}, bf16[4,128,2048]{2,1,0:T(8,128)(2,1)}, u32[]{:S(2)}, u32[]{:S(2)}) collective-permute-start(bf16[4,128,2048]{2,1,0:T(8,128)(2,1)} %fusion.12), channel_id=1, source_target_pairs={{0,4},{4,0},{8,12},{12,8},{16,20},{20,16},{24,28},{28,24},{1,5},{5... | collective-permute-start | bytes 6291464 | tf_op jit(solution)/shard_map/ppermute | solution.py:1263
  456.4 5.7 copy-start.21
  461.8 186.8 %copy-start.35 = (f32[128]{0:T(128)}, f32[128]{0:T(128)S(1)}, u32[]{:S(2)}) copy-start(f32[128]{0:T(128)S(1)} %broadcast_multiply_fusion.3) | copy-start | bytes 1540
  462.1 186.5 %copy-start.37 = (f32[128]{0:T(128)}, f32[128]{0:T(128)S(1)}, u32[]{:S(2)}) copy-start(f32[128]{0:T(128)S(1)} %add_rsqrt_fusion.1) | copy-start | bytes 1540
  473.6 167.1 %collective-permute-start.3 = (bf16[2,128,2048]{2,1,0:T(8,128)(2,1)}, bf16[2,128,2048]{2,1,0:T(8,128)(2,1)}, u32[]{:S(2)}, u32[]{:S(2)}) collective-permute-start(bf16[2,128,2048]{2,1,0:T(8,128)(2,1)} %pad_maximum_fusion.6), channel_id=1, source_target_pairs={{0,2},{1,3},{2,0},{3,1},{4,6},{5,7},{6,4},{7,5},{8,10},{9,11},{10,... | collective-permute-start | bytes 3145736 | tf_op jit(solution)/shard_map/ppermute | solution.py:1266
  476.1 166.0 %collective-permute-start.4 = (bf16[2,128,2048]{2,1,0:T(8,128)(2,1)}, bf16[2,128,2048]{2,1,0:T(8,128)(2,1)}, u32[]{:S(2)}, u32[]{:S(2)}) collective-permute-start(bf16[2,128,2048]{2,1,0:T(8,128)(2,1)} %pad_maximum_fusion.7), channel_id=1, source_target_pairs={{0,3},{1,2},{2,1},{3,0},{4,7},{5,6},{6,5},{7,4},{8,11},{9,10},{10,... | collective-permute-start | bytes 3145736 | tf_op jit(solution)/shard_map/ppermute | solution.py:1266
  478.7 165.0 %collective-permute-start.2 = (bf16[2,128,2048]{2,1,0:T(8,128)(2,1)}, bf16[2,128,2048]{2,1,0:T(8,128)(2,1)}, u32[]{:S(2)}, u32[]{:S(2)}) collective-permute-start(bf16[2,128,2048]{2,1,0:T(8,128)(2,1)} %pad_maximum_fusion.5), channel_id=1, source_target_pairs={{0,1},{1,0},{2,3},{3,2},{4,5},{5,4},{6,7},{7,6},{8,9},{9,8},{10,11... | collective-permute-start | bytes 3145736 | tf_op jit(solution)/shard_map/ppermute | solution.py:1266
  479.2 153.6 %copy-start.15 = (f32[1280,512]{1,0:T(8,128)S(1)}, f32[1280,512]{1,0:T(8,128)}, u32[]{:S(2)}) copy-start(f32[1280,512]{1,0:T(8,128)} %param.31) | copy-start | bytes 7864324
  651.0 105.7 %copy-start.26 = (f32[7,2,8,128]{3,1,2,0:T(2,128)S(1)}, f32[7,2,8,128]{3,1,2,0:T(2,128)}, u32[]{:S(2)}) copy-start(f32[7,2,8,128]{3,1,2,0:T(2,128)} %copy.60) | copy-start | bytes 172036
  651.0 105.7 %copy-start.32 = (f32[1,2048]{1,0:T(1,128)S(1)}, f32[1,2048]{1,0:T(1,128)}, u32[]{:S(2)}) copy-start(f32[1,2048]{1,0:T(1,128)} %fusion.65) | copy-start | bytes 24580
  768.1 139.1 %copy-start.24 = (f32[20480]{0:T(1024)S(1)}, f32[20480]{0:T(1024)}, u32[]{:S(2)}) copy-start(f32[20480]{0:T(1024)} %param.36) | copy-start | bytes 245764
  768.1 139.1 %copy-start.30 = (f32[20480]{0:T(1024)S(1)}, f32[20480]{0:T(1024)}, u32[]{:S(2)}) copy-start(f32[20480]{0:T(1024)} %param.38) | copy-start | bytes 245764
  768.1 139.1 %copy-start.31 = (f32[20480]{0:T(1024)S(1)}, f32[20480]{0:T(1024)}, u32[]{:S(2)}) copy-start(f32[20480]{0:T(1024)} %param.37) | copy-start | bytes 245764
  768.1 141.6 %copy-start.4 = (f32[128,2048]{1,0:T(8,128)S(1)}, f32[128,2048]{1,0:T(8,128)}, u32[]{:S(2)}) copy-start(f32[128,2048]{1,0:T(8,128)} %copy-done.3) | copy-start | bytes 3145732
  768.2 141.6 %copy-start.6 = (bf16[1,128,2048]{2,1,0:T(8,128)(2,1)S(1)}, bf16[1,128,2048]{2,1,0:T(8,128)(2,1)}, u32[]{:S(2)}) copy-start(bf16[1,128,2048]{2,1,0:T(8,128)(2,1)} %param.24) | copy-start | bytes 1572868
  768.2 141.5 %copy-start.14 = (f32[128,2048]{1,0:T(8,128)S(1)}, f32[128,2048]{1,0:T(8,128)}, u32[]{:S(2)}) copy-start(f32[128,2048]{1,0:T(8,128)} %get-tuple-element.58) | copy-start | bytes 3145732
  768.2 141.5 %copy-start.22 = (bf16[1,128,2048]{2,1,0:T(8,128)(2,1)S(1)}, bf16[1,128,2048]{2,1,0:T(8,128)(2,1)}, u32[]{:S(2)}) copy-start(bf16[1,128,2048]{2,1,0:T(8,128)(2,1)} %param.25) | copy-start | bytes 1572868
  768.2 141.5 %copy-start.29 = (f32[2048]{0:T(1024)S(1)}, f32[2048]{0:T(1024)}, u32[]{:S(2)}) copy-start(f32[2048]{0:T(1024)} %copy-done.27) | copy-start | bytes 24580
  768.2 141.5 %copy-start.33 = (f32[2048]{0:T(1024)S(1)}, f32[2048]{0:T(1024)}, u32[]{:S(2)}) copy-start(f32[2048]{0:T(1024)} %get-tuple-element.103) | copy-start | bytes 24580
  768.2 141.5 %copy-start.36 = (f32[128]{0:T(128)S(1)}, f32[128]{0:T(128)}, u32[]{:S(2)}) copy-start(f32[128]{0:T(128)} %copy-done.35) | copy-start | bytes 1540
  768.2 141.5 %copy-start.38 = (f32[128]{0:T(128)S(1)}, f32[128]{0:T(128)}, u32[]{:S(2)}) copy-start(f32[128]{0:T(128)} %copy-done.37) | copy-start | bytes 1540
  768.2 141.5 %copy-start.42 = (f32[128]{0:T(128)S(1)}, f32[128]{0:T(128)}, u32[]{:S(2)}) copy-start(f32[128]{0:T(128)} %broadcast_multiply_fusion.1) | copy-start | bytes 1540
  768.2 141.5 %copy-start.43 = (f32[128]{0:T(128)S(1)}, f32[128]{0:T(128)}, u32[]{:S(2)}) copy-start(f32[128]{0:T(128)} %broadcast_multiply_fusion.2) | copy-start | bytes 1540
  907.3 18.8 %slice-start = ((s8[10485760]{0:T(1024)(128)(4,1)}), s8[4194304]{0:T(1024)(128)(4,1)S(1)}, s32[]{:S(2)}) async-start(s8[10485760]{0:T(1024)(128)(4,1)} %bitcast.87), calls=%async_computation | async-start | bytes 8388608
  912.0 14.1 %slice-start.1 = ((s8[10485760]{0:T(1024)(128)(4,1)}), s8[4194304]{0:T(1024)(128)(4,1)S(1)}, s32[]{:S(2)}) async-start(s8[10485760]{0:T(1024)(128)(4,1)} %bitcast.87), calls=%async_computation.1 | async-start | bytes 8388608
  912.0 14.1 %slice-start.2 = ((s8[10485760]{0:T(1024)(128)(4,1)}), s8[2097152]{0:T(1024)(128)(4,1)S(1)}, s32[]{:S(2)}) async-start(s8[10485760]{0:T(1024)(128)(4,1)} %bitcast.87), calls=%async_computation.2 | async-start | bytes 4194304
  (24 other events, 97.4 us)

commit v9 on v8

--- a/solution.py
+++ b/solution.py
@@ -140,14 +140,58 @@
     return cosine, jnp.where(lower, -sine, 0.0), jnp.where(lower, 0.0, sine)
 
 
-def rotate(values, tables):
-    half = ROT // 2
-    cosine, from_above, from_below = tables
-    return (
-        values * cosine
-        + jnp.roll(values, -half, axis=1) * from_above
-        + jnp.roll(values, half, axis=1) * from_below
-    )
+def across(table, width):
+    return jnp.concatenate([table] * (width // table.shape[1]), axis=1)
+
+
+def prepare_kernel(
+    tok, grad, weight, back, bias, gain, shift, cosine, from_above, from_below, normed_ref, out_ref
+):
+    half, width = ROT // 2, back.shape[0]
+    contract_last = (((1,), (1,)), ((), ()))
+    normed = (normalize(tok[...])[0] * gain[...] + shift[...]).astype(bf16)
+    normed_ref[...] = normed
+    hidden = jnp.dot(normed, weight[...], preferred_element_type=f32) + bias[...]
+    tables = [across(ref[...], width) for ref in (cosine, from_above, from_below)]
+    for number in range(2):
+        values = hidden[:, number * width : (number + 1) * width]
+        out_ref[:, number * width : (number + 1) * width] = (
+            values * tables[0]
+            + pltpu.roll(values, width - half, 1) * tables[1]
+            + pltpu.roll(values, half, 1) * tables[2]
+        ).astype(bf16)
+    out_ref[:, 2 * width : 3 * width] = hidden[:, 2 * width :].astype(bf16)
+    out_ref[:, 3 * width :] = lax.dot_general(
+        grad[...], back[...], contract_last, preferred_element_type=f32
+    ).astype(bf16)
+
+
+def prepare(tokens, grad, weight, back, bias, gain, shift, tables):
+    length, width, block = tokens.shape[0], back.shape[0], tables[0].shape[0]
+    rows = lambda columns: pl.BlockSpec((block, columns), lambda i: (i, 0))
+    fixed = lambda height, columns: pl.BlockSpec((height, columns), lambda i: (0, 0))
+    return pl.pallas_call(
+        prepare_kernel,
+        grid=(length // block,),
+        in_specs=[
+            rows(D),
+            rows(D),
+            fixed(D, 3 * width),
+            fixed(width, D),
+            fixed(1, 3 * width),
+            fixed(1, D),
+            fixed(1, D),
+        ]
+        + [fixed(block, tables[0].shape[1])] * 3,
+        out_specs=[rows(D), rows(4 * width)],
+        out_shape=[
+            jax.ShapeDtypeStruct((length, D), bf16),
+            jax.ShapeDtypeStruct((length, 4 * width), bf16),
+        ],
+        cost_estimate=pl.CostEstimate(
+            flops=8 * length * width * D, transcendentals=0, bytes_accessed=16 * length * D
+        ),
+    )(tokens, grad, weight, back, bias, gain, shift, *tables)
 
 
 def attention_kernel(
@@ -166,9 +210,9 @@
 
     def turn_back(values, at):
         return (
-            values * cosine[at, :]
-            + pltpu.roll(values * from_above[at, :], half, 1)
-            + pltpu.roll(values * from_below[at, :], width - half, 1)
+            values * across(cosine[at, :], width)
+            + pltpu.roll(values * across(from_above[at, :], width), half, 1)
+            + pltpu.roll(values * across(from_below[at, :], width), width - half, 1)
         ).astype(bf16)
 
     allowed = (pos_k[...] <= pos_q[...]) & (seg_k[...] == seg_q[...])
@@ -212,7 +256,7 @@
     return pl.pallas_call(
         attention_kernel,
         grid=(length // block,),
-        in_specs=[whole(4 * width), column, line, column, line] + [whole(width)] * 3,
+        in_specs=[whole(4 * width), column, line, column, line] + [whole(tables[0].shape[1])] * 3,
         out_specs=whole(4 * width),
         out_shape=jax.ShapeDtypeStruct((length, 4 * width), bf16),
         scratch_shapes=[
@@ -1272,8 +1316,6 @@
     block_tokens = doc_ids.shape[1] // blocks
     offsets = jnp.arange(block_tokens, dtype=jnp.int32)
     positions_all = (block_order[:, None] * block_tokens + offsets[None, :]).reshape(planes, share)
-    own_positions = at(positions_all, z)
-    plane_positions = jnp.tile(own_positions, shards)
 
     plane_tokens, plane_grad, documents, weight_local, back_attention = gather_first(
         plan, tokens[0], cotangent[0], doc_ids.astype(f32), front_weight, back_weight
@@ -1281,28 +1323,29 @@
     plane_tokens = plane_tokens.reshape(plane_rows, D)
     plane_grad = plane_grad.reshape(plane_rows, D)
 
-    normed = (normalize(plane_tokens)[0] * norm_gain + norm_shift).astype(bf16)
-
     unit_table = pick(plan.rank_units, p)
     bias_local = jnp.take(bias_front, unit_table, axis=0).reshape(-1)
 
-    hidden = jnp.dot(normed, weight_local[:, : 3 * unit], preferred_element_type=f32) + bias_local[: 3 * unit]
-    tables = rotation_tables(plane_positions, unit)
-    query = rotate(hidden[:, :unit], tables).astype(bf16)
-    key = rotate(hidden[:, unit : 2 * unit], tables).astype(bf16)
-    attended_grad = lax.dot_general(
-        plane_grad, back_attention, contract_last, preferred_element_type=f32
-    ).astype(bf16)
-    qkvg = jnp.concatenate([query, key, hidden[:, 2 * unit :].astype(bf16), attended_grad], axis=1)
+    seq_positions = positions_all.reshape(-1)
+    tables = rotation_tables(seq_positions, 2 * HEAD_DIM)
+    normed, qkvg = prepare(
+        plane_tokens,
+        plane_grad,
+        weight_local,
+        back_attention,
+        bias_local[None, : 3 * unit],
+        norm_gain[None],
+        norm_shift[None],
+        [lax.dynamic_slice(table, (z * share, 0), (share, 2 * HEAD_DIM)) for table in tables],
+    )
     qkvg, back_up, activation, slope = exchange_first(
         plan, qkvg.reshape(planes, share, -1), normed, weight_local, bias_local[None, 3 * unit :], back_weight
     )
     qkvg = qkvg.reshape(planes * share, -1)
 
-    seq_positions = positions_all.reshape(-1)
     doc_row = documents[0].astype(jnp.int32)
     seq_documents = jnp.take(doc_row.reshape(blocks, block_tokens), block_order, axis=0).reshape(-1)
-    returned = attention(qkvg, seq_positions, seq_documents, rotation_tables(seq_positions, unit))
+    returned = attention(qkvg, seq_positions, seq_documents, tables)
     returned, up_grad = exchange_back(
         plan, returned.reshape(planes, share, -1), plane_grad, back_up, slope
     )

time: 940 us -> 916 us (0.974)
  other arithmetic: 69.9 us -> 54.2 us
  matrix products: 37.8 us -> 27.1 us
  Pallas kernels: 767 us -> 777 us
    pallas_call x0 -> x1, Pallas kernels: none -> 11.1 us  [prepare(): pl.pallas_call(prepare_kernel, grid=(length // block,), in_specs=[rows(D)...]
    dot_general x2 -> x0, matrix products: 10.7 us -> none  [the longest x1 6.82 us: per_device(): jnp.dot(normed, weight_local[:, :3 * unit], preferred_element_type=f32)]
    unnamed x110 -> x92, local copies, waits for them, and re-layouts: 27.2 us -> 27.1 us
  transfers between devices with their start and end apart: 5 -> 5, of which waited for: 0 -> 0; matrix products, arithmetic and copies ran while one was open for 5% -> 5% of each run, Pallas kernels for 27% -> 28%
where the time goes in v9:
time: 916 us; the launch traced here: 910 us
  Pallas kernels  777 us (85%)
  other arithmetic  54.2 us (6%)
  local copies, waits for them, and re-layouts  45.6 us (5%)
  matrix products  27.1 us (3%)
    pallas_call x1, Pallas kernels, front_sums(): pl.pallas_call(functools.partial(front_sum_kernel, plan, rows), in_specs=...  154 us
    pallas_call x1, Pallas kernels, front_nexts(): pl.pallas_call(functools.partial(front_next_kernel, plan), in_specs=[VMEM...  139 us
    pallas_call x1, Pallas kernels, gather_first(): pl.pallas_call(functools.partial(gather_kernel, plan), in_specs=[VMEM_BLO...  118 us
    pallas_call x1, Pallas kernels, back_nexts(): pl.pallas_call(functools.partial(back_next_kernel, plan), in_specs=[VMEM_...  106 us
    pallas_call x1, Pallas kernels, back_sums(): pl.pallas_call(functools.partial(back_sum_kernel, plan, width), in_specs=...  102 us
    pallas_call x1, Pallas kernels, exchange_first(): pl.pallas_call(functools.partial(exchange_kernel, plan), in_specs=[VMEM_B...  60.5 us
    pallas_call x1, Pallas kernels, exchange_back(): pl.pallas_call(functools.partial(exchange_back_kernel, plan), in_specs=[V...  59.4 us
    pallas_call x1, Pallas kernels, attention(): pl.pallas_call(attention_kernel, grid=(length // block,), in_specs=[whole...  28.2 us
  transfers between devices with their start and end apart: 5, of which 0 were waited for; matrix products, arithmetic and copies ran while one was open for 5% of the time, Pallas kernels for 28%

profile of v9, /device:TPU:0, one launch (start us, length us, event | category | flops | bytes accessed | tf_op | source)
XLA Modules:
  0.0 910.4 jit_solution(5000516704641266240)
XLA Ops:
  9.5 118.3 %shard_map.324 = (bf16[4,2,128,2048]{3,2,1,0:T(8,128)(2,1)}, bf16[4,2,128,2048]{3,2,1,0:T(8,128)(2,1)}, f32[1,1024]{1,0:T(1,128)}, bf16[2048,1792]{1,0:T(8,128)(2,1)}, bf16[256,2048]{1,0:T(8,128)(2,1)}) custom-call(bf16[128,2048]{1,0:T(8,128)(2,1)} %bitcast.77, bf16[128,2048]{1,0:T(8,128)(2,1)} %bitcast.88, f32[1,1024]{1,0:T(1,128)} %convert_element_type.112.doc, ...), custom_call_target="tpu_custom_call" | custom-call | flops 117000003584 | tf_op jit(solution)/shard_map/pallas_call | solution.py:593
  132.5 2.0 fusion.26
  136.0 11.1 %shard_map.325 = (bf16[1024,2048]{1,0:T(8,128)(2,1)}, bf16[1024,1024]{1,0:T(8,128)(2,1)}) custom-call(bf16[1024,2048]{1,0:T(8,128)(2,1)} %bitcast.85, bf16[1024,2048]{1,0:T(8,128)(2,1)} %bitcast.82, bf16[2048,1792]{1,0:T(8,128)(2,1)} %get-tuple-element.45.weight, bf16[256,2048]{1,0:T(8,128)(2,1)} %get-tuple-element.46.back, f32[1,768]{1,0:T(1,128)} %bitcast.95, ...), custom_call_target="tpu_custom_call" | custom-call | flops 4294967296 | bytes 33554432 | tf_op jit(solution)/shard_map/pallas_call | solution.py:173
  147.1 60.5 %shard_map.326 = (bf16[4,256,1024]{2,1,0:T(8,128)(2,1)}, bf16[1024,2048]{1,0:T(8,128)(2,1)}, bf16[1024,1024]{1,0:T(8,128)(2,1)}, f32[1024,1024]{1,0:T(8,128)}) custom-call(bf16[4,256,1024]{2,1,0:T(8,128)(2,1)} %bitcast.97, bf16[1024,2048]{1,0:T(8,128)(2,1)} %get-tuple-element.48.normed, bf16[2048,1792]{1,0:T(8,128)(2,1)} %get-tuple-element.45.weight, ...), custom_call_target="tpu_custom_call" | custom-call | flops 44999999488 | tf_op jit(solution)/shard_map/pallas_call | solution.py:668
  207.6 28.2 %shard_map.327 = bf16[1024,1024]{1,0:T(8,128)(2,1)} custom-call(bf16[1024,1024]{1,0:T(8,128)(2,1)} %bitcast.98, s32[1024,1]{1,0:T(8,128)} %add.253.pos_q, s32[1,1024]{1,0:T(1,128)} %add.214.pos_k, s32[1024,1]{1,0:T(8,128)} %select_n.129.seg_q, s32[1,1024]{1,0:T(1,128)} %select_n.122.seg_k, f32[1024,128]{1,0:T(8,128)} %copy-done.17, f32[1024,128]{1,0:T(8,128)} %copy-done.16, ...), custom_call_target="tpu_custom_call" | custom-call | flops 3758096384 | bytes 5242880 | tf_op jit(solution)/shard_map/pallas_call | solution.py:256
  235.8 59.4 %shard_map.328 = (bf16[4,256,1024]{2,1,0:T(8,128)(2,1)}, bf16[1024,1024]{1,0:T(8,128)(2,1)}) custom-call(bf16[4,256,1024]{2,1,0:T(8,128)(2,1)} %bitcast.99, bf16[1024,2048]{1,0:T(8,128)(2,1)} %bitcast.83, bf16[1024,2048]{1,0:T(8,128)(2,1)} %get-tuple-element.51.rows, f32[1024,1024]{1,0:T(8,128)} %get-tuple-element.52.slope), custom_call_target="tpu_custom_call" | custom-call | flops 44999999488 | tf_op jit(solution)/shard_map/pallas_call | solution.py:709
  295.1 1.5 slice.76
  296.7 10.9 %fusion.44 = f32[1024,2048]{1,0:T(8,128)S(1)} fusion(bf16[2048,1792]{1,0:T(8,128)(2,1)} %get-tuple-element.45.weight, bf16[1024,1024]{1,0:T(8,128)(2,1)} %get-tuple-element.55, bf16[1024,768]{1,0:T(8,128)(2,1)S(1)} %slice.76), kind=kOutput, calls=%fused_computation.109 | convolution fusion | flops 7523532800 | bytes 19398656 | tf_op jit(solution)/shard_map/dot_general | solution.py:1374
  307.6 1.6 fusion.7
  309.2 3.1 slice.75
  312.3 5.6 fusion
  318.0 3.5 copy-done.7
  321.5 1.6 fusion.6
  323.1 2.1 pad_maximum_fusion.grad
  326.6 7.6 convolution_convert_fusion.src
  334.3 101.7 %shard_map.329 = (bf16[1280,512]{1,0:T(8,128)(2,1)}, bf16[2048,1792]{1,0:T(8,128)(2,1)}) custom-call(bf16[1280,2048]{1,0:T(8,128)(2,1)} %convolution_convert_fusion.src, bf16[1024,2048]{1,0:T(8,128)(2,1)} %get-tuple-element.48.normed, bf16[1024,1792]{1,0:T(8,128)(2,1)} %pad_maximum_fusion.grad), custom_call_target="tpu_custom_call" | custom-call | flops 80999997440 | tf_op jit(solution)/shard_map/pallas_call | solution.py:1082
  436.8 2.2 convolution_reduce_fusion
  442.5 3.4 bitcast_add_fusion
  446.0 4.9 bitcast_add_fusion.1
  453.3 1.5 collective-permute-start.3
  458.9 153.6 %shard_map.330 = (bf16[512,1792]{1,0:T(8,128)(2,1)}, bf16[1280,512]{1,0:T(8,128)(2,1)}) custom-call(bf16[2048,1792]{1,0:T(8,128)(2,1)} %get-tuple-element.56.src, bf16[1280,512]{1,0:T(8,128)(2,1)} %get-tuple-element.58.back), custom_call_target="tpu_custom_call" | custom-call | flops 108000002048 | tf_op jit(solution)/shard_map/pallas_call | solution.py:1112
  612.5 7.9 fusion.48
  621.9 1.5 convert_element_type.132
  623.4 1.5 convert_element_type.126
  624.8 3.4 fusion.22
  630.7 105.7 %shard_map.331 = (bf16[10240,512]{1,0:T(8,128)(2,1)}, bf16[256,3584]{1,0:T(8,128)(2,1)}) custom-call(bf16[1280,512]{1,0:T(8,128)(2,1)} %get-tuple-element.82.own, bf16[512,1792]{1,0:T(8,128)(2,1)} %get-tuple-element.65.src), custom_call_target="tpu_custom_call" | custom-call | flops 80999997440 | tf_op jit(solution)/shard_map/pallas_call | solution.py:1139
  737.1 10.8 %fusion.46 = (bf16[256,3584]{1,0:T(8,128)(2,1)}, f32[256,3584]{1,0:T(8,128)}, f32[256,3584]{1,0:T(8,128)}, f32[256,3584]{1,0:T(8,128)}, f32[256,3584]{1,0:T(8,128)}) fusion(f32[256,3584]{1,0:T(8,128)} %param.27, f32[]{:T(128)} %bitcast.25, f32[]{:T(128)} %bitcast.24, f32[]{:T(128)} %bitcast.26, f32[256,3584]{1,0:T(8,128)} %param.31, f32[256,3584]{1,0:T(8,128)} %param.29, ...), kind=kLoop, calls=%fused_computation.110 | loop fusion | flops 15597568 | bytes 29360140 | tf_op jit(solution)/shard_map/convert_element_type | solution.py:1423
  748.0 139.0 %shard_map.332 = (bf16[2048,3584]{1,0:T(8,128)(2,1)}, f32[160,128]{1,0:T(8,128)}) custom-call(bf16[256,3584]{1,0:T(8,128)(2,1)} %get-tuple-element.77.own, f32[160,128]{1,0:T(8,128)} %maximum_bitcast_fusion.vector), custom_call_target="tpu_custom_call" | custom-call | flops 108000002048 | tf_op jit(solution)/shard_map/pallas_call | solution.py:1223
  887.0 2.4 multiply_subtract_fusion.2
  889.6 1.6 fusion.30
  891.8 14.1 %copy.55 = bf16[2048,3584]{1,0:T(8,128)(2,1)} copy(bf16[2048,3584]{1,0:T(8,128)(2,1)} %get-tuple-element.142) | data formatting | bytes 29360128
  905.9 4.1 copy.56
  (143 shorter events, 31.6 us)
Async XLA Ops:
  9.5 122.9 %copy-start.32 = (f32[128]{0:T(128)S(1)}, f32[128]{0:T(128)}, u32[]{:S(2)}) copy-start(f32[128]{0:T(128)} %constant.173) | copy-start | bytes 1540
  9.5 122.9 %copy-start.33 = (pred[128]{0:T(512)(128)(4,1)S(1)}, pred[128]{0:T(512)(128)(4,1)}, u32[]{:S(2)}) copy-start(pred[128]{0:T(512)(128)(4,1)} %constant.168.clone) | copy-start | bytes 388
  9.5 122.9 %copy-start.34 = (pred[128]{0:T(512)(128)(4,1)S(1)}, pred[128]{0:T(512)(128)(4,1)}, u32[]{:S(2)}) copy-start(pred[128]{0:T(512)(128)(4,1)} %constant.167.clone) | copy-start | bytes 388
  134.4 12.7 %copy-start.15 = (f32[1024,128]{1,0:T(8,128)}, f32[1024,128]{1,0:T(8,128)S(1)}, u32[]{:S(2)}) copy-start(f32[1024,128]{1,0:T(8,128)S(1)} %get-tuple-element.100.from_below) | copy-start | bytes 1572868
  134.4 12.7 %copy-start.16 = (f32[1024,128]{1,0:T(8,128)}, f32[1024,128]{1,0:T(8,128)S(1)}, u32[]{:S(2)}) copy-start(f32[1024,128]{1,0:T(8,128)S(1)} %get-tuple-element.101.from_above) | copy-start | bytes 1572868
  296.7 15.6 %copy-start.38 = (bf16[1024,2048]{1,0:T(8,128)(2,1)S(1)}, bf16[1024,2048]{1,0:T(8,128)(2,1)}, u32[]{:S(2)}) copy-start(bf16[1024,2048]{1,0:T(8,128)(2,1)} %get-tuple-element.51.rows) | copy-start | bytes 12582916
  309.2 133.3 %collective-permute-start.1 = (bf16[4,128,2048]{2,1,0:T(8,128)(2,1)}, bf16[4,128,2048]{2,1,0:T(8,128)(2,1)}, u32[]{:S(2)}, u32[]{:S(2)}) collective-permute-start(bf16[4,128,2048]{2,1,0:T(8,128)(2,1)} %fusion.7), channel_id=1, source_target_pairs={{0,4},{4,0},{8,12},{12,8},{16,20},{20,16},{24,28},{28,24},{1,5},{5... | collective-permute-start | bytes 6291464 | tf_op jit(solution)/shard_map/ppermute | solution.py:1307
  323.1 122.9 %collective-permute-start = (bf16[4,128,2048]{2,1,0:T(8,128)(2,1)}, bf16[4,128,2048]{2,1,0:T(8,128)(2,1)}, u32[]{:S(2)}, u32[]{:S(2)}) collective-permute-start(bf16[4,128,2048]{2,1,0:T(8,128)(2,1)} %fusion.6), channel_id=1, source_target_pairs={{0,4},{4,0},{8,12},{12,8},{16,20},{20,16},{24,28},{28,24},{1,5},{5... | collective-permute-start | bytes 6291464 | tf_op jit(solution)/shard_map/ppermute | solution.py:1307
  441.4 186.8 %copy-start.28 = (f32[128]{0:T(128)}, f32[128]{0:T(128)S(1)}, u32[]{:S(2)}) copy-start(f32[128]{0:T(128)S(1)} %broadcast_multiply_fusion.2) | copy-start | bytes 1540
  441.7 186.5 %copy-start.30 = (f32[128]{0:T(128)}, f32[128]{0:T(128)S(1)}, u32[]{:S(2)}) copy-start(f32[128]{0:T(128)S(1)} %add_rsqrt_fusion) | copy-start | bytes 1540
  453.3 167.1 %collective-permute-start.3 = (bf16[2,128,2048]{2,1,0:T(8,128)(2,1)}, bf16[2,128,2048]{2,1,0:T(8,128)(2,1)}, u32[]{:S(2)}, u32[]{:S(2)}) collective-permute-start(bf16[2,128,2048]{2,1,0:T(8,128)(2,1)} %pad_maximum_fusion.5), channel_id=1, source_target_pairs={{0,2},{1,3},{2,0},{3,1},{4,6},{5,7},{6,4},{7,5},{8,10},{9,11},{10,... | collective-permute-start | bytes 3145736 | tf_op jit(solution)/shard_map/ppermute | solution.py:1310
  455.8 166.1 %collective-permute-start.4 = (bf16[2,128,2048]{2,1,0:T(8,128)(2,1)}, bf16[2,128,2048]{2,1,0:T(8,128)(2,1)}, u32[]{:S(2)}, u32[]{:S(2)}) collective-permute-start(bf16[2,128,2048]{2,1,0:T(8,128)(2,1)} %pad_maximum_fusion.6), channel_id=1, source_target_pairs={{0,3},{1,2},{2,1},{3,0},{4,7},{5,6},{6,5},{7,4},{8,11},{9,10},{10,... | collective-permute-start | bytes 3145736 | tf_op jit(solution)/shard_map/ppermute | solution.py:1310
  458.3 165.0 %collective-permute-start.2 = (bf16[2,128,2048]{2,1,0:T(8,128)(2,1)}, bf16[2,128,2048]{2,1,0:T(8,128)(2,1)}, u32[]{:S(2)}, u32[]{:S(2)}) collective-permute-start(bf16[2,128,2048]{2,1,0:T(8,128)(2,1)} %pad_maximum_fusion.4), channel_id=1, source_target_pairs={{0,1},{1,0},{2,3},{3,2},{4,5},{5,4},{6,7},{7,6},{8,9},{9,8},{10,11... | collective-permute-start | bytes 3145736 | tf_op jit(solution)/shard_map/ppermute | solution.py:1310
  458.9 153.6 %copy-start.10 = (f32[1280,512]{1,0:T(8,128)S(1)}, f32[1280,512]{1,0:T(8,128)}, u32[]{:S(2)}) copy-start(f32[1280,512]{1,0:T(8,128)} %param.28) | copy-start | bytes 7864324
  630.7 105.7 %copy-start.20 = (f32[7,2,8,128]{3,1,2,0:T(2,128)S(1)}, f32[7,2,8,128]{3,1,2,0:T(2,128)}, u32[]{:S(2)}) copy-start(f32[7,2,8,128]{3,1,2,0:T(2,128)} %copy.49) | copy-start | bytes 172036
  630.7 105.7 %copy-start.25 = (f32[1,2048]{1,0:T(1,128)S(1)}, f32[1,2048]{1,0:T(1,128)}, u32[]{:S(2)}) copy-start(f32[1,2048]{1,0:T(1,128)} %fusion.37) | copy-start | bytes 24580
  747.9 139.1 %copy-start.18 = (f32[20480]{0:T(1024)S(1)}, f32[20480]{0:T(1024)}, u32[]{:S(2)}) copy-start(f32[20480]{0:T(1024)} %param.33) | copy-start | bytes 245764
  747.9 139.1 %copy-start.23 = (f32[20480]{0:T(1024)S(1)}, f32[20480]{0:T(1024)}, u32[]{:S(2)}) copy-start(f32[20480]{0:T(1024)} %param.35) | copy-start | bytes 245764
  747.9 139.1 %copy-start.24 = (f32[20480]{0:T(1024)S(1)}, f32[20480]{0:T(1024)}, u32[]{:S(2)}) copy-start(f32[20480]{0:T(1024)} %param.34) | copy-start | bytes 245764
  747.9 141.6 %copy-start.3 = (f32[128,2048]{1,0:T(8,128)S(1)}, f32[128,2048]{1,0:T(8,128)}, u32[]{:S(2)}) copy-start(f32[128,2048]{1,0:T(8,128)} %copy-done.2) | copy-start | bytes 3145732
  747.9 141.6 %copy-start.5 = (bf16[1,128,2048]{2,1,0:T(8,128)(2,1)S(1)}, bf16[1,128,2048]{2,1,0:T(8,128)(2,1)}, u32[]{:S(2)}) copy-start(bf16[1,128,2048]{2,1,0:T(8,128)(2,1)} %param.21) | copy-start | bytes 1572868
  747.9 141.6 %copy-start.9 = (f32[128,2048]{1,0:T(8,128)S(1)}, f32[128,2048]{1,0:T(8,128)}, u32[]{:S(2)}) copy-start(f32[128,2048]{1,0:T(8,128)} %get-tuple-element.62) | copy-start | bytes 3145732
  747.9 141.6 %copy-start.13 = (bf16[1,128,2048]{2,1,0:T(8,128)(2,1)S(1)}, bf16[1,128,2048]{2,1,0:T(8,128)(2,1)}, u32[]{:S(2)}) copy-start(bf16[1,128,2048]{2,1,0:T(8,128)(2,1)} %param.22) | copy-start | bytes 1572868
  747.9 141.6 %copy-start.22 = (f32[2048]{0:T(1024)S(1)}, f32[2048]{0:T(1024)}, u32[]{:S(2)}) copy-start(f32[2048]{0:T(1024)} %get-tuple-element.99) | copy-start | bytes 24580
  747.9 141.6 %copy-start.26 = (f32[2048]{0:T(1024)S(1)}, f32[2048]{0:T(1024)}, u32[]{:S(2)}) copy-start(f32[2048]{0:T(1024)} %get-tuple-element.97) | copy-start | bytes 24580
  748.0 141.6 %copy-start.29 = (f32[128]{0:T(128)S(1)}, f32[128]{0:T(128)}, u32[]{:S(2)}) copy-start(f32[128]{0:T(128)} %copy-done.28) | copy-start | bytes 1540
  748.0 141.6 %copy-start.31 = (f32[128]{0:T(128)S(1)}, f32[128]{0:T(128)}, u32[]{:S(2)}) copy-start(f32[128]{0:T(128)} %copy-done.30) | copy-start | bytes 1540
  748.0 141.6 %copy-start.35 = (f32[128]{0:T(128)S(1)}, f32[128]{0:T(128)}, u32[]{:S(2)}) copy-start(f32[128]{0:T(128)} %broadcast_multiply_fusion) | copy-start | bytes 1540
  748.0 141.6 %copy-start.36 = (f32[128]{0:T(128)S(1)}, f32[128]{0:T(128)}, u32[]{:S(2)}) copy-start(f32[128]{0:T(128)} %broadcast_multiply_fusion.1) | copy-start | bytes 1540
  887.0 18.8 %slice-start = ((s8[10485760]{0:T(1024)(128)(4,1)}), s8[4194304]{0:T(1024)(128)(4,1)S(1)}, s32[]{:S(2)}) async-start(s8[10485760]{0:T(1024)(128)(4,1)} %bitcast.75), calls=%async_computation | async-start | bytes 8388608
  891.8 14.1 %slice-start.1 = ((s8[10485760]{0:T(1024)(128)(4,1)}), s8[4194304]{0:T(1024)(128)(4,1)S(1)}, s32[]{:S(2)}) async-start(s8[10485760]{0:T(1024)(128)(4,1)} %bitcast.75), calls=%async_computation.1 | async-start | bytes 8388608
  891.8 14.1 %slice-start.2 = ((s8[10485760]{0:T(1024)(128)(4,1)}), s8[2097152]{0:T(1024)(128)(4,1)S(1)}, s32[]{:S(2)}) async-start(s8[10485760]{0:T(1024)(128)(4,1)} %bitcast.75), calls=%async_computation.2 | async-start | bytes 4194304
  (15 other events, 77.5 us)

commit v10 on v9

--- a/solution.py
+++ b/solution.py
@@ -44,7 +44,8 @@
                 keep, home[f] = home[f][:4], home[f][4:]
                 pairs[2 * f], pairs[2 * f + 1] = keep[:2], keep[2:]
             elif home[f]:
-                keep, home[f] = home[f], []
+                some = (len(home[f]) + 1) // 2
+                keep, home[f] = home[f][:some], home[f][some:]
                 for i, g in enumerate(keep):
                     pairs[2 * f + i % 2][(i + i // 2) % 2] = g
         for s in range(2):
@@ -56,7 +57,7 @@
                         continue
                     options = sorted(
                         (h for h in range(fsdp) if home[h]),
-                        key=lambda h: (h in used, bin(h ^ f).count("1"), -len(home[h])),
+                        key=lambda h: (h in used, h == f, bin(h ^ f).count("1"), -len(home[h])),
                     )
                     used.add(options[0])
                     pairs[p][s] = home[options[0]].pop(0)
@@ -88,28 +89,6 @@
             for p in range(r)
         ]
         self.back_units = [[p] + [g - 2 * r for g in self.rank_units[p][3:]] for p in range(r)]
-        self.matchings = []
-        left = {p: list(range(5)) for p in range(r)}
-        own = lambda p, j: self.back_units[p][j] // 5
-        for _ in range(5):
-            match = {}
-
-            def assign(p, seen):
-                for j in left[p]:
-                    c = own(p, j)
-                    if c in seen:
-                        continue
-                    seen.add(c)
-                    if c not in match or assign(match[c][0], seen):
-                        match[c] = (p, j)
-                        return True
-                return False
-
-            for p in range(r):
-                assert assign(p, set())
-            for c, (p, j) in match.items():
-                left[p].remove(j)
-            self.matchings.append(match)
 
     def device(self, z, k, f):
         return (2 * z + k) * self.fsdp + f

time: 916 us -> 907 us (level)
    pallas_call x1, Pallas kernels: 118 us -> 107 us  [gather_first(): pl.pallas_call(functools.partial(gather_kernel, plan), in_specs=[VMEM_BLO...]
where the time goes in v10:
time: 907 us; the launch traced here: 901 us
  Pallas kernels  768 us (85%)
  other arithmetic  54.2 us (6%)
  local copies, waits for them, and re-layouts  45.6 us (5%)
  matrix products  27.1 us (3%)
    pallas_call x1, Pallas kernels, front_sums(): pl.pallas_call(functools.partial(front_sum_kernel, plan, rows), in_specs=...  154 us
    pallas_call x1, Pallas kernels, front_nexts(): pl.pallas_call(functools.partial(front_next_kernel, plan), in_specs=[VMEM...  139 us
    pallas_call x1, Pallas kernels, gather_first(): pl.pallas_call(functools.partial(gather_kernel, plan), in_specs=[VMEM_BLO...  107 us
    pallas_call x1, Pallas kernels, back_nexts(): pl.pallas_call(functools.partial(back_next_kernel, plan), in_specs=[VMEM_...  106 us
    pallas_call x1, Pallas kernels, back_sums(): pl.pallas_call(functools.partial(back_sum_kernel, plan, width), in_specs=...  102 us
    pallas_call x1, Pallas kernels, exchange_first(): pl.pallas_call(functools.partial(exchange_kernel, plan), in_specs=[VMEM_B...  62.7 us
    pallas_call x1, Pallas kernels, exchange_back(): pl.pallas_call(functools.partial(exchange_back_kernel, plan), in_specs=[V...  59.4 us
    pallas_call x1, Pallas kernels, attention(): pl.pallas_call(attention_kernel, grid=(length // block,), in_specs=[whole...  28.2 us
  transfers between devices with their start and end apart: 5, of which 0 were waited for; matrix products, arithmetic and copies ran while one was open for 5% of the time, Pallas kernels for 28%

profile of v10, /device:TPU:0, one launch (start us, length us, event | category | flops | bytes accessed | tf_op | source)
XLA Modules:
  0.0 901.1 jit_solution(3417327049357285167)
XLA Ops:
  9.5 106.8 %shard_map.324 = (bf16[4,2,128,2048]{3,2,1,0:T(8,128)(2,1)}, bf16[4,2,128,2048]{3,2,1,0:T(8,128)(2,1)}, f32[1,1024]{1,0:T(1,128)}, bf16[2048,1792]{1,0:T(8,128)(2,1)}, bf16[256,2048]{1,0:T(8,128)(2,1)}) custom-call(bf16[128,2048]{1,0:T(8,128)(2,1)} %bitcast.77, bf16[128,2048]{1,0:T(8,128)(2,1)} %bitcast.88, f32[1,1024]{1,0:T(1,128)} %convert_element_type.112.doc, ...), custom_call_target="tpu_custom_call" | custom-call | flops 117000003584 | tf_op jit(solution)/shard_map/pallas_call | solution.py:572
  120.9 2.0 fusion.26
  124.5 11.1 %shard_map.325 = (bf16[1024,2048]{1,0:T(8,128)(2,1)}, bf16[1024,1024]{1,0:T(8,128)(2,1)}) custom-call(bf16[1024,2048]{1,0:T(8,128)(2,1)} %bitcast.85, bf16[1024,2048]{1,0:T(8,128)(2,1)} %bitcast.82, bf16[2048,1792]{1,0:T(8,128)(2,1)} %get-tuple-element.45.weight, bf16[256,2048]{1,0:T(8,128)(2,1)} %get-tuple-element.46.back, f32[1,768]{1,0:T(1,128)} %bitcast.95, ...), custom_call_target="tpu_custom_call" | custom-call | flops 4294967296 | bytes 33554432 | tf_op jit(solution)/shard_map/pallas_call | solution.py:152
  135.6 62.7 %shard_map.326 = (bf16[4,256,1024]{2,1,0:T(8,128)(2,1)}, bf16[1024,2048]{1,0:T(8,128)(2,1)}, bf16[1024,1024]{1,0:T(8,128)(2,1)}, f32[1024,1024]{1,0:T(8,128)}) custom-call(bf16[4,256,1024]{2,1,0:T(8,128)(2,1)} %bitcast.97, bf16[1024,2048]{1,0:T(8,128)(2,1)} %get-tuple-element.48.normed, bf16[2048,1792]{1,0:T(8,128)(2,1)} %get-tuple-element.45.weight, ...), custom_call_target="tpu_custom_call" | custom-call | flops 44999999488 | tf_op jit(solution)/shard_map/pallas_call | solution.py:647
  198.3 28.2 %shard_map.327 = bf16[1024,1024]{1,0:T(8,128)(2,1)} custom-call(bf16[1024,1024]{1,0:T(8,128)(2,1)} %bitcast.98, s32[1024,1]{1,0:T(8,128)} %add.253.pos_q, s32[1,1024]{1,0:T(1,128)} %add.214.pos_k, s32[1024,1]{1,0:T(8,128)} %select_n.129.seg_q, s32[1,1024]{1,0:T(1,128)} %select_n.122.seg_k, f32[1024,128]{1,0:T(8,128)} %copy-done.17, f32[1024,128]{1,0:T(8,128)} %copy-done.16, ...), custom_call_target="tpu_custom_call" | custom-call | flops 3758096384 | bytes 5242880 | tf_op jit(solution)/shard_map/pallas_call | solution.py:235
  226.5 59.4 %shard_map.328 = (bf16[4,256,1024]{2,1,0:T(8,128)(2,1)}, bf16[1024,1024]{1,0:T(8,128)(2,1)}) custom-call(bf16[4,256,1024]{2,1,0:T(8,128)(2,1)} %bitcast.99, bf16[1024,2048]{1,0:T(8,128)(2,1)} %bitcast.83, bf16[1024,2048]{1,0:T(8,128)(2,1)} %get-tuple-element.51.rows, f32[1024,1024]{1,0:T(8,128)} %get-tuple-element.52.slope), custom_call_target="tpu_custom_call" | custom-call | flops 44999999488 | tf_op jit(solution)/shard_map/pallas_call | solution.py:688
  285.8 1.5 slice.76
  287.4 10.9 %fusion.44 = f32[1024,2048]{1,0:T(8,128)S(1)} fusion(bf16[2048,1792]{1,0:T(8,128)(2,1)} %get-tuple-element.45.weight, bf16[1024,1024]{1,0:T(8,128)(2,1)} %get-tuple-element.55, bf16[1024,768]{1,0:T(8,128)(2,1)S(1)} %slice.76), kind=kOutput, calls=%fused_computation.109 | convolution fusion | flops 7523532800 | bytes 19398656 | tf_op jit(solution)/shard_map/dot_general | solution.py:1353
  298.3 1.6 fusion.7
  299.9 3.1 slice.75
  303.0 5.6 fusion
  308.7 3.5 copy-done.7
  312.2 1.6 fusion.6
  313.8 2.1 pad_maximum_fusion.grad
  317.3 7.6 convolution_convert_fusion.src
  325.0 101.7 %shard_map.329 = (bf16[1280,512]{1,0:T(8,128)(2,1)}, bf16[2048,1792]{1,0:T(8,128)(2,1)}) custom-call(bf16[1280,2048]{1,0:T(8,128)(2,1)} %convolution_convert_fusion.src, bf16[1024,2048]{1,0:T(8,128)(2,1)} %get-tuple-element.48.normed, bf16[1024,1792]{1,0:T(8,128)(2,1)} %pad_maximum_fusion.grad), custom_call_target="tpu_custom_call" | custom-call | flops 80999997440 | tf_op jit(solution)/shard_map/pallas_call | solution.py:1061
  427.5 2.2 convolution_reduce_fusion
  433.2 3.4 bitcast_add_fusion
  436.7 4.9 bitcast_add_fusion.1
  443.9 1.5 collective-permute-start.3
  449.6 153.6 %shard_map.330 = (bf16[512,1792]{1,0:T(8,128)(2,1)}, bf16[1280,512]{1,0:T(8,128)(2,1)}) custom-call(bf16[2048,1792]{1,0:T(8,128)(2,1)} %get-tuple-element.56.src, bf16[1280,512]{1,0:T(8,128)(2,1)} %get-tuple-element.58.back), custom_call_target="tpu_custom_call" | custom-call | flops 108000002048 | tf_op jit(solution)/shard_map/pallas_call | solution.py:1091
  603.2 7.9 fusion.48
  612.6 1.5 convert_element_type.132
  614.0 1.5 convert_element_type.126
  615.5 3.4 fusion.22
  621.4 105.7 %shard_map.331 = (bf16[10240,512]{1,0:T(8,128)(2,1)}, bf16[256,3584]{1,0:T(8,128)(2,1)}) custom-call(bf16[1280,512]{1,0:T(8,128)(2,1)} %get-tuple-element.82.own, bf16[512,1792]{1,0:T(8,128)(2,1)} %get-tuple-element.65.src), custom_call_target="tpu_custom_call" | custom-call | flops 80999997440 | tf_op jit(solution)/shard_map/pallas_call | solution.py:1118
  727.8 10.8 %fusion.46 = (bf16[256,3584]{1,0:T(8,128)(2,1)}, f32[256,3584]{1,0:T(8,128)}, f32[256,3584]{1,0:T(8,128)}, f32[256,3584]{1,0:T(8,128)}, f32[256,3584]{1,0:T(8,128)}) fusion(f32[256,3584]{1,0:T(8,128)} %param.27, f32[]{:T(128)} %bitcast.25, f32[]{:T(128)} %bitcast.24, f32[]{:T(128)} %bitcast.26, f32[256,3584]{1,0:T(8,128)} %param.31, f32[256,3584]{1,0:T(8,128)} %param.29, ...), kind=kLoop, calls=%fused_computation.110 | loop fusion | flops 15597568 | bytes 29360140 | tf_op jit(solution)/shard_map/convert_element_type | solution.py:1402
  738.7 139.0 %shard_map.332 = (bf16[2048,3584]{1,0:T(8,128)(2,1)}, f32[160,128]{1,0:T(8,128)}) custom-call(bf16[256,3584]{1,0:T(8,128)(2,1)} %get-tuple-element.77.own, f32[160,128]{1,0:T(8,128)} %maximum_bitcast_fusion.vector), custom_call_target="tpu_custom_call" | custom-call | flops 108000002048 | tf_op jit(solution)/shard_map/pallas_call | solution.py:1202
  877.7 2.4 multiply_subtract_fusion.2
  880.3 1.6 fusion.30
  882.5 14.1 %copy.55 = bf16[2048,3584]{1,0:T(8,128)(2,1)} copy(bf16[2048,3584]{1,0:T(8,128)(2,1)} %get-tuple-element.142) | data formatting | bytes 29360128
  896.6 4.1 copy.56
  (143 shorter events, 31.6 us)
Async XLA Ops:
  9.5 111.4 %copy-start.32 = (f32[128]{0:T(128)S(1)}, f32[128]{0:T(128)}, u32[]{:S(2)}) copy-start(f32[128]{0:T(128)} %constant.173) | copy-start | bytes 1540
  9.5 111.4 %copy-start.33 = (pred[128]{0:T(512)(128)(4,1)S(1)}, pred[128]{0:T(512)(128)(4,1)}, u32[]{:S(2)}) copy-start(pred[128]{0:T(512)(128)(4,1)} %constant.168.clone) | copy-start | bytes 388
  9.5 111.4 %copy-start.34 = (pred[128]{0:T(512)(128)(4,1)S(1)}, pred[128]{0:T(512)(128)(4,1)}, u32[]{:S(2)}) copy-start(pred[128]{0:T(512)(128)(4,1)} %constant.167.clone) | copy-start | bytes 388
  122.9 12.7 %copy-start.15 = (f32[1024,128]{1,0:T(8,128)}, f32[1024,128]{1,0:T(8,128)S(1)}, u32[]{:S(2)}) copy-start(f32[1024,128]{1,0:T(8,128)S(1)} %get-tuple-element.100.from_below) | copy-start | bytes 1572868
  122.9 12.7 %copy-start.16 = (f32[1024,128]{1,0:T(8,128)}, f32[1024,128]{1,0:T(8,128)S(1)}, u32[]{:S(2)}) copy-start(f32[1024,128]{1,0:T(8,128)S(1)} %get-tuple-element.101.from_above) | copy-start | bytes 1572868
  287.4 15.6 %copy-start.38 = (bf16[1024,2048]{1,0:T(8,128)(2,1)S(1)}, bf16[1024,2048]{1,0:T(8,128)(2,1)}, u32[]{:S(2)}) copy-start(bf16[1024,2048]{1,0:T(8,128)(2,1)} %get-tuple-element.51.rows) | copy-start | bytes 12582916
  299.9 133.3 %collective-permute-start.1 = (bf16[4,128,2048]{2,1,0:T(8,128)(2,1)}, bf16[4,128,2048]{2,1,0:T(8,128)(2,1)}, u32[]{:S(2)}, u32[]{:S(2)}) collective-permute-start(bf16[4,128,2048]{2,1,0:T(8,128)(2,1)} %fusion.7), channel_id=1, source_target_pairs={{0,4},{4,0},{8,12},{12,8},{16,20},{20,16},{24,28},{28,24},{1,5},{5... | collective-permute-start | bytes 6291464 | tf_op jit(solution)/shard_map/ppermute | solution.py:1286
  313.8 122.9 %collective-permute-start = (bf16[4,128,2048]{2,1,0:T(8,128)(2,1)}, bf16[4,128,2048]{2,1,0:T(8,128)(2,1)}, u32[]{:S(2)}, u32[]{:S(2)}) collective-permute-start(bf16[4,128,2048]{2,1,0:T(8,128)(2,1)} %fusion.6), channel_id=1, source_target_pairs={{0,4},{4,0},{8,12},{12,8},{16,20},{20,16},{24,28},{28,24},{1,5},{5... | collective-permute-start | bytes 6291464 | tf_op jit(solution)/shard_map/ppermute | solution.py:1286
  432.1 186.8 %copy-start.28 = (f32[128]{0:T(128)}, f32[128]{0:T(128)S(1)}, u32[]{:S(2)}) copy-start(f32[128]{0:T(128)S(1)} %broadcast_multiply_fusion.2) | copy-start | bytes 1540
  432.4 186.5 %copy-start.30 = (f32[128]{0:T(128)}, f32[128]{0:T(128)S(1)}, u32[]{:S(2)}) copy-start(f32[128]{0:T(128)S(1)} %add_rsqrt_fusion) | copy-start | bytes 1540
  443.9 167.1 %collective-permute-start.3 = (bf16[2,128,2048]{2,1,0:T(8,128)(2,1)}, bf16[2,128,2048]{2,1,0:T(8,128)(2,1)}, u32[]{:S(2)}, u32[]{:S(2)}) collective-permute-start(bf16[2,128,2048]{2,1,0:T(8,128)(2,1)} %pad_maximum_fusion.5), channel_id=1, source_target_pairs={{0,2},{1,3},{2,0},{3,1},{4,6},{5,7},{6,4},{7,5},{8,10},{9,11},{10,... | collective-permute-start | bytes 3145736 | tf_op jit(solution)/shard_map/ppermute | solution.py:1289
  446.5 166.0 %collective-permute-start.4 = (bf16[2,128,2048]{2,1,0:T(8,128)(2,1)}, bf16[2,128,2048]{2,1,0:T(8,128)(2,1)}, u32[]{:S(2)}, u32[]{:S(2)}) collective-permute-start(bf16[2,128,2048]{2,1,0:T(8,128)(2,1)} %pad_maximum_fusion.6), channel_id=1, source_target_pairs={{0,3},{1,2},{2,1},{3,0},{4,7},{5,6},{6,5},{7,4},{8,11},{9,10},{10,... | collective-permute-start | bytes 3145736 | tf_op jit(solution)/shard_map/ppermute | solution.py:1289
  449.0 165.0 %collective-permute-start.2 = (bf16[2,128,2048]{2,1,0:T(8,128)(2,1)}, bf16[2,128,2048]{2,1,0:T(8,128)(2,1)}, u32[]{:S(2)}, u32[]{:S(2)}) collective-permute-start(bf16[2,128,2048]{2,1,0:T(8,128)(2,1)} %pad_maximum_fusion.4), channel_id=1, source_target_pairs={{0,1},{1,0},{2,3},{3,2},{4,5},{5,4},{6,7},{7,6},{8,9},{9,8},{10,11... | collective-permute-start | bytes 3145736 | tf_op jit(solution)/shard_map/ppermute | solution.py:1289
  449.6 153.6 %copy-start.10 = (f32[1280,512]{1,0:T(8,128)S(1)}, f32[1280,512]{1,0:T(8,128)}, u32[]{:S(2)}) copy-start(f32[1280,512]{1,0:T(8,128)} %param.28) | copy-start | bytes 7864324
  621.4 105.7 %copy-start.20 = (f32[7,2,8,128]{3,1,2,0:T(2,128)S(1)}, f32[7,2,8,128]{3,1,2,0:T(2,128)}, u32[]{:S(2)}) copy-start(f32[7,2,8,128]{3,1,2,0:T(2,128)} %copy.49) | copy-start | bytes 172036
  621.4 105.7 %copy-start.25 = (f32[1,2048]{1,0:T(1,128)S(1)}, f32[1,2048]{1,0:T(1,128)}, u32[]{:S(2)}) copy-start(f32[1,2048]{1,0:T(1,128)} %fusion.37) | copy-start | bytes 24580
  738.6 139.1 %copy-start.18 = (f32[20480]{0:T(1024)S(1)}, f32[20480]{0:T(1024)}, u32[]{:S(2)}) copy-start(f32[20480]{0:T(1024)} %param.33) | copy-start | bytes 245764
  738.6 139.1 %copy-start.23 = (f32[20480]{0:T(1024)S(1)}, f32[20480]{0:T(1024)}, u32[]{:S(2)}) copy-start(f32[20480]{0:T(1024)} %param.35) | copy-start | bytes 245764
  738.6 139.1 %copy-start.24 = (f32[20480]{0:T(1024)S(1)}, f32[20480]{0:T(1024)}, u32[]{:S(2)}) copy-start(f32[20480]{0:T(1024)} %param.34) | copy-start | bytes 245764
  738.6 141.6 %copy-start.3 = (f32[128,2048]{1,0:T(8,128)S(1)}, f32[128,2048]{1,0:T(8,128)}, u32[]{:S(2)}) copy-start(f32[128,2048]{1,0:T(8,128)} %copy-done.2) | copy-start | bytes 3145732
  738.6 141.6 %copy-start.5 = (bf16[1,128,2048]{2,1,0:T(8,128)(2,1)S(1)}, bf16[1,128,2048]{2,1,0:T(8,128)(2,1)}, u32[]{:S(2)}) copy-start(bf16[1,128,2048]{2,1,0:T(8,128)(2,1)} %param.21) | copy-start | bytes 1572868
  738.6 141.6 %copy-start.9 = (f32[128,2048]{1,0:T(8,128)S(1)}, f32[128,2048]{1,0:T(8,128)}, u32[]{:S(2)}) copy-start(f32[128,2048]{1,0:T(8,128)} %get-tuple-element.62) | copy-start | bytes 3145732
  738.6 141.6 %copy-start.13 = (bf16[1,128,2048]{2,1,0:T(8,128)(2,1)S(1)}, bf16[1,128,2048]{2,1,0:T(8,128)(2,1)}, u32[]{:S(2)}) copy-start(bf16[1,128,2048]{2,1,0:T(8,128)(2,1)} %param.22) | copy-start | bytes 1572868
  738.6 141.6 %copy-start.22 = (f32[2048]{0:T(1024)S(1)}, f32[2048]{0:T(1024)}, u32[]{:S(2)}) copy-start(f32[2048]{0:T(1024)} %get-tuple-element.99) | copy-start | bytes 24580
  738.6 141.6 %copy-start.26 = (f32[2048]{0:T(1024)S(1)}, f32[2048]{0:T(1024)}, u32[]{:S(2)}) copy-start(f32[2048]{0:T(1024)} %get-tuple-element.97) | copy-start | bytes 24580
  738.6 141.6 %copy-start.29 = (f32[128]{0:T(128)S(1)}, f32[128]{0:T(128)}, u32[]{:S(2)}) copy-start(f32[128]{0:T(128)} %copy-done.28) | copy-start | bytes 1540
  738.7 141.6 %copy-start.31 = (f32[128]{0:T(128)S(1)}, f32[128]{0:T(128)}, u32[]{:S(2)}) copy-start(f32[128]{0:T(128)} %copy-done.30) | copy-start | bytes 1540
  738.7 141.6 %copy-start.35 = (f32[128]{0:T(128)S(1)}, f32[128]{0:T(128)}, u32[]{:S(2)}) copy-start(f32[128]{0:T(128)} %broadcast_multiply_fusion) | copy-start | bytes 1540
  738.7 141.6 %copy-start.36 = (f32[128]{0:T(128)S(1)}, f32[128]{0:T(128)}, u32[]{:S(2)}) copy-start(f32[128]{0:T(128)} %broadcast_multiply_fusion.1) | copy-start | bytes 1540
  877.7 18.8 %slice-start = ((s8[10485760]{0:T(1024)(128)(4,1)}), s8[4194304]{0:T(1024)(128)(4,1)S(1)}, s32[]{:S(2)}) async-start(s8[10485760]{0:T(1024)(128)(4,1)} %bitcast.75), calls=%async_computation | async-start | bytes 8388608
  882.5 14.1 %slice-start.1 = ((s8[10485760]{0:T(1024)(128)(4,1)}), s8[4194304]{0:T(1024)(128)(4,1)S(1)}, s32[]{:S(2)}) async-start(s8[10485760]{0:T(1024)(128)(4,1)} %bitcast.75), calls=%async_computation.1 | async-start | bytes 8388608
  882.5 14.1 %slice-start.2 = ((s8[10485760]{0:T(1024)(128)(4,1)}), s8[2097152]{0:T(1024)(128)(4,1)S(1)}, s32[]{:S(2)}) async-start(s8[10485760]{0:T(1024)(128)(4,1)} %bitcast.75), calls=%async_computation.2 | async-start | bytes 4194304
  (15 other events, 77.5 us)
